TPU v7x, 32 devices: a whole 2x2x4 slice. The times are simulated.
32 devices in a mesh: axial: 16 (over z, x, core), azim: 2 (over y).
Axes of the slice: x: 2, y: 2, z: 4, core: 2. Of those that a mesh axis runs over, the one named last changes fastest.
Arguments:
- velocity: float32 [3, 8, 8, 8, 16, 2, 128], P(None, None, None, None, 'axial', 'azim'), may hold values from -6 to 6
- diffusivity: float32 [8, 8, 8, 16, 2, 128], P(None, None, None, 'axial', 'azim'), may hold values from 1 to 10
- coarse_factor: float32 [32, 32], P(('axial', 'azim')), may hold values from -0.0625 to 0.0625
Outputs:
- pressure: float32 [8, 8, 8, 16, 2, 128], P(None, None, None, 'axial', 'azim')
- residual: float32 [8, 8, 8, 16, 2, 128], P(None, None, None, 'axial', 'azim')
- direction: float32 [8, 8, 8, 16, 2, 128], P(None, None, None, 'axial', 'azim')
All inputs are finite; a program needn't handle non-finite values.
Results may differ from a plain program's by a relative error of at most 0.02.
Values sent between devices are 32-bit elements; how exact they have to be, the bound alone decides.
No kernel may reach another device: no remote copies, remote signals or barrier semaphores. Data moves between devices by JAX's collectives and lax.ppermute only.
A program may use at most 128 MiB of HBM per device.

v0:
```python
import math

import jax
import jax.numpy as jnp
import numpy as np
from jax import lax
from jax.experimental import pallas as pl
from jax.experimental.pallas import tpu as pltpu
from jax.sharding import PartitionSpec as P

ALL = ("axial", "azim")
time_increment = 0.02
mass_shift = 0.05
VMEM_GRANT = 20 << 20
gll_points = [
    -1.0,
    -0.8717401485096066,
    -0.5917001814331423,
    -0.20929921790247888,
    0.20929921790247888,
    0.5917001814331423,
    0.8717401485096066,
    1.0,
]


def legendre_value(order, point):
    before = 1.0
    current = point
    for step_idx in range(1, order):
        after = ((2 * step_idx + 1) * point * current - step_idx * before) / (step_idx + 1)
        before = current
        current = after
    return current


def jacobi_eigen(matrix):
    size_n = len(matrix)
    work = [list(row) for row in matrix]
    vectors = [
        [1.0 if row_idx == col_idx else 0.0 for col_idx in range(size_n)]
        for row_idx in range(size_n)
    ]
    for sweep_idx in range(15):
        for row_idx in range(size_n):
            for col_idx in range(row_idx + 1, size_n):
                off_value = work[row_idx][col_idx]
                if off_value != 0.0:
                    theta = (work[col_idx][col_idx] - work[row_idx][row_idx]) / (2.0 * off_value)
                    root_val = math.sqrt(theta * theta + 1.0)
                    tangent = 1.0 / (theta + root_val) if theta >= 0.0 else 1.0 / (theta - root_val)
                    cosine = 1.0 / math.sqrt(tangent * tangent + 1.0)
                    sine = tangent * cosine
                    for other in range(size_n):
                        left_val = work[other][row_idx]
                        right_val = work[other][col_idx]
                        work[other][row_idx] = cosine * left_val - sine * right_val
                        work[other][col_idx] = sine * left_val + cosine * right_val
                    for other in range(size_n):
                        left_val = work[row_idx][other]
                        right_val = work[col_idx][other]
                        work[row_idx][other] = cosine * left_val - sine * right_val
                        work[col_idx][other] = sine * left_val + cosine * right_val
                    for other in range(size_n):
                        left_val = vectors[other][row_idx]
                        right_val = vectors[other][col_idx]
                        vectors[other][row_idx] = cosine * left_val - sine * right_val
                        vectors[other][col_idx] = sine * left_val + cosine * right_val
    return ([work[row_idx][row_idx] for row_idx in range(size_n)], vectors)


def gll_tables():
    degree = 7
    points = degree + 1
    legendre_at = [legendre_value(degree, node_val) for node_val in gll_points]
    weights = [2.0 / (degree * (degree + 1) * value * value) for value in legendre_at]
    derivative = [[0.0] * points for row_idx in range(points)]
    for row_idx in range(points):
        for col_idx in range(points):
            if row_idx != col_idx:
                derivative[row_idx][col_idx] = legendre_at[row_idx] / (
                    legendre_at[col_idx] * (gll_points[row_idx] - gll_points[col_idx])
                )
    derivative[0][0] = -degree * (degree + 1) / 4.0
    derivative[degree][degree] = degree * (degree + 1) / 4.0
    stiffness = [
        [
            sum(
                (
                    derivative[mid_idx][row_idx] * weights[mid_idx] * derivative[mid_idx][col_idx]
                    for mid_idx in range(points)
                )
            )
            for col_idx in range(points)
        ]
        for row_idx in range(points)
    ]
    line_len = 3 * degree + 1
    big_stiff = [[0.0] * line_len for row_idx in range(line_len)]
    big_mass = [0.0] * line_len
    for element in range(3):
        offset = element * degree
        for row_idx in range(points):
            big_mass[offset + row_idx] += weights[row_idx]
            for col_idx in range(points):
                big_stiff[offset + row_idx][offset + col_idx] += stiffness[row_idx][col_idx]
    start_node = degree - 1
    box_len = degree + 3
    scaling = [1.0 / math.sqrt(big_mass[start_node + row_idx]) for row_idx in range(box_len)]
    symmetric = [
        [
            scaling[row_idx]
            * big_stiff[start_node + row_idx][start_node + col_idx]
            * scaling[col_idx]
            for col_idx in range(box_len)
        ]
        for row_idx in range(box_len)
    ]
    eigval, eigvec = jacobi_eigen(symmetric)
    fdm_basis = [
        [scaling[row_idx] * eigvec[row_idx][col_idx] for col_idx in range(box_len)]
        for row_idx in range(box_len)
    ]
    return (weights, derivative, fdm_basis, eigval)

WEIGHTS, DERIV, BASIS, EIGVAL = (np.asarray(t, np.float64) for t in gll_tables())


def f32(table):
    return jnp.asarray(table, jnp.float32)


F32 = jnp.float32
BF16 = jnp.bfloat16
LANES = 128
INTERPRET = False


def split_terms(table, depth):
    padded = np.zeros((table.shape[0], depth))
    padded[:, : table.shape[1]] = table
    high = padded.astype(jnp.bfloat16)
    low = (padded - high.astype(np.float64)).astype(jnp.bfloat16)
    return jnp.asarray(np.concatenate([high, high, low], axis=1))


def box_tables():
    pairs = [(b + 1, c + 1) for b in range(8) for c in range(8)]
    pairs += [(b + 1, {6: 0, 1: 9}.get(c)) for b in range(8) for c in range(8)]
    pairs += [(0, c + 1) for c in range(8)] + [(9, c + 1) for c in range(8)]
    table = np.zeros((144, 112))
    for row, (b, c) in enumerate(pairs):
        if c is not None:
            table[row, :100] = np.outer(BASIS[b], BASIS[c]).reshape(100)
    sums = np.ones(112)
    sums[:100] = (EIGVAL[:, None] + EIGVAL[None, :]).reshape(100)
    return table, sums


EYE = np.eye(8)
GRAD = np.concatenate([np.kron(DERIV, EYE), np.kron(EYE, DERIV)])
BOX_ROWS, SPECTRUM = box_tables()
EVEN = [bool(abs(BASIS[0, i] - BASIS[9, i]) < abs(BASIS[0, i] + BASIS[9, i])) for i in range(10)]


def constant_tables(radial):
    plane = (WEIGHTS[:, None] * WEIGHTS[None, :]).reshape(64, 1)
    mult_r = np.ones((8, radial))
    mult_r[0, 1:] = 2.0
    mult_r[7, :-1] = 2.0
    ends = np.array([2.0, 1, 1, 1, 1, 1, 1, 2.0])
    mult = (ends[:, None, None] * mult_r[None]).reshape(64, radial)
    return dict(
        plane=f32(np.broadcast_to(plane, (64, radial))),
        over=f32(1.0 / mult),
        spectrum=f32(np.broadcast_to(SPECTRUM[:, None], (112, radial))),
        grad=split_terms(GRAD, 64),
        div=split_terms(GRAD.T, 128),
        into=split_terms(BOX_ROWS.T, 144),
        outof=split_terms(BOX_ROWS, 112),
    )


def product(table_ref, values):
    high = values.astype(BF16)
    low = (values - high.astype(F32)).astype(BF16)
    return jnp.dot(
        table_ref[...], jnp.concatenate([high, low, high], axis=0), preferred_element_type=F32
    )


def combine(coefs, terms):
    total = None
    for coef, term in zip(coefs, terms):
        scaled = float(coef) * term
        total = scaled if total is None else total + scaled
    return total


def skew_apply(matrix, parts):
    plus = [parts[b] + parts[7 - b] for b in range(4)]
    minus = [parts[b] - parts[7 - b] for b in range(4)]
    result = [None] * 8
    for a in range(4):
        even = combine([0.5 * (matrix[a, b] + matrix[a, 7 - b]) for b in range(4)], plus)
        odd = combine([0.5 * (matrix[a, b] - matrix[a, 7 - b]) for b in range(4)], minus)
        result[a] = even + odd
        result[7 - a] = odd - even
    return result


def to_spectral(parts):
    plus = [parts[a] + parts[9 - a] for a in range(5)]
    minus = [parts[a] - parts[9 - a] for a in range(5)]
    return [combine(BASIS[:5, i], plus if EVEN[i] else minus) for i in range(10)]


def from_spectral(parts):
    evens = [i for i in range(10) if EVEN[i]]
    odds = [i for i in range(10) if not EVEN[i]]
    result = [None] * 10
    for a in range(5):
        even = combine(BASIS[a, evens], [parts[i] for i in evens])
        odd = combine(BASIS[a, odds], [parts[i] for i in odds])
        result[a] = even + odd
        result[9 - a] = even - odd
    return result


def masks(rows):
    layer = lax.broadcasted_iota(jnp.int32, (rows, LANES), 0) % 8
    elem = lax.broadcasted_iota(jnp.int32, (rows, LANES), 1)
    return layer, elem > 0, elem < LANES - 1


def spread(values, first, last):
    layer, has_before, has_after = masks(values.shape[0])
    before = pltpu.roll(values, 1, axis=1)
    after = pltpu.roll(values, LANES - 1, axis=1)
    return jnp.where(
        (layer == first) & has_before,
        before,
        jnp.where((layer == last) & has_after, after, 0.0),
    )


def radial_sum(values):
    rows = values.shape[0]
    layer, _, _ = masks(rows)
    cubes = values.reshape(rows // 8, 8, LANES)
    up = pltpu.roll(cubes, 1, axis=1).reshape(rows, LANES)
    down = pltpu.roll(cubes, 7, axis=1).reshape(rows, LANES)
    return values + spread(jnp.where(layer == 0, up, down), 0, 7)


def total(values):
    return jnp.sum(values, axis=(0, 1), keepdims=True)


def add_rows(block, extra):
    pieces = []
    for b in range(8):
        piece = block[8 * b : 8 * b + 8]
        pieces.append(piece + extra[b] if b in extra else piece)
    return jnp.concatenate(pieces, axis=0)


def is_even():
    return lax.axis_index("axial") % 2 == 0


def send_axial(inner_ref, outer_ref, low, high):
    even = is_even()
    row = 0
    for low_piece, high_piece in zip(low, high):
        size = low_piece.shape[0]
        inner_ref[row : row + size] = jnp.where(even, high_piece, low_piece)
        outer_ref[row : row + size] = jnp.where(even, low_piece, high_piece)
        row += size


def got_axial(inner_ref, outer_ref):
    even = is_even()

    def before(start, size):
        return jnp.where(even, outer_ref[start : start + size], inner_ref[start : start + size])

    def after(start, size):
        return jnp.where(even, inner_ref[start : start + size], outer_ref[start : start + size])

    return before, after


def conv_kernel(u_ref, diff_ref, row_ref, plane_ref, grad_ref, conv_ref, kbar_ref, in_ref, out_ref, az_ref):
    plane = plane_ref[...]
    fields = [[u_ref[d, a] for a in range(8)] for d in range(3)]
    low, high = [], []
    for comp in range(3):
        parts = fields[comp]
        flat = product(grad_ref, jnp.concatenate(parts, axis=1))
        along_a = skew_apply(DERIV, parts)
        for a in range(8):
            cols = slice(LANES * a, LANES * a + LANES)
            value = (
                fields[0][a] * along_a[a]
                + fields[1][a] * flat[:64, cols]
                + fields[2][a] * flat[64:, cols]
            )
            value = radial_sum(float(WEIGHTS[a]) * plane * value)
            conv_ref[comp, a] = value
            start = 64 * comp + 8 * a
            az_ref[0, start : start + 8] = value[:8]
            az_ref[1, start : start + 8] = value[56:]
            if a == 0:
                low.append(value)
            if a == 7:
                high.append(value)
    row = row_ref[...]
    send_axial(in_ref, out_ref, low + [row], high + [row])
    mean = diff_ref[0]
    for a in range(1, 8):
        mean = mean + diff_ref[a]
    mean = jnp.sum(mean, axis=0, keepdims=True) * (1.0 / 512.0)
    kbar_ref[...] = jnp.broadcast_to(mean, (8, LANES))


def conv_side_kernel(in_ref, out_ref, az_ref, row_ref, send_ref):
    before, after = got_axial(in_ref, out_ref)
    count = row_ref.shape[0]
    for side, b in ((0, 0), (1, 7)):
        for comp in range(3):
            start = 64 * comp
            send_ref[side, start : start + 8] = az_ref[side, start : start + 8] + before(start + 8 * b, 8)
            send_ref[side, start + 8 : start + 56] = az_ref[side, start + 8 : start + 56]
            send_ref[side, start + 56 : start + 64] = az_ref[side, start + 56 : start + 64] + after(start + 8 * b, 8)
        for place, rows in enumerate((before(192, count), row_ref[...], after(192, count))):
            start = 192 + place * count
            send_ref[side, start : start + count] = rows


def coarse_share(raw, near_ref):
    middle = raw[1]
    for a in range(2, 7):
        middle = middle + raw[a]
    per_axial = (0.5 * raw[0], middle + 0.5 * (raw[0] + raw[7]), 0.5 * raw[7])
    rows = []
    for part in per_axial:
        inner = part[8:16]
        for b in range(2, 7):
            inner = inner + part[8 * b : 8 * b + 8]
        ends = (part[:8], part[56:])
        for piece in (0.5 * ends[0], inner + 0.5 * (ends[0] + ends[1]), 0.5 * ends[1]):
            rows.append(jnp.sum(piece, axis=0, keepdims=True))
    rows = jnp.concatenate(rows + [jnp.zeros((7, LANES), F32)], axis=0)
    shares = jnp.sum(rows, axis=1, keepdims=True)
    return jnp.sum(shares * near_ref[...], axis=0, keepdims=True)


def send_sums(pay_ref, row, scalars):
    width = pay_ref.shape[1]
    place = lax.broadcasted_iota(jnp.int32, (1, width), 1)
    for k, value in enumerate(scalars):
        row = jnp.where(place == width - 1 - k, value, row)
    pay_ref[...] = jnp.broadcast_to(row, pay_ref.shape)


def got_sums(ref, scalars):
    row = jnp.sum(ref[...], axis=0, keepdims=True)
    width = row.shape[1]
    place = lax.broadcasted_iota(jnp.int32, (1, width), 1)
    values = [
        jnp.sum(jnp.where(place == width - 1 - k, row, 0.0), axis=1, keepdims=True)
        for k in range(scalars)
    ]
    return jnp.where(place >= width - 4, 0.0, row), values


def send_raw(raw, g_ref, in_ref, out_ref, az_ref):
    parts = [radial_sum(raw[a]) for a in range(8)]
    for a in range(8):
        g_ref[a] = parts[a]
        for side, (edge, inner) in enumerate(((0, 1), (7, 6))):
            az_ref[side, 8 + 8 * a : 16 + 8 * a] = parts[a][8 * edge : 8 * edge + 8]
            az_ref[side, 80 + 8 * a : 88 + 8 * a] = parts[a][8 * inner : 8 * inner + 8]
    zero = jnp.zeros((8, LANES), F32)
    for side in range(2):
        az_ref[side, :8] = zero
        az_ref[side, 72:80] = zero
    send_axial(in_ref, out_ref, [parts[0], parts[1]], [parts[7], parts[6]])


def raw_side_kernel(in_ref, out_ref, az_ref, send_ref):
    before, after = got_axial(in_ref, out_ref)
    for side, (edge, inner) in enumerate(((0, 1), (7, 6))):
        send_ref[side, :8] = before(64 + 8 * edge, 8)
        send_ref[side, 8:16] = az_ref[side, 8:16] + before(8 * edge, 8)
        send_ref[side, 16:64] = az_ref[side, 16:64]
        send_ref[side, 64:72] = az_ref[side, 64:72] + after(8 * edge, 8)
        send_ref[side, 72:80] = after(64 + 8 * edge, 8)
        send_ref[side, 80:88] = az_ref[side, 80:88] + before(8 * inner, 8)
        send_ref[side, 88:136] = az_ref[side, 88:136]
        send_ref[side, 136:144] = az_ref[side, 136:144] + after(8 * inner, 8)


def divergence_kernel(
    conv_ref, u_ref, in_ref, out_ref, az_ref, row_ref, plane_ref, over_ref, div_ref,
    g_ref, send_in_ref, send_out_ref, send_az_ref, near_ref, pay_ref,
):
    before, after = got_axial(in_ref, out_ref)
    plane, over = plane_ref[...], over_ref[...]
    moved = []
    for comp in range(3):
        parts = []
        for a in range(8):
            value = conv_ref[comp, a]
            if a == 0:
                value = value + before(64 * comp, 64)
            if a == 7:
                value = value + after(64 * comp, 64)
            start = 64 * comp + 8 * a
            value = add_rows(value, {0: az_ref[1, start : start + 8], 7: az_ref[0, start : start + 8]})
            scale = time_increment * (0.5 if a in (0, 7) else 1.0)
            parts.append(float(WEIGHTS[a]) * plane * u_ref[comp, a] - scale * over * value)
        moved.append(parts)
    flat = product(
        div_ref,
        jnp.concatenate([jnp.concatenate(moved[1], axis=1), jnp.concatenate(moved[2], axis=1)], axis=0),
    )
    along_a = skew_apply(DERIV.T, moved[0])
    raw = [along_a[a] + flat[:, LANES * a : LANES * a + LANES] for a in range(8)]
    send_raw(raw, g_ref, send_in_ref, send_out_ref, send_az_ref)
    count = (az_ref.shape[1] - 192) // 3
    width = near_ref.shape[1] // LANES
    near_ref[...] = jnp.zeros(near_ref.shape, F32)
    for i in range(3):
        start = 192 + i * count
        middle = (before(192, count), row_ref[...], after(192, count))[i]
        sides = (az_ref[1, start : start + count], middle, az_ref[0, start : start + count])
        for j, rows in enumerate(sides):
            for k in range(width):
                near_ref[3 * i + j : 3 * i + j + 1, LANES * k : LANES * k + LANES] = rows[k : k + 1]
    send_sums(pay_ref, coarse_share(raw, near_ref), [])


def got_box(g_ref, in_ref, out_ref, az_ref):
    before, after = got_axial(in_ref, out_ref)
    center = []
    for a in range(8):
        value = g_ref[a]
        if a == 0:
            value = value + before(0, 64)
        if a == 7:
            value = value + after(0, 64)
        start = 8 + 8 * a
        center.append(
            add_rows(value, {0: az_ref[1, start : start + 8], 7: az_ref[0, start : start + 8]})
        )
    outer_a = [
        add_rows(before(64, 64), {0: az_ref[1, :8], 7: az_ref[0, :8]}),
        add_rows(after(64, 64), {0: az_ref[1, 72:80], 7: az_ref[0, 72:80]}),
    ]
    outer_b = [
        jnp.concatenate(
            [az_ref[1, 80 + 8 * a : 88 + 8 * a], az_ref[0, 80 + 8 * a : 88 + 8 * a]], axis=0
        )
        for a in range(8)
    ]
    return center, outer_a, outer_b


def put_box(box, center_ref, outer_a_ref, outer_b_ref):
    center, outer_a, outer_b = box
    for a in range(8):
        center_ref[a] = center[a]
        outer_b_ref[a] = outer_b[a]
    for k in range(2):
        outer_a_ref[k] = outer_a[k]


def take_box(center_ref, outer_a_ref, outer_b_ref):
    return (
        [center_ref[a] for a in range(8)],
        [outer_a_ref[k] for k in range(2)],
        [outer_b_ref[a] for a in range(8)],
    )


def add_box(first, scale, second):
    return tuple([x + scale * y for x, y in zip(xs, ys)] for xs, ys in zip(first, second))


def solve(box, kbar_ref, into_ref, outof_ref, spectrum_ref):
    center, outer_a, outer_b = box
    zero = jnp.zeros((80, LANES), F32)
    planes = [jnp.concatenate([outer_a[0], zero], axis=0)]
    for a in range(8):
        planes.append(jnp.concatenate([center[a], spread(center[a], 6, 1), outer_b[a]], axis=0))
    planes.append(jnp.concatenate([outer_a[1], zero], axis=0))
    rows = jnp.concatenate(planes, axis=1)
    flat = product(into_ref, rows)
    parts = to_spectral([flat[:, LANES * a : LANES * a + LANES] for a in range(10)])
    kbar = kbar_ref[0:1, :]
    plane_spectrum = kbar * spectrum_ref[...] + mass_shift
    parts = [parts[i] / (plane_spectrum + float(EIGVAL[i]) * kbar) for i in range(10)]
    parts = from_spectral(parts)
    flat = product(outof_ref, jnp.concatenate(parts, axis=1))
    solved = [flat[:, LANES * a : LANES * a + LANES] for a in range(10)]
    dot = None
    for a in range(10):
        stop = 64 if a in (0, 9) else 144
        term = planes[a][:stop] * solved[a][:stop]
        term = jnp.sum(term.reshape(stop // 8, 8, LANES), axis=0)
        dot = term if dot is None else dot + term
    return solved, dot


def send_solved(solved, part_ref, in_ref, out_ref, az_ref):
    outer_a = [radial_sum(solved[0][:64]), radial_sum(solved[9][:64])]
    edges = []
    for a in range(8):
        rows = solved[a + 1]
        value = radial_sum(rows[:64] + spread(rows[64:128], 1, 6))
        outer_b = radial_sum(rows[128:144])
        part_ref[a] = value
        az_ref[0, 8 * a : 8 * a + 8] = value[:8]
        az_ref[1, 8 * a : 8 * a + 8] = value[56:]
        az_ref[0, 64 + 8 * a : 72 + 8 * a] = outer_b[:8]
        az_ref[1, 64 + 8 * a : 72 + 8 * a] = outer_b[8:]
        if a in (0, 7):
            edges.append((value, outer_b))
    send_axial(
        in_ref,
        out_ref,
        [edges[0][0], outer_a[0], edges[0][1]],
        [edges[1][0], outer_a[1], edges[1][1]],
    )


def solved_side_kernel(in_ref, out_ref, az_ref, send_ref):
    before, after = got_axial(in_ref, out_ref)
    for side, b in ((0, 0), (1, 7)):
        row = 8 * b
        send_ref[side, :8] = az_ref[side, :8] + before(row, 8)
        send_ref[side, 8:16] = az_ref[side, 8:16] + before(64 + row, 8)
        send_ref[side, 16:48] = az_ref[side, 16:48]
        send_ref[side, 48:56] = az_ref[side, 48:56] + after(64 + row, 8)
        send_ref[side, 56:64] = az_ref[side, 56:64] + after(row, 8)
        send_ref[side, 64:72] = az_ref[side, 64:72] + before(128 + 8 * side, 8)
        send_ref[side, 72:120] = az_ref[side, 72:120]
        send_ref[side, 120:128] = az_ref[side, 120:128] + after(128 + 8 * side, 8)


def got_solved(part_ref, in_ref, out_ref, az_ref):
    before, after = got_axial(in_ref, out_ref)
    extra = {0: (before, 0), 1: (before, 64), 6: (after, 64), 7: (after, 0)}
    result = []
    for a in range(8):
        value = part_ref[a]
        if a in extra:
            side, start = extra[a]
            value = value + side(start, 64)
        rows = slice(8 * a, 8 * a + 8)
        faces = slice(64 + 8 * a, 72 + 8 * a)
        result.append(
            add_rows(
                value,
                {0: az_ref[1, rows], 1: az_ref[1, faces], 6: az_ref[0, faces], 7: az_ref[0, rows]},
            )
        )
    return result


def add_coarse(parts, row, near_ref):
    values = jnp.sum(near_ref[...] * row, axis=1, keepdims=True)
    own = [[values[3 * i + j : 3 * i + j + 1] for j in range(3)] for i in range(3)]
    b = lax.broadcasted_iota(jnp.int32, (64, LANES), 0) // 8
    fields = []
    for i in range(3):
        ends = [0.5 * (own[i][1] + own[i][j]) for j in (0, 2)]
        fields.append(jnp.where(b == 0, ends[0], jnp.where(b == 7, ends[1], own[i][1])))
    first, last = 0.5 * (fields[0] + fields[1]), 0.5 * (fields[1] + fields[2])
    return [
        parts[a] + (first if a == 0 else last if a == 7 else fields[1]) for a in range(8)
    ]


def apply_operator(values, diff_ref, plane_ref, grad_ref, div_ref):
    plane = plane_ref[...]
    coef = [float(WEIGHTS[a]) * plane * diff_ref[a] for a in range(8)]
    flat = product(grad_ref, jnp.concatenate(values, axis=1))
    along_a = skew_apply(DERIV, values)
    flux = jnp.concatenate(
        [
            jnp.concatenate([coef[a], coef[a]], axis=0) * flat[:, LANES * a : LANES * a + LANES]
            for a in range(8)
        ],
        axis=1,
    )
    flat = product(div_ref, flux)
    along_a = skew_apply(DERIV.T, [coef[a] * along_a[a] for a in range(8)])
    return [
        along_a[a]
        + flat[:, LANES * a : LANES * a + LANES]
        + (mass_shift * float(WEIGHTS[a])) * plane * values[a]
        for a in range(8)
    ]


def dot_parts(first, second):
    result = first[0] * second[0]
    for a in range(1, 8):
        result = result + first[a] * second[a]
    return total(result)


def norm(row):
    return jnp.sum(row * row, axis=1, keepdims=True)


def keep(ref, row, scalars):
    ref[0:1] = row
    for k, value in enumerate(scalars):
        ref[k + 1 : k + 2] = jnp.broadcast_to(value, row.shape)


def first_solve_kernel(
    g_ref, in_ref, out_ref, az_ref, kbar_ref, into_ref, outof_ref, spectrum_ref,
    center_ref, outer_a_ref, outer_b_ref, part_ref, send_in_ref, send_out_ref, send_az_ref, dot_ref,
):
    box = got_box(g_ref, in_ref, out_ref, az_ref)
    put_box(box, center_ref, outer_a_ref, outer_b_ref)
    solved, dot = solve(box, kbar_ref, into_ref, outof_ref, spectrum_ref)
    dot_ref[...] = dot
    send_solved(solved, part_ref, send_in_ref, send_out_ref, send_az_ref)


def second_solve_kernel(
    g_ref, in_ref, out_ref, az_ref, kbar_ref, into_ref, outof_ref, spectrum_ref,
    old_center_ref, old_a_ref, old_b_ref, sums_ref, state_ref,
    center_ref, outer_a_ref, outer_b_ref, q_center_ref, q_a_ref, q_b_ref,
    part_ref, send_in_ref, send_out_ref, send_az_ref, dot_ref, new_state_ref,
):
    row_q, (local_rz, curv) = got_sums(sums_ref, 2)
    row_r = state_ref[0:1]
    rz = local_rz + norm(row_r)
    alpha = rz / curv
    image = got_box(g_ref, in_ref, out_ref, az_ref)
    put_box(image, q_center_ref, q_a_ref, q_b_ref)
    box = add_box(take_box(old_center_ref, old_a_ref, old_b_ref), -alpha, image)
    put_box(box, center_ref, outer_a_ref, outer_b_ref)
    solved, dot = solve(box, kbar_ref, into_ref, outof_ref, spectrum_ref)
    dot_ref[...] = dot
    keep(new_state_ref, row_r - alpha * row_q, [rz, curv, alpha])
    new_state_ref[4:5] = row_q
    send_solved(solved, part_ref, send_in_ref, send_out_ref, send_az_ref)


def third_solve_kernel(
    g_ref, in_ref, out_ref, az_ref, kbar_ref, into_ref, outof_ref, spectrum_ref,
    old_center_ref, old_a_ref, old_b_ref, q_center_ref, q_a_ref, q_b_ref, sums_ref, state_ref,
    center_ref, part_ref, send_in_ref, send_out_ref, send_az_ref, new_state_ref, pay_ref,
):
    row_w, (local_rz, first_curv, cross) = got_sums(sums_ref, 3)
    row_r, row_q = state_ref[0:1], state_ref[4:5]
    rz_before, curv_before = state_ref[1:2, 0:1], state_ref[2:3, 0:1]
    rz = local_rz + norm(row_r)
    beta = rz / rz_before
    curv = first_curv + beta * (2.0 * cross + beta * curv_before)
    alpha = rz / curv
    image = got_box(g_ref, in_ref, out_ref, az_ref)
    image = add_box(image, beta, take_box(q_center_ref, q_a_ref, q_b_ref))
    box = add_box(take_box(old_center_ref, old_a_ref, old_b_ref), -alpha, image)
    for a in range(8):
        center_ref[a] = box[0][a]
    solved, dot = solve(box, kbar_ref, into_ref, outof_ref, spectrum_ref)
    keep(new_state_ref, row_r - alpha * (row_w + beta * row_q), [rz, beta, alpha])
    send_sums(pay_ref, jnp.zeros((1, pay_ref.shape[1]), F32), [total(dot)])
    send_solved(solved, part_ref, send_in_ref, send_out_ref, send_az_ref)


def first_apply_kernel(
    part_ref, in_ref, out_ref, az_ref, near_ref, diff_ref, plane_ref, grad_ref, div_ref,
    sums_ref, dot_ref,
    z_ref, raw_ref, g_ref, send_in_ref, send_out_ref, send_az_ref, state_ref, pay_ref,
):
    row, _ = got_sums(sums_ref, 0)
    values = add_coarse(got_solved(part_ref, in_ref, out_ref, az_ref), row, near_ref)
    raw = apply_operator(values, diff_ref, plane_ref, grad_ref, div_ref)
    for a in range(8):
        z_ref[a] = values[a]
        raw_ref[a] = raw[a]
    keep(state_ref, row, [])
    send_sums(pay_ref, coarse_share(raw, near_ref), [total(dot_ref[...]), dot_parts(values, raw)])
    send_raw(raw, g_ref, send_in_ref, send_out_ref, send_az_ref)


def second_apply_kernel(
    part_ref, in_ref, out_ref, az_ref, near_ref, diff_ref, plane_ref, grad_ref, div_ref,
    state_ref, dot_ref, old_raw_ref,
    z_ref, g_ref, send_in_ref, send_out_ref, send_az_ref, pay_ref,
):
    row = state_ref[0:1]
    values = add_coarse(got_solved(part_ref, in_ref, out_ref, az_ref), row, near_ref)
    raw = apply_operator(values, diff_ref, plane_ref, grad_ref, div_ref)
    for a in range(8):
        z_ref[a] = values[a]
    scalars = [
        total(dot_ref[...]),
        dot_parts(values, raw),
        dot_parts(values, [old_raw_ref[a] for a in range(8)]),
    ]
    send_sums(pay_ref, coarse_share(raw, near_ref), scalars)
    send_raw(raw, g_ref, send_in_ref, send_out_ref, send_az_ref)


def last_kernel(
    part_ref, in_ref, out_ref, az_ref, near_ref, sums_ref, state_ref, old_state_ref, z0_ref, z1_ref,
    pressure_ref, direction_ref,
):
    _, (local_rz,) = got_sums(sums_ref, 1)
    row = state_ref[0:1]
    rz_before, beta, alpha = (state_ref[k : k + 1, 0:1] for k in (1, 2, 3))
    alpha_before = old_state_ref[3:4, 0:1]
    ratio = (local_rz + norm(row)) / rz_before
    values = add_coarse(got_solved(part_ref, in_ref, out_ref, az_ref), row, near_ref)
    for a in range(8):
        first = z0_ref[a]
        second = z1_ref[a] + beta * first
        pressure_ref[a] = alpha_before * first + alpha * second
        direction_ref[a] = values[a] + ratio * second


def kernel_call(kernel, out_shapes, *args):
    outs = [jax.ShapeDtypeStruct(shape, F32) for shape in out_shapes]
    return pl.pallas_call(
        kernel,
        out_shape=outs,
        compiler_params=pltpu.CompilerParams(vmem_limit_bytes=VMEM_GRANT),
        interpret=INTERPRET,
    )(*args)


def axial_swap(inner_rows, outer_rows):
    count = lax.axis_size("axial")
    inner = [(i, i ^ 1) for i in range(count)]
    outer = [((2 * i + 1) % count, (2 * i + 2) % count) for i in range(count // 2)]
    outer = outer + [(b, a) for a, b in outer]
    from_outer = lax.ppermute(outer_rows, "axial", outer)
    from_inner = lax.ppermute(inner_rows, "axial", inner)
    return from_inner, from_outer


def azim_swap(sides):
    count = lax.axis_size("azim")
    if count == 2:
        return lax.ppermute(sides, "azim", [(0, 1), (1, 0)])
    after = lax.ppermute(sides[0], "azim", [((i + 1) % count, i) for i in range(count)])
    before = lax.ppermute(sides[1], "azim", [(i, (i + 1) % count) for i in range(count)])
    return jnp.stack([after, before])


def gather_sums(rows):
    return lax.all_to_all(rows, ALL, 0, 0, tiled=True)


def per_device(velocity, diffusivity, coarse_factor):
    shape = diffusivity.shape
    devices = lax.axis_size("axial") * lax.axis_size("azim")
    u = velocity.reshape(3, 8, 64, LANES)
    diff = diffusivity.reshape(8, 64, LANES)
    tables = constant_tables(LANES)
    plane, over, spectrum = tables["plane"], tables["over"], tables["spectrum"]
    grad, div, into, outof = tables["grad"], tables["div"], tables["into"], tables["outof"]
    coarse_size = coarse_factor.shape[1]
    width = -(-(coarse_size + 4) // LANES)
    count = 8 * -(-width // 8)
    row = jnp.pad(coarse_factor[0], (0, count * LANES - coarse_size)).reshape(count, LANES)

    field, sums, state = (8, 64, LANES), (devices, width * LANES), (8, width * LANES)
    box = [field, (2, 64, LANES), (8, 16, LANES)]
    raw_sends = [(128, LANES), (128, LANES), (2, 144, LANES)]
    solved_sends = [(144, LANES), (144, LANES), (2, 128, LANES)]

    conv, kbar, inner, outer, azim = kernel_call(
        conv_kernel,
        [(3,) + field, (8, LANES), (192 + count, LANES), (192 + count, LANES), (2, 192, LANES)],
        u, diff, row, plane, grad,
    )
    inner, outer = axial_swap(inner, outer)
    (azim,) = kernel_call(conv_side_kernel, [(2, 192 + 3 * count, LANES)], inner, outer, azim, row)
    azim = azim_swap(azim)
    g, send_in, send_out, send_az, near, pay = kernel_call(
        divergence_kernel,
        [field] + raw_sends + [(16, width * LANES), sums],
        conv, u, inner, outer, azim, row, plane, over, div,
    )

    def finish_raw(send_in, send_out, send_az, pay):
        inner, outer = axial_swap(send_in, send_out)
        pay = gather_sums(pay)
        (azim,) = kernel_call(raw_side_kernel, [(2, 144, LANES)], inner, outer, send_az)
        return inner, outer, azim_swap(azim), pay

    def finish_solved(send_in, send_out, send_az):
        inner, outer = axial_swap(send_in, send_out)
        (azim,) = kernel_call(solved_side_kernel, [(2, 128, LANES)], inner, outer, send_az)
        return inner, outer, azim_swap(azim)

    solver = (kbar, into, outof, spectrum)
    operator = (near, diff, plane, grad, div)
    inner, outer, azim, pay = finish_raw(send_in, send_out, send_az, pay)
    *old, part, send_in, send_out, send_az, dot = kernel_call(
        first_solve_kernel,
        box + [field] + solved_sends + [(8, LANES)],
        g, inner, outer, azim, *solver,
    )
    moved = finish_solved(send_in, send_out, send_az)
    z0, raw0, g, send_in, send_out, send_az, state0, pay = kernel_call(
        first_apply_kernel,
        [field, field, field] + raw_sends + [state, sums],
        part, *moved, *operator, pay, dot,
    )
    inner, outer, azim, pay = finish_raw(send_in, send_out, send_az, pay)
    *new, part, send_in, send_out, send_az, dot, state1 = kernel_call(
        second_solve_kernel,
        box + box + [field] + solved_sends + [(8, LANES), state],
        g, inner, outer, azim, *solver, *old, pay, state0,
    )
    moved = finish_solved(send_in, send_out, send_az)
    z1, g, send_in, send_out, send_az, pay = kernel_call(
        second_apply_kernel,
        [field, field] + raw_sends + [sums],
        part, *moved, *operator, state1, dot, raw0,
    )
    inner, outer, azim, pay = finish_raw(send_in, send_out, send_az, pay)
    residual, part, send_in, send_out, send_az, state2, pay = kernel_call(
        third_solve_kernel,
        [field, field] + solved_sends + [state, sums],
        g, inner, outer, azim, *solver, *new, pay, state1,
    )
    moved = finish_solved(send_in, send_out, send_az)
    pressure, direction = kernel_call(
        last_kernel, [field, field], part, *moved, near, gather_sums(pay), state2, state1, z0, z1
    )
    return pressure.reshape(shape), residual.reshape(shape), direction.reshape(shape)


def solution(mesh):
    split = P(None, None, None, "axial", "azim", None)
    in_specs = (P(None, None, None, None, "axial", "azim", None), split, P(ALL, None))
    return jax.shard_map(
        per_device, mesh=mesh, in_specs=in_specs, out_specs=(split, split, split), check_vma=False
    )
```

profile of v0, /device:TPU:0, one launch (start us, length us, event | category | flops | bytes accessed | tf_op | source)
XLA Modules:
  0.0 117.7 jit_solution(2912826112486293044)
XLA Ops:
  1.3 1.1 copy-done
  2.4 0.9 copy-done.2
  3.4 0.8 copy-done.6
  4.2 0.8 copy-done.8
  5.0 0.9 shard_map.121
  6.4 5.6 %collective-permute-start.1 = (f32[200,128]{1,0:T(8,128)S(1)}, f32[200,128]{1,0:T(8,128)S(1)}, u32[]{:S(2)}, u32[]{:S(2)}) collective-permute-start(f32[200,128]{1,0:T(8,128)S(1)} %get-tuple-element.59), channel_id=1, source_target_pairs={{2,4},{6,8},{10,12},{14,16},{18,20},{22,24},{26,28},{30,0},{4,2},{... | collective-permute-start | bytes 307208 | tf_op jit(solution)/shard_map/ppermute | solution.py:748
  12.1 2.3 %collective-permute-done.1.out_ref = f32[200,128]{1,0:T(8,128)S(1)} collective-permute-done((f32[200,128]{1,0:T(8,128)S(1)}, f32[200,128]{1,0:T(8,128)S(1)}, u32[]{:S(2)}, u32[]{:S(2)}) %collective-permute-start.1) | collective-permute-done | bytes 102432 | tf_op jit(solution)/shard_map/ppermute | solution.py:748
  14.4 1.6 %collective-permute-start.2 = (f32[2,216,128]{2,1,0:T(8,128)S(1)}, f32[2,216,128]{2,1,0:T(8,128)S(1)}, u32[]{:S(2)}, u32[]{:S(2)}) collective-permute-start(f32[2,216,128]{2,1,0:T(8,128)S(1)} %shard_map.122), channel_id=1, source_target_pairs={{0,1},{1,0},{2,3},{3,2},{4,5},{5,4},{6,7},{7,6},{8,9},{9,8},{10,11... | collective-permute-start | bytes 663560 | tf_op jit(solution)/shard_map/ppermute | solution.py:756
  16.0 4.4 %collective-permute-done.2.az_ref = f32[2,216,128]{2,1,0:T(8,128)S(1)} collective-permute-done((f32[2,216,128]{2,1,0:T(8,128)S(1)}, f32[2,216,128]{2,1,0:T(8,128)S(1)}, u32[]{:S(2)}, u32[]{:S(2)}) %collective-permute-start.2) | collective-permute-done | bytes 221216 | tf_op jit(solution)/shard_map/ppermute | solution.py:756
  21.1 3.6 %collective-permute-start.4 = (f32[128,128]{1,0:T(8,128)S(1)}, f32[128,128]{1,0:T(8,128)S(1)}, u32[]{:S(2)}, u32[]{:S(2)}) collective-permute-start(f32[128,128]{1,0:T(8,128)S(1)} %get-tuple-element.63), channel_id=1, source_target_pairs={{2,4},{6,8},{10,12},{14,16},{18,20},{22,24},{26,28},{30,0},{4,2},{... | collective-permute-start | bytes 196616 | tf_op jit(solution)/shard_map/ppermute | solution.py:748
  24.6 2.9 %collective-permute-done.4.out_ref = f32[128,128]{1,0:T(8,128)S(1)} collective-permute-done((f32[128,128]{1,0:T(8,128)S(1)}, f32[128,128]{1,0:T(8,128)S(1)}, u32[]{:S(2)}, u32[]{:S(2)}) %collective-permute-start.4) | collective-permute-done | bytes 65568 | tf_op jit(solution)/shard_map/ppermute | solution.py:748
  27.5 1.6 %collective-permute-start.5 = (f32[2,144,128]{2,1,0:T(8,128)S(1)}, f32[2,144,128]{2,1,0:T(8,128)S(1)}, u32[]{:S(2)}, u32[]{:S(2)}) collective-permute-start(f32[2,144,128]{2,1,0:T(8,128)S(1)} %shard_map.124), channel_id=1, source_target_pairs={{0,1},{1,0},{2,3},{3,2},{4,5},{5,4},{6,7},{7,6},{8,9},{9,8},{10,11... | collective-permute-start | bytes 442376 | tf_op jit(solution)/shard_map/ppermute | solution.py:756
  29.1 3.6 %collective-permute-done.5.az_ref = f32[2,144,128]{2,1,0:T(8,128)S(1)} collective-permute-done((f32[2,144,128]{2,1,0:T(8,128)S(1)}, f32[2,144,128]{2,1,0:T(8,128)S(1)}, u32[]{:S(2)}, u32[]{:S(2)}) %collective-permute-start.5) | collective-permute-done | bytes 147488 | tf_op jit(solution)/shard_map/ppermute | solution.py:756
  32.8 1.5 %shard_map.125 = (f32[8,64,128]{2,1,0:T(8,128)S(1)}, f32[2,64,128]{2,1,0:T(8,128)S(1)}, f32[8,16,128]{2,1,0:T(8,128)S(1)}, f32[8,64,128]{2,1,0:T(8,128)S(1)}, f3...) custom-call(f32[8,64,128]{2,1,0:T(8,128)S(1)} %get-tuple-element.61.g_ref, ...), custom_call_target="tpu_custom_call" | custom-call | tf_op jit(solution)/shard_map/pallas_call | solution.py:735
  34.4 2.4 %collective-permute-start.7 = (f32[144,128]{1,0:T(8,128)S(1)}, f32[144,128]{1,0:T(8,128)S(1)}, u32[]{:S(2)}, u32[]{:S(2)}) collective-permute-start(f32[144,128]{1,0:T(8,128)S(1)} %get-tuple-element.68), channel_id=1, source_target_pairs={{2,4},{6,8},{10,12},{14,16},{18,20},{22,24},{26,28},{30,0},{4,2},{... | collective-permute-start | bytes 221192 | tf_op jit(solution)/shard_map/ppermute | solution.py:748
  36.8 4.1 %collective-permute-done.7.out_ref = f32[144,128]{1,0:T(8,128)S(1)} collective-permute-done((f32[144,128]{1,0:T(8,128)S(1)}, f32[144,128]{1,0:T(8,128)S(1)}, u32[]{:S(2)}, u32[]{:S(2)}) %collective-permute-start.7) | collective-permute-done | bytes 73760 | tf_op jit(solution)/shard_map/ppermute | solution.py:748
  40.9 1.6 %collective-permute-start.8 = (f32[2,128,128]{2,1,0:T(8,128)S(1)}, f32[2,128,128]{2,1,0:T(8,128)S(1)}, u32[]{:S(2)}, u32[]{:S(2)}) collective-permute-start(f32[2,128,128]{2,1,0:T(8,128)S(1)} %shard_map.126), channel_id=1, source_target_pairs={{0,1},{1,0},{2,3},{3,2},{4,5},{5,4},{6,7},{7,6},{8,9},{9,8},{10,11... | collective-permute-start | bytes 393224 | tf_op jit(solution)/shard_map/ppermute | solution.py:756
  42.5 9.4 %all_to_all.44 = f32[32,1,128]{2,1,0:T(1,128)S(1)} all-to-all(f32[32,1,128]{2,1,0:T(1,128)S(1)} %bitcast.39), channel_id=1, replica_groups=mesh['axial'=16,'azim'=2] {'axial','azim'}, dimensions={0} | all-to-all | bytes 32768 | tf_op jit(solution)/shard_map/all_to_all | solution.py:763
  52.0 0.8 shard_map.127
  54.1 5.2 %collective-permute-done.10.out_ref = f32[128,128]{1,0:T(8,128)S(1)} collective-permute-done((f32[128,128]{1,0:T(8,128)S(1)}, f32[128,128]{1,0:T(8,128)S(1)}, u32[]{:S(2)}, u32[]{:S(2)}) %collective-permute-start.10) | collective-permute-done | bytes 65568 | tf_op jit(solution)/shard_map/ppermute | solution.py:748
  59.9 8.9 %all_to_all.45 = f32[32,1,128]{2,1,0:T(1,128)S(1)} all-to-all(f32[32,1,128]{2,1,0:T(1,128)S(1)} %bitcast.42), channel_id=1, replica_groups=mesh['axial'=16,'azim'=2] {'axial','azim'}, dimensions={0} | all-to-all | bytes 32768 | tf_op jit(solution)/shard_map/all_to_all | solution.py:763
  68.8 1.6 %shard_map.129 = (f32[8,64,128]{2,1,0:T(8,128)S(1)}, f32[2,64,128]{2,1,0:T(8,128)S(1)}, f32[8,16,128]{2,1,0:T(8,128)S(1)}, f32[8,64,128]{2,1,0:T(8,128)S(1)}, f3...) custom-call(f32[8,64,128]{2,1,0:T(8,128)S(1)} %get-tuple-element.73., ...), custom_call_target="tpu_custom_call" | custom-call | tf_op jit(solution)/shard_map/pallas_call | solution.py:735
  71.7 5.3 %collective-permute-done.13.out_ref = f32[144,128]{1,0:T(8,128)S(1)} collective-permute-done((f32[144,128]{1,0:T(8,128)S(1)}, f32[144,128]{1,0:T(8,128)S(1)}, u32[]{:S(2)}, u32[]{:S(2)}) %collective-permute-start.13) | collective-permute-done | bytes 73760 | tf_op jit(solution)/shard_map/ppermute | solution.py:748
  77.6 4.5 %collective-permute-done.14.az_ref = f32[2,128,128]{2,1,0:T(8,128)S(1)} collective-permute-done((f32[2,128,128]{2,1,0:T(8,128)S(1)}, f32[2,128,128]{2,1,0:T(8,128)S(1)}, u32[]{:S(2)}, u32[]{:S(2)}) %collective-permute-start.14) | collective-permute-done | bytes 131104 | tf_op jit(solution)/shard_map/ppermute | solution.py:756
  82.1 0.8 shard_map.131
  83.1 1.2 collective-permute-done.15.in_ref
  84.2 5.2 %collective-permute-done.16.out_ref = f32[128,128]{1,0:T(8,128)S(1)} collective-permute-done((f32[128,128]{1,0:T(8,128)S(1)}, f32[128,128]{1,0:T(8,128)S(1)}, u32[]{:S(2)}, u32[]{:S(2)}) %collective-permute-start.16) | collective-permute-done | bytes 65568 | tf_op jit(solution)/shard_map/ppermute | solution.py:748
  90.0 8.9 %all_to_all.46 = f32[32,1,128]{2,1,0:T(1,128)S(1)} all-to-all(f32[32,1,128]{2,1,0:T(1,128)S(1)} %bitcast.41), channel_id=1, replica_groups=mesh['axial'=16,'azim'=2] {'axial','azim'}, dimensions={0} | all-to-all | bytes 32768 | tf_op jit(solution)/shard_map/all_to_all | solution.py:763
  98.9 1.6 %shard_map.133 = (f32[8,64,128]{2,1,0:T(8,128)}, f32[8,64,128]{2,1,0:T(8,128)S(1)}, f32[144,128]{1,0:T(8,128)S(1)}, f32[144,128]{1,0:T(8,128)S(1)}, f32[2,128,12...) custom-call(f32[8,64,128]{2,1,0:T(8,128)S(1)} %get-tuple-element.89.g_ref, ...), custom_call_target="tpu_custom_call" | custom-call | tf_op jit(solution)/shard_map/pallas_call | solution.py:735
  101.9 5.3 %collective-permute-done.19.out_ref = f32[144,128]{1,0:T(8,128)S(1)} collective-permute-done((f32[144,128]{1,0:T(8,128)S(1)}, f32[144,128]{1,0:T(8,128)S(1)}, u32[]{:S(2)}, u32[]{:S(2)}) %collective-permute-start.19) | collective-permute-done | bytes 73760 | tf_op jit(solution)/shard_map/ppermute | solution.py:748
  107.8 8.9 %all_to_all.47 = f32[32,1,128]{2,1,0:T(1,128)S(1)} all-to-all(f32[32,1,128]{2,1,0:T(1,128)S(1)} %bitcast.40), channel_id=1, replica_groups=mesh['axial'=16,'azim'=2] {'axial','azim'}, dimensions={0} | all-to-all | bytes 32768 | tf_op jit(solution)/shard_map/all_to_all | solution.py:763
  116.7 1.0 shard_map.135
  (58 shorter events, 8.4 us)
Async XLA Ops:
  1.3 1.1 copy-start
  2.4 0.9 copy-start.2
  5.0 15.5 %copy-start.1 = (f32[3,8,8,8,1,1,128]{6,5,4,3,2,1,0:T(1,128)S(1)}, f32[3,8,8,8,1,1,128]{6,5,4,3,2,1,0:T(1,128)}, u32[]{:S(2)}) copy-start(f32[3,8,8,8,1,1,128]{6,5,4,3,2,1,0:T(1,128)} %param.10) | copy-start | bytes 2359300
  5.9 6.2 %collective-permute-start = (f32[200,128]{1,0:T(8,128)S(1)}, f32[200,128]{1,0:T(8,128)S(1)}, u32[]{:S(2)}, u32[]{:S(2)}) collective-permute-start(f32[200,128]{1,0:T(8,128)S(1)} %get-tuple-element.58), channel_id=1, source_target_pairs={{0,2},{2,0},{4,6},{6,4},{8,10},{10,8},{12,14},{14,12},{16,18},{18,... | collective-permute-start | bytes 307208 | tf_op jit(solution)/shard_map/ppermute | solution.py:749
  6.4 8.0 %collective-permute-start.1 = (f32[200,128]{1,0:T(8,128)S(1)}, f32[200,128]{1,0:T(8,128)S(1)}, u32[]{:S(2)}, u32[]{:S(2)}) collective-permute-start(f32[200,128]{1,0:T(8,128)S(1)} %get-tuple-element.59), channel_id=1, source_target_pairs={{2,4},{6,8},{10,12},{14,16},{18,20},{22,24},{26,28},{30,0},{4,2},{... | collective-permute-start | bytes 307208 | tf_op jit(solution)/shard_map/ppermute | solution.py:748
  14.4 6.0 %copy-start.9 = (f32[64,128]{1,0:T(8,128)S(1)}, f32[64,128]{1,0:T(8,128)}, u32[]{:S(2)}) copy-start(f32[64,128]{1,0:T(8,128)} %constant.17.clone.plane_ref) | copy-start | bytes 98308
  14.4 6.0 %copy-start.11 = (bf16[64,384]{1,0:T(8,128)(2,1)S(1)}, bf16[64,384]{1,0:T(8,128)(2,1)}, u32[]{:S(2)}) copy-start(bf16[64,384]{1,0:T(8,128)(2,1)} %constant.21.clone.div_ref) | copy-start | bytes 147460
  14.4 6.0 %copy-start.12 = (f32[64,128]{1,0:T(8,128)S(1)}, f32[64,128]{1,0:T(8,128)}, u32[]{:S(2)}) copy-start(f32[64,128]{1,0:T(8,128)} %constant.18.clone.over_ref) | copy-start | bytes 98308
  14.4 6.0 %collective-permute-start.2 = (f32[2,216,128]{2,1,0:T(8,128)S(1)}, f32[2,216,128]{2,1,0:T(8,128)S(1)}, u32[]{:S(2)}, u32[]{:S(2)}) collective-permute-start(f32[2,216,128]{2,1,0:T(8,128)S(1)} %shard_map.122), channel_id=1, source_target_pairs={{0,1},{1,0},{2,3},{3,2},{4,5},{5,4},{6,7},{7,6},{8,9},{9,8},{10,11... | collective-permute-start | bytes 663560 | tf_op jit(solution)/shard_map/ppermute | solution.py:756
  21.0 3.6 %collective-permute-start.3 = (f32[128,128]{1,0:T(8,128)S(1)}, f32[128,128]{1,0:T(8,128)S(1)}, u32[]{:S(2)}, u32[]{:S(2)}) collective-permute-start(f32[128,128]{1,0:T(8,128)S(1)} %get-tuple-element.62), channel_id=1, source_target_pairs={{0,2},{2,0},{4,6},{6,4},{8,10},{10,8},{12,14},{14,12},{16,18},{18,... | collective-permute-start | bytes 196616 | tf_op jit(solution)/shard_map/ppermute | solution.py:749
  21.1 6.5 %collective-permute-start.4 = (f32[128,128]{1,0:T(8,128)S(1)}, f32[128,128]{1,0:T(8,128)S(1)}, u32[]{:S(2)}, u32[]{:S(2)}) collective-permute-start(f32[128,128]{1,0:T(8,128)S(1)} %get-tuple-element.63), channel_id=1, source_target_pairs={{2,4},{6,8},{10,12},{14,16},{18,20},{22,24},{26,28},{30,0},{4,2},{... | collective-permute-start | bytes 196616 | tf_op jit(solution)/shard_map/ppermute | solution.py:748
  27.5 5.2 %copy-start.4 = (bf16[112,432]{1,0:T(8,128)(2,1)S(1)}, bf16[112,432]{1,0:T(8,128)(2,1)}, u32[]{:S(2)}) copy-start(bf16[112,432]{1,0:T(8,128)(2,1)} %constant.22.clone.into_ref) | copy-start | bytes 290308
  27.5 5.2 %copy-start.5 = (bf16[144,336]{1,0:T(8,128)(2,1)S(1)}, bf16[144,336]{1,0:T(8,128)(2,1)}, u32[]{:S(2)}) copy-start(bf16[144,336]{1,0:T(8,128)(2,1)} %constant.23.clone.outof_ref) | copy-start | bytes 290308
  27.5 5.2 %copy-start.10 = (f32[112,128]{1,0:T(8,128)S(1)}, f32[112,128]{1,0:T(8,128)}, u32[]{:S(2)}) copy-start(f32[112,128]{1,0:T(8,128)} %constant.19.clone.spectrum_ref) | copy-start | bytes 172036
  27.5 5.2 %collective-permute-start.5 = (f32[2,144,128]{2,1,0:T(8,128)S(1)}, f32[2,144,128]{2,1,0:T(8,128)S(1)}, u32[]{:S(2)}, u32[]{:S(2)}) collective-permute-start(f32[2,144,128]{2,1,0:T(8,128)S(1)} %shard_map.124), channel_id=1, source_target_pairs={{0,1},{1,0},{2,3},{3,2},{4,5},{5,4},{6,7},{7,6},{8,9},{9,8},{10,11... | collective-permute-start | bytes 442376 | tf_op jit(solution)/shard_map/ppermute | solution.py:756
  34.3 17.7 %copy-start.3 = (f32[8,8,8,1,1,128]{5,4,3,2,1,0:T(1,128)S(1)}, f32[8,8,8,1,1,128]{5,4,3,2,1,0:T(1,128)}, u32[]{:S(2)}) copy-start(f32[8,8,8,1,1,128]{5,4,3,2,1,0:T(1,128)} %param.11) | copy-start | bytes 786436
  34.3 2.5 %collective-permute-start.6 = (f32[144,128]{1,0:T(8,128)S(1)}, f32[144,128]{1,0:T(8,128)S(1)}, u32[]{:S(2)}, u32[]{:S(2)}) collective-permute-start(f32[144,128]{1,0:T(8,128)S(1)} %get-tuple-element.67), channel_id=1, source_target_pairs={{0,2},{2,0},{4,6},{6,4},{8,10},{10,8},{12,14},{14,12},{16,18},{18,... | collective-permute-start | bytes 221192 | tf_op jit(solution)/shard_map/ppermute | solution.py:749
  34.4 6.5 %collective-permute-start.7 = (f32[144,128]{1,0:T(8,128)S(1)}, f32[144,128]{1,0:T(8,128)S(1)}, u32[]{:S(2)}, u32[]{:S(2)}) collective-permute-start(f32[144,128]{1,0:T(8,128)S(1)} %get-tuple-element.68), channel_id=1, source_target_pairs={{2,4},{6,8},{10,12},{14,16},{18,20},{22,24},{26,28},{30,0},{4,2},{... | collective-permute-start | bytes 221192 | tf_op jit(solution)/shard_map/ppermute | solution.py:748
  40.9 11.1 %copy-start.7 = (bf16[128,192]{1,0:T(8,128)(2,1)S(1)}, bf16[128,192]{1,0:T(8,128)(2,1)}, u32[]{:S(2)}) copy-start(bf16[128,192]{1,0:T(8,128)(2,1)} %constant.20.clone.grad_ref) | copy-start | bytes 147460
  40.9 11.0 %collective-permute-start.8 = (f32[2,128,128]{2,1,0:T(8,128)S(1)}, f32[2,128,128]{2,1,0:T(8,128)S(1)}, u32[]{:S(2)}, u32[]{:S(2)}) collective-permute-start(f32[2,128,128]{2,1,0:T(8,128)S(1)} %shard_map.126), channel_id=1, source_target_pairs={{0,1},{1,0},{2,3},{3,2},{4,5},{5,4},{6,7},{7,6},{8,9},{9,8},{10,11... | collective-permute-start | bytes 393224 | tf_op jit(solution)/shard_map/ppermute | solution.py:756
  52.8 1.3 %collective-permute-start.9 = (f32[128,128]{1,0:T(8,128)S(1)}, f32[128,128]{1,0:T(8,128)S(1)}, u32[]{:S(2)}, u32[]{:S(2)}) collective-permute-start(f32[128,128]{1,0:T(8,128)S(1)} %get-tuple-element.74), channel_id=1, source_target_pairs={{0,2},{2,0},{4,6},{6,4},{8,10},{10,8},{12,14},{14,12},{16,18},{18,... | collective-permute-start | bytes 196616 | tf_op jit(solution)/shard_map/ppermute | solution.py:749
  52.9 6.5 %collective-permute-start.10 = (f32[128,128]{1,0:T(8,128)S(1)}, f32[128,128]{1,0:T(8,128)S(1)}, u32[]{:S(2)}, u32[]{:S(2)}) collective-permute-start(f32[128,128]{1,0:T(8,128)S(1)} %get-tuple-element.75), channel_id=1, source_target_pairs={{2,4},{6,8},{10,12},{14,16},{18,20},{22,24},{26,28},{30,0},{4,2},{... | collective-permute-start | bytes 196616 | tf_op jit(solution)/shard_map/ppermute | solution.py:748
  59.4 9.5 %collective-permute-start.11 = (f32[2,144,128]{2,1,0:T(8,128)S(1)}, f32[2,144,128]{2,1,0:T(8,128)S(1)}, u32[]{:S(2)}, u32[]{:S(2)}) collective-permute-start(f32[2,144,128]{2,1,0:T(8,128)S(1)} %shard_map.128), channel_id=1, source_target_pairs={{0,1},{1,0},{2,3},{3,2},{4,5},{5,4},{6,7},{7,6},{8,9},{9,8},{10,11... | collective-permute-start | bytes 442376 | tf_op jit(solution)/shard_map/ppermute | solution.py:756
  70.4 1.3 %collective-permute-start.12 = (f32[144,128]{1,0:T(8,128)S(1)}, f32[144,128]{1,0:T(8,128)S(1)}, u32[]{:S(2)}, u32[]{:S(2)}) collective-permute-start(f32[144,128]{1,0:T(8,128)S(1)} %get-tuple-element.83), channel_id=1, source_target_pairs={{0,2},{2,0},{4,6},{6,4},{8,10},{10,8},{12,14},{14,12},{16,18},{18,... | collective-permute-start | bytes 221192 | tf_op jit(solution)/shard_map/ppermute | solution.py:749
  70.5 6.5 %collective-permute-start.13 = (f32[144,128]{1,0:T(8,128)S(1)}, f32[144,128]{1,0:T(8,128)S(1)}, u32[]{:S(2)}, u32[]{:S(2)}) collective-permute-start(f32[144,128]{1,0:T(8,128)S(1)} %get-tuple-element.84), channel_id=1, source_target_pairs={{2,4},{6,8},{10,12},{14,16},{18,20},{22,24},{26,28},{30,0},{4,2},{... | collective-permute-start | bytes 221192 | tf_op jit(solution)/shard_map/ppermute | solution.py:748
  77.0 5.0 %collective-permute-start.14 = (f32[2,128,128]{2,1,0:T(8,128)S(1)}, f32[2,128,128]{2,1,0:T(8,128)S(1)}, u32[]{:S(2)}, u32[]{:S(2)}) collective-permute-start(f32[2,128,128]{2,1,0:T(8,128)S(1)} %shard_map.130), channel_id=1, source_target_pairs={{0,1},{1,0},{2,3},{3,2},{4,5},{5,4},{6,7},{7,6},{8,9},{9,8},{10,11... | collective-permute-start | bytes 393224 | tf_op jit(solution)/shard_map/ppermute | solution.py:756
  82.9 1.3 %collective-permute-start.15 = (f32[128,128]{1,0:T(8,128)S(1)}, f32[128,128]{1,0:T(8,128)S(1)}, u32[]{:S(2)}, u32[]{:S(2)}) collective-permute-start(f32[128,128]{1,0:T(8,128)S(1)} %get-tuple-element.90), channel_id=1, source_target_pairs={{0,2},{2,0},{4,6},{6,4},{8,10},{10,8},{12,14},{14,12},{16,18},{18,... | collective-permute-start | bytes 196616 | tf_op jit(solution)/shard_map/ppermute | solution.py:749
  83.0 6.5 %collective-permute-start.16 = (f32[128,128]{1,0:T(8,128)S(1)}, f32[128,128]{1,0:T(8,128)S(1)}, u32[]{:S(2)}, u32[]{:S(2)}) collective-permute-start(f32[128,128]{1,0:T(8,128)S(1)} %get-tuple-element.91), channel_id=1, source_target_pairs={{2,4},{6,8},{10,12},{14,16},{18,20},{22,24},{26,28},{30,0},{4,2},{... | collective-permute-start | bytes 196616 | tf_op jit(solution)/shard_map/ppermute | solution.py:748
  89.5 9.5 %collective-permute-start.17 = (f32[2,144,128]{2,1,0:T(8,128)S(1)}, f32[2,144,128]{2,1,0:T(8,128)S(1)}, u32[]{:S(2)}, u32[]{:S(2)}) collective-permute-start(f32[2,144,128]{2,1,0:T(8,128)S(1)} %shard_map.132), channel_id=1, source_target_pairs={{0,1},{1,0},{2,3},{3,2},{4,5},{5,4},{6,7},{7,6},{8,9},{9,8},{10,11... | collective-permute-start | bytes 442376 | tf_op jit(solution)/shard_map/ppermute | solution.py:756
  100.6 1.3 %collective-permute-start.18 = (f32[144,128]{1,0:T(8,128)S(1)}, f32[144,128]{1,0:T(8,128)S(1)}, u32[]{:S(2)}, u32[]{:S(2)}) collective-permute-start(f32[144,128]{1,0:T(8,128)S(1)} %get-tuple-element.101), channel_id=1, source_target_pairs={{0,2},{2,0},{4,6},{6,4},{8,10},{10,8},{12,14},{14,12},{16,18},{18,... | collective-permute-start | bytes 221192 | tf_op jit(solution)/shard_map/ppermute | solution.py:749
  100.6 6.5 %collective-permute-start.19 = (f32[144,128]{1,0:T(8,128)S(1)}, f32[144,128]{1,0:T(8,128)S(1)}, u32[]{:S(2)}, u32[]{:S(2)}) collective-permute-start(f32[144,128]{1,0:T(8,128)S(1)} %get-tuple-element.102), channel_id=1, source_target_pairs={{2,4},{6,8},{10,12},{14,16},{18,20},{22,24},{26,28},{30,0},{4,2},{... | collective-permute-start | bytes 221192 | tf_op jit(solution)/shard_map/ppermute | solution.py:748
  107.2 9.5 %collective-permute-start.20 = (f32[2,128,128]{2,1,0:T(8,128)S(1)}, f32[2,128,128]{2,1,0:T(8,128)S(1)}, u32[]{:S(2)}, u32[]{:S(2)}) collective-permute-start(f32[2,128,128]{2,1,0:T(8,128)S(1)} %shard_map.134), channel_id=1, source_target_pairs={{0,1},{1,0},{2,3},{3,2},{4,5},{5,4},{6,7},{7,6},{8,9},{9,8},{10,11... | collective-permute-start | bytes 393224 | tf_op jit(solution)/shard_map/ppermute | solution.py:756
  (3 other events, 2.3 us)
where the time goes:
time: 118 us
  waiting for transfers between devices  45.9 us (39%)
  blocking collectives  36.1 us (31%)
  starting transfers between devices  21.6 us (18%)
  Pallas kernels  8.94 us (8%)
  local copies, waits for them, and re-layouts  4.36 us (4%)
    all_to_all x4, blocking collectives, gather_sums(): return lax.all_to_all(rows, ALL, 0, 0, tiled=True)  36.1 us
    ppermute x7, waiting for transfers between devices, axial_swap(): from_outer = lax.ppermute(outer_rows, 'axial', outer)  30.3 us
    ppermute x7, starting transfers between devices, axial_swap(): from_outer = lax.ppermute(outer_rows, 'axial', outer)  13.6 us
    ppermute x7, waiting for transfers between devices, azim_swap(): return lax.ppermute(sides, 'azim', [(0, 1), (1, 0)])  12.5 us
    pallas_call x15, Pallas kernels, kernel_call(): pl.pallas_call(kernel, out_shape=outs, compiler_params=pltpu.CompilerPara...  8.94 us
    ppermute x7, starting transfers between devices, azim_swap(): return lax.ppermute(sides, 'azim', [(0, 1), (1, 0)])  7.05 us
    unnamed x28, local copies, waits for them, and re-layouts  4.36 us
    ppermute x7, waiting for transfers between devices, axial_swap(): from_inner = lax.ppermute(inner_rows, 'axial', inner)  3.03 us
  transfers between devices with their start and end apart: 21, of which 14 were waited for; matrix products, arithmetic and copies ran while one was open for 0% of the time, Pallas kernels for 0%

commit v1 on v0

--- a/solution.py
+++ b/solution.py
@@ -12,6 +12,7 @@
 time_increment = 0.02
 mass_shift = 0.05
 VMEM_GRANT = 20 << 20
+TAIL = 16
 gll_points = [
     -1.0,
     -0.8717401485096066,
@@ -291,7 +292,26 @@
     return before, after
 
 
-def conv_kernel(u_ref, diff_ref, row_ref, plane_ref, grad_ref, conv_ref, kbar_ref, in_ref, out_ref, az_ref):
+def conv_kernel(
+    u_hbm, row_hbm, plane_hbm, grad_hbm,
+    conv_ref, row_ref, in_ref, out_ref, early_ref, late_ref,
+    u_ref, small_ref, plane_ref, grad_ref, sems,
+):
+    copies = [
+        pltpu.make_async_copy(source, target, sems.at[k])
+        for k, (source, target) in enumerate(
+            ((u_hbm, u_ref), (plane_hbm, plane_ref), (grad_hbm, grad_ref), (row_hbm, small_ref))
+        )
+    ]
+    for copy in copies:
+        copy.start()
+    row_ref[...] = jnp.zeros(row_ref.shape, F32)
+    for copy in copies:
+        copy.wait()
+    size = small_ref.shape[1]
+    for k in range(-(-size // LANES)):
+        stop = min(LANES, size - LANES * k)
+        row_ref[k : k + 1, :stop] = small_ref[:, LANES * k : LANES * k + stop]
     plane = plane_ref[...]
     fields = [[u_ref[d, a] for a in range(8)] for d in range(3)]
     low, high = [], []
@@ -308,15 +328,22 @@
             )
             value = radial_sum(float(WEIGHTS[a]) * plane * value)
             conv_ref[comp, a] = value
-            start = 64 * comp + 8 * a
-            az_ref[0, start : start + 8] = value[:8]
-            az_ref[1, start : start + 8] = value[56:]
+            for side, rows in enumerate((value[:8], value[56:])):
+                if a in (0, 7):
+                    start = 16 * comp + (8 if a else 0)
+                    late_ref[side, start : start + 8] = rows
+                else:
+                    start = 48 * comp + 8 * (a - 1)
+                    early_ref[side, start : start + 8] = rows
             if a == 0:
                 low.append(value)
             if a == 7:
                 high.append(value)
     row = row_ref[...]
     send_axial(in_ref, out_ref, low + [row], high + [row])
+
+
+def mean_kernel(diff_ref, kbar_ref):
     mean = diff_ref[0]
     for a in range(1, 8):
         mean = mean + diff_ref[a]
@@ -324,17 +351,18 @@
     kbar_ref[...] = jnp.broadcast_to(mean, (8, LANES))
 
 
-def conv_side_kernel(in_ref, out_ref, az_ref, row_ref, send_ref):
+def conv_side_kernel(in_ref, out_ref, late_ref, row_ref, send_ref):
     before, after = got_axial(in_ref, out_ref)
     count = row_ref.shape[0]
     for side, b in ((0, 0), (1, 7)):
         for comp in range(3):
-            start = 64 * comp
-            send_ref[side, start : start + 8] = az_ref[side, start : start + 8] + before(start + 8 * b, 8)
-            send_ref[side, start + 8 : start + 56] = az_ref[side, start + 8 : start + 56]
-            send_ref[side, start + 56 : start + 64] = az_ref[side, start + 56 : start + 64] + after(start + 8 * b, 8)
+            first = slice(16 * comp, 16 * comp + 8)
+            last = slice(16 * comp + 8, 16 * comp + 16)
+            row = 64 * comp + 8 * b
+            send_ref[side, first] = late_ref[side, first] + before(row, 8)
+            send_ref[side, last] = late_ref[side, last] + after(row, 8)
         for place, rows in enumerate((before(192, count), row_ref[...], after(192, count))):
-            start = 192 + place * count
+            start = 48 + place * count
             send_ref[side, start : start + count] = rows
 
 
@@ -372,42 +400,51 @@
         jnp.sum(jnp.where(place == width - 1 - k, row, 0.0), axis=1, keepdims=True)
         for k in range(scalars)
     ]
-    return jnp.where(place >= width - 4, 0.0, row), values
-
-
-def send_raw(raw, g_ref, in_ref, out_ref, az_ref):
+    return jnp.where(place >= width - TAIL, 0.0, row), values
+
+
+def send_raw(raw, g_ref, in_ref, out_ref, early_ref, late_ref):
     parts = [radial_sum(raw[a]) for a in range(8)]
     for a in range(8):
         g_ref[a] = parts[a]
-        for side, (edge, inner) in enumerate(((0, 1), (7, 6))):
-            az_ref[side, 8 + 8 * a : 16 + 8 * a] = parts[a][8 * edge : 8 * edge + 8]
-            az_ref[side, 80 + 8 * a : 88 + 8 * a] = parts[a][8 * inner : 8 * inner + 8]
-    zero = jnp.zeros((8, LANES), F32)
-    for side in range(2):
-        az_ref[side, :8] = zero
-        az_ref[side, 72:80] = zero
     send_axial(in_ref, out_ref, [parts[0], parts[1]], [parts[7], parts[6]])
-
-
-def raw_side_kernel(in_ref, out_ref, az_ref, send_ref):
+    for side, (edge, inner) in enumerate(((0, 1), (7, 6))):
+        edges = [part[8 * edge : 8 * edge + 8] for part in parts]
+        inners = [part[8 * inner : 8 * inner + 8] for part in parts]
+        for a in range(1, 7):
+            early_ref[side, 8 * a - 8 : 8 * a] = edges[a]
+            early_ref[side, 40 + 8 * a : 48 + 8 * a] = inners[a]
+        late_ref[side, :8] = edges[0]
+        late_ref[side, 8:16] = edges[7]
+        late_ref[side, 16:24] = inners[0]
+        late_ref[side, 24:32] = inners[7]
+
+
+def raw_side_kernel(in_ref, out_ref, late_ref, send_ref):
     before, after = got_axial(in_ref, out_ref)
     for side, (edge, inner) in enumerate(((0, 1), (7, 6))):
         send_ref[side, :8] = before(64 + 8 * edge, 8)
-        send_ref[side, 8:16] = az_ref[side, 8:16] + before(8 * edge, 8)
-        send_ref[side, 16:64] = az_ref[side, 16:64]
-        send_ref[side, 64:72] = az_ref[side, 64:72] + after(8 * edge, 8)
-        send_ref[side, 72:80] = after(64 + 8 * edge, 8)
-        send_ref[side, 80:88] = az_ref[side, 80:88] + before(8 * inner, 8)
-        send_ref[side, 88:136] = az_ref[side, 88:136]
-        send_ref[side, 136:144] = az_ref[side, 136:144] + after(8 * inner, 8)
+        send_ref[side, 8:16] = late_ref[side, :8] + before(8 * edge, 8)
+        send_ref[side, 16:24] = late_ref[side, 8:16] + after(8 * edge, 8)
+        send_ref[side, 24:32] = after(64 + 8 * edge, 8)
+        send_ref[side, 32:40] = late_ref[side, 16:24] + before(8 * inner, 8)
+        send_ref[side, 40:48] = late_ref[side, 24:32] + after(8 * inner, 8)
 
 
 def divergence_kernel(
-    conv_ref, u_ref, in_ref, out_ref, az_ref, row_ref, plane_ref, over_ref, div_ref,
-    g_ref, send_in_ref, send_out_ref, send_az_ref, near_ref, pay_ref,
+    conv_ref, u_ref, in_ref, out_ref, early_ref, late_ref, row_ref, plane_ref, over_ref, div_ref,
+    g_ref, send_in_ref, send_out_ref, send_early_ref, send_late_ref, near_ref, pay_ref,
 ):
     before, after = got_axial(in_ref, out_ref)
     plane, over = plane_ref[...], over_ref[...]
+
+    def side_rows(side, comp, a):
+        if a in (0, 7):
+            start = 16 * comp + (8 if a else 0)
+            return late_ref[side, start : start + 8]
+        start = 48 * comp + 8 * (a - 1)
+        return early_ref[side, start : start + 8]
+
     moved = []
     for comp in range(3):
         parts = []
@@ -417,8 +454,7 @@
                 value = value + before(64 * comp, 64)
             if a == 7:
                 value = value + after(64 * comp, 64)
-            start = 64 * comp + 8 * a
-            value = add_rows(value, {0: az_ref[1, start : start + 8], 7: az_ref[0, start : start + 8]})
+            value = add_rows(value, {0: side_rows(1, comp, a), 7: side_rows(0, comp, a)})
             scale = time_increment * (0.5 if a in (0, 7) else 1.0)
             parts.append(float(WEIGHTS[a]) * plane * u_ref[comp, a] - scale * over * value)
         moved.append(parts)
@@ -428,93 +464,74 @@
     )
     along_a = skew_apply(DERIV.T, moved[0])
     raw = [along_a[a] + flat[:, LANES * a : LANES * a + LANES] for a in range(8)]
-    send_raw(raw, g_ref, send_in_ref, send_out_ref, send_az_ref)
-    count = (az_ref.shape[1] - 192) // 3
+    send_raw(raw, g_ref, send_in_ref, send_out_ref, send_early_ref, send_late_ref)
+    count = row_ref.shape[0]
     width = near_ref.shape[1] // LANES
     near_ref[...] = jnp.zeros(near_ref.shape, F32)
     for i in range(3):
-        start = 192 + i * count
+        start = 48 + i * count
         middle = (before(192, count), row_ref[...], after(192, count))[i]
-        sides = (az_ref[1, start : start + count], middle, az_ref[0, start : start + count])
+        sides = (late_ref[1, start : start + count], middle, late_ref[0, start : start + count])
         for j, rows in enumerate(sides):
             for k in range(width):
                 near_ref[3 * i + j : 3 * i + j + 1, LANES * k : LANES * k + LANES] = rows[k : k + 1]
     send_sums(pay_ref, coarse_share(raw, near_ref), [])
 
 
-def got_box(g_ref, in_ref, out_ref, az_ref):
+def got_planes(g_ref, in_ref, out_ref, early_ref, late_ref):
     before, after = got_axial(in_ref, out_ref)
-    center = []
-    for a in range(8):
-        value = g_ref[a]
-        if a == 0:
+
+    def edge_rows(side, e):
+        if e in (0, 1, 8, 9):
+            start = 8 * (0, 1, 8, 9).index(e)
+            return late_ref[side, start : start + 8]
+        return early_ref[side, 8 * e - 16 : 8 * e - 8]
+
+    def inner_rows(side, a):
+        if a in (0, 7):
+            start = 40 if a else 32
+            return late_ref[side, start : start + 8]
+        return early_ref[side, 40 + 8 * a : 48 + 8 * a]
+
+    zero = jnp.zeros((80, LANES), F32)
+    planes = []
+    for e in range(10):
+        if e == 0:
+            value = before(64, 64)
+        elif e == 9:
+            value = after(64, 64)
+        else:
+            value = g_ref[e - 1]
+        if e == 1:
             value = value + before(0, 64)
-        if a == 7:
+        if e == 8:
             value = value + after(0, 64)
-        start = 8 + 8 * a
-        center.append(
-            add_rows(value, {0: az_ref[1, start : start + 8], 7: az_ref[0, start : start + 8]})
-        )
-    outer_a = [
-        add_rows(before(64, 64), {0: az_ref[1, :8], 7: az_ref[0, :8]}),
-        add_rows(after(64, 64), {0: az_ref[1, 72:80], 7: az_ref[0, 72:80]}),
-    ]
-    outer_b = [
-        jnp.concatenate(
-            [az_ref[1, 80 + 8 * a : 88 + 8 * a], az_ref[0, 80 + 8 * a : 88 + 8 * a]], axis=0
-        )
-        for a in range(8)
-    ]
-    return center, outer_a, outer_b
-
-
-def put_box(box, center_ref, outer_a_ref, outer_b_ref):
-    center, outer_a, outer_b = box
-    for a in range(8):
-        center_ref[a] = center[a]
-        outer_b_ref[a] = outer_b[a]
-    for k in range(2):
-        outer_a_ref[k] = outer_a[k]
-
-
-def take_box(center_ref, outer_a_ref, outer_b_ref):
-    return (
-        [center_ref[a] for a in range(8)],
-        [outer_a_ref[k] for k in range(2)],
-        [outer_b_ref[a] for a in range(8)],
-    )
-
-
-def add_box(first, scale, second):
-    return tuple([x + scale * y for x, y in zip(xs, ys)] for xs, ys in zip(first, second))
-
-
-def solve(box, kbar_ref, into_ref, outof_ref, spectrum_ref):
-    center, outer_a, outer_b = box
-    zero = jnp.zeros((80, LANES), F32)
-    planes = [jnp.concatenate([outer_a[0], zero], axis=0)]
-    for a in range(8):
-        planes.append(jnp.concatenate([center[a], spread(center[a], 6, 1), outer_b[a]], axis=0))
-    planes.append(jnp.concatenate([outer_a[1], zero], axis=0))
-    rows = jnp.concatenate(planes, axis=1)
-    flat = product(into_ref, rows)
-    parts = to_spectral([flat[:, LANES * a : LANES * a + LANES] for a in range(10)])
+        value = add_rows(value, {0: edge_rows(1, e), 7: edge_rows(0, e)})
+        if e in (0, 9):
+            rows = [value, zero]
+        else:
+            rows = [value, spread(value, 6, 1), inner_rows(1, e - 1), inner_rows(0, e - 1)]
+        planes.append(jnp.concatenate(rows, axis=0))
+    return planes
+
+
+def solve_kernel(
+    g_ref, in_ref, out_ref, early_ref, late_ref, kbar_ref, into_ref, outof_ref, spectrum_ref,
+    planes_ref, solved_ref, part_ref, send_in_ref, send_out_ref, send_early_ref, send_late_ref,
+):
+    planes = got_planes(g_ref, in_ref, out_ref, early_ref, late_ref)
+    for e in range(10):
+        planes_ref[e] = planes[e]
+    flat = product(into_ref, jnp.concatenate(planes, axis=1))
+    parts = to_spectral([flat[:, LANES * e : LANES * e + LANES] for e in range(10)])
     kbar = kbar_ref[0:1, :]
     plane_spectrum = kbar * spectrum_ref[...] + mass_shift
     parts = [parts[i] / (plane_spectrum + float(EIGVAL[i]) * kbar) for i in range(10)]
     parts = from_spectral(parts)
     flat = product(outof_ref, jnp.concatenate(parts, axis=1))
-    solved = [flat[:, LANES * a : LANES * a + LANES] for a in range(10)]
-    dot = None
-    for a in range(10):
-        stop = 64 if a in (0, 9) else 144
-        term = planes[a][:stop] * solved[a][:stop]
-        term = jnp.sum(term.reshape(stop // 8, 8, LANES), axis=0)
-        dot = term if dot is None else dot + term
-    return solved, dot
-
-
-def send_solved(solved, part_ref, in_ref, out_ref, az_ref):
+    solved = [flat[:, LANES * e : LANES * e + LANES] for e in range(10)]
+    for e in range(10):
+        solved_ref[e] = solved[e]
     outer_a = [radial_sum(solved[0][:64]), radial_sum(solved[9][:64])]
     edges = []
     for a in range(8):
@@ -522,49 +539,67 @@
         value = radial_sum(rows[:64] + spread(rows[64:128], 1, 6))
         outer_b = radial_sum(rows[128:144])
         part_ref[a] = value
-        az_ref[0, 8 * a : 8 * a + 8] = value[:8]
-        az_ref[1, 8 * a : 8 * a + 8] = value[56:]
-        az_ref[0, 64 + 8 * a : 72 + 8 * a] = outer_b[:8]
-        az_ref[1, 64 + 8 * a : 72 + 8 * a] = outer_b[8:]
+        for side in range(2):
+            edge = value[56 * side : 56 * side + 8]
+            face = outer_b[8 * side : 8 * side + 8]
+            if a in (0, 1, 6, 7):
+                start = 8 * (0, 1, 6, 7).index(a)
+                send_late_ref[side, start : start + 8] = edge
+            else:
+                send_early_ref[side, 8 * a - 16 : 8 * a - 8] = edge
+            if a in (0, 7):
+                start = 40 if a else 32
+                send_late_ref[side, start : start + 8] = face
+            else:
+                send_early_ref[side, 24 + 8 * a : 32 + 8 * a] = face
         if a in (0, 7):
             edges.append((value, outer_b))
     send_axial(
-        in_ref,
-        out_ref,
+        send_in_ref,
+        send_out_ref,
         [edges[0][0], outer_a[0], edges[0][1]],
         [edges[1][0], outer_a[1], edges[1][1]],
     )
 
 
-def solved_side_kernel(in_ref, out_ref, az_ref, send_ref):
+def solved_side_kernel(in_ref, out_ref, late_ref, send_ref):
     before, after = got_axial(in_ref, out_ref)
     for side, b in ((0, 0), (1, 7)):
         row = 8 * b
-        send_ref[side, :8] = az_ref[side, :8] + before(row, 8)
-        send_ref[side, 8:16] = az_ref[side, 8:16] + before(64 + row, 8)
-        send_ref[side, 16:48] = az_ref[side, 16:48]
-        send_ref[side, 48:56] = az_ref[side, 48:56] + after(64 + row, 8)
-        send_ref[side, 56:64] = az_ref[side, 56:64] + after(row, 8)
-        send_ref[side, 64:72] = az_ref[side, 64:72] + before(128 + 8 * side, 8)
-        send_ref[side, 72:120] = az_ref[side, 72:120]
-        send_ref[side, 120:128] = az_ref[side, 120:128] + after(128 + 8 * side, 8)
-
-
-def got_solved(part_ref, in_ref, out_ref, az_ref):
+        send_ref[side, :8] = late_ref[side, :8] + before(row, 8)
+        send_ref[side, 8:16] = late_ref[side, 8:16] + before(64 + row, 8)
+        send_ref[side, 16:24] = late_ref[side, 16:24] + after(64 + row, 8)
+        send_ref[side, 24:32] = late_ref[side, 24:32] + after(row, 8)
+        send_ref[side, 32:40] = late_ref[side, 32:40] + before(128 + 8 * side, 8)
+        send_ref[side, 40:48] = late_ref[side, 40:48] + after(128 + 8 * side, 8)
+
+
+def got_solved(part_ref, in_ref, out_ref, early_ref, late_ref):
     before, after = got_axial(in_ref, out_ref)
     extra = {0: (before, 0), 1: (before, 64), 6: (after, 64), 7: (after, 0)}
+
+    def edge_rows(side, a):
+        if a in extra:
+            start = 8 * (0, 1, 6, 7).index(a)
+            return late_ref[side, start : start + 8]
+        return early_ref[side, 8 * a - 16 : 8 * a - 8]
+
+    def face_rows(side, a):
+        if a in (0, 7):
+            start = 40 if a else 32
+            return late_ref[side, start : start + 8]
+        return early_ref[side, 24 + 8 * a : 32 + 8 * a]
+
     result = []
     for a in range(8):
         value = part_ref[a]
         if a in extra:
             side, start = extra[a]
             value = value + side(start, 64)
-        rows = slice(8 * a, 8 * a + 8)
-        faces = slice(64 + 8 * a, 72 + 8 * a)
         result.append(
             add_rows(
                 value,
-                {0: az_ref[1, rows], 1: az_ref[1, faces], 6: az_ref[0, faces], 7: az_ref[0, rows]},
+                {0: edge_rows(1, a), 1: face_rows(1, a), 6: face_rows(0, a), 7: edge_rows(0, a)},
             )
         )
     return result
@@ -617,126 +652,149 @@
     return jnp.sum(row * row, axis=1, keepdims=True)
 
 
-def keep(ref, row, scalars):
-    ref[0:1] = row
-    for k, value in enumerate(scalars):
-        ref[k + 1 : k + 2] = jnp.broadcast_to(value, row.shape)
-
-
-def first_solve_kernel(
-    g_ref, in_ref, out_ref, az_ref, kbar_ref, into_ref, outof_ref, spectrum_ref,
-    center_ref, outer_a_ref, outer_b_ref, part_ref, send_in_ref, send_out_ref, send_az_ref, dot_ref,
-):
-    box = got_box(g_ref, in_ref, out_ref, az_ref)
-    put_box(box, center_ref, outer_a_ref, outer_b_ref)
-    solved, dot = solve(box, kbar_ref, into_ref, outof_ref, spectrum_ref)
-    dot_ref[...] = dot
-    send_solved(solved, part_ref, send_in_ref, send_out_ref, send_az_ref)
-
-
-def second_solve_kernel(
-    g_ref, in_ref, out_ref, az_ref, kbar_ref, into_ref, outof_ref, spectrum_ref,
-    old_center_ref, old_a_ref, old_b_ref, sums_ref, state_ref,
-    center_ref, outer_a_ref, outer_b_ref, q_center_ref, q_a_ref, q_b_ref,
-    part_ref, send_in_ref, send_out_ref, send_az_ref, dot_ref, new_state_ref,
-):
-    row_q, (local_rz, curv) = got_sums(sums_ref, 2)
-    row_r = state_ref[0:1]
-    rz = local_rz + norm(row_r)
-    alpha = rz / curv
-    image = got_box(g_ref, in_ref, out_ref, az_ref)
-    put_box(image, q_center_ref, q_a_ref, q_b_ref)
-    box = add_box(take_box(old_center_ref, old_a_ref, old_b_ref), -alpha, image)
-    put_box(box, center_ref, outer_a_ref, outer_b_ref)
-    solved, dot = solve(box, kbar_ref, into_ref, outof_ref, spectrum_ref)
-    dot_ref[...] = dot
-    keep(new_state_ref, row_r - alpha * row_q, [rz, curv, alpha])
-    new_state_ref[4:5] = row_q
-    send_solved(solved, part_ref, send_in_ref, send_out_ref, send_az_ref)
-
-
-def third_solve_kernel(
-    g_ref, in_ref, out_ref, az_ref, kbar_ref, into_ref, outof_ref, spectrum_ref,
-    old_center_ref, old_a_ref, old_b_ref, q_center_ref, q_a_ref, q_b_ref, sums_ref, state_ref,
-    center_ref, part_ref, send_in_ref, send_out_ref, send_az_ref, new_state_ref, pay_ref,
-):
-    row_w, (local_rz, first_curv, cross) = got_sums(sums_ref, 3)
-    row_r, row_q = state_ref[0:1], state_ref[4:5]
-    rz_before, curv_before = state_ref[1:2, 0:1], state_ref[2:3, 0:1]
-    rz = local_rz + norm(row_r)
-    beta = rz / rz_before
-    curv = first_curv + beta * (2.0 * cross + beta * curv_before)
-    alpha = rz / curv
-    image = got_box(g_ref, in_ref, out_ref, az_ref)
-    image = add_box(image, beta, take_box(q_center_ref, q_a_ref, q_b_ref))
-    box = add_box(take_box(old_center_ref, old_a_ref, old_b_ref), -alpha, image)
-    for a in range(8):
-        center_ref[a] = box[0][a]
-    solved, dot = solve(box, kbar_ref, into_ref, outof_ref, spectrum_ref)
-    keep(new_state_ref, row_r - alpha * (row_w + beta * row_q), [rz, beta, alpha])
-    send_sums(pay_ref, jnp.zeros((1, pay_ref.shape[1]), F32), [total(dot)])
-    send_solved(solved, part_ref, send_in_ref, send_out_ref, send_az_ref)
+def dot_planes(first, second):
+    result = None
+    for e in range(10):
+        stop = 64 if e in (0, 9) else 144
+        term = first[e][:stop] * second[e][:stop]
+        term = jnp.sum(term.reshape(stop // 8, 8, LANES), axis=0)
+        result = term if result is None else result + term
+    return total(result)
 
 
 def first_apply_kernel(
-    part_ref, in_ref, out_ref, az_ref, near_ref, diff_ref, plane_ref, grad_ref, div_ref,
-    sums_ref, dot_ref,
-    z_ref, raw_ref, g_ref, send_in_ref, send_out_ref, send_az_ref, state_ref, pay_ref,
+    part_ref, in_ref, out_ref, early_ref, late_ref, near_ref, diff_ref, plane_ref, grad_ref, div_ref,
+    sums_ref, planes_ref, solved_ref,
+    z_ref, raw_ref, g_ref, send_in_ref, send_out_ref, send_early_ref, send_late_ref, row_ref, pay_ref,
 ):
     row, _ = got_sums(sums_ref, 0)
-    values = add_coarse(got_solved(part_ref, in_ref, out_ref, az_ref), row, near_ref)
+    values = got_solved(part_ref, in_ref, out_ref, early_ref, late_ref)
+    values = add_coarse(values, row, near_ref)
     raw = apply_operator(values, diff_ref, plane_ref, grad_ref, div_ref)
+    send_raw(raw, g_ref, send_in_ref, send_out_ref, send_early_ref, send_late_ref)
     for a in range(8):
         z_ref[a] = values[a]
         raw_ref[a] = raw[a]
-    keep(state_ref, row, [])
-    send_sums(pay_ref, coarse_share(raw, near_ref), [total(dot_ref[...]), dot_parts(values, raw)])
-    send_raw(raw, g_ref, send_in_ref, send_out_ref, send_az_ref)
+    row_ref[0:1] = row
+    scalars = [dot_planes(planes_ref, solved_ref), dot_parts(values, raw)]
+    send_sums(pay_ref, coarse_share(raw, near_ref), scalars)
+
+
+def first_step(sums_ref, row_ref):
+    row_q, (local_rz, curv) = got_sums(sums_ref, 2)
+    row_r = row_ref[0:1]
+    rz = local_rz + norm(row_r)
+    return row_r, row_q, rz, curv, rz / curv
 
 
 def second_apply_kernel(
-    part_ref, in_ref, out_ref, az_ref, near_ref, diff_ref, plane_ref, grad_ref, div_ref,
-    state_ref, dot_ref, old_raw_ref,
-    z_ref, g_ref, send_in_ref, send_out_ref, send_az_ref, pay_ref,
+    part_ref, in_ref, out_ref, early_ref, late_ref, near_ref, diff_ref, plane_ref, grad_ref, div_ref,
+    sums_ref, row_ref, z0_ref,
+    y_ref, z_ref, raw_ref, g_ref, send_in_ref, send_out_ref, send_early_ref, send_late_ref,
 ):
-    row = state_ref[0:1]
-    values = add_coarse(got_solved(part_ref, in_ref, out_ref, az_ref), row, near_ref)
+    _, row_q, _, _, alpha = first_step(sums_ref, row_ref)
+    change = got_solved(part_ref, in_ref, out_ref, early_ref, late_ref)
+    change = add_coarse(change, row_q, near_ref)
+    values = [z0_ref[a] - alpha * change[a] for a in range(8)]
     raw = apply_operator(values, diff_ref, plane_ref, grad_ref, div_ref)
+    send_raw(raw, g_ref, send_in_ref, send_out_ref, send_early_ref, send_late_ref)
     for a in range(8):
+        y_ref[a] = change[a]
         z_ref[a] = values[a]
+        raw_ref[a] = raw[a]
+
+
+def first_dots_kernel(
+    sums_ref, row_ref, near_ref, planes_r_ref, planes_q_ref, solved_r_ref, solved_q_ref,
+    z_ref, raw_ref, old_raw_ref,
+    planes_ref, solved_ref, pay_ref,
+):
+    alpha = first_step(sums_ref, row_ref)[4]
+    planes, solved = [], []
+    for e in range(10):
+        planes.append(planes_r_ref[e] - alpha * planes_q_ref[e])
+        solved.append(solved_r_ref[e] - alpha * solved_q_ref[e])
+        planes_ref[e] = planes[e]
+        solved_ref[e] = solved[e]
+    values = [z_ref[a] for a in range(8)]
+    raw = [raw_ref[a] for a in range(8)]
     scalars = [
-        total(dot_ref[...]),
+        dot_planes(planes, solved),
+        dot_planes(planes, solved_q_ref),
+        dot_planes(planes_q_ref, solved),
+        dot_planes(planes_q_ref, solved_q_ref),
         dot_parts(values, raw),
         dot_parts(values, [old_raw_ref[a] for a in range(8)]),
     ]
     send_sums(pay_ref, coarse_share(raw, near_ref), scalars)
-    send_raw(raw, g_ref, send_in_ref, send_out_ref, send_az_ref)
+
+
+def second_dots_kernel(
+    pay_in_ref, planes_r_ref, planes_q_ref, planes_w_ref, solved_r_ref, solved_q_ref, solved_w_ref,
+    pay_ref,
+):
+    scalars = [
+        dot_planes(planes_r_ref, solved_w_ref),
+        dot_planes(planes_q_ref, solved_w_ref),
+        dot_planes(planes_w_ref, solved_r_ref),
+        dot_planes(planes_w_ref, solved_q_ref),
+        dot_planes(planes_w_ref, solved_w_ref),
+    ]
+    row = pay_in_ref[0:1]
+    width = row.shape[1]
+    place = lax.broadcasted_iota(jnp.int32, (1, width), 1)
+    for k, value in enumerate(scalars):
+        row = jnp.where(place == width - 7 - k, value, row)
+    pay_ref[...] = jnp.broadcast_to(row, pay_ref.shape)
 
 
 def last_kernel(
-    part_ref, in_ref, out_ref, az_ref, near_ref, sums_ref, state_ref, old_state_ref, z0_ref, z1_ref,
-    pressure_ref, direction_ref,
+    part_ref, in_ref, out_ref, early_ref, late_ref, near_ref, sums_ref, old_sums_ref, row_ref,
+    y_ref, z0_ref, z1_ref, planes_r_ref, planes_q_ref, planes_w_ref,
+    pressure_ref, residual_ref, direction_ref,
 ):
-    _, (local_rz,) = got_sums(sums_ref, 1)
-    row = state_ref[0:1]
-    rz_before, beta, alpha = (state_ref[k : k + 1, 0:1] for k in (1, 2, 3))
-    alpha_before = old_state_ref[3:4, 0:1]
-    ratio = (local_rz + norm(row)) / rz_before
-    values = add_coarse(got_solved(part_ref, in_ref, out_ref, az_ref), row, near_ref)
+    row_r, row_q, rz0, curv0, alpha0 = first_step(old_sums_ref, row_ref)
+    row_w, scalars = got_sums(sums_ref, 11)
+    rr, rq, qr, qq, first_curv, cross, rw, qw, wr, wq, ww = scalars
+    row_r = row_r - alpha0 * row_q
+    rz1 = rr + norm(row_r)
+    beta0 = rz1 / rz0
+    curv1 = first_curv + beta0 * (2.0 * cross + beta0 * curv0)
+    alpha1 = rz1 / curv1
+    row = row_w + beta0 * row_q
+    row_r = row_r - alpha1 * row
+    step = -alpha1 * beta0
+    rz2 = (
+        rr
+        - alpha1 * (rw + wr)
+        + step * (rq + qr)
+        + alpha1 * alpha1 * ww
+        - alpha1 * step * (wq + qw)
+        + step * step * qq
+        + norm(row_r)
+    )
+    beta1 = rz2 / rz1
+    change = got_solved(part_ref, in_ref, out_ref, early_ref, late_ref)
+    change = add_coarse(change, row_w, near_ref)
     for a in range(8):
         first = z0_ref[a]
-        second = z1_ref[a] + beta * first
-        pressure_ref[a] = alpha_before * first + alpha * second
-        direction_ref[a] = values[a] + ratio * second
-
-
-def kernel_call(kernel, out_shapes, *args):
+        second = z1_ref[a] + beta0 * first
+        image = planes_w_ref[a + 1, :64] + beta0 * planes_q_ref[a + 1, :64]
+        residual_ref[a] = planes_r_ref[a + 1, :64] - alpha1 * image
+        pressure_ref[a] = alpha0 * first + alpha1 * second
+        direction_ref[a] = (
+            z1_ref[a] - alpha1 * (change[a] + beta0 * y_ref[a]) + beta1 * second
+        )
+
+
+def kernel_call(kernel, out_shapes, *args, **options):
     outs = [jax.ShapeDtypeStruct(shape, F32) for shape in out_shapes]
     return pl.pallas_call(
         kernel,
         out_shape=outs,
         compiler_params=pltpu.CompilerParams(vmem_limit_bytes=VMEM_GRANT),
         interpret=INTERPRET,
+        **options,
     )(*args)
 
 
@@ -772,75 +830,81 @@
     plane, over, spectrum = tables["plane"], tables["over"], tables["spectrum"]
     grad, div, into, outof = tables["grad"], tables["div"], tables["into"], tables["outof"]
     coarse_size = coarse_factor.shape[1]
-    width = -(-(coarse_size + 4) // LANES)
+    width = -(-(coarse_size + TAIL) // LANES)
     count = 8 * -(-width // 8)
-    row = jnp.pad(coarse_factor[0], (0, count * LANES - coarse_size)).reshape(count, LANES)
-
-    field, sums, state = (8, 64, LANES), (devices, width * LANES), (8, width * LANES)
-    box = [field, (2, 64, LANES), (8, 16, LANES)]
-    raw_sends = [(128, LANES), (128, LANES), (2, 144, LANES)]
-    solved_sends = [(144, LANES), (144, LANES), (2, 128, LANES)]
-
-    conv, kbar, inner, outer, azim = kernel_call(
+
+    field, sums, row_shape = (8, 64, LANES), (devices, width * LANES), (8, width * LANES)
+    boxes = [(10, 144, LANES), (10, 144, LANES)]
+    raw_sends = [(128, LANES), (128, LANES), (2, 96, LANES), (2, 32, LANES)]
+    solved_sends = [(144, LANES), (144, LANES), (2, 80, LANES), (2, 48, LANES)]
+
+    far = pl.BlockSpec(memory_space=pltpu.HBM)
+    conv, row, *sends = kernel_call(
         conv_kernel,
-        [(3,) + field, (8, LANES), (192 + count, LANES), (192 + count, LANES), (2, 192, LANES)],
-        u, diff, row, plane, grad,
-    )
-    inner, outer = axial_swap(inner, outer)
-    (azim,) = kernel_call(conv_side_kernel, [(2, 192 + 3 * count, LANES)], inner, outer, azim, row)
-    azim = azim_swap(azim)
-    g, send_in, send_out, send_az, near, pay = kernel_call(
+        [(3,) + field, (count, LANES), (192 + count, LANES), (192 + count, LANES)]
+        + [(2, 144, LANES), (2, 48, LANES)],
+        u, coarse_factor, plane, grad,
+        in_specs=[far] * 4,
+        scratch_shapes=[
+            pltpu.VMEM((3,) + field, F32),
+            pltpu.VMEM((1, coarse_size), F32),
+            pltpu.VMEM(plane.shape, F32),
+            pltpu.VMEM(grad.shape, BF16),
+            pltpu.SemaphoreType.DMA((4,)),
+        ],
+    )
+    (kbar,) = kernel_call(mean_kernel, [(8, LANES)], diff)
+
+    def exchange(side_kernel, late_rows, send_in, send_out, send_early, send_late, *more):
+        inner, outer = axial_swap(send_in, send_out)
+        early = azim_swap(send_early)
+        (late,) = kernel_call(side_kernel, [(2, late_rows, LANES)], inner, outer, send_late, *more)
+        return inner, outer, early, azim_swap(late)
+
+    moved = exchange(conv_side_kernel, 48 + 3 * count, *sends, row)
+    g, *sends, near, pay = kernel_call(
         divergence_kernel,
         [field] + raw_sends + [(16, width * LANES), sums],
-        conv, u, inner, outer, azim, row, plane, over, div,
-    )
-
-    def finish_raw(send_in, send_out, send_az, pay):
-        inner, outer = axial_swap(send_in, send_out)
-        pay = gather_sums(pay)
-        (azim,) = kernel_call(raw_side_kernel, [(2, 144, LANES)], inner, outer, send_az)
-        return inner, outer, azim_swap(azim), pay
-
-    def finish_solved(send_in, send_out, send_az):
-        inner, outer = axial_swap(send_in, send_out)
-        (azim,) = kernel_call(solved_side_kernel, [(2, 128, LANES)], inner, outer, send_az)
-        return inner, outer, azim_swap(azim)
-
+        conv, u, *moved, row, plane, over, div,
+    )
     solver = (kbar, into, outof, spectrum)
     operator = (near, diff, plane, grad, div)
-    inner, outer, azim, pay = finish_raw(send_in, send_out, send_az, pay)
-    *old, part, send_in, send_out, send_az, dot = kernel_call(
-        first_solve_kernel,
-        box + [field] + solved_sends + [(8, LANES)],
-        g, inner, outer, azim, *solver,
-    )
-    moved = finish_solved(send_in, send_out, send_az)
-    z0, raw0, g, send_in, send_out, send_az, state0, pay = kernel_call(
+    solve_shapes = boxes + [field] + solved_sends
+
+    moved = exchange(raw_side_kernel, 48, *sends)
+    pay = gather_sums(pay)
+    planes_r, solved_r, part, *sends = kernel_call(solve_kernel, solve_shapes, g, *moved, *solver)
+    moved = exchange(solved_side_kernel, 48, *sends)
+    z0, raw0, g, *sends, row_r, pay = kernel_call(
         first_apply_kernel,
-        [field, field, field] + raw_sends + [state, sums],
-        part, *moved, *operator, pay, dot,
-    )
-    inner, outer, azim, pay = finish_raw(send_in, send_out, send_az, pay)
-    *new, part, send_in, send_out, send_az, dot, state1 = kernel_call(
-        second_solve_kernel,
-        box + box + [field] + solved_sends + [(8, LANES), state],
-        g, inner, outer, azim, *solver, *old, pay, state0,
-    )
-    moved = finish_solved(send_in, send_out, send_az)
-    z1, g, send_in, send_out, send_az, pay = kernel_call(
+        [field, field, field] + raw_sends + [row_shape, sums],
+        part, *moved, *operator, pay, planes_r, solved_r,
+    )
+    moved = exchange(raw_side_kernel, 48, *sends)
+    first_sums = gather_sums(pay)
+    planes_q, solved_q, part, *sends = kernel_call(solve_kernel, solve_shapes, g, *moved, *solver)
+    moved = exchange(solved_side_kernel, 48, *sends)
+    y, z1, raw1, g, *sends = kernel_call(
         second_apply_kernel,
-        [field, field] + raw_sends + [sums],
-        part, *moved, *operator, state1, dot, raw0,
-    )
-    inner, outer, azim, pay = finish_raw(send_in, send_out, send_az, pay)
-    residual, part, send_in, send_out, send_az, state2, pay = kernel_call(
-        third_solve_kernel,
-        [field, field] + solved_sends + [state, sums],
-        g, inner, outer, azim, *solver, *new, pay, state1,
-    )
-    moved = finish_solved(send_in, send_out, send_az)
-    pressure, direction = kernel_call(
-        last_kernel, [field, field], part, *moved, near, gather_sums(pay), state2, state1, z0, z1
+        [field, field, field, field] + raw_sends,
+        part, *moved, *operator, first_sums, row_r, z0,
+    )
+    planes_r, solved_r, pay = kernel_call(
+        first_dots_kernel,
+        boxes + [sums],
+        first_sums, row_r, near, planes_r, planes_q, solved_r, solved_q, z1, raw1, raw0,
+    )
+    moved = exchange(raw_side_kernel, 48, *sends)
+    planes_w, solved_w, part, *sends = kernel_call(solve_kernel, solve_shapes, g, *moved, *solver)
+    (pay,) = kernel_call(
+        second_dots_kernel, [sums], pay, planes_r, planes_q, planes_w, solved_r, solved_q, solved_w
+    )
+    moved = exchange(solved_side_kernel, 48, *sends)
+    pressure, residual, direction = kernel_call(
+        last_kernel,
+        [field, field, field],
+        part, *moved, near, gather_sums(pay), first_sums, row_r,
+        y, z0, z1, planes_r, planes_q, planes_w,
     )
     return pressure.reshape(shape), residual.reshape(shape), direction.reshape(shape)
 

time: 118 us -> 109 us (0.924)
  blocking collectives: 36.1 us -> 27 us
  waiting for transfers between devices: 45.9 us -> 40.1 us
  starting transfers between devices: 21.6 us -> 27.3 us
  Pallas kernels: 8.94 us -> 10.3 us
    all_to_all x4 -> x3, blocking collectives: 36.1 us -> 27 us  [gather_sums(): return lax.all_to_all(rows, ALL, 0, 0, tiled=True)]
    ppermute x7 -> x14, starting transfers between devices: 7.05 us -> 13.8 us  [azim_swap(): return lax.ppermute(sides, 'azim', [(0, 1), (1, 0)])]
    ppermute x7, waiting for transfers between devices: 30.3 us -> 26.2 us  [axial_swap(): from_outer = lax.ppermute(outer_rows, 'axial', outer)]
    ppermute x7, waiting for transfers between devices: 3.03 us -> 1.35 us  [axial_swap(): from_inner = lax.ppermute(inner_rows, 'axial', inner)]
    pallas_call x15 -> x18, Pallas kernels: 8.94 us -> 10.3 us  [kernel_call(): pl.pallas_call(kernel, out_shape=outs, compiler_params=pltpu.CompilerPara...]
    unnamed x28 -> x26, local copies, waits for them, and re-layouts: 4.36 us -> 3.41 us
    ppermute x7 -> x14, waiting for transfers between devices: 12.5 us -> 12.6 us  [azim_swap(): return lax.ppermute(sides, 'azim', [(0, 1), (1, 0)])]
  transfers between devices with their start and end apart: 21 -> 28, of which waited for: 14 -> 17; matrix products, arithmetic and copies ran while one was open for 0% -> 0% of each run, Pallas kernels for 0% -> 1%
where the time goes in v1:
time: 109 us
  waiting for transfers between devices  40.1 us (37%)
  starting transfers between devices  27.3 us (25%)
  blocking collectives  27 us (25%)
  Pallas kernels  10.3 us (9%)
  local copies, waits for them, and re-layouts  3.41 us (3%)
    all_to_all x3, blocking collectives, gather_sums(): return lax.all_to_all(rows, ALL, 0, 0, tiled=True)  27 us
    ppermute x7, waiting for transfers between devices, axial_swap(): from_outer = lax.ppermute(outer_rows, 'axial', outer)  26.2 us
    ppermute x14, starting transfers between devices, azim_swap(): return lax.ppermute(sides, 'azim', [(0, 1), (1, 0)])  13.8 us
    ppermute x7, starting transfers between devices, axial_swap(): from_outer = lax.ppermute(outer_rows, 'axial', outer)  12.6 us
    ppermute x14, waiting for transfers between devices, azim_swap(): return lax.ppermute(sides, 'azim', [(0, 1), (1, 0)])  12.6 us
    pallas_call x18, Pallas kernels, kernel_call(): pl.pallas_call(kernel, out_shape=outs, compiler_params=pltpu.CompilerPara...  10.3 us
    unnamed x26, local copies, waits for them, and re-layouts  3.41 us
  transfers between devices with their start and end apart: 28, of which 17 were waited for; matrix products, arithmetic and copies ran while one was open for 0% of the time, Pallas kernels for 1%

profile of v1, /device:TPU:0, one launch (start us, length us, event | category | flops | bytes accessed | tf_op | source)
XLA Modules:
  0.0 109.0 jit_solution(2061303686074690859)
XLA Ops:
  1.3 1.1 %copy-done = f32[3,8,8,8,1,1,128]{6,5,4,3,2,1,0:T(1,128)S(1)} copy-done((f32[3,8,8,8,1,1,128]{6,5,4,3,2,1,0:T(1,128)S(1)}, f32[3,8,8,8,1,1,128]{6,5,4,3,2,1,0:T(1,128)}, u32[]{:S(2)}) %copy-start) | copy-done | bytes 786456
  2.4 0.8 copy-done.5
  4.0 1.1 %shard_map.121 = (f32[3,8,64,128]{3,2,1,0:T(8,128)S(1)}, f32[8,128]{1,0:T(8,128)S(1)}, f32[200,128]{1,0:T(8,128)S(1)}, f32[200,128]{1,0:T(8,128)S(1)}, f32[2,144...) custom-call(f32[3,8,64,128]{3,2,1,0:T(8,128)S(1)} %bitcast.23, f32[1,32]{1,0:T(1,128)S(1)} %copy-done.12, ...), custom_call_target="tpu_custom_call" | custom-call | tf_op jit(solution)/shard_map/pallas_call | solution.py:792
  5.7 5.6 %collective-permute-start.1 = (f32[200,128]{1,0:T(8,128)S(1)}, f32[200,128]{1,0:T(8,128)S(1)}, u32[]{:S(2)}, u32[]{:S(2)}) collective-permute-start(f32[200,128]{1,0:T(8,128)S(1)} %get-tuple-element.62), channel_id=1, source_target_pairs={{2,4},{6,8},{10,12},{14,16},{18,20},{22,24},{26,28},{30,0},{4,2},{... | collective-permute-start | bytes 307208 | tf_op jit(solution)/shard_map/ppermute | solution.py:806
  11.3 1.5 %collective-permute-start.2 = (f32[2,144,128]{2,1,0:T(8,128)S(1)}, f32[2,144,128]{2,1,0:T(8,128)S(1)}, u32[]{:S(2)}, u32[]{:S(2)}) collective-permute-start(f32[2,144,128]{2,1,0:T(8,128)S(1)} %get-tuple-element.63), channel_id=1, source_target_pairs={{0,1},{1,0},{2,3},{3,2},{4,5},{5,4},{6,7},{7,6},{8,9},{9,8},{10,11... | collective-permute-start | bytes 442376 | tf_op jit(solution)/shard_map/ppermute | solution.py:814
  12.8 0.8 collective-permute-done.1.out_ref
  13.7 1.6 %collective-permute-start.3 = (f32[2,72,128]{2,1,0:T(8,128)S(1)}, f32[2,72,128]{2,1,0:T(8,128)S(1)}, u32[]{:S(2)}, u32[]{:S(2)}) collective-permute-start(f32[2,72,128]{2,1,0:T(8,128)S(1)} %shard_map.122), channel_id=1, source_target_pairs={{0,1},{1,0},{2,3},{3,2},{4,5},{5,4},{6,7},{7,6},{8,9},{9,8},{10,11... | collective-permute-start | bytes 221192 | tf_op jit(solution)/shard_map/ppermute | solution.py:814
  15.3 1.2 %collective-permute-done.2.early_ref = f32[2,144,128]{2,1,0:T(8,128)S(1)} collective-permute-done((f32[2,144,128]{2,1,0:T(8,128)S(1)}, f32[2,144,128]{2,1,0:T(8,128)S(1)}, u32[]{:S(2)}, u32[]{:S(2)}) %collective-permute-start.2) | collective-permute-done | bytes 147488 | tf_op jit(solution)/shard_map/ppermute | solution.py:814
  16.5 1.6 %collective-permute-done.3.late_ref = f32[2,72,128]{2,1,0:T(8,128)S(1)} collective-permute-done((f32[2,72,128]{2,1,0:T(8,128)S(1)}, f32[2,72,128]{2,1,0:T(8,128)S(1)}, u32[]{:S(2)}, u32[]{:S(2)}) %collective-permute-start.3) | collective-permute-done | bytes 73760 | tf_op jit(solution)/shard_map/ppermute | solution.py:814
  18.8 3.4 %collective-permute-start.5 = (f32[128,128]{1,0:T(8,128)S(1)}, f32[128,128]{1,0:T(8,128)S(1)}, u32[]{:S(2)}, u32[]{:S(2)}) collective-permute-start(f32[128,128]{1,0:T(8,128)S(1)} %get-tuple-element.68), channel_id=1, source_target_pairs={{2,4},{6,8},{10,12},{14,16},{18,20},{22,24},{26,28},{30,0},{4,2},{... | collective-permute-start | bytes 196616 | tf_op jit(solution)/shard_map/ppermute | solution.py:806
  22.1 1.5 %collective-permute-start.6 = (f32[2,96,128]{2,1,0:T(8,128)S(1)}, f32[2,96,128]{2,1,0:T(8,128)S(1)}, u32[]{:S(2)}, u32[]{:S(2)}) collective-permute-start(f32[2,96,128]{2,1,0:T(8,128)S(1)} %get-tuple-element.69), channel_id=1, source_target_pairs={{0,1},{1,0},{2,3},{3,2},{4,5},{5,4},{6,7},{7,6},{8,9},{9,8},{10,11... | collective-permute-start | bytes 294920 | tf_op jit(solution)/shard_map/ppermute | solution.py:814
  23.6 1.6 %collective-permute-done.5.out_ref = f32[128,128]{1,0:T(8,128)S(1)} collective-permute-done((f32[128,128]{1,0:T(8,128)S(1)}, f32[128,128]{1,0:T(8,128)S(1)}, u32[]{:S(2)}, u32[]{:S(2)}) %collective-permute-start.5) | collective-permute-done | bytes 65568 | tf_op jit(solution)/shard_map/ppermute | solution.py:806
  25.2 1.6 %collective-permute-start.7 = (f32[2,48,128]{2,1,0:T(8,128)S(1)}, f32[2,48,128]{2,1,0:T(8,128)S(1)}, u32[]{:S(2)}, u32[]{:S(2)}) collective-permute-start(f32[2,48,128]{2,1,0:T(8,128)S(1)} %shard_map.124), channel_id=1, source_target_pairs={{0,1},{1,0},{2,3},{3,2},{4,5},{5,4},{6,7},{7,6},{8,9},{9,8},{10,11... | collective-permute-start | bytes 147464 | tf_op jit(solution)/shard_map/ppermute | solution.py:814
  27.2 2.2 %collective-permute-done.7.late_ref = f32[2,48,128]{2,1,0:T(8,128)S(1)} collective-permute-done((f32[2,48,128]{2,1,0:T(8,128)S(1)}, f32[2,48,128]{2,1,0:T(8,128)S(1)}, u32[]{:S(2)}, u32[]{:S(2)}) %collective-permute-start.7) | collective-permute-done | bytes 49184 | tf_op jit(solution)/shard_map/ppermute | solution.py:814
  29.4 1.5 %shard_map.126 = (f32[10,144,128]{2,1,0:T(8,128)S(1)}, f32[10,144,128]{2,1,0:T(8,128)S(1)}, f32[8,64,128]{2,1,0:T(8,128)S(1)}, f32[144,128]{1,0:T(8,128)S(1)}, f...) custom-call(f32[8,64,128]{2,1,0:T(8,128)S(1)} %get-tuple-element.66.g_ref, ...), custom_call_target="tpu_custom_call" | custom-call | tf_op jit(solution)/shard_map/pallas_call | solution.py:792
  31.0 2.2 %collective-permute-start.9 = (f32[144,128]{1,0:T(8,128)S(1)}, f32[144,128]{1,0:T(8,128)S(1)}, u32[]{:S(2)}, u32[]{:S(2)}) collective-permute-start(f32[144,128]{1,0:T(8,128)S(1)} %get-tuple-element.73), channel_id=1, source_target_pairs={{2,4},{6,8},{10,12},{14,16},{18,20},{22,24},{26,28},{30,0},{4,2},{... | collective-permute-start | bytes 221192 | tf_op jit(solution)/shard_map/ppermute | solution.py:806
  33.2 1.5 %collective-permute-start.10 = (f32[2,80,128]{2,1,0:T(8,128)S(1)}, f32[2,80,128]{2,1,0:T(8,128)S(1)}, u32[]{:S(2)}, u32[]{:S(2)}) collective-permute-start(f32[2,80,128]{2,1,0:T(8,128)S(1)} %get-tuple-element.74), channel_id=1, source_target_pairs={{0,1},{1,0},{2,3},{3,2},{4,5},{5,4},{6,7},{7,6},{8,9},{9,8},{10,11... | collective-permute-start | bytes 245768 | tf_op jit(solution)/shard_map/ppermute | solution.py:814
  34.7 2.8 %collective-permute-done.9.out_ref = f32[144,128]{1,0:T(8,128)S(1)} collective-permute-done((f32[144,128]{1,0:T(8,128)S(1)}, f32[144,128]{1,0:T(8,128)S(1)}, u32[]{:S(2)}, u32[]{:S(2)}) %collective-permute-start.9) | collective-permute-done | bytes 73760 | tf_op jit(solution)/shard_map/ppermute | solution.py:806
  37.5 1.6 %collective-permute-start.11 = (f32[2,48,128]{2,1,0:T(8,128)S(1)}, f32[2,48,128]{2,1,0:T(8,128)S(1)}, u32[]{:S(2)}, u32[]{:S(2)}) collective-permute-start(f32[2,48,128]{2,1,0:T(8,128)S(1)} %shard_map.127), channel_id=1, source_target_pairs={{0,1},{1,0},{2,3},{3,2},{4,5},{5,4},{6,7},{7,6},{8,9},{9,8},{10,11... | collective-permute-start | bytes 147464 | tf_op jit(solution)/shard_map/ppermute | solution.py:814
  39.1 9.2 %all_to_all.33 = f32[32,1,128]{2,1,0:T(1,128)S(1)} all-to-all(f32[32,1,128]{2,1,0:T(1,128)S(1)} %bitcast.34), channel_id=1, replica_groups=mesh['axial'=16,'azim'=2] {'axial','azim'}, dimensions={0} | all-to-all | bytes 32768 | tf_op jit(solution)/shard_map/all_to_all | solution.py:821
  48.3 0.9 shard_map.128
  50.6 5.2 %collective-permute-done.13.out_ref = f32[128,128]{1,0:T(8,128)S(1)} collective-permute-done((f32[128,128]{1,0:T(8,128)S(1)}, f32[128,128]{1,0:T(8,128)S(1)}, u32[]{:S(2)}, u32[]{:S(2)}) %collective-permute-start.13) | collective-permute-done | bytes 65568 | tf_op jit(solution)/shard_map/ppermute | solution.py:806
  56.4 3.6 %collective-permute-done.15.late_ref = f32[2,48,128]{2,1,0:T(8,128)S(1)} collective-permute-done((f32[2,48,128]{2,1,0:T(8,128)S(1)}, f32[2,48,128]{2,1,0:T(8,128)S(1)}, u32[]{:S(2)}, u32[]{:S(2)}) %collective-permute-start.15) | collective-permute-done | bytes 49184 | tf_op jit(solution)/shard_map/ppermute | solution.py:814
  59.9 1.5 %shard_map.130 = (f32[10,144,128]{2,1,0:T(8,128)S(1)}, f32[10,144,128]{2,1,0:T(8,128)S(1)}, f32[8,64,128]{2,1,0:T(8,128)S(1)}, f32[144,128]{1,0:T(8,128)S(1)}, f...) custom-call(f32[8,64,128]{2,1,0:T(8,128)S(1)} %get-tuple-element.80.g_ref, ...), custom_call_target="tpu_custom_call" | custom-call | tf_op jit(solution)/shard_map/pallas_call | solution.py:792
  62.8 5.3 %collective-permute-done.17.out_ref = f32[144,128]{1,0:T(8,128)S(1)} collective-permute-done((f32[144,128]{1,0:T(8,128)S(1)}, f32[144,128]{1,0:T(8,128)S(1)}, u32[]{:S(2)}, u32[]{:S(2)}) %collective-permute-start.17) | collective-permute-done | bytes 73760 | tf_op jit(solution)/shard_map/ppermute | solution.py:806
  68.6 8.9 %all_to_all.34 = f32[32,1,128]{2,1,0:T(1,128)S(1)} all-to-all(f32[32,1,128]{2,1,0:T(1,128)S(1)} %bitcast.35), channel_id=1, replica_groups=mesh['axial'=16,'azim'=2] {'axial','azim'}, dimensions={0} | all-to-all | bytes 32768 | tf_op jit(solution)/shard_map/all_to_all | solution.py:821
  79.6 5.2 %collective-permute-done.21.out_ref = f32[128,128]{1,0:T(8,128)S(1)} collective-permute-done((f32[128,128]{1,0:T(8,128)S(1)}, f32[128,128]{1,0:T(8,128)S(1)}, u32[]{:S(2)}, u32[]{:S(2)}) %collective-permute-start.21) | collective-permute-done | bytes 65568 | tf_op jit(solution)/shard_map/ppermute | solution.py:806
  85.4 3.6 %collective-permute-done.23.late_ref = f32[2,48,128]{2,1,0:T(8,128)S(1)} collective-permute-done((f32[2,48,128]{2,1,0:T(8,128)S(1)}, f32[2,48,128]{2,1,0:T(8,128)S(1)}, u32[]{:S(2)}, u32[]{:S(2)}) %collective-permute-start.23) | collective-permute-done | bytes 49184 | tf_op jit(solution)/shard_map/ppermute | solution.py:814
  89.0 1.5 %shard_map.134 = (f32[10,144,128]{2,1,0:T(8,128)S(1)}, f32[10,144,128]{2,1,0:T(8,128)S(1)}, f32[8,64,128]{2,1,0:T(8,128)S(1)}, f32[144,128]{1,0:T(8,128)S(1)}, f...) custom-call(f32[8,64,128]{2,1,0:T(8,128)S(1)} %get-tuple-element.93.g_ref, ...), custom_call_target="tpu_custom_call" | custom-call | tf_op jit(solution)/shard_map/pallas_call | solution.py:792
  91.8 5.3 %collective-permute-done.25.out_ref = f32[144,128]{1,0:T(8,128)S(1)} collective-permute-done((f32[144,128]{1,0:T(8,128)S(1)}, f32[144,128]{1,0:T(8,128)S(1)}, u32[]{:S(2)}, u32[]{:S(2)}) %collective-permute-start.25) | collective-permute-done | bytes 73760 | tf_op jit(solution)/shard_map/ppermute | solution.py:806
  98.9 8.9 %all_to_all.35 = f32[32,1,128]{2,1,0:T(1,128)S(1)} all-to-all(f32[32,1,128]{2,1,0:T(1,128)S(1)} %bitcast.33), channel_id=1, replica_groups=mesh['axial'=16,'azim'=2] {'axial','azim'}, dimensions={0} | all-to-all | bytes 32768 | tf_op jit(solution)/shard_map/all_to_all | solution.py:821
  107.9 1.1 %shard_map.138 = (f32[8,64,128]{2,1,0:T(8,128)}, f32[8,64,128]{2,1,0:T(8,128)}, f32[8,64,128]{2,1,0:T(8,128)}) custom-call(f32[8,64,128]{2,1,0:T(8,128)S(1)} %get-tuple-element.98.part_ref, f32[144,128]{1,0:T(8,128)S(1)} %collective-permute-done.24.in_ref, f32[144,128]{1,0:T(8,128)S(1)} %collective-permute-done.25.out_ref, ...), custom_call_target="tpu_custom_call" | custom-call | tf_op jit(solution)/shard_map/pallas_call | solution.py:792
  (71 shorter events, 12.7 us)
Async XLA Ops:
  4.0 14.1 %copy-start.1 = (f32[3,8,8,8,1,1,128]{6,5,4,3,2,1,0:T(1,128)S(1)}, f32[3,8,8,8,1,1,128]{6,5,4,3,2,1,0:T(1,128)}, u32[]{:S(2)}) copy-start(f32[3,8,8,8,1,1,128]{6,5,4,3,2,1,0:T(1,128)} %param.10) | copy-start | bytes 2359300
  5.2 7.7 %collective-permute-start = (f32[200,128]{1,0:T(8,128)S(1)}, f32[200,128]{1,0:T(8,128)S(1)}, u32[]{:S(2)}, u32[]{:S(2)}) collective-permute-start(f32[200,128]{1,0:T(8,128)S(1)} %get-tuple-element.61), channel_id=1, source_target_pairs={{0,2},{2,0},{4,6},{6,4},{8,10},{10,8},{12,14},{14,12},{16,18},{18,... | collective-permute-start | bytes 307208 | tf_op jit(solution)/shard_map/ppermute | solution.py:807
  5.7 8.0 %collective-permute-start.1 = (f32[200,128]{1,0:T(8,128)S(1)}, f32[200,128]{1,0:T(8,128)S(1)}, u32[]{:S(2)}, u32[]{:S(2)}) collective-permute-start(f32[200,128]{1,0:T(8,128)S(1)} %get-tuple-element.62), channel_id=1, source_target_pairs={{2,4},{6,8},{10,12},{14,16},{18,20},{22,24},{26,28},{30,0},{4,2},{... | collective-permute-start | bytes 307208 | tf_op jit(solution)/shard_map/ppermute | solution.py:806
  11.3 5.1 %collective-permute-start.2 = (f32[2,144,128]{2,1,0:T(8,128)S(1)}, f32[2,144,128]{2,1,0:T(8,128)S(1)}, u32[]{:S(2)}, u32[]{:S(2)}) collective-permute-start(f32[2,144,128]{2,1,0:T(8,128)S(1)} %get-tuple-element.63), channel_id=1, source_target_pairs={{0,1},{1,0},{2,3},{3,2},{4,5},{5,4},{6,7},{7,6},{8,9},{9,8},{10,11... | collective-permute-start | bytes 442376 | tf_op jit(solution)/shard_map/ppermute | solution.py:814
  13.7 4.5 %copy-start.11 = (f32[64,128]{1,0:T(8,128)S(1)}, f32[64,128]{1,0:T(8,128)}, u32[]{:S(2)}) copy-start(f32[64,128]{1,0:T(8,128)} %constant.15.clone.over_ref) | copy-start | bytes 98308
  13.7 4.4 %collective-permute-start.3 = (f32[2,72,128]{2,1,0:T(8,128)S(1)}, f32[2,72,128]{2,1,0:T(8,128)S(1)}, u32[]{:S(2)}, u32[]{:S(2)}) collective-permute-start(f32[2,72,128]{2,1,0:T(8,128)S(1)} %shard_map.122), channel_id=1, source_target_pairs={{0,1},{1,0},{2,3},{3,2},{4,5},{5,4},{6,7},{7,6},{8,9},{9,8},{10,11... | collective-permute-start | bytes 221192 | tf_op jit(solution)/shard_map/ppermute | solution.py:814
  18.1 8.7 %copy-start.2 = (f32[8,8,8,1,1,128]{5,4,3,2,1,0:T(1,128)S(1)}, f32[8,8,8,1,1,128]{5,4,3,2,1,0:T(1,128)}, u32[]{:S(2)}) copy-start(f32[8,8,8,1,1,128]{5,4,3,2,1,0:T(1,128)} %param.11) | copy-start | bytes 786436
  18.7 5.0 %collective-permute-start.4 = (f32[128,128]{1,0:T(8,128)S(1)}, f32[128,128]{1,0:T(8,128)S(1)}, u32[]{:S(2)}, u32[]{:S(2)}) collective-permute-start(f32[128,128]{1,0:T(8,128)S(1)} %get-tuple-element.67), channel_id=1, source_target_pairs={{0,2},{2,0},{4,6},{6,4},{8,10},{10,8},{12,14},{14,12},{16,18},{18,... | collective-permute-start | bytes 196616 | tf_op jit(solution)/shard_map/ppermute | solution.py:807
  18.8 6.5 %collective-permute-start.5 = (f32[128,128]{1,0:T(8,128)S(1)}, f32[128,128]{1,0:T(8,128)S(1)}, u32[]{:S(2)}, u32[]{:S(2)}) collective-permute-start(f32[128,128]{1,0:T(8,128)S(1)} %get-tuple-element.68), channel_id=1, source_target_pairs={{2,4},{6,8},{10,12},{14,16},{18,20},{22,24},{26,28},{30,0},{4,2},{... | collective-permute-start | bytes 196616 | tf_op jit(solution)/shard_map/ppermute | solution.py:806
  22.1 5.1 %collective-permute-start.6 = (f32[2,96,128]{2,1,0:T(8,128)S(1)}, f32[2,96,128]{2,1,0:T(8,128)S(1)}, u32[]{:S(2)}, u32[]{:S(2)}) collective-permute-start(f32[2,96,128]{2,1,0:T(8,128)S(1)} %get-tuple-element.69), channel_id=1, source_target_pairs={{0,1},{1,0},{2,3},{3,2},{4,5},{5,4},{6,7},{7,6},{8,9},{9,8},{10,11... | collective-permute-start | bytes 294920 | tf_op jit(solution)/shard_map/ppermute | solution.py:814
  25.2 4.2 %collective-permute-start.7 = (f32[2,48,128]{2,1,0:T(8,128)S(1)}, f32[2,48,128]{2,1,0:T(8,128)S(1)}, u32[]{:S(2)}, u32[]{:S(2)}) collective-permute-start(f32[2,48,128]{2,1,0:T(8,128)S(1)} %shard_map.124), channel_id=1, source_target_pairs={{0,1},{1,0},{2,3},{3,2},{4,5},{5,4},{6,7},{7,6},{8,9},{9,8},{10,11... | collective-permute-start | bytes 147464 | tf_op jit(solution)/shard_map/ppermute | solution.py:814
  30.9 3.8 %collective-permute-start.8 = (f32[144,128]{1,0:T(8,128)S(1)}, f32[144,128]{1,0:T(8,128)S(1)}, u32[]{:S(2)}, u32[]{:S(2)}) collective-permute-start(f32[144,128]{1,0:T(8,128)S(1)} %get-tuple-element.72), channel_id=1, source_target_pairs={{0,2},{2,0},{4,6},{6,4},{8,10},{10,8},{12,14},{14,12},{16,18},{18,... | collective-permute-start | bytes 221192 | tf_op jit(solution)/shard_map/ppermute | solution.py:807
  31.0 6.5 %collective-permute-start.9 = (f32[144,128]{1,0:T(8,128)S(1)}, f32[144,128]{1,0:T(8,128)S(1)}, u32[]{:S(2)}, u32[]{:S(2)}) collective-permute-start(f32[144,128]{1,0:T(8,128)S(1)} %get-tuple-element.73), channel_id=1, source_target_pairs={{2,4},{6,8},{10,12},{14,16},{18,20},{22,24},{26,28},{30,0},{4,2},{... | collective-permute-start | bytes 221192 | tf_op jit(solution)/shard_map/ppermute | solution.py:806
  33.2 15.2 %collective-permute-start.10 = (f32[2,80,128]{2,1,0:T(8,128)S(1)}, f32[2,80,128]{2,1,0:T(8,128)S(1)}, u32[]{:S(2)}, u32[]{:S(2)}) collective-permute-start(f32[2,80,128]{2,1,0:T(8,128)S(1)} %get-tuple-element.74), channel_id=1, source_target_pairs={{0,1},{1,0},{2,3},{3,2},{4,5},{5,4},{6,7},{7,6},{8,9},{9,8},{10,11... | collective-permute-start | bytes 245768 | tf_op jit(solution)/shard_map/ppermute | solution.py:814
  37.5 10.8 %copy-start.6 = (bf16[128,192]{1,0:T(8,128)(2,1)S(1)}, bf16[128,192]{1,0:T(8,128)(2,1)}, u32[]{:S(2)}) copy-start(bf16[128,192]{1,0:T(8,128)(2,1)} %constant.17.clone.grad_hbm.grad_ref) | copy-start | bytes 147460
  37.5 10.8 %collective-permute-start.11 = (f32[2,48,128]{2,1,0:T(8,128)S(1)}, f32[2,48,128]{2,1,0:T(8,128)S(1)}, u32[]{:S(2)}, u32[]{:S(2)}) collective-permute-start(f32[2,48,128]{2,1,0:T(8,128)S(1)} %shard_map.127), channel_id=1, source_target_pairs={{0,1},{1,0},{2,3},{3,2},{4,5},{5,4},{6,7},{7,6},{8,9},{9,8},{10,11... | collective-permute-start | bytes 147464 | tf_op jit(solution)/shard_map/ppermute | solution.py:814
  49.2 1.3 %collective-permute-start.12 = (f32[128,128]{1,0:T(8,128)S(1)}, f32[128,128]{1,0:T(8,128)S(1)}, u32[]{:S(2)}, u32[]{:S(2)}) collective-permute-start(f32[128,128]{1,0:T(8,128)S(1)} %get-tuple-element.81), channel_id=1, source_target_pairs={{0,2},{2,0},{4,6},{6,4},{8,10},{10,8},{12,14},{14,12},{16,18},{18,... | collective-permute-start | bytes 196616 | tf_op jit(solution)/shard_map/ppermute | solution.py:807
  49.3 6.5 %collective-permute-start.13 = (f32[128,128]{1,0:T(8,128)S(1)}, f32[128,128]{1,0:T(8,128)S(1)}, u32[]{:S(2)}, u32[]{:S(2)}) collective-permute-start(f32[128,128]{1,0:T(8,128)S(1)} %get-tuple-element.82), channel_id=1, source_target_pairs={{2,4},{6,8},{10,12},{14,16},{18,20},{22,24},{26,28},{30,0},{4,2},{... | collective-permute-start | bytes 196616 | tf_op jit(solution)/shard_map/ppermute | solution.py:806
  50.0 6.4 %collective-permute-start.14 = (f32[2,96,128]{2,1,0:T(8,128)S(1)}, f32[2,96,128]{2,1,0:T(8,128)S(1)}, u32[]{:S(2)}, u32[]{:S(2)}) collective-permute-start(f32[2,96,128]{2,1,0:T(8,128)S(1)} %get-tuple-element.83), channel_id=1, source_target_pairs={{0,1},{1,0},{2,3},{3,2},{4,5},{5,4},{6,7},{7,6},{8,9},{9,8},{10,11... | collective-permute-start | bytes 294920 | tf_op jit(solution)/shard_map/ppermute | solution.py:814
  55.8 4.2 %collective-permute-start.15 = (f32[2,48,128]{2,1,0:T(8,128)S(1)}, f32[2,48,128]{2,1,0:T(8,128)S(1)}, u32[]{:S(2)}, u32[]{:S(2)}) collective-permute-start(f32[2,48,128]{2,1,0:T(8,128)S(1)} %shard_map.129), channel_id=1, source_target_pairs={{0,1},{1,0},{2,3},{3,2},{4,5},{5,4},{6,7},{7,6},{8,9},{9,8},{10,11... | collective-permute-start | bytes 147464 | tf_op jit(solution)/shard_map/ppermute | solution.py:814
  61.4 1.3 %collective-permute-start.16 = (f32[144,128]{1,0:T(8,128)S(1)}, f32[144,128]{1,0:T(8,128)S(1)}, u32[]{:S(2)}, u32[]{:S(2)}) collective-permute-start(f32[144,128]{1,0:T(8,128)S(1)} %get-tuple-element.86), channel_id=1, source_target_pairs={{0,2},{2,0},{4,6},{6,4},{8,10},{10,8},{12,14},{14,12},{16,18},{18,... | collective-permute-start | bytes 221192 | tf_op jit(solution)/shard_map/ppermute | solution.py:807
  61.5 6.5 %collective-permute-start.17 = (f32[144,128]{1,0:T(8,128)S(1)}, f32[144,128]{1,0:T(8,128)S(1)}, u32[]{:S(2)}, u32[]{:S(2)}) collective-permute-start(f32[144,128]{1,0:T(8,128)S(1)} %get-tuple-element.87), channel_id=1, source_target_pairs={{2,4},{6,8},{10,12},{14,16},{18,20},{22,24},{26,28},{30,0},{4,2},{... | collective-permute-start | bytes 221192 | tf_op jit(solution)/shard_map/ppermute | solution.py:806
  61.6 15.9 %collective-permute-start.18 = (f32[2,80,128]{2,1,0:T(8,128)S(1)}, f32[2,80,128]{2,1,0:T(8,128)S(1)}, u32[]{:S(2)}, u32[]{:S(2)}) collective-permute-start(f32[2,80,128]{2,1,0:T(8,128)S(1)} %get-tuple-element.88), channel_id=1, source_target_pairs={{0,1},{1,0},{2,3},{3,2},{4,5},{5,4},{6,7},{7,6},{8,9},{9,8},{10,11... | collective-permute-start | bytes 245768 | tf_op jit(solution)/shard_map/ppermute | solution.py:814
  68.1 9.5 %collective-permute-start.19 = (f32[2,48,128]{2,1,0:T(8,128)S(1)}, f32[2,48,128]{2,1,0:T(8,128)S(1)}, u32[]{:S(2)}, u32[]{:S(2)}) collective-permute-start(f32[2,48,128]{2,1,0:T(8,128)S(1)} %shard_map.131), channel_id=1, source_target_pairs={{0,1},{1,0},{2,3},{3,2},{4,5},{5,4},{6,7},{7,6},{8,9},{9,8},{10,11... | collective-permute-start | bytes 147464 | tf_op jit(solution)/shard_map/ppermute | solution.py:814
  78.3 1.3 %collective-permute-start.20 = (f32[128,128]{1,0:T(8,128)S(1)}, f32[128,128]{1,0:T(8,128)S(1)}, u32[]{:S(2)}, u32[]{:S(2)}) collective-permute-start(f32[128,128]{1,0:T(8,128)S(1)} %get-tuple-element.94), channel_id=1, source_target_pairs={{0,2},{2,0},{4,6},{6,4},{8,10},{10,8},{12,14},{14,12},{16,18},{18,... | collective-permute-start | bytes 196616 | tf_op jit(solution)/shard_map/ppermute | solution.py:807
  78.4 6.5 %collective-permute-start.21 = (f32[128,128]{1,0:T(8,128)S(1)}, f32[128,128]{1,0:T(8,128)S(1)}, u32[]{:S(2)}, u32[]{:S(2)}) collective-permute-start(f32[128,128]{1,0:T(8,128)S(1)} %get-tuple-element.95), channel_id=1, source_target_pairs={{2,4},{6,8},{10,12},{14,16},{18,20},{22,24},{26,28},{30,0},{4,2},{... | collective-permute-start | bytes 196616 | tf_op jit(solution)/shard_map/ppermute | solution.py:806
  79.0 6.4 %collective-permute-start.22 = (f32[2,96,128]{2,1,0:T(8,128)S(1)}, f32[2,96,128]{2,1,0:T(8,128)S(1)}, u32[]{:S(2)}, u32[]{:S(2)}) collective-permute-start(f32[2,96,128]{2,1,0:T(8,128)S(1)} %get-tuple-element.96), channel_id=1, source_target_pairs={{0,1},{1,0},{2,3},{3,2},{4,5},{5,4},{6,7},{7,6},{8,9},{9,8},{10,11... | collective-permute-start | bytes 294920 | tf_op jit(solution)/shard_map/ppermute | solution.py:814
  84.9 4.2 %collective-permute-start.23 = (f32[2,48,128]{2,1,0:T(8,128)S(1)}, f32[2,48,128]{2,1,0:T(8,128)S(1)}, u32[]{:S(2)}, u32[]{:S(2)}) collective-permute-start(f32[2,48,128]{2,1,0:T(8,128)S(1)} %shard_map.133), channel_id=1, source_target_pairs={{0,1},{1,0},{2,3},{3,2},{4,5},{5,4},{6,7},{7,6},{8,9},{9,8},{10,11... | collective-permute-start | bytes 147464 | tf_op jit(solution)/shard_map/ppermute | solution.py:814
  90.5 1.3 %collective-permute-start.24 = (f32[144,128]{1,0:T(8,128)S(1)}, f32[144,128]{1,0:T(8,128)S(1)}, u32[]{:S(2)}, u32[]{:S(2)}) collective-permute-start(f32[144,128]{1,0:T(8,128)S(1)} %get-tuple-element.99), channel_id=1, source_target_pairs={{0,2},{2,0},{4,6},{6,4},{8,10},{10,8},{12,14},{14,12},{16,18},{18,... | collective-permute-start | bytes 221192 | tf_op jit(solution)/shard_map/ppermute | solution.py:807
  90.6 6.5 %collective-permute-start.25 = (f32[144,128]{1,0:T(8,128)S(1)}, f32[144,128]{1,0:T(8,128)S(1)}, u32[]{:S(2)}, u32[]{:S(2)}) collective-permute-start(f32[144,128]{1,0:T(8,128)S(1)} %get-tuple-element.100), channel_id=1, source_target_pairs={{2,4},{6,8},{10,12},{14,16},{18,20},{22,24},{26,28},{30,0},{4,2},{... | collective-permute-start | bytes 221192 | tf_op jit(solution)/shard_map/ppermute | solution.py:806
  90.7 17.2 %collective-permute-start.26 = (f32[2,80,128]{2,1,0:T(8,128)S(1)}, f32[2,80,128]{2,1,0:T(8,128)S(1)}, u32[]{:S(2)}, u32[]{:S(2)}) collective-permute-start(f32[2,80,128]{2,1,0:T(8,128)S(1)} %get-tuple-element.101), channel_id=1, source_target_pairs={{0,1},{1,0},{2,3},{3,2},{4,5},{5,4},{6,7},{7,6},{8,9},{9,8},{10,11... | collective-permute-start | bytes 245768 | tf_op jit(solution)/shard_map/ppermute | solution.py:814
  97.1 10.7 %collective-permute-start.27 = (f32[2,48,128]{2,1,0:T(8,128)S(1)}, f32[2,48,128]{2,1,0:T(8,128)S(1)}, u32[]{:S(2)}, u32[]{:S(2)}) collective-permute-start(f32[2,48,128]{2,1,0:T(8,128)S(1)} %shard_map.135), channel_id=1, source_target_pairs={{0,1},{1,0},{2,3},{3,2},{4,5},{5,4},{6,7},{7,6},{8,9},{9,8},{10,11... | collective-permute-start | bytes 147464 | tf_op jit(solution)/shard_map/ppermute | solution.py:814
  (9 other events, 21.6 us)

commit v2 on v1

--- a/solution.py
+++ b/solution.py
@@ -420,7 +420,8 @@
         late_ref[side, 24:32] = inners[7]
 
 
-def raw_side_kernel(in_ref, out_ref, late_ref, send_ref):
+def raw_side_kernel(in_ref, out_ref, late_ref, row_ref, send_ref, pass_ref):
+    pass_ref[...] = row_ref[...]
     before, after = got_axial(in_ref, out_ref)
     for side, (edge, inner) in enumerate(((0, 1), (7, 6))):
         send_ref[side, :8] = before(64 + 8 * edge, 8)
@@ -516,9 +517,12 @@
 
 
 def solve_kernel(
-    g_ref, in_ref, out_ref, early_ref, late_ref, kbar_ref, into_ref, outof_ref, spectrum_ref,
+    g_ref, in_ref, out_ref, early_ref, late_ref, row_ref,
+    kbar_ref, into_ref, outof_ref, spectrum_ref,
     planes_ref, solved_ref, part_ref, send_in_ref, send_out_ref, send_early_ref, send_late_ref,
+    pass_ref,
 ):
+    pass_ref[...] = row_ref[...]
     planes = got_planes(g_ref, in_ref, out_ref, early_ref, late_ref)
     for e in range(10):
         planes_ref[e] = planes[e]
@@ -562,7 +566,8 @@
     )
 
 
-def solved_side_kernel(in_ref, out_ref, late_ref, send_ref):
+def solved_side_kernel(in_ref, out_ref, late_ref, row_ref, send_ref, pass_ref):
+    pass_ref[...] = row_ref[...]
     before, after = got_axial(in_ref, out_ref)
     for side, b in ((0, 0), (1, 7)):
         row = 8 * b
@@ -730,7 +735,7 @@
 
 
 def second_dots_kernel(
-    pay_in_ref, planes_r_ref, planes_q_ref, planes_w_ref, solved_r_ref, solved_q_ref, solved_w_ref,
+    row_ref, planes_r_ref, planes_q_ref, planes_w_ref, solved_r_ref, solved_q_ref, solved_w_ref,
     pay_ref,
 ):
     scalars = [
@@ -740,7 +745,7 @@
         dot_planes(planes_w_ref, solved_q_ref),
         dot_planes(planes_w_ref, solved_w_ref),
     ]
-    row = pay_in_ref[0:1]
+    row = row_ref[...]
     width = row.shape[1]
     place = lax.broadcasted_iota(jnp.int32, (1, width), 1)
     for k, value in enumerate(scalars):
@@ -817,6 +822,29 @@
     return jnp.stack([after, before])
 
 
+def sum_steps():
+    azim = lax.axis_size("azim")
+    count = lax.axis_size("axial") * azim
+    steps, step = [], 2 * azim
+    while step < count:
+        steps.append(step)
+        step *= 2
+    step = 1
+    while step < azim:
+        steps.append(step)
+        step *= 2
+    groups = [steps[k::4] for k in range(4)]
+    groups[0] = groups[0] + [azim]
+    return groups
+
+
+def partial_sum(row, steps):
+    count = lax.axis_size("axial") * lax.axis_size("azim")
+    for step in steps:
+        row = row + lax.ppermute(row, ALL, [(i, i ^ step) for i in range(count)])
+    return row
+
+
 def gather_sums(rows):
     return lax.all_to_all(rows, ALL, 0, 0, tiled=True)
 
@@ -843,7 +871,7 @@
         conv_kernel,
         [(3,) + field, (count, LANES), (192 + count, LANES), (192 + count, LANES)]
         + [(2, 144, LANES), (2, 48, LANES)],
-        u, coarse_factor, plane, grad,
+        *(pltpu.with_memory_space_constraint(x, pltpu.HBM) for x in (u, coarse_factor, plane, grad)),
         in_specs=[far] * 4,
         scratch_shapes=[
             pltpu.VMEM((3,) + field, F32),
@@ -855,35 +883,46 @@
     )
     (kbar,) = kernel_call(mean_kernel, [(8, LANES)], diff)
 
-    def exchange(side_kernel, late_rows, send_in, send_out, send_early, send_late, *more):
+    def exchange(side_kernel, late_rows, sends, extra, extra_shape=None):
+        send_in, send_out, send_early, send_late = sends
         inner, outer = axial_swap(send_in, send_out)
         early = azim_swap(send_early)
-        (late,) = kernel_call(side_kernel, [(2, late_rows, LANES)], inner, outer, send_late, *more)
-        return inner, outer, early, azim_swap(late)
-
-    moved = exchange(conv_side_kernel, 48 + 3 * count, *sends, row)
+        shapes = [(2, late_rows, LANES)]
+        shapes = shapes if extra_shape is None else shapes + [extra_shape]
+        late, *passed = kernel_call(side_kernel, shapes, inner, outer, send_late, extra)
+        return [inner, outer, early, azim_swap(late)] + passed
+
+    one = (1, width * LANES)
+    groups = sum_steps()
+    moved = exchange(conv_side_kernel, 48 + 3 * count, sends, row)
     g, *sends, near, pay = kernel_call(
         divergence_kernel,
-        [field] + raw_sends + [(16, width * LANES), sums],
+        [field] + raw_sends + [(16, width * LANES), one],
         conv, u, *moved, row, plane, over, div,
     )
     solver = (kbar, into, outof, spectrum)
     operator = (near, diff, plane, grad, div)
-    solve_shapes = boxes + [field] + solved_sends
-
-    moved = exchange(raw_side_kernel, 48, *sends)
-    pay = gather_sums(pay)
-    planes_r, solved_r, part, *sends = kernel_call(solve_kernel, solve_shapes, g, *moved, *solver)
-    moved = exchange(solved_side_kernel, 48, *sends)
+    solve_shapes = boxes + [field] + solved_sends + [one]
+
+    *moved, pay = exchange(raw_side_kernel, 48, sends, partial_sum(pay, groups[0]), one)
+    pay = partial_sum(pay, groups[1])
+    planes_r, solved_r, part, *sends, pay = kernel_call(
+        solve_kernel, solve_shapes, g, *moved, pay, *solver
+    )
+    *moved, pay = exchange(solved_side_kernel, 48, sends, partial_sum(pay, groups[2]), one)
+    pay = partial_sum(pay, groups[3])
     z0, raw0, g, *sends, row_r, pay = kernel_call(
         first_apply_kernel,
-        [field, field, field] + raw_sends + [row_shape, sums],
+        [field, field, field] + raw_sends + [row_shape, one],
         part, *moved, *operator, pay, planes_r, solved_r,
     )
-    moved = exchange(raw_side_kernel, 48, *sends)
-    first_sums = gather_sums(pay)
-    planes_q, solved_q, part, *sends = kernel_call(solve_kernel, solve_shapes, g, *moved, *solver)
-    moved = exchange(solved_side_kernel, 48, *sends)
+    *moved, pay = exchange(raw_side_kernel, 48, sends, partial_sum(pay, groups[0]), one)
+    pay = partial_sum(pay, groups[1])
+    planes_q, solved_q, part, *sends, pay = kernel_call(
+        solve_kernel, solve_shapes, g, *moved, pay, *solver
+    )
+    *moved, pay = exchange(solved_side_kernel, 48, sends, partial_sum(pay, groups[2]), one)
+    first_sums = partial_sum(pay, groups[3])
     y, z1, raw1, g, *sends = kernel_call(
         second_apply_kernel,
         [field, field, field, field] + raw_sends,
@@ -891,19 +930,21 @@
     )
     planes_r, solved_r, pay = kernel_call(
         first_dots_kernel,
-        boxes + [sums],
+        boxes + [one],
         first_sums, row_r, near, planes_r, planes_q, solved_r, solved_q, z1, raw1, raw0,
     )
-    moved = exchange(raw_side_kernel, 48, *sends)
-    planes_w, solved_w, part, *sends = kernel_call(solve_kernel, solve_shapes, g, *moved, *solver)
+    *moved, pay = exchange(raw_side_kernel, 48, sends, pay, one)
+    planes_w, solved_w, part, *sends, pay = kernel_call(
+        solve_kernel, solve_shapes, g, *moved, pay, *solver
+    )
     (pay,) = kernel_call(
         second_dots_kernel, [sums], pay, planes_r, planes_q, planes_w, solved_r, solved_q, solved_w
     )
-    moved = exchange(solved_side_kernel, 48, *sends)
+    *moved, pay = exchange(solved_side_kernel, 48, sends, gather_sums(pay), sums)
     pressure, residual, direction = kernel_call(
         last_kernel,
         [field, field, field],
-        part, *moved, near, gather_sums(pay), first_sums, row_r,
+        part, *moved, near, pay, first_sums, row_r,
         y, z0, z1, planes_r, planes_q, planes_w,
     )
     return pressure.reshape(shape), residual.reshape(shape), direction.reshape(shape)

time: 109 us -> 102 us (0.936)
  blocking collectives: 27 us -> 12.2 us
  starting transfers between devices: 27.3 us -> 34.9 us
  local copies, waits for them, and re-layouts: 3.41 us -> 0.04 us
  waiting for transfers between devices: 40.1 us -> 42.3 us
    ppermute x0 -> x10, waiting for transfers between devices: none -> 27.1 us  [partial_sum(): row = row + lax.ppermute(row, ALL, [(i, i ^ step) for i in range(count)])]
    ppermute x7, waiting for transfers between devices: 26.2 us -> 5.23 us  [axial_swap(): from_outer = lax.ppermute(outer_rows, 'axial', outer)]
    all_to_all x3 -> x1, blocking collectives: 27 us -> 12.2 us  [gather_sums(): return lax.all_to_all(rows, ALL, 0, 0, tiled=True)]
    ppermute x0 -> x10, starting transfers between devices: none -> 5.18 us  [partial_sum(): row = row + lax.ppermute(row, ALL, [(i, i ^ step) for i in range(count)])]
    unnamed x26 -> x18, local copies, waits for them, and re-layouts: 3.41 us -> 0.04 us
    ppermute x14, waiting for transfers between devices: 12.6 us -> 9.89 us  [azim_swap(): return lax.ppermute(sides, 'azim', [(0, 1), (1, 0)])]
    ppermute x14, starting transfers between devices: 13.8 us -> 15.2 us  [azim_swap(): return lax.ppermute(sides, 'azim', [(0, 1), (1, 0)])]
    ppermute x7, waiting for transfers between devices: 1.35 us -> 0.02 us  [axial_swap(): from_inner = lax.ppermute(inner_rows, 'axial', inner)]
  transfers between devices with their start and end apart: 28 -> 38, of which waited for: 17 -> 17; matrix products, arithmetic and copies ran while one was open for 0% -> 0% of each run, Pallas kernels for 1% -> 1%
where the time goes in v2:
time: 102 us
  waiting for transfers between devices  42.3 us (41%)
  starting transfers between devices  34.9 us (34%)
  blocking collectives  12.2 us (12%)
  Pallas kernels  11.2 us (11%)
    ppermute x10, waiting for transfers between devices, partial_sum(): row = row + lax.ppermute(row, ALL, [(i, i ^ step) for i in range(count)])  27.1 us
    ppermute x14, starting transfers between devices, azim_swap(): return lax.ppermute(sides, 'azim', [(0, 1), (1, 0)])  15.2 us
    ppermute x7, starting transfers between devices, axial_swap(): from_outer = lax.ppermute(outer_rows, 'axial', outer)  13.6 us
    all_to_all x1, blocking collectives, gather_sums(): return lax.all_to_all(rows, ALL, 0, 0, tiled=True)  12.2 us
    pallas_call x18, Pallas kernels, kernel_call(): pl.pallas_call(kernel, out_shape=outs, compiler_params=pltpu.CompilerPara...  11.2 us
    ppermute x14, waiting for transfers between devices, azim_swap(): return lax.ppermute(sides, 'azim', [(0, 1), (1, 0)])  9.89 us
    ppermute x7, waiting for transfers between devices, axial_swap(): from_outer = lax.ppermute(outer_rows, 'axial', outer)  5.23 us
    ppermute x10, starting transfers between devices, partial_sum(): row = row + lax.ppermute(row, ALL, [(i, i ^ step) for i in range(count)])  5.18 us
  transfers between devices with their start and end apart: 38, of which 17 were waited for; matrix products, arithmetic and copies ran while one was open for 0% of the time, Pallas kernels for 1%

profile of v2, /device:TPU:0, one launch (start us, length us, event | category | flops | bytes accessed | tf_op | source)
XLA Modules:
  0.0 101.6 jit_solution(7526253871192889340)
XLA Ops:
  0.6 2.2 %shard_map.121 = (f32[3,8,64,128]{3,2,1,0:T(8,128)S(1)}, f32[8,128]{1,0:T(8,128)S(1)}, f32[200,128]{1,0:T(8,128)S(1)}, f32[200,128]{1,0:T(8,128)S(1)}, f32[2,144...) custom-call(f32[3,8,64,128]{3,2,1,0:T(8,128)} %bitcast.15, f32[1,32]{1,0:T(1,128)} %row_hbm.1, ...), custom_call_target="tpu_custom_call" | custom-call | tf_op jit(solution)/shard_map/pallas_call | solution.py:797
  3.3 5.6 %collective-permute-start.1 = (f32[200,128]{1,0:T(8,128)S(1)}, f32[200,128]{1,0:T(8,128)S(1)}, u32[]{:S(2)}, u32[]{:S(2)}) collective-permute-start(f32[200,128]{1,0:T(8,128)S(1)} %get-tuple-element.77), channel_id=1, source_target_pairs={{2,4},{6,8},{10,12},{14,16},{18,20},{22,24},{26,28},{30,0},{4,2},{... | collective-permute-start | bytes 307208 | tf_op jit(solution)/shard_map/ppermute | solution.py:811
  9.0 1.5 %collective-permute-start.2 = (f32[2,144,128]{2,1,0:T(8,128)S(1)}, f32[2,144,128]{2,1,0:T(8,128)S(1)}, u32[]{:S(2)}, u32[]{:S(2)}) collective-permute-start(f32[2,144,128]{2,1,0:T(8,128)S(1)} %get-tuple-element.78), channel_id=1, source_target_pairs={{0,1},{1,0},{2,3},{3,2},{4,5},{5,4},{6,7},{7,6},{8,9},{9,8},{10,11... | collective-permute-start | bytes 442376 | tf_op jit(solution)/shard_map/ppermute | solution.py:819
  11.3 1.6 %collective-permute-start.3 = (f32[2,72,128]{2,1,0:T(8,128)S(1)}, f32[2,72,128]{2,1,0:T(8,128)S(1)}, u32[]{:S(2)}, u32[]{:S(2)}) collective-permute-start(f32[2,72,128]{2,1,0:T(8,128)S(1)} %shard_map.122), channel_id=1, source_target_pairs={{0,1},{1,0},{2,3},{3,2},{4,5},{5,4},{6,7},{7,6},{8,9},{9,8},{10,11... | collective-permute-start | bytes 221192 | tf_op jit(solution)/shard_map/ppermute | solution.py:819
  12.9 1.2 %collective-permute-done.2.early_ref = f32[2,144,128]{2,1,0:T(8,128)S(1)} collective-permute-done((f32[2,144,128]{2,1,0:T(8,128)S(1)}, f32[2,144,128]{2,1,0:T(8,128)S(1)}, u32[]{:S(2)}, u32[]{:S(2)}) %collective-permute-start.2) | collective-permute-done | bytes 147488 | tf_op jit(solution)/shard_map/ppermute | solution.py:819
  14.1 1.6 %collective-permute-done.3.late_ref = f32[2,72,128]{2,1,0:T(8,128)S(1)} collective-permute-done((f32[2,72,128]{2,1,0:T(8,128)S(1)}, f32[2,72,128]{2,1,0:T(8,128)S(1)}, u32[]{:S(2)}, u32[]{:S(2)}) %collective-permute-start.3) | collective-permute-done | bytes 73760 | tf_op jit(solution)/shard_map/ppermute | solution.py:819
  16.4 3.4 %collective-permute-start.5 = (f32[128,128]{1,0:T(8,128)S(1)}, f32[128,128]{1,0:T(8,128)S(1)}, u32[]{:S(2)}, u32[]{:S(2)}) collective-permute-start(f32[128,128]{1,0:T(8,128)S(1)} %get-tuple-element.83), channel_id=1, source_target_pairs={{2,4},{6,8},{10,12},{14,16},{18,20},{22,24},{26,28},{30,0},{4,2},{... | collective-permute-start | bytes 196616 | tf_op jit(solution)/shard_map/ppermute | solution.py:811
  19.8 1.5 %collective-permute-start.6 = (f32[2,96,128]{2,1,0:T(8,128)S(1)}, f32[2,96,128]{2,1,0:T(8,128)S(1)}, u32[]{:S(2)}, u32[]{:S(2)}) collective-permute-start(f32[2,96,128]{2,1,0:T(8,128)S(1)} %get-tuple-element.84), channel_id=1, source_target_pairs={{0,1},{1,0},{2,3},{3,2},{4,5},{5,4},{6,7},{7,6},{8,9},{9,8},{10,11... | collective-permute-start | bytes 294920 | tf_op jit(solution)/shard_map/ppermute | solution.py:819
  21.3 3.5 %collective-permute-done.7 = f32[1,128]{1,0:T(1,128)S(1)} collective-permute-done((f32[1,128]{1,0:T(1,128)S(1)}, f32[1,128]{1,0:T(1,128)S(1)}, u32[]{:S(2)}, u32[]{:S(2)}) %collective-permute-start.7) | collective-permute-done | bytes 544 | tf_op jit(solution)/shard_map/ppermute | solution.py:844
  26.6 3.5 %collective-permute-done.10 = f32[1,128]{1,0:T(1,128)S(1)} collective-permute-done((f32[1,128]{1,0:T(1,128)S(1)}, f32[1,128]{1,0:T(1,128)S(1)}, u32[]{:S(2)}, u32[]{:S(2)}) %collective-permute-start.10) | collective-permute-done | bytes 544 | tf_op jit(solution)/shard_map/ppermute | solution.py:844
  30.2 1.5 %shard_map.126 = (f32[10,144,128]{2,1,0:T(8,128)S(1)}, f32[10,144,128]{2,1,0:T(8,128)S(1)}, f32[8,64,128]{2,1,0:T(8,128)S(1)}, f32[144,128]{1,0:T(8,128)S(1)}, f...) custom-call(f32[8,64,128]{2,1,0:T(8,128)S(1)} %get-tuple-element.81.g_ref, ...), custom_call_target="tpu_custom_call" | custom-call | tf_op jit(solution)/shard_map/pallas_call | solution.py:797
  32.5 1.5 %collective-permute-start.13 = (f32[2,80,128]{2,1,0:T(8,128)S(1)}, f32[2,80,128]{2,1,0:T(8,128)S(1)}, u32[]{:S(2)}, u32[]{:S(2)}) collective-permute-start(f32[2,80,128]{2,1,0:T(8,128)S(1)} %get-tuple-element.92), channel_id=1, source_target_pairs={{0,1},{1,0},{2,3},{3,2},{4,5},{5,4},{6,7},{7,6},{8,9},{9,8},{10,11... | collective-permute-start | bytes 245768 | tf_op jit(solution)/shard_map/ppermute | solution.py:819
  34.2 4.2 %collective-permute-done.14 = f32[1,128]{1,0:T(1,128)S(1)} collective-permute-done((f32[1,128]{1,0:T(1,128)S(1)}, f32[1,128]{1,0:T(1,128)S(1)}, u32[]{:S(2)}, u32[]{:S(2)}) %collective-permute-start.14) | collective-permute-done | bytes 544 | tf_op jit(solution)/shard_map/ppermute | solution.py:844
  38.5 1.4 %collective-permute-start.15 = (f32[2,48,128]{2,1,0:T(8,128)S(1)}, f32[2,48,128]{2,1,0:T(8,128)S(1)}, u32[]{:S(2)}, u32[]{:S(2)}) collective-permute-start(f32[2,48,128]{2,1,0:T(8,128)S(1)} %get-tuple-element.95), channel_id=1, source_target_pairs={{0,1},{1,0},{2,3},{3,2},{4,5},{5,4},{6,7},{7,6},{8,9},{9,8},{10,11... | collective-permute-start | bytes 147464 | tf_op jit(solution)/shard_map/ppermute | solution.py:819
  40.6 2.9 %collective-permute-done.16 = f32[1,128]{1,0:T(1,128)S(1)} collective-permute-done((f32[1,128]{1,0:T(1,128)S(1)}, f32[1,128]{1,0:T(1,128)S(1)}, u32[]{:S(2)}, u32[]{:S(2)}) %collective-permute-start.16) | collective-permute-done | bytes 544 | tf_op jit(solution)/shard_map/ppermute | solution.py:844
  44.9 1.1 %collective-permute-start.19 = (f32[2,96,128]{2,1,0:T(8,128)S(1)}, f32[2,96,128]{2,1,0:T(8,128)S(1)}, u32[]{:S(2)}, u32[]{:S(2)}) collective-permute-start(f32[2,96,128]{2,1,0:T(8,128)S(1)} %get-tuple-element.103), channel_id=1, source_target_pairs={{0,1},{1,0},{2,3},{3,2},{4,5},{5,4},{6,7},{7,6},{8,9},{9,8},{10,11... | collective-permute-start | bytes 294920 | tf_op jit(solution)/shard_map/ppermute | solution.py:819
  46.1 1.1 %collective-permute-start.20 = (f32[1,128]{1,0:T(1,128)S(1)}, f32[1,128]{1,0:T(1,128)S(1)}, u32[]{:S(2)}, u32[]{:S(2)}) collective-permute-start(f32[1,128]{1,0:T(1,128)S(1)} %get-tuple-element.105), channel_id=1, source_target_pairs={{0,4},{1,5},{2,6},{3,7},{4,0},{5,1},{6,2},{7,3},{8,12},{9,13},{10,... | collective-permute-start | bytes 1544 | tf_op jit(solution)/shard_map/ppermute | solution.py:844
  47.2 2.4 %collective-permute-done.20 = f32[1,128]{1,0:T(1,128)S(1)} collective-permute-done((f32[1,128]{1,0:T(1,128)S(1)}, f32[1,128]{1,0:T(1,128)S(1)}, u32[]{:S(2)}, u32[]{:S(2)}) %collective-permute-start.20) | collective-permute-done | bytes 544 | tf_op jit(solution)/shard_map/ppermute | solution.py:844
  49.6 1.1 %collective-permute-done.21 = f32[1,128]{1,0:T(1,128)S(1)} collective-permute-done((f32[1,128]{1,0:T(1,128)S(1)}, f32[1,128]{1,0:T(1,128)S(1)}, u32[]{:S(2)}, u32[]{:S(2)}) %collective-permute-start.21) | collective-permute-done | bytes 544 | tf_op jit(solution)/shard_map/ppermute | solution.py:844
  51.7 1.7 %collective-permute-start.23 = (f32[1,128]{1,0:T(1,128)S(1)}, f32[1,128]{1,0:T(1,128)S(1)}, u32[]{:S(2)}, u32[]{:S(2)}) collective-permute-start(f32[1,128]{1,0:T(1,128)S(1)} %get-tuple-element.107), channel_id=1, source_target_pairs={{0,8},{1,9},{2,10},{3,11},{4,12},{5,13},{6,14},{7,15},{8,0},{9,1},... | collective-permute-start | bytes 1544 | tf_op jit(solution)/shard_map/ppermute | solution.py:844
  53.4 1.8 %collective-permute-done.23 = f32[1,128]{1,0:T(1,128)S(1)} collective-permute-done((f32[1,128]{1,0:T(1,128)S(1)}, f32[1,128]{1,0:T(1,128)S(1)}, u32[]{:S(2)}, u32[]{:S(2)}) %collective-permute-start.23) | collective-permute-done | bytes 544 | tf_op jit(solution)/shard_map/ppermute | solution.py:844
  55.3 1.5 %shard_map.130 = (f32[10,144,128]{2,1,0:T(8,128)S(1)}, f32[10,144,128]{2,1,0:T(8,128)S(1)}, f32[8,64,128]{2,1,0:T(8,128)S(1)}, f32[144,128]{1,0:T(8,128)S(1)}, f...) custom-call(f32[8,64,128]{2,1,0:T(8,128)S(1)} %get-tuple-element.100.g_ref,, ...), custom_call_target="tpu_custom_call" | custom-call | tf_op jit(solution)/shard_map/pallas_call | solution.py:797
  56.9 2.7 %collective-permute-start.25 = (f32[144,128]{1,0:T(8,128)S(1)}, f32[144,128]{1,0:T(8,128)S(1)}, u32[]{:S(2)}, u32[]{:S(2)}) collective-permute-start(f32[144,128]{1,0:T(8,128)S(1)} %get-tuple-element.110), channel_id=1, source_target_pairs={{2,4},{6,8},{10,12},{14,16},{18,20},{22,24},{26,28},{30,0},{4,2},{... | collective-permute-start | bytes 221192 | tf_op jit(solution)/shard_map/ppermute | solution.py:811
  61.0 3.7 %collective-permute-done.27 = f32[1,128]{1,0:T(1,128)S(1)} collective-permute-done((f32[1,128]{1,0:T(1,128)S(1)}, f32[1,128]{1,0:T(1,128)S(1)}, u32[]{:S(2)}, u32[]{:S(2)}) %collective-permute-start.27) | collective-permute-done | bytes 544 | tf_op jit(solution)/shard_map/ppermute | solution.py:844
  64.8 1.4 %collective-permute-start.28 = (f32[2,48,128]{2,1,0:T(8,128)S(1)}, f32[2,48,128]{2,1,0:T(8,128)S(1)}, u32[]{:S(2)}, u32[]{:S(2)}) collective-permute-start(f32[2,48,128]{2,1,0:T(8,128)S(1)} %get-tuple-element.114), channel_id=1, source_target_pairs={{0,1},{1,0},{2,3},{3,2},{4,5},{5,4},{6,7},{7,6},{8,9},{9,8},{10,11... | collective-permute-start | bytes 147464 | tf_op jit(solution)/shard_map/ppermute | solution.py:819
  66.9 2.9 %collective-permute-done.29 = f32[1,128]{1,0:T(1,128)S(1)} collective-permute-done((f32[1,128]{1,0:T(1,128)S(1)}, f32[1,128]{1,0:T(1,128)S(1)}, u32[]{:S(2)}, u32[]{:S(2)}) %collective-permute-start.29) | collective-permute-done | bytes 544 | tf_op jit(solution)/shard_map/ppermute | solution.py:844
  72.7 4.3 %collective-permute-done.31.out_ref = f32[128,128]{1,0:T(8,128)S(1)} collective-permute-done((f32[128,128]{1,0:T(8,128)S(1)}, f32[128,128]{1,0:T(8,128)S(1)}, u32[]{:S(2)}, u32[]{:S(2)}) %collective-permute-start.31) | collective-permute-done | bytes 65568 | tf_op jit(solution)/shard_map/ppermute | solution.py:811
  77.8 3.4 %collective-permute-done.33.late_ref = f32[2,48,128]{2,1,0:T(8,128)S(1)} collective-permute-done((f32[2,48,128]{2,1,0:T(8,128)S(1)}, f32[2,48,128]{2,1,0:T(8,128)S(1)}, u32[]{:S(2)}, u32[]{:S(2)}) %collective-permute-start.33) | collective-permute-done | bytes 49184 | tf_op jit(solution)/shard_map/ppermute | solution.py:819
  81.2 1.5 %shard_map.135 = (f32[10,144,128]{2,1,0:T(8,128)S(1)}, f32[10,144,128]{2,1,0:T(8,128)S(1)}, f32[8,64,128]{2,1,0:T(8,128)S(1)}, f32[144,128]{1,0:T(8,128)S(1)}, f...) custom-call(f32[8,64,128]{2,1,0:T(8,128)S(1)} %get-tuple-element.118.g_ref,, ...), custom_call_target="tpu_custom_call" | custom-call | tf_op jit(solution)/shard_map/pallas_call | solution.py:797
  84.1 12.2 %all_to_all.11 = f32[32,1,128]{2,1,0:T(1,128)S(1)} all-to-all(f32[32,1,128]{2,1,0:T(1,128)S(1)} %bitcast.20), channel_id=1, replica_groups=mesh['axial'=16,'azim'=2] {'axial','azim'}, dimensions={0} | all-to-all | bytes 32768 | tf_op jit(solution)/shard_map/all_to_all | solution.py:849
  96.9 3.6 %collective-permute-done.37.late_ref = f32[2,48,128]{2,1,0:T(8,128)S(1)} collective-permute-done((f32[2,48,128]{2,1,0:T(8,128)S(1)}, f32[2,48,128]{2,1,0:T(8,128)S(1)}, u32[]{:S(2)}, u32[]{:S(2)}) %collective-permute-start.37) | collective-permute-done | bytes 49184 | tf_op jit(solution)/shard_map/ppermute | solution.py:819
  100.5 1.1 %shard_map.138 = (f32[8,64,128]{2,1,0:T(8,128)}, f32[8,64,128]{2,1,0:T(8,128)}, f32[8,64,128]{2,1,0:T(8,128)}) custom-call(f32[8,64,128]{2,1,0:T(8,128)S(1)} %get-tuple-element.131.part_ref, f32[144,128]{1,0:T(8,128)S(1)} %collective-permute-done.34.in_ref, f32[144,128]{1,0:T(8,128)S(1)} %collective-permute-done.35.out_ref, ...), custom_call_target="tpu_custom_call" | custom-call | tf_op jit(solution)/shard_map/pallas_call | solution.py:797
  (91 shorter events, 15.9 us)
Async XLA Ops:
  2.8 7.7 %collective-permute-start = (f32[200,128]{1,0:T(8,128)S(1)}, f32[200,128]{1,0:T(8,128)S(1)}, u32[]{:S(2)}, u32[]{:S(2)}) collective-permute-start(f32[200,128]{1,0:T(8,128)S(1)} %get-tuple-element.76), channel_id=1, source_target_pairs={{0,2},{2,0},{4,6},{6,4},{8,10},{10,8},{12,14},{14,12},{16,18},{18,... | collective-permute-start | bytes 307208 | tf_op jit(solution)/shard_map/ppermute | solution.py:812
  3.3 8.0 %collective-permute-start.1 = (f32[200,128]{1,0:T(8,128)S(1)}, f32[200,128]{1,0:T(8,128)S(1)}, u32[]{:S(2)}, u32[]{:S(2)}) collective-permute-start(f32[200,128]{1,0:T(8,128)S(1)} %get-tuple-element.77), channel_id=1, source_target_pairs={{2,4},{6,8},{10,12},{14,16},{18,20},{22,24},{26,28},{30,0},{4,2},{... | collective-permute-start | bytes 307208 | tf_op jit(solution)/shard_map/ppermute | solution.py:811
  9.0 5.1 %collective-permute-start.2 = (f32[2,144,128]{2,1,0:T(8,128)S(1)}, f32[2,144,128]{2,1,0:T(8,128)S(1)}, u32[]{:S(2)}, u32[]{:S(2)}) collective-permute-start(f32[2,144,128]{2,1,0:T(8,128)S(1)} %get-tuple-element.78), channel_id=1, source_target_pairs={{0,1},{1,0},{2,3},{3,2},{4,5},{5,4},{6,7},{7,6},{8,9},{9,8},{10,11... | collective-permute-start | bytes 442376 | tf_op jit(solution)/shard_map/ppermute | solution.py:819
  11.3 4.4 %collective-permute-start.3 = (f32[2,72,128]{2,1,0:T(8,128)S(1)}, f32[2,72,128]{2,1,0:T(8,128)S(1)}, u32[]{:S(2)}, u32[]{:S(2)}) collective-permute-start(f32[2,72,128]{2,1,0:T(8,128)S(1)} %shard_map.122), channel_id=1, source_target_pairs={{0,1},{1,0},{2,3},{3,2},{4,5},{5,4},{6,7},{7,6},{8,9},{9,8},{10,11... | collective-permute-start | bytes 221192 | tf_op jit(solution)/shard_map/ppermute | solution.py:819
  16.3 9.6 %collective-permute-start.4 = (f32[128,128]{1,0:T(8,128)S(1)}, f32[128,128]{1,0:T(8,128)S(1)}, u32[]{:S(2)}, u32[]{:S(2)}) collective-permute-start(f32[128,128]{1,0:T(8,128)S(1)} %get-tuple-element.82), channel_id=1, source_target_pairs={{0,2},{2,0},{4,6},{6,4},{8,10},{10,8},{12,14},{14,12},{16,18},{18,... | collective-permute-start | bytes 196616 | tf_op jit(solution)/shard_map/ppermute | solution.py:812
  16.4 9.6 %collective-permute-start.5 = (f32[128,128]{1,0:T(8,128)S(1)}, f32[128,128]{1,0:T(8,128)S(1)}, u32[]{:S(2)}, u32[]{:S(2)}) collective-permute-start(f32[128,128]{1,0:T(8,128)S(1)} %get-tuple-element.83), channel_id=1, source_target_pairs={{2,4},{6,8},{10,12},{14,16},{18,20},{22,24},{26,28},{30,0},{4,2},{... | collective-permute-start | bytes 196616 | tf_op jit(solution)/shard_map/ppermute | solution.py:811
  19.8 10.4 %collective-permute-start.6 = (f32[2,96,128]{2,1,0:T(8,128)S(1)}, f32[2,96,128]{2,1,0:T(8,128)S(1)}, u32[]{:S(2)}, u32[]{:S(2)}) collective-permute-start(f32[2,96,128]{2,1,0:T(8,128)S(1)} %get-tuple-element.84), channel_id=1, source_target_pairs={{0,1},{1,0},{2,3},{3,2},{4,5},{5,4},{6,7},{7,6},{8,9},{9,8},{10,11... | collective-permute-start | bytes 294920 | tf_op jit(solution)/shard_map/ppermute | solution.py:819
  21.3 3.5 %collective-permute-start.7 = (f32[1,128]{1,0:T(1,128)S(1)}, f32[1,128]{1,0:T(1,128)S(1)}, u32[]{:S(2)}, u32[]{:S(2)}) collective-permute-start(f32[1,128]{1,0:T(1,128)S(1)} %get-tuple-element.86), channel_id=1, source_target_pairs={{0,4},{1,5},{2,6},{3,7},{4,0},{5,1},{6,2},{7,3},{8,12},{9,13},{10,... | collective-permute-start | bytes 1544 | tf_op jit(solution)/shard_map/ppermute | solution.py:844
  26.0 4.2 %collective-permute-start.9 = (f32[2,48,128]{2,1,0:T(8,128)S(1)}, f32[2,48,128]{2,1,0:T(8,128)S(1)}, u32[]{:S(2)}, u32[]{:S(2)}) collective-permute-start(f32[2,48,128]{2,1,0:T(8,128)S(1)} %get-tuple-element.87), channel_id=1, source_target_pairs={{0,1},{1,0},{2,3},{3,2},{4,5},{5,4},{6,7},{7,6},{8,9},{9,8},{10,11... | collective-permute-start | bytes 147464 | tf_op jit(solution)/shard_map/ppermute | solution.py:819
  26.6 3.5 %collective-permute-start.10 = (f32[1,128]{1,0:T(1,128)S(1)}, f32[1,128]{1,0:T(1,128)S(1)}, u32[]{:S(2)}, u32[]{:S(2)}) collective-permute-start(f32[1,128]{1,0:T(1,128)S(1)} %get-tuple-element.88), channel_id=1, source_target_pairs={{0,8},{1,9},{2,10},{3,11},{4,12},{5,13},{6,14},{7,15},{8,0},{9,1},... | collective-permute-start | bytes 1544 | tf_op jit(solution)/shard_map/ppermute | solution.py:844
  31.6 6.8 %collective-permute-start.11 = (f32[144,128]{1,0:T(8,128)S(1)}, f32[144,128]{1,0:T(8,128)S(1)}, u32[]{:S(2)}, u32[]{:S(2)}) collective-permute-start(f32[144,128]{1,0:T(8,128)S(1)} %get-tuple-element.90), channel_id=1, source_target_pairs={{0,2},{2,0},{4,6},{6,4},{8,10},{10,8},{12,14},{14,12},{16,18},{18,... | collective-permute-start | bytes 221192 | tf_op jit(solution)/shard_map/ppermute | solution.py:812
  31.7 6.7 %collective-permute-start.12 = (f32[144,128]{1,0:T(8,128)S(1)}, f32[144,128]{1,0:T(8,128)S(1)}, u32[]{:S(2)}, u32[]{:S(2)}) collective-permute-start(f32[144,128]{1,0:T(8,128)S(1)} %get-tuple-element.91), channel_id=1, source_target_pairs={{2,4},{6,8},{10,12},{14,16},{18,20},{22,24},{26,28},{30,0},{4,2},{... | collective-permute-start | bytes 221192 | tf_op jit(solution)/shard_map/ppermute | solution.py:811
  32.5 11.0 %collective-permute-start.13 = (f32[2,80,128]{2,1,0:T(8,128)S(1)}, f32[2,80,128]{2,1,0:T(8,128)S(1)}, u32[]{:S(2)}, u32[]{:S(2)}) collective-permute-start(f32[2,80,128]{2,1,0:T(8,128)S(1)} %get-tuple-element.92), channel_id=1, source_target_pairs={{0,1},{1,0},{2,3},{3,2},{4,5},{5,4},{6,7},{7,6},{8,9},{9,8},{10,11... | collective-permute-start | bytes 245768 | tf_op jit(solution)/shard_map/ppermute | solution.py:819
  34.0 4.4 %collective-permute-start.14 = (f32[1,128]{1,0:T(1,128)S(1)}, f32[1,128]{1,0:T(1,128)S(1)}, u32[]{:S(2)}, u32[]{:S(2)}) collective-permute-start(f32[1,128]{1,0:T(1,128)S(1)} %get-tuple-element.94), channel_id=1, source_target_pairs={{0,16},{1,17},{2,18},{3,19},{4,20},{5,21},{6,22},{7,23},{8,24},{9,... | collective-permute-start | bytes 1544 | tf_op jit(solution)/shard_map/ppermute | solution.py:844
  38.5 5.0 %collective-permute-start.15 = (f32[2,48,128]{2,1,0:T(8,128)S(1)}, f32[2,48,128]{2,1,0:T(8,128)S(1)}, u32[]{:S(2)}, u32[]{:S(2)}) collective-permute-start(f32[2,48,128]{2,1,0:T(8,128)S(1)} %get-tuple-element.95), channel_id=1, source_target_pairs={{0,1},{1,0},{2,3},{3,2},{4,5},{5,4},{6,7},{7,6},{8,9},{9,8},{10,11... | collective-permute-start | bytes 147464 | tf_op jit(solution)/shard_map/ppermute | solution.py:819
  39.9 3.5 %collective-permute-start.16 = (f32[1,128]{1,0:T(1,128)S(1)}, f32[1,128]{1,0:T(1,128)S(1)}, u32[]{:S(2)}, u32[]{:S(2)}) collective-permute-start(f32[1,128]{1,0:T(1,128)S(1)} %get-tuple-element.97), channel_id=1, source_target_pairs={{0,1},{1,0},{2,3},{3,2},{4,5},{5,4},{6,7},{7,6},{8,9},{9,8},{10,11... | collective-permute-start | bytes 1544 | tf_op jit(solution)/shard_map/ppermute | solution.py:844
  44.3 6.4 %collective-permute-start.17 = (f32[128,128]{1,0:T(8,128)S(1)}, f32[128,128]{1,0:T(8,128)S(1)}, u32[]{:S(2)}, u32[]{:S(2)}) collective-permute-start(f32[128,128]{1,0:T(8,128)S(1)} %get-tuple-element.101), channel_id=1, source_target_pairs={{0,2},{2,0},{4,6},{6,4},{8,10},{10,8},{12,14},{14,12},{16,18},{18,... | collective-permute-start | bytes 196616 | tf_op jit(solution)/shard_map/ppermute | solution.py:812
  44.4 6.5 %collective-permute-start.18 = (f32[128,128]{1,0:T(8,128)S(1)}, f32[128,128]{1,0:T(8,128)S(1)}, u32[]{:S(2)}, u32[]{:S(2)}) collective-permute-start(f32[128,128]{1,0:T(8,128)S(1)} %get-tuple-element.102), channel_id=1, source_target_pairs={{2,4},{6,8},{10,12},{14,16},{18,20},{22,24},{26,28},{30,0},{4,2},{... | collective-permute-start | bytes 196616 | tf_op jit(solution)/shard_map/ppermute | solution.py:811
  44.9 10.3 %collective-permute-start.19 = (f32[2,96,128]{2,1,0:T(8,128)S(1)}, f32[2,96,128]{2,1,0:T(8,128)S(1)}, u32[]{:S(2)}, u32[]{:S(2)}) collective-permute-start(f32[2,96,128]{2,1,0:T(8,128)S(1)} %get-tuple-element.103), channel_id=1, source_target_pairs={{0,1},{1,0},{2,3},{3,2},{4,5},{5,4},{6,7},{7,6},{8,9},{9,8},{10,11... | collective-permute-start | bytes 294920 | tf_op jit(solution)/shard_map/ppermute | solution.py:819
  50.9 4.4 %collective-permute-start.22 = (f32[2,48,128]{2,1,0:T(8,128)S(1)}, f32[2,48,128]{2,1,0:T(8,128)S(1)}, u32[]{:S(2)}, u32[]{:S(2)}) collective-permute-start(f32[2,48,128]{2,1,0:T(8,128)S(1)} %get-tuple-element.106), channel_id=1, source_target_pairs={{0,1},{1,0},{2,3},{3,2},{4,5},{5,4},{6,7},{7,6},{8,9},{9,8},{10,11... | collective-permute-start | bytes 147464 | tf_op jit(solution)/shard_map/ppermute | solution.py:819
  56.8 7.9 %collective-permute-start.24 = (f32[144,128]{1,0:T(8,128)S(1)}, f32[144,128]{1,0:T(8,128)S(1)}, u32[]{:S(2)}, u32[]{:S(2)}) collective-permute-start(f32[144,128]{1,0:T(8,128)S(1)} %get-tuple-element.109), channel_id=1, source_target_pairs={{0,2},{2,0},{4,6},{6,4},{8,10},{10,8},{12,14},{14,12},{16,18},{18,... | collective-permute-start | bytes 221192 | tf_op jit(solution)/shard_map/ppermute | solution.py:812
  56.9 7.9 %collective-permute-start.25 = (f32[144,128]{1,0:T(8,128)S(1)}, f32[144,128]{1,0:T(8,128)S(1)}, u32[]{:S(2)}, u32[]{:S(2)}) collective-permute-start(f32[144,128]{1,0:T(8,128)S(1)} %get-tuple-element.110), channel_id=1, source_target_pairs={{2,4},{6,8},{10,12},{14,16},{18,20},{22,24},{26,28},{30,0},{4,2},{... | collective-permute-start | bytes 221192 | tf_op jit(solution)/shard_map/ppermute | solution.py:811
  59.6 10.1 %collective-permute-start.26 = (f32[2,80,128]{2,1,0:T(8,128)S(1)}, f32[2,80,128]{2,1,0:T(8,128)S(1)}, u32[]{:S(2)}, u32[]{:S(2)}) collective-permute-start(f32[2,80,128]{2,1,0:T(8,128)S(1)} %get-tuple-element.111), channel_id=1, source_target_pairs={{0,1},{1,0},{2,3},{3,2},{4,5},{5,4},{6,7},{7,6},{8,9},{9,8},{10,11... | collective-permute-start | bytes 245768 | tf_op jit(solution)/shard_map/ppermute | solution.py:819
  60.3 4.4 %collective-permute-start.27 = (f32[1,128]{1,0:T(1,128)S(1)}, f32[1,128]{1,0:T(1,128)S(1)}, u32[]{:S(2)}, u32[]{:S(2)}) collective-permute-start(f32[1,128]{1,0:T(1,128)S(1)} %get-tuple-element.113), channel_id=1, source_target_pairs={{0,16},{1,17},{2,18},{3,19},{4,20},{5,21},{6,22},{7,23},{8,24},{9,... | collective-permute-start | bytes 1544 | tf_op jit(solution)/shard_map/ppermute | solution.py:844
  64.8 5.0 %collective-permute-start.28 = (f32[2,48,128]{2,1,0:T(8,128)S(1)}, f32[2,48,128]{2,1,0:T(8,128)S(1)}, u32[]{:S(2)}, u32[]{:S(2)}) collective-permute-start(f32[2,48,128]{2,1,0:T(8,128)S(1)} %get-tuple-element.114), channel_id=1, source_target_pairs={{0,1},{1,0},{2,3},{3,2},{4,5},{5,4},{6,7},{7,6},{8,9},{9,8},{10,11... | collective-permute-start | bytes 147464 | tf_op jit(solution)/shard_map/ppermute | solution.py:819
  70.6 6.5 %collective-permute-start.31 = (f32[128,128]{1,0:T(8,128)S(1)}, f32[128,128]{1,0:T(8,128)S(1)}, u32[]{:S(2)}, u32[]{:S(2)}) collective-permute-start(f32[128,128]{1,0:T(8,128)S(1)} %get-tuple-element.120), channel_id=1, source_target_pairs={{2,4},{6,8},{10,12},{14,16},{18,20},{22,24},{26,28},{30,0},{4,2},{... | collective-permute-start | bytes 196616 | tf_op jit(solution)/shard_map/ppermute | solution.py:811
  71.1 6.7 %collective-permute-start.32 = (f32[2,96,128]{2,1,0:T(8,128)S(1)}, f32[2,96,128]{2,1,0:T(8,128)S(1)}, u32[]{:S(2)}, u32[]{:S(2)}) collective-permute-start(f32[2,96,128]{2,1,0:T(8,128)S(1)} %get-tuple-element.121), channel_id=1, source_target_pairs={{0,1},{1,0},{2,3},{3,2},{4,5},{5,4},{6,7},{7,6},{8,9},{9,8},{10,11... | collective-permute-start | bytes 294920 | tf_op jit(solution)/shard_map/ppermute | solution.py:819
  77.0 4.2 %collective-permute-start.33 = (f32[2,48,128]{2,1,0:T(8,128)S(1)}, f32[2,48,128]{2,1,0:T(8,128)S(1)}, u32[]{:S(2)}, u32[]{:S(2)}) collective-permute-start(f32[2,48,128]{2,1,0:T(8,128)S(1)} %get-tuple-element.129), channel_id=1, source_target_pairs={{0,1},{1,0},{2,3},{3,2},{4,5},{5,4},{6,7},{7,6},{8,9},{9,8},{10,11... | collective-permute-start | bytes 147464 | tf_op jit(solution)/shard_map/ppermute | solution.py:819
  82.7 13.6 %collective-permute-start.34 = (f32[144,128]{1,0:T(8,128)S(1)}, f32[144,128]{1,0:T(8,128)S(1)}, u32[]{:S(2)}, u32[]{:S(2)}) collective-permute-start(f32[144,128]{1,0:T(8,128)S(1)} %get-tuple-element.132), channel_id=1, source_target_pairs={{0,2},{2,0},{4,6},{6,4},{8,10},{10,8},{12,14},{14,12},{16,18},{18,... | collective-permute-start | bytes 221192 | tf_op jit(solution)/shard_map/ppermute | solution.py:812
  82.8 13.5 %collective-permute-start.35 = (f32[144,128]{1,0:T(8,128)S(1)}, f32[144,128]{1,0:T(8,128)S(1)}, u32[]{:S(2)}, u32[]{:S(2)}) collective-permute-start(f32[144,128]{1,0:T(8,128)S(1)} %get-tuple-element.133), channel_id=1, source_target_pairs={{2,4},{6,8},{10,12},{14,16},{18,20},{22,24},{26,28},{30,0},{4,2},{... | collective-permute-start | bytes 221192 | tf_op jit(solution)/shard_map/ppermute | solution.py:811
  82.8 14.1 %collective-permute-start.36 = (f32[2,80,128]{2,1,0:T(8,128)S(1)}, f32[2,80,128]{2,1,0:T(8,128)S(1)}, u32[]{:S(2)}, u32[]{:S(2)}) collective-permute-start(f32[2,80,128]{2,1,0:T(8,128)S(1)} %get-tuple-element.134), channel_id=1, source_target_pairs={{0,1},{1,0},{2,3},{3,2},{4,5},{5,4},{6,7},{7,6},{8,9},{9,8},{10,11... | collective-permute-start | bytes 245768 | tf_op jit(solution)/shard_map/ppermute | solution.py:819
  96.3 4.2 %collective-permute-start.37 = (f32[2,48,128]{2,1,0:T(8,128)S(1)}, f32[2,48,128]{2,1,0:T(8,128)S(1)}, u32[]{:S(2)}, u32[]{:S(2)}) collective-permute-start(f32[2,48,128]{2,1,0:T(8,128)S(1)} %get-tuple-element.141), channel_id=1, source_target_pairs={{0,1},{1,0},{2,3},{3,2},{4,5},{5,4},{6,7},{7,6},{8,9},{9,8},{10,11... | collective-permute-start | bytes 147464 | tf_op jit(solution)/shard_map/ppermute | solution.py:819
  (15 other events, 70.8 us)

commit v3 on v2

--- a/solution.py
+++ b/solution.py
@@ -228,30 +228,35 @@
     return result
 
 
-def masks(rows):
-    layer = lax.broadcasted_iota(jnp.int32, (rows, LANES), 0) % 8
-    elem = lax.broadcasted_iota(jnp.int32, (rows, LANES), 1)
+def masks():
+    layer = lax.broadcasted_iota(jnp.int32, (8, LANES), 0)
+    elem = lax.broadcasted_iota(jnp.int32, (8, LANES), 1)
     return layer, elem > 0, elem < LANES - 1
 
 
 def spread(values, first, last):
-    layer, has_before, has_after = masks(values.shape[0])
-    before = pltpu.roll(values, 1, axis=1)
-    after = pltpu.roll(values, LANES - 1, axis=1)
-    return jnp.where(
-        (layer == first) & has_before,
-        before,
-        jnp.where((layer == last) & has_after, after, 0.0),
-    )
+    layer, has_before, has_after = masks()
+    cubes = values.reshape(values.shape[0] // 8, 8, LANES)
+    before = pltpu.roll(cubes, 1, axis=2)
+    after = pltpu.roll(cubes, LANES - 1, axis=2)
+    before_mask = ((layer == first) & has_before)[None]
+    after_mask = ((layer == last) & has_after)[None]
+    result = jnp.where(before_mask, before, jnp.where(after_mask, after, 0.0))
+    return result.reshape(values.shape)
 
 
 def radial_sum(values):
-    rows = values.shape[0]
-    layer, _, _ = masks(rows)
-    cubes = values.reshape(rows // 8, 8, LANES)
-    up = pltpu.roll(cubes, 1, axis=1).reshape(rows, LANES)
-    down = pltpu.roll(cubes, 7, axis=1).reshape(rows, LANES)
-    return values + spread(jnp.where(layer == 0, up, down), 0, 7)
+    layer, has_before, has_after = masks()
+    cubes = values.reshape(values.shape[0] // 8, 8, LANES)
+    up = pltpu.roll(cubes, 1, axis=1)
+    down = pltpu.roll(cubes, 7, axis=1)
+    ends = jnp.where((layer == 0)[None], up, down)
+    before = pltpu.roll(ends, 1, axis=2)
+    after = pltpu.roll(ends, LANES - 1, axis=2)
+    before_mask = ((layer == 0) & has_before)[None]
+    after_mask = ((layer == 7) & has_after)[None]
+    ends = jnp.where(before_mask, before, jnp.where(after_mask, after, 0.0))
+    return (cubes + ends).reshape(values.shape)
 
 
 def total(values):
@@ -294,7 +299,7 @@
 
 def conv_kernel(
     u_hbm, row_hbm, plane_hbm, grad_hbm,
-    conv_ref, row_ref, in_ref, out_ref, early_ref, late_ref,
+    conv_ref, row_ref, out_ref, early_ref, in_ref, late_ref,
     u_ref, small_ref, plane_ref, grad_ref, sems,
 ):
     copies = [
@@ -343,15 +348,17 @@
     send_axial(in_ref, out_ref, low + [row], high + [row])
 
 
-def mean_kernel(diff_ref, kbar_ref):
+def inverse_kernel(diff_ref, spectrum_ref, inverse_ref):
     mean = diff_ref[0]
     for a in range(1, 8):
         mean = mean + diff_ref[a]
-    mean = jnp.sum(mean, axis=0, keepdims=True) * (1.0 / 512.0)
-    kbar_ref[...] = jnp.broadcast_to(mean, (8, LANES))
-
-
-def conv_side_kernel(in_ref, out_ref, late_ref, row_ref, send_ref):
+    kbar = jnp.sum(mean, axis=0, keepdims=True) * (1.0 / 512.0)
+    plane_spectrum = kbar * spectrum_ref[...] + mass_shift
+    for i in range(10):
+        inverse_ref[i] = 1.0 / (plane_spectrum + float(EIGVAL[i]) * kbar)
+
+
+def conv_side_kernel(out_ref, in_ref, late_ref, row_ref, send_ref):
     before, after = got_axial(in_ref, out_ref)
     count = row_ref.shape[0]
     for side, b in ((0, 0), (1, 7)):
@@ -420,7 +427,7 @@
         late_ref[side, 24:32] = inners[7]
 
 
-def raw_side_kernel(in_ref, out_ref, late_ref, row_ref, send_ref, pass_ref):
+def raw_side_kernel(out_ref, in_ref, late_ref, row_ref, send_ref, pass_ref):
     pass_ref[...] = row_ref[...]
     before, after = got_axial(in_ref, out_ref)
     for side, (edge, inner) in enumerate(((0, 1), (7, 6))):
@@ -433,8 +440,8 @@
 
 
 def divergence_kernel(
-    conv_ref, u_ref, in_ref, out_ref, early_ref, late_ref, row_ref, plane_ref, over_ref, div_ref,
-    g_ref, send_in_ref, send_out_ref, send_early_ref, send_late_ref, near_ref, pay_ref,
+    conv_ref, u_ref, out_ref, in_ref, early_ref, late_ref, row_ref, plane_ref, over_ref, div_ref,
+    g_ref, send_out_ref, send_early_ref, send_in_ref, send_late_ref, near_ref, pay_ref,
 ):
     before, after = got_axial(in_ref, out_ref)
     plane, over = plane_ref[...], over_ref[...]
@@ -517,9 +524,9 @@
 
 
 def solve_kernel(
-    g_ref, in_ref, out_ref, early_ref, late_ref, row_ref,
-    kbar_ref, into_ref, outof_ref, spectrum_ref,
-    planes_ref, solved_ref, part_ref, send_in_ref, send_out_ref, send_early_ref, send_late_ref,
+    g_ref, out_ref, in_ref, early_ref, late_ref, row_ref,
+    inverse_ref, into_ref, outof_ref,
+    planes_ref, solved_ref, part_ref, send_out_ref, send_early_ref, send_in_ref, send_late_ref,
     pass_ref,
 ):
     pass_ref[...] = row_ref[...]
@@ -528,9 +535,7 @@
         planes_ref[e] = planes[e]
     flat = product(into_ref, jnp.concatenate(planes, axis=1))
     parts = to_spectral([flat[:, LANES * e : LANES * e + LANES] for e in range(10)])
-    kbar = kbar_ref[0:1, :]
-    plane_spectrum = kbar * spectrum_ref[...] + mass_shift
-    parts = [parts[i] / (plane_spectrum + float(EIGVAL[i]) * kbar) for i in range(10)]
+    parts = [parts[i] * inverse_ref[i] for i in range(10)]
     parts = from_spectral(parts)
     flat = product(outof_ref, jnp.concatenate(parts, axis=1))
     solved = [flat[:, LANES * e : LANES * e + LANES] for e in range(10)]
@@ -566,7 +571,7 @@
     )
 
 
-def solved_side_kernel(in_ref, out_ref, late_ref, row_ref, send_ref, pass_ref):
+def solved_side_kernel(out_ref, in_ref, late_ref, row_ref, send_ref, pass_ref):
     pass_ref[...] = row_ref[...]
     before, after = got_axial(in_ref, out_ref)
     for side, b in ((0, 0), (1, 7)):
@@ -613,11 +618,11 @@
 def add_coarse(parts, row, near_ref):
     values = jnp.sum(near_ref[...] * row, axis=1, keepdims=True)
     own = [[values[3 * i + j : 3 * i + j + 1] for j in range(3)] for i in range(3)]
-    b = lax.broadcasted_iota(jnp.int32, (64, LANES), 0) // 8
     fields = []
     for i in range(3):
         ends = [0.5 * (own[i][1] + own[i][j]) for j in (0, 2)]
-        fields.append(jnp.where(b == 0, ends[0], jnp.where(b == 7, ends[1], own[i][1])))
+        rows = [jnp.broadcast_to(value, (8, LANES)) for value in (ends[0], own[i][1], ends[1])]
+        fields.append(jnp.concatenate([rows[0]] + [rows[1]] * 6 + [rows[2]], axis=0))
     first, last = 0.5 * (fields[0] + fields[1]), 0.5 * (fields[1] + fields[2])
     return [
         parts[a] + (first if a == 0 else last if a == 7 else fields[1]) for a in range(8)
@@ -668,9 +673,9 @@
 
 
 def first_apply_kernel(
-    part_ref, in_ref, out_ref, early_ref, late_ref, near_ref, diff_ref, plane_ref, grad_ref, div_ref,
+    part_ref, out_ref, in_ref, early_ref, late_ref, near_ref, diff_ref, plane_ref, grad_ref, div_ref,
     sums_ref, planes_ref, solved_ref,
-    z_ref, raw_ref, g_ref, send_in_ref, send_out_ref, send_early_ref, send_late_ref, row_ref, pay_ref,
+    z_ref, raw_ref, g_ref, send_out_ref, send_early_ref, send_in_ref, send_late_ref, row_ref, pay_ref,
 ):
     row, _ = got_sums(sums_ref, 0)
     values = got_solved(part_ref, in_ref, out_ref, early_ref, late_ref)
@@ -693,9 +698,9 @@
 
 
 def second_apply_kernel(
-    part_ref, in_ref, out_ref, early_ref, late_ref, near_ref, diff_ref, plane_ref, grad_ref, div_ref,
+    part_ref, out_ref, in_ref, early_ref, late_ref, near_ref, diff_ref, plane_ref, grad_ref, div_ref,
     sums_ref, row_ref, z0_ref,
-    y_ref, z_ref, raw_ref, g_ref, send_in_ref, send_out_ref, send_early_ref, send_late_ref,
+    y_ref, z_ref, raw_ref, g_ref, send_out_ref, send_early_ref, send_in_ref, send_late_ref,
 ):
     _, row_q, _, _, alpha = first_step(sums_ref, row_ref)
     change = got_solved(part_ref, in_ref, out_ref, early_ref, late_ref)
@@ -754,7 +759,7 @@
 
 
 def last_kernel(
-    part_ref, in_ref, out_ref, early_ref, late_ref, near_ref, sums_ref, old_sums_ref, row_ref,
+    part_ref, out_ref, in_ref, early_ref, late_ref, near_ref, sums_ref, old_sums_ref, row_ref,
     y_ref, z0_ref, z1_ref, planes_r_ref, planes_q_ref, planes_w_ref,
     pressure_ref, residual_ref, direction_ref,
 ):
@@ -863,14 +868,14 @@
 
     field, sums, row_shape = (8, 64, LANES), (devices, width * LANES), (8, width * LANES)
     boxes = [(10, 144, LANES), (10, 144, LANES)]
-    raw_sends = [(128, LANES), (128, LANES), (2, 96, LANES), (2, 32, LANES)]
-    solved_sends = [(144, LANES), (144, LANES), (2, 80, LANES), (2, 48, LANES)]
+    raw_sends = [(128, LANES), (2, 96, LANES), (128, LANES), (2, 32, LANES)]
+    solved_sends = [(144, LANES), (2, 80, LANES), (144, LANES), (2, 48, LANES)]
 
     far = pl.BlockSpec(memory_space=pltpu.HBM)
     conv, row, *sends = kernel_call(
         conv_kernel,
-        [(3,) + field, (count, LANES), (192 + count, LANES), (192 + count, LANES)]
-        + [(2, 144, LANES), (2, 48, LANES)],
+        [(3,) + field, (count, LANES), (192 + count, LANES), (2, 144, LANES)]
+        + [(192 + count, LANES), (2, 48, LANES)],
         *(pltpu.with_memory_space_constraint(x, pltpu.HBM) for x in (u, coarse_factor, plane, grad)),
         in_specs=[far] * 4,
         scratch_shapes=[
@@ -881,16 +886,16 @@
             pltpu.SemaphoreType.DMA((4,)),
         ],
     )
-    (kbar,) = kernel_call(mean_kernel, [(8, LANES)], diff)
+    (inverse,) = kernel_call(inverse_kernel, [(10, 112, LANES)], diff, spectrum)
 
     def exchange(side_kernel, late_rows, sends, extra, extra_shape=None):
-        send_in, send_out, send_early, send_late = sends
+        send_out, send_early, send_in, send_late = sends
         inner, outer = axial_swap(send_in, send_out)
         early = azim_swap(send_early)
         shapes = [(2, late_rows, LANES)]
         shapes = shapes if extra_shape is None else shapes + [extra_shape]
-        late, *passed = kernel_call(side_kernel, shapes, inner, outer, send_late, extra)
-        return [inner, outer, early, azim_swap(late)] + passed
+        late, *passed = kernel_call(side_kernel, shapes, outer, inner, send_late, extra)
+        return [outer, inner, early, azim_swap(late)] + passed
 
     one = (1, width * LANES)
     groups = sum_steps()
@@ -900,7 +905,7 @@
         [field] + raw_sends + [(16, width * LANES), one],
         conv, u, *moved, row, plane, over, div,
     )
-    solver = (kbar, into, outof, spectrum)
+    solver = (inverse, into, outof)
     operator = (near, diff, plane, grad, div)
     solve_shapes = boxes + [field] + solved_sends + [one]
 
@@ -938,13 +943,14 @@
         solve_kernel, solve_shapes, g, *moved, pay, *solver
     )
     (pay,) = kernel_call(
-        second_dots_kernel, [sums], pay, planes_r, planes_q, planes_w, solved_r, solved_q, solved_w
-    )
-    *moved, pay = exchange(solved_side_kernel, 48, sends, gather_sums(pay), sums)
+        second_dots_kernel, [one], pay, planes_r, planes_q, planes_w, solved_r, solved_q, solved_w
+    )
+    gathered = gather_sums(jnp.broadcast_to(pay, sums))
+    *moved, _ = exchange(solved_side_kernel, 48, sends, pay, one)
     pressure, residual, direction = kernel_call(
         last_kernel,
         [field, field, field],
-        part, *moved, near, pay, first_sums, row_r,
+        part, *moved, near, gathered, first_sums, row_r,
         y, z0, z1, planes_r, planes_q, planes_w,
     )
     return pressure.reshape(shape), residual.reshape(shape), direction.reshape(shape)

time: 102 us -> 101 us (level)
  blocking collectives: 12.2 us -> 8.89 us
  starting transfers between devices: 34.9 us -> 36.5 us
    ppermute x7, waiting for transfers between devices: 5.23 us -> 9.4 us  [axial_swap(): from_outer = lax.ppermute(outer_rows, 'axial', outer)]
    ppermute x14, waiting for transfers between devices: 9.89 us -> 6.1 us  [azim_swap(): return lax.ppermute(sides, 'azim', [(0, 1), (1, 0)])]
    all_to_all x1, blocking collectives: 12.2 us -> 8.89 us  [gather_sums(): return lax.all_to_all(rows, ALL, 0, 0, tiled=True)]
    ppermute x14, starting transfers between devices: 15.2 us -> 18.5 us  [azim_swap(): return lax.ppermute(sides, 'azim', [(0, 1), (1, 0)])]
    ppermute x7, starting transfers between devices: 13.6 us -> 12.1 us  [axial_swap(): from_outer = lax.ppermute(outer_rows, 'axial', outer)]
  transfers between devices with their start and end apart: 38 -> 38, of which waited for: 17 -> 16; matrix products, arithmetic and copies ran while one was open for 0% -> 0% of each run, Pallas kernels for 1% -> 2%
where the time goes in v3:
time: 101 us; the launch traced here: 100 us
  waiting for transfers between devices  42 us (42%)
  starting transfers between devices  36.5 us (36%)
  Pallas kernels  11.8 us (12%)
  blocking collectives  8.89 us (9%)
    ppermute x10, waiting for transfers between devices, partial_sum(): row = row + lax.ppermute(row, ALL, [(i, i ^ step) for i in range(count)])  26.5 us
    ppermute x14, starting transfers between devices, azim_swap(): return lax.ppermute(sides, 'azim', [(0, 1), (1, 0)])  18.5 us
    ppermute x7, starting transfers between devices, axial_swap(): from_outer = lax.ppermute(outer_rows, 'axial', outer)  12.1 us
    pallas_call x18, Pallas kernels, kernel_call(): pl.pallas_call(kernel, out_shape=outs, compiler_params=pltpu.CompilerPara...  11.8 us
    ppermute x7, waiting for transfers between devices, axial_swap(): from_outer = lax.ppermute(outer_rows, 'axial', outer)  9.4 us
    all_to_all x1, blocking collectives, gather_sums(): return lax.all_to_all(rows, ALL, 0, 0, tiled=True)  8.89 us
    ppermute x14, waiting for transfers between devices, azim_swap(): return lax.ppermute(sides, 'azim', [(0, 1), (1, 0)])  6.1 us
    ppermute x10, starting transfers between devices, partial_sum(): row = row + lax.ppermute(row, ALL, [(i, i ^ step) for i in range(count)])  5.69 us
  transfers between devices with their start and end apart: 38, of which 16 were waited for; matrix products, arithmetic and copies ran while one was open for 0% of the time, Pallas kernels for 2%

profile of v3, /device:TPU:0, one launch (start us, length us, event | category | flops | bytes accessed | tf_op | source)
XLA Modules:
  0.0 100.3 jit_solution(17236195147669412338)
XLA Ops:
  0.6 2.1 %shard_map.121 = (f32[3,8,64,128]{3,2,1,0:T(8,128)S(1)}, f32[8,128]{1,0:T(8,128)S(1)}, f32[200,128]{1,0:T(8,128)S(1)}, f32[2,144,128]{2,1,0:T(8,128)S(1)}, f32[2...) custom-call(f32[3,8,64,128]{3,2,1,0:T(8,128)} %bitcast.13, f32[1,32]{1,0:T(1,128)} %row_hbm.1, ...), custom_call_target="tpu_custom_call" | custom-call | tf_op jit(solution)/shard_map/pallas_call | solution.py:802
  2.8 5.5 %collective-permute-start = (f32[200,128]{1,0:T(8,128)S(1)}, f32[200,128]{1,0:T(8,128)S(1)}, u32[]{:S(2)}, u32[]{:S(2)}) collective-permute-start(f32[200,128]{1,0:T(8,128)S(1)} %get-tuple-element.75), channel_id=1, source_target_pairs={{2,4},{6,8},{10,12},{14,16},{18,20},{22,24},{26,28},{30,0},{4,2},{... | collective-permute-start | bytes 307208 | tf_op jit(solution)/shard_map/ppermute | solution.py:816
  8.3 1.5 %collective-permute-start.2 = (f32[2,144,128]{2,1,0:T(8,128)S(1)}, f32[2,144,128]{2,1,0:T(8,128)S(1)}, u32[]{:S(2)}, u32[]{:S(2)}) collective-permute-start(f32[2,144,128]{2,1,0:T(8,128)S(1)} %get-tuple-element.77), channel_id=1, source_target_pairs={{0,1},{1,0},{2,3},{3,2},{4,5},{5,4},{6,7},{7,6},{8,9},{9,8},{10,11... | collective-permute-start | bytes 442376 | tf_op jit(solution)/shard_map/ppermute | solution.py:824
  10.7 2.0 %collective-permute-start.3 = (f32[2,72,128]{2,1,0:T(8,128)S(1)}, f32[2,72,128]{2,1,0:T(8,128)S(1)}, u32[]{:S(2)}, u32[]{:S(2)}) collective-permute-start(f32[2,72,128]{2,1,0:T(8,128)S(1)} %shard_map.122), channel_id=1, source_target_pairs={{0,1},{1,0},{2,3},{3,2},{4,5},{5,4},{6,7},{7,6},{8,9},{9,8},{10,11... | collective-permute-start | bytes 221192 | tf_op jit(solution)/shard_map/ppermute | solution.py:824
  12.7 2.2 %collective-permute-done.2.early_ref = f32[2,144,128]{2,1,0:T(8,128)S(1)} collective-permute-done((f32[2,144,128]{2,1,0:T(8,128)S(1)}, f32[2,144,128]{2,1,0:T(8,128)S(1)}, u32[]{:S(2)}, u32[]{:S(2)}) %collective-permute-start.2) | collective-permute-done | bytes 147488 | tf_op jit(solution)/shard_map/ppermute | solution.py:824
  16.7 2.3 %collective-permute-start.4 = (f32[128,128]{1,0:T(8,128)S(1)}, f32[128,128]{1,0:T(8,128)S(1)}, u32[]{:S(2)}, u32[]{:S(2)}) collective-permute-start(f32[128,128]{1,0:T(8,128)S(1)} %get-tuple-element.81), channel_id=1, source_target_pairs={{2,4},{6,8},{10,12},{14,16},{18,20},{22,24},{26,28},{30,0},{4,2},{... | collective-permute-start | bytes 196616 | tf_op jit(solution)/shard_map/ppermute | solution.py:816
  19.0 1.5 %collective-permute-start.6 = (f32[2,96,128]{2,1,0:T(8,128)S(1)}, f32[2,96,128]{2,1,0:T(8,128)S(1)}, u32[]{:S(2)}, u32[]{:S(2)}) collective-permute-start(f32[2,96,128]{2,1,0:T(8,128)S(1)} %get-tuple-element.83), channel_id=1, source_target_pairs={{0,1},{1,0},{2,3},{3,2},{4,5},{5,4},{6,7},{7,6},{8,9},{9,8},{10,11... | collective-permute-start | bytes 294920 | tf_op jit(solution)/shard_map/ppermute | solution.py:824
  20.5 3.5 %collective-permute-done.7 = f32[1,128]{1,0:T(1,128)S(1)} collective-permute-done((f32[1,128]{1,0:T(1,128)S(1)}, f32[1,128]{1,0:T(1,128)S(1)}, u32[]{:S(2)}, u32[]{:S(2)}) %collective-permute-start.7) | collective-permute-done | bytes 544 | tf_op jit(solution)/shard_map/ppermute | solution.py:849
  26.1 3.3 %collective-permute-done.10 = f32[1,128]{1,0:T(1,128)S(1)} collective-permute-done((f32[1,128]{1,0:T(1,128)S(1)}, f32[1,128]{1,0:T(1,128)S(1)}, u32[]{:S(2)}, u32[]{:S(2)}) %collective-permute-start.10) | collective-permute-done | bytes 544 | tf_op jit(solution)/shard_map/ppermute | solution.py:849
  29.5 1.5 %shard_map.126 = (f32[10,144,128]{2,1,0:T(8,128)S(1)}, f32[10,144,128]{2,1,0:T(8,128)S(1)}, f32[8,64,128]{2,1,0:T(8,128)S(1)}, f32[144,128]{1,0:T(8,128)S(1)}, f...) custom-call(f32[8,64,128]{2,1,0:T(8,128)S(1)} %get-tuple-element.80.g_ref, ...), custom_call_target="tpu_custom_call" | custom-call | tf_op jit(solution)/shard_map/pallas_call | solution.py:802
  32.2 1.5 %collective-permute-start.13 = (f32[2,80,128]{2,1,0:T(8,128)S(1)}, f32[2,80,128]{2,1,0:T(8,128)S(1)}, u32[]{:S(2)}, u32[]{:S(2)}) collective-permute-start(f32[2,80,128]{2,1,0:T(8,128)S(1)} %get-tuple-element.91), channel_id=1, source_target_pairs={{0,1},{1,0},{2,3},{3,2},{4,5},{5,4},{6,7},{7,6},{8,9},{9,8},{10,11... | collective-permute-start | bytes 245768 | tf_op jit(solution)/shard_map/ppermute | solution.py:824
  34.2 3.9 %collective-permute-done.14 = f32[1,128]{1,0:T(1,128)S(1)} collective-permute-done((f32[1,128]{1,0:T(1,128)S(1)}, f32[1,128]{1,0:T(1,128)S(1)}, u32[]{:S(2)}, u32[]{:S(2)}) %collective-permute-start.14) | collective-permute-done | bytes 544 | tf_op jit(solution)/shard_map/ppermute | solution.py:849
  39.0 1.3 %collective-permute-start.16 = (f32[1,128]{1,0:T(1,128)S(1)}, f32[1,128]{1,0:T(1,128)S(1)}, u32[]{:S(2)}, u32[]{:S(2)}) collective-permute-start(f32[1,128]{1,0:T(1,128)S(1)} %get-tuple-element.96), channel_id=1, source_target_pairs={{0,1},{1,0},{2,3},{3,2},{4,5},{5,4},{6,7},{7,6},{8,9},{9,8},{10,11... | collective-permute-start | bytes 1544 | tf_op jit(solution)/shard_map/ppermute | solution.py:849
  40.3 2.3 %collective-permute-done.16 = f32[1,128]{1,0:T(1,128)S(1)} collective-permute-done((f32[1,128]{1,0:T(1,128)S(1)}, f32[1,128]{1,0:T(1,128)S(1)}, u32[]{:S(2)}, u32[]{:S(2)}) %collective-permute-start.16) | collective-permute-done | bytes 544 | tf_op jit(solution)/shard_map/ppermute | solution.py:849
  46.0 2.8 %collective-permute-done.20 = f32[1,128]{1,0:T(1,128)S(1)} collective-permute-done((f32[1,128]{1,0:T(1,128)S(1)}, f32[1,128]{1,0:T(1,128)S(1)}, u32[]{:S(2)}, u32[]{:S(2)}) %collective-permute-start.20) | collective-permute-done | bytes 544 | tf_op jit(solution)/shard_map/ppermute | solution.py:849
  50.0 1.3 %collective-permute-start.22 = (f32[2,48,128]{2,1,0:T(8,128)S(1)}, f32[2,48,128]{2,1,0:T(8,128)S(1)}, u32[]{:S(2)}, u32[]{:S(2)}) collective-permute-start(f32[2,48,128]{2,1,0:T(8,128)S(1)} %get-tuple-element.105), channel_id=1, source_target_pairs={{0,1},{1,0},{2,3},{3,2},{4,5},{5,4},{6,7},{7,6},{8,9},{9,8},{10,11... | collective-permute-start | bytes 147464 | tf_op jit(solution)/shard_map/ppermute | solution.py:824
  52.1 2.7 %collective-permute-done.23 = f32[1,128]{1,0:T(1,128)S(1)} collective-permute-done((f32[1,128]{1,0:T(1,128)S(1)}, f32[1,128]{1,0:T(1,128)S(1)}, u32[]{:S(2)}, u32[]{:S(2)}) %collective-permute-start.23) | collective-permute-done | bytes 544 | tf_op jit(solution)/shard_map/ppermute | solution.py:849
  54.8 1.5 %shard_map.130 = (f32[10,144,128]{2,1,0:T(8,128)S(1)}, f32[10,144,128]{2,1,0:T(8,128)S(1)}, f32[8,64,128]{2,1,0:T(8,128)S(1)}, f32[144,128]{1,0:T(8,128)S(1)}, f...) custom-call(f32[8,64,128]{2,1,0:T(8,128)S(1)} %get-tuple-element.99.g_ref, ...), custom_call_target="tpu_custom_call" | custom-call | tf_op jit(solution)/shard_map/pallas_call | solution.py:802
  56.3 2.4 %collective-permute-start.24 = (f32[144,128]{1,0:T(8,128)S(1)}, f32[144,128]{1,0:T(8,128)S(1)}, u32[]{:S(2)}, u32[]{:S(2)}) collective-permute-start(f32[144,128]{1,0:T(8,128)S(1)} %get-tuple-element.108), channel_id=1, source_target_pairs={{2,4},{6,8},{10,12},{14,16},{18,20},{22,24},{26,28},{30,0},{4,2},{... | collective-permute-start | bytes 221192 | tf_op jit(solution)/shard_map/ppermute | solution.py:816
  58.7 1.5 %collective-permute-start.26 = (f32[2,80,128]{2,1,0:T(8,128)S(1)}, f32[2,80,128]{2,1,0:T(8,128)S(1)}, u32[]{:S(2)}, u32[]{:S(2)}) collective-permute-start(f32[2,80,128]{2,1,0:T(8,128)S(1)} %get-tuple-element.110), channel_id=1, source_target_pairs={{0,1},{1,0},{2,3},{3,2},{4,5},{5,4},{6,7},{7,6},{8,9},{9,8},{10,11... | collective-permute-start | bytes 245768 | tf_op jit(solution)/shard_map/ppermute | solution.py:824
  61.0 3.7 %collective-permute-done.27 = f32[1,128]{1,0:T(1,128)S(1)} collective-permute-done((f32[1,128]{1,0:T(1,128)S(1)}, f32[1,128]{1,0:T(1,128)S(1)}, u32[]{:S(2)}, u32[]{:S(2)}) %collective-permute-start.27) | collective-permute-done | bytes 544 | tf_op jit(solution)/shard_map/ppermute | solution.py:849
  65.3 1.5 %collective-permute-start.29 = (f32[1,128]{1,0:T(1,128)S(1)}, f32[1,128]{1,0:T(1,128)S(1)}, u32[]{:S(2)}, u32[]{:S(2)}) collective-permute-start(f32[1,128]{1,0:T(1,128)S(1)} %get-tuple-element.114), channel_id=1, source_target_pairs={{0,1},{1,0},{2,3},{3,2},{4,5},{5,4},{6,7},{7,6},{8,9},{9,8},{10,11... | collective-permute-start | bytes 1544 | tf_op jit(solution)/shard_map/ppermute | solution.py:849
  66.8 2.1 %collective-permute-done.29 = f32[1,128]{1,0:T(1,128)S(1)} collective-permute-done((f32[1,128]{1,0:T(1,128)S(1)}, f32[1,128]{1,0:T(1,128)S(1)}, u32[]{:S(2)}, u32[]{:S(2)}) %collective-permute-start.29) | collective-permute-done | bytes 544 | tf_op jit(solution)/shard_map/ppermute | solution.py:849
  69.9 1.5 %collective-permute-start.32 = (f32[2,96,128]{2,1,0:T(8,128)S(1)}, f32[2,96,128]{2,1,0:T(8,128)S(1)}, u32[]{:S(2)}, u32[]{:S(2)}) collective-permute-start(f32[2,96,128]{2,1,0:T(8,128)S(1)} %get-tuple-element.120), channel_id=1, source_target_pairs={{0,1},{1,0},{2,3},{3,2},{4,5},{5,4},{6,7},{7,6},{8,9},{9,8},{10,11... | collective-permute-start | bytes 294920 | tf_op jit(solution)/shard_map/ppermute | solution.py:824
  72.0 4.1 %collective-permute-done.30.out_ref = f32[128,128]{1,0:T(8,128)S(1)} collective-permute-done((f32[128,128]{1,0:T(8,128)S(1)}, f32[128,128]{1,0:T(8,128)S(1)}, u32[]{:S(2)}, u32[]{:S(2)}) %collective-permute-start.30) | collective-permute-done | bytes 65568 | tf_op jit(solution)/shard_map/ppermute | solution.py:816
  76.2 1.5 %collective-permute-start.33 = (f32[2,48,128]{2,1,0:T(8,128)S(1)}, f32[2,48,128]{2,1,0:T(8,128)S(1)}, u32[]{:S(2)}, u32[]{:S(2)}) collective-permute-start(f32[2,48,128]{2,1,0:T(8,128)S(1)} %get-tuple-element.128), channel_id=1, source_target_pairs={{0,1},{1,0},{2,3},{3,2},{4,5},{5,4},{6,7},{7,6},{8,9},{9,8},{10,11... | collective-permute-start | bytes 147464 | tf_op jit(solution)/shard_map/ppermute | solution.py:824
  77.6 2.7 %collective-permute-done.33.late_ref = f32[2,48,128]{2,1,0:T(8,128)S(1)} collective-permute-done((f32[2,48,128]{2,1,0:T(8,128)S(1)}, f32[2,48,128]{2,1,0:T(8,128)S(1)}, u32[]{:S(2)}, u32[]{:S(2)}) %collective-permute-start.33) | collective-permute-done | bytes 49184 | tf_op jit(solution)/shard_map/ppermute | solution.py:824
  80.3 1.5 %shard_map.135 = (f32[10,144,128]{2,1,0:T(8,128)S(1)}, f32[10,144,128]{2,1,0:T(8,128)S(1)}, f32[8,64,128]{2,1,0:T(8,128)S(1)}, f32[144,128]{1,0:T(8,128)S(1)}, f...) custom-call(f32[8,64,128]{2,1,0:T(8,128)S(1)} %get-tuple-element.117.g_ref,, ...), custom_call_target="tpu_custom_call" | custom-call | tf_op jit(solution)/shard_map/pallas_call | solution.py:802
  81.9 1.5 %collective-permute-start.36 = (f32[2,80,128]{2,1,0:T(8,128)S(1)}, f32[2,80,128]{2,1,0:T(8,128)S(1)}, u32[]{:S(2)}, u32[]{:S(2)}) collective-permute-start(f32[2,80,128]{2,1,0:T(8,128)S(1)} %get-tuple-element.133), channel_id=1, source_target_pairs={{0,1},{1,0},{2,3},{3,2},{4,5},{5,4},{6,7},{7,6},{8,9},{9,8},{10,11... | collective-permute-start | bytes 245768 | tf_op jit(solution)/shard_map/ppermute | solution.py:824
  83.9 4.4 %collective-permute-done.34.out_ref = f32[144,128]{1,0:T(8,128)S(1)} collective-permute-done((f32[144,128]{1,0:T(8,128)S(1)}, f32[144,128]{1,0:T(8,128)S(1)}, u32[]{:S(2)}, u32[]{:S(2)}) %collective-permute-start.34) | collective-permute-done | bytes 73760 | tf_op jit(solution)/shard_map/ppermute | solution.py:816
  88.8 1.4 %collective-permute-start.37 = (f32[2,48,128]{2,1,0:T(8,128)S(1)}, f32[2,48,128]{2,1,0:T(8,128)S(1)}, u32[]{:S(2)}, u32[]{:S(2)}) collective-permute-start(f32[2,48,128]{2,1,0:T(8,128)S(1)} %get-tuple-element.140), channel_id=1, source_target_pairs={{0,1},{1,0},{2,3},{3,2},{4,5},{5,4},{6,7},{7,6},{8,9},{9,8},{10,11... | collective-permute-start | bytes 147464 | tf_op jit(solution)/shard_map/ppermute | solution.py:824
  90.3 8.9 %all_to_all.8 = f32[32,1,128]{2,1,0:T(1,128)S(1)} all-to-all(f32[32,1,128]{2,1,0:T(1,128)S(1)} %broadcast_in_dim.2), channel_id=1, replica_groups=mesh['axial'=16,'azim'=2] {'axial','azim'}, dimensions={0} | all-to-all | bytes 32768 | tf_op jit(solution)/shard_map/all_to_all | solution.py:854
  (92 shorter events, 18.1 us)
Async XLA Ops:
  2.8 7.8 %collective-permute-start = (f32[200,128]{1,0:T(8,128)S(1)}, f32[200,128]{1,0:T(8,128)S(1)}, u32[]{:S(2)}, u32[]{:S(2)}) collective-permute-start(f32[200,128]{1,0:T(8,128)S(1)} %get-tuple-element.75), channel_id=1, source_target_pairs={{2,4},{6,8},{10,12},{14,16},{18,20},{22,24},{26,28},{30,0},{4,2},{... | collective-permute-start | bytes 307208 | tf_op jit(solution)/shard_map/ppermute | solution.py:816
  8.3 6.6 %collective-permute-start.2 = (f32[2,144,128]{2,1,0:T(8,128)S(1)}, f32[2,144,128]{2,1,0:T(8,128)S(1)}, u32[]{:S(2)}, u32[]{:S(2)}) collective-permute-start(f32[2,144,128]{2,1,0:T(8,128)S(1)} %get-tuple-element.77), channel_id=1, source_target_pairs={{0,1},{1,0},{2,3},{3,2},{4,5},{5,4},{6,7},{7,6},{8,9},{9,8},{10,11... | collective-permute-start | bytes 442376 | tf_op jit(solution)/shard_map/ppermute | solution.py:824
  10.7 5.5 %collective-permute-start.3 = (f32[2,72,128]{2,1,0:T(8,128)S(1)}, f32[2,72,128]{2,1,0:T(8,128)S(1)}, u32[]{:S(2)}, u32[]{:S(2)}) collective-permute-start(f32[2,72,128]{2,1,0:T(8,128)S(1)} %shard_map.122), channel_id=1, source_target_pairs={{0,1},{1,0},{2,3},{3,2},{4,5},{5,4},{6,7},{7,6},{8,9},{9,8},{10,11... | collective-permute-start | bytes 221192 | tf_op jit(solution)/shard_map/ppermute | solution.py:824
  16.7 8.5 %collective-permute-start.4 = (f32[128,128]{1,0:T(8,128)S(1)}, f32[128,128]{1,0:T(8,128)S(1)}, u32[]{:S(2)}, u32[]{:S(2)}) collective-permute-start(f32[128,128]{1,0:T(8,128)S(1)} %get-tuple-element.81), channel_id=1, source_target_pairs={{2,4},{6,8},{10,12},{14,16},{18,20},{22,24},{26,28},{30,0},{4,2},{... | collective-permute-start | bytes 196616 | tf_op jit(solution)/shard_map/ppermute | solution.py:816
  19.0 6.2 %collective-permute-start.5 = (f32[128,128]{1,0:T(8,128)S(1)}, f32[128,128]{1,0:T(8,128)S(1)}, u32[]{:S(2)}, u32[]{:S(2)}) collective-permute-start(f32[128,128]{1,0:T(8,128)S(1)} %get-tuple-element.82), channel_id=1, source_target_pairs={{0,2},{2,0},{4,6},{6,4},{8,10},{10,8},{12,14},{14,12},{16,18},{18,... | collective-permute-start | bytes 196616 | tf_op jit(solution)/shard_map/ppermute | solution.py:817
  19.0 10.4 %collective-permute-start.6 = (f32[2,96,128]{2,1,0:T(8,128)S(1)}, f32[2,96,128]{2,1,0:T(8,128)S(1)}, u32[]{:S(2)}, u32[]{:S(2)}) collective-permute-start(f32[2,96,128]{2,1,0:T(8,128)S(1)} %get-tuple-element.83), channel_id=1, source_target_pairs={{0,1},{1,0},{2,3},{3,2},{4,5},{5,4},{6,7},{7,6},{8,9},{9,8},{10,11... | collective-permute-start | bytes 294920 | tf_op jit(solution)/shard_map/ppermute | solution.py:824
  25.2 4.2 %collective-permute-start.9 = (f32[2,48,128]{2,1,0:T(8,128)S(1)}, f32[2,48,128]{2,1,0:T(8,128)S(1)}, u32[]{:S(2)}, u32[]{:S(2)}) collective-permute-start(f32[2,48,128]{2,1,0:T(8,128)S(1)} %get-tuple-element.86), channel_id=1, source_target_pairs={{0,1},{1,0},{2,3},{3,2},{4,5},{5,4},{6,7},{7,6},{8,9},{9,8},{10,11... | collective-permute-start | bytes 147464 | tf_op jit(solution)/shard_map/ppermute | solution.py:824
  25.9 3.5 %collective-permute-start.10 = (f32[1,128]{1,0:T(1,128)S(1)}, f32[1,128]{1,0:T(1,128)S(1)}, u32[]{:S(2)}, u32[]{:S(2)}) collective-permute-start(f32[1,128]{1,0:T(1,128)S(1)} %get-tuple-element.87), channel_id=1, source_target_pairs={{0,8},{1,9},{2,10},{3,11},{4,12},{5,13},{6,14},{7,15},{8,0},{9,1},... | collective-permute-start | bytes 1544 | tf_op jit(solution)/shard_map/ppermute | solution.py:849
  30.9 7.2 %collective-permute-start.11 = (f32[144,128]{1,0:T(8,128)S(1)}, f32[144,128]{1,0:T(8,128)S(1)}, u32[]{:S(2)}, u32[]{:S(2)}) collective-permute-start(f32[144,128]{1,0:T(8,128)S(1)} %get-tuple-element.89), channel_id=1, source_target_pairs={{2,4},{6,8},{10,12},{14,16},{18,20},{22,24},{26,28},{30,0},{4,2},{... | collective-permute-start | bytes 221192 | tf_op jit(solution)/shard_map/ppermute | solution.py:816
  32.2 6.0 %collective-permute-start.12 = (f32[144,128]{1,0:T(8,128)S(1)}, f32[144,128]{1,0:T(8,128)S(1)}, u32[]{:S(2)}, u32[]{:S(2)}) collective-permute-start(f32[144,128]{1,0:T(8,128)S(1)} %get-tuple-element.90), channel_id=1, source_target_pairs={{0,2},{2,0},{4,6},{6,4},{8,10},{10,8},{12,14},{14,12},{16,18},{18,... | collective-permute-start | bytes 221192 | tf_op jit(solution)/shard_map/ppermute | solution.py:817
  32.2 10.4 %collective-permute-start.13 = (f32[2,80,128]{2,1,0:T(8,128)S(1)}, f32[2,80,128]{2,1,0:T(8,128)S(1)}, u32[]{:S(2)}, u32[]{:S(2)}) collective-permute-start(f32[2,80,128]{2,1,0:T(8,128)S(1)} %get-tuple-element.91), channel_id=1, source_target_pairs={{0,1},{1,0},{2,3},{3,2},{4,5},{5,4},{6,7},{7,6},{8,9},{9,8},{10,11... | collective-permute-start | bytes 245768 | tf_op jit(solution)/shard_map/ppermute | solution.py:824
  33.7 4.4 %collective-permute-start.14 = (f32[1,128]{1,0:T(1,128)S(1)}, f32[1,128]{1,0:T(1,128)S(1)}, u32[]{:S(2)}, u32[]{:S(2)}) collective-permute-start(f32[1,128]{1,0:T(1,128)S(1)} %get-tuple-element.93), channel_id=1, source_target_pairs={{0,16},{1,17},{2,18},{3,19},{4,20},{5,21},{6,22},{7,23},{8,24},{9,... | collective-permute-start | bytes 1544 | tf_op jit(solution)/shard_map/ppermute | solution.py:849
  38.2 4.4 %collective-permute-start.15 = (f32[2,48,128]{2,1,0:T(8,128)S(1)}, f32[2,48,128]{2,1,0:T(8,128)S(1)}, u32[]{:S(2)}, u32[]{:S(2)}) collective-permute-start(f32[2,48,128]{2,1,0:T(8,128)S(1)} %get-tuple-element.94), channel_id=1, source_target_pairs={{0,1},{1,0},{2,3},{3,2},{4,5},{5,4},{6,7},{7,6},{8,9},{9,8},{10,11... | collective-permute-start | bytes 147464 | tf_op jit(solution)/shard_map/ppermute | solution.py:824
  43.5 6.5 %collective-permute-start.17 = (f32[128,128]{1,0:T(8,128)S(1)}, f32[128,128]{1,0:T(8,128)S(1)}, u32[]{:S(2)}, u32[]{:S(2)}) collective-permute-start(f32[128,128]{1,0:T(8,128)S(1)} %get-tuple-element.100), channel_id=1, source_target_pairs={{2,4},{6,8},{10,12},{14,16},{18,20},{22,24},{26,28},{30,0},{4,2},{... | collective-permute-start | bytes 196616 | tf_op jit(solution)/shard_map/ppermute | solution.py:816
  44.0 5.9 %collective-permute-start.18 = (f32[128,128]{1,0:T(8,128)S(1)}, f32[128,128]{1,0:T(8,128)S(1)}, u32[]{:S(2)}, u32[]{:S(2)}) collective-permute-start(f32[128,128]{1,0:T(8,128)S(1)} %get-tuple-element.101), channel_id=1, source_target_pairs={{0,2},{2,0},{4,6},{6,4},{8,10},{10,8},{12,14},{14,12},{16,18},{18,... | collective-permute-start | bytes 196616 | tf_op jit(solution)/shard_map/ppermute | solution.py:817
  44.0 10.8 %collective-permute-start.19 = (f32[2,96,128]{2,1,0:T(8,128)S(1)}, f32[2,96,128]{2,1,0:T(8,128)S(1)}, u32[]{:S(2)}, u32[]{:S(2)}) collective-permute-start(f32[2,96,128]{2,1,0:T(8,128)S(1)} %get-tuple-element.102), channel_id=1, source_target_pairs={{0,1},{1,0},{2,3},{3,2},{4,5},{5,4},{6,7},{7,6},{8,9},{9,8},{10,11... | collective-permute-start | bytes 294920 | tf_op jit(solution)/shard_map/ppermute | solution.py:824
  45.2 3.5 %collective-permute-start.20 = (f32[1,128]{1,0:T(1,128)S(1)}, f32[1,128]{1,0:T(1,128)S(1)}, u32[]{:S(2)}, u32[]{:S(2)}) collective-permute-start(f32[1,128]{1,0:T(1,128)S(1)} %get-tuple-element.104), channel_id=1, source_target_pairs={{0,4},{1,5},{2,6},{3,7},{4,0},{5,1},{6,2},{7,3},{8,12},{9,13},{10,... | collective-permute-start | bytes 1544 | tf_op jit(solution)/shard_map/ppermute | solution.py:849
  50.0 4.9 %collective-permute-start.22 = (f32[2,48,128]{2,1,0:T(8,128)S(1)}, f32[2,48,128]{2,1,0:T(8,128)S(1)}, u32[]{:S(2)}, u32[]{:S(2)}) collective-permute-start(f32[2,48,128]{2,1,0:T(8,128)S(1)} %get-tuple-element.105), channel_id=1, source_target_pairs={{0,1},{1,0},{2,3},{3,2},{4,5},{5,4},{6,7},{7,6},{8,9},{9,8},{10,11... | collective-permute-start | bytes 147464 | tf_op jit(solution)/shard_map/ppermute | solution.py:824
  56.3 8.4 %collective-permute-start.24 = (f32[144,128]{1,0:T(8,128)S(1)}, f32[144,128]{1,0:T(8,128)S(1)}, u32[]{:S(2)}, u32[]{:S(2)}) collective-permute-start(f32[144,128]{1,0:T(8,128)S(1)} %get-tuple-element.108), channel_id=1, source_target_pairs={{2,4},{6,8},{10,12},{14,16},{18,20},{22,24},{26,28},{30,0},{4,2},{... | collective-permute-start | bytes 221192 | tf_op jit(solution)/shard_map/ppermute | solution.py:816
  58.7 6.0 %collective-permute-start.25 = (f32[144,128]{1,0:T(8,128)S(1)}, f32[144,128]{1,0:T(8,128)S(1)}, u32[]{:S(2)}, u32[]{:S(2)}) collective-permute-start(f32[144,128]{1,0:T(8,128)S(1)} %get-tuple-element.109), channel_id=1, source_target_pairs={{0,2},{2,0},{4,6},{6,4},{8,10},{10,8},{12,14},{14,12},{16,18},{18,... | collective-permute-start | bytes 221192 | tf_op jit(solution)/shard_map/ppermute | solution.py:817
  58.7 10.2 %collective-permute-start.26 = (f32[2,80,128]{2,1,0:T(8,128)S(1)}, f32[2,80,128]{2,1,0:T(8,128)S(1)}, u32[]{:S(2)}, u32[]{:S(2)}) collective-permute-start(f32[2,80,128]{2,1,0:T(8,128)S(1)} %get-tuple-element.110), channel_id=1, source_target_pairs={{0,1},{1,0},{2,3},{3,2},{4,5},{5,4},{6,7},{7,6},{8,9},{9,8},{10,11... | collective-permute-start | bytes 245768 | tf_op jit(solution)/shard_map/ppermute | solution.py:824
  60.2 4.4 %collective-permute-start.27 = (f32[1,128]{1,0:T(1,128)S(1)}, f32[1,128]{1,0:T(1,128)S(1)}, u32[]{:S(2)}, u32[]{:S(2)}) collective-permute-start(f32[1,128]{1,0:T(1,128)S(1)} %get-tuple-element.112), channel_id=1, source_target_pairs={{0,16},{1,17},{2,18},{3,19},{4,20},{5,21},{6,22},{7,23},{8,24},{9,... | collective-permute-start | bytes 1544 | tf_op jit(solution)/shard_map/ppermute | solution.py:849
  64.7 4.2 %collective-permute-start.28 = (f32[2,48,128]{2,1,0:T(8,128)S(1)}, f32[2,48,128]{2,1,0:T(8,128)S(1)}, u32[]{:S(2)}, u32[]{:S(2)}) collective-permute-start(f32[2,48,128]{2,1,0:T(8,128)S(1)} %get-tuple-element.113), channel_id=1, source_target_pairs={{0,1},{1,0},{2,3},{3,2},{4,5},{5,4},{6,7},{7,6},{8,9},{9,8},{10,11... | collective-permute-start | bytes 147464 | tf_op jit(solution)/shard_map/ppermute | solution.py:824
  65.3 3.6 %collective-permute-start.29 = (f32[1,128]{1,0:T(1,128)S(1)}, f32[1,128]{1,0:T(1,128)S(1)}, u32[]{:S(2)}, u32[]{:S(2)}) collective-permute-start(f32[1,128]{1,0:T(1,128)S(1)} %get-tuple-element.114), channel_id=1, source_target_pairs={{0,1},{1,0},{2,3},{3,2},{4,5},{5,4},{6,7},{7,6},{8,9},{9,8},{10,11... | collective-permute-start | bytes 1544 | tf_op jit(solution)/shard_map/ppermute | solution.py:849
  69.7 6.5 %collective-permute-start.30 = (f32[128,128]{1,0:T(8,128)S(1)}, f32[128,128]{1,0:T(8,128)S(1)}, u32[]{:S(2)}, u32[]{:S(2)}) collective-permute-start(f32[128,128]{1,0:T(8,128)S(1)} %get-tuple-element.118), channel_id=1, source_target_pairs={{2,4},{6,8},{10,12},{14,16},{18,20},{22,24},{26,28},{30,0},{4,2},{... | collective-permute-start | bytes 196616 | tf_op jit(solution)/shard_map/ppermute | solution.py:816
  69.8 6.4 %collective-permute-start.31 = (f32[128,128]{1,0:T(8,128)S(1)}, f32[128,128]{1,0:T(8,128)S(1)}, u32[]{:S(2)}, u32[]{:S(2)}) collective-permute-start(f32[128,128]{1,0:T(8,128)S(1)} %get-tuple-element.119), channel_id=1, source_target_pairs={{0,2},{2,0},{4,6},{6,4},{8,10},{10,8},{12,14},{14,12},{16,18},{18,... | collective-permute-start | bytes 196616 | tf_op jit(solution)/shard_map/ppermute | solution.py:817
  69.9 7.8 %collective-permute-start.32 = (f32[2,96,128]{2,1,0:T(8,128)S(1)}, f32[2,96,128]{2,1,0:T(8,128)S(1)}, u32[]{:S(2)}, u32[]{:S(2)}) collective-permute-start(f32[2,96,128]{2,1,0:T(8,128)S(1)} %get-tuple-element.120), channel_id=1, source_target_pairs={{0,1},{1,0},{2,3},{3,2},{4,5},{5,4},{6,7},{7,6},{8,9},{9,8},{10,11... | collective-permute-start | bytes 294920 | tf_op jit(solution)/shard_map/ppermute | solution.py:824
  76.2 4.2 %collective-permute-start.33 = (f32[2,48,128]{2,1,0:T(8,128)S(1)}, f32[2,48,128]{2,1,0:T(8,128)S(1)}, u32[]{:S(2)}, u32[]{:S(2)}) collective-permute-start(f32[2,48,128]{2,1,0:T(8,128)S(1)} %get-tuple-element.128), channel_id=1, source_target_pairs={{0,1},{1,0},{2,3},{3,2},{4,5},{5,4},{6,7},{7,6},{8,9},{9,8},{10,11... | collective-permute-start | bytes 147464 | tf_op jit(solution)/shard_map/ppermute | solution.py:824
  81.8 6.5 %collective-permute-start.34 = (f32[144,128]{1,0:T(8,128)S(1)}, f32[144,128]{1,0:T(8,128)S(1)}, u32[]{:S(2)}, u32[]{:S(2)}) collective-permute-start(f32[144,128]{1,0:T(8,128)S(1)} %get-tuple-element.131), channel_id=1, source_target_pairs={{2,4},{6,8},{10,12},{14,16},{18,20},{22,24},{26,28},{30,0},{4,2},{... | collective-permute-start | bytes 221192 | tf_op jit(solution)/shard_map/ppermute | solution.py:816
  81.9 6.5 %collective-permute-start.35 = (f32[144,128]{1,0:T(8,128)S(1)}, f32[144,128]{1,0:T(8,128)S(1)}, u32[]{:S(2)}, u32[]{:S(2)}) collective-permute-start(f32[144,128]{1,0:T(8,128)S(1)} %get-tuple-element.132), channel_id=1, source_target_pairs={{0,2},{2,0},{4,6},{6,4},{8,10},{10,8},{12,14},{14,12},{16,18},{18,... | collective-permute-start | bytes 221192 | tf_op jit(solution)/shard_map/ppermute | solution.py:817
  81.9 17.2 %collective-permute-start.36 = (f32[2,80,128]{2,1,0:T(8,128)S(1)}, f32[2,80,128]{2,1,0:T(8,128)S(1)}, u32[]{:S(2)}, u32[]{:S(2)}) collective-permute-start(f32[2,80,128]{2,1,0:T(8,128)S(1)} %get-tuple-element.133), channel_id=1, source_target_pairs={{0,1},{1,0},{2,3},{3,2},{4,5},{5,4},{6,7},{7,6},{8,9},{9,8},{10,11... | collective-permute-start | bytes 245768 | tf_op jit(solution)/shard_map/ppermute | solution.py:824
  88.8 10.3 %collective-permute-start.37 = (f32[2,48,128]{2,1,0:T(8,128)S(1)}, f32[2,48,128]{2,1,0:T(8,128)S(1)}, u32[]{:S(2)}, u32[]{:S(2)}) collective-permute-start(f32[2,48,128]{2,1,0:T(8,128)S(1)} %get-tuple-element.140), channel_id=1, source_target_pairs={{0,1},{1,0},{2,3},{3,2},{4,5},{5,4},{6,7},{7,6},{8,9},{9,8},{10,11... | collective-permute-start | bytes 147464 | tf_op jit(solution)/shard_map/ppermute | solution.py:824
  (15 other events, 69.0 us)

commit v4 on v3

--- a/solution.py
+++ b/solution.py
@@ -13,6 +13,7 @@
 mass_shift = 0.05
 VMEM_GRANT = 20 << 20
 TAIL = 16
+SUM_ROWS = 32
 gll_points = [
     -1.0,
     -0.8717401485096066,
@@ -529,7 +530,7 @@
     planes_ref, solved_ref, part_ref, send_out_ref, send_early_ref, send_in_ref, send_late_ref,
     pass_ref,
 ):
-    pass_ref[...] = row_ref[...]
+    pass_ref[...] = jnp.broadcast_to(row_ref[...], pass_ref.shape)
     planes = got_planes(g_ref, in_ref, out_ref, early_ref, late_ref)
     for e in range(10):
         planes_ref[e] = planes[e]
@@ -846,7 +847,7 @@
 def partial_sum(row, steps):
     count = lax.axis_size("axial") * lax.axis_size("azim")
     for step in steps:
-        row = row + lax.ppermute(row, ALL, [(i, i ^ step) for i in range(count)])
+        row = row[:1] + lax.ppermute(row, ALL, [(i, i ^ step) for i in range(count)])[:1]
     return row
 
 
@@ -897,17 +898,17 @@
         late, *passed = kernel_call(side_kernel, shapes, outer, inner, send_late, extra)
         return [outer, inner, early, azim_swap(late)] + passed
 
-    one = (1, width * LANES)
+    one, copies = (1, width * LANES), (SUM_ROWS, width * LANES)
     groups = sum_steps()
     moved = exchange(conv_side_kernel, 48 + 3 * count, sends, row)
     g, *sends, near, pay = kernel_call(
         divergence_kernel,
-        [field] + raw_sends + [(16, width * LANES), one],
+        [field] + raw_sends + [(16, width * LANES), copies],
         conv, u, *moved, row, plane, over, div,
     )
     solver = (inverse, into, outof)
     operator = (near, diff, plane, grad, div)
-    solve_shapes = boxes + [field] + solved_sends + [one]
+    solve_shapes = boxes + [field] + solved_sends + [copies]
 
     *moved, pay = exchange(raw_side_kernel, 48, sends, partial_sum(pay, groups[0]), one)
     pay = partial_sum(pay, groups[1])
@@ -918,7 +919,7 @@
     pay = partial_sum(pay, groups[3])
     z0, raw0, g, *sends, row_r, pay = kernel_call(
         first_apply_kernel,
-        [field, field, field] + raw_sends + [row_shape, one],
+        [field, field, field] + raw_sends + [row_shape, copies],
         part, *moved, *operator, pay, planes_r, solved_r,
     )
     *moved, pay = exchange(raw_side_kernel, 48, sends, partial_sum(pay, groups[0]), one)
@@ -943,7 +944,7 @@
         solve_kernel, solve_shapes, g, *moved, pay, *solver
     )
     (pay,) = kernel_call(
-        second_dots_kernel, [one], pay, planes_r, planes_q, planes_w, solved_r, solved_q, solved_w
+        second_dots_kernel, [one], pay[:1], planes_r, planes_q, planes_w, solved_r, solved_q, solved_w
     )
     gathered = gather_sums(jnp.broadcast_to(pay, sums))
     *moved, _ = exchange(solved_side_kernel, 48, sends, pay, one)

time: 101 us -> 97.1 us (0.961)
  starting transfers between devices: 36.5 us -> 32.9 us
    ppermute x7, waiting for transfers between devices: 9.4 us -> 16.4 us  [axial_swap(): from_outer = lax.ppermute(outer_rows, 'axial', outer)]
    ppermute x10, waiting for transfers between devices: 26.5 us -> 19.8 us  [partial_sum(): lax.ppermute(row, ALL, [(i, i ^ step) for i in range(count)])[:1]]
    ppermute x7, starting transfers between devices: 12.1 us -> 8.95 us  [axial_swap(): from_outer = lax.ppermute(outer_rows, 'axial', outer)]
    ppermute x7, starting transfers between devices: 0.19 us -> 2.95 us  [axial_swap(): from_inner = lax.ppermute(inner_rows, 'axial', inner)]
    ppermute x10, starting transfers between devices: 5.69 us -> 3.48 us  [partial_sum(): lax.ppermute(row, ALL, [(i, i ^ step) for i in range(count)])[:1]]
    ppermute x14, starting transfers between devices: 18.5 us -> 17.5 us  [azim_swap(): return lax.ppermute(sides, 'azim', [(0, 1), (1, 0)])]
  transfers between devices with their start and end apart: 38 -> 38, of which waited for: 16 -> 19; matrix products, arithmetic and copies ran while one was open for 0% -> 0% of each run, Pallas kernels for 2% -> 2%
where the time goes in v4:
time: 97.1 us; the launch traced here: 97 us
  waiting for transfers between devices  42.5 us (44%)
  starting transfers between devices  32.9 us (34%)
  Pallas kernels  11.8 us (12%)
  blocking collectives  8.89 us (9%)
    ppermute x10, waiting for transfers between devices, partial_sum(): lax.ppermute(row, ALL, [(i, i ^ step) for i in range(count)])[:1]  19.8 us
    ppermute x14, starting transfers between devices, azim_swap(): return lax.ppermute(sides, 'azim', [(0, 1), (1, 0)])  17.5 us
    ppermute x7, waiting for transfers between devices, axial_swap(): from_outer = lax.ppermute(outer_rows, 'axial', outer)  16.4 us
    pallas_call x18, Pallas kernels, kernel_call(): pl.pallas_call(kernel, out_shape=outs, compiler_params=pltpu.CompilerPara...  11.8 us
    ppermute x7, starting transfers between devices, axial_swap(): from_outer = lax.ppermute(outer_rows, 'axial', outer)  8.95 us
    all_to_all x1, blocking collectives, gather_sums(): return lax.all_to_all(rows, ALL, 0, 0, tiled=True)  8.89 us
    ppermute x14, waiting for transfers between devices, azim_swap(): return lax.ppermute(sides, 'azim', [(0, 1), (1, 0)])  6.18 us
    ppermute x10, starting transfers between devices, partial_sum(): lax.ppermute(row, ALL, [(i, i ^ step) for i in range(count)])[:1]  3.48 us
  transfers between devices with their start and end apart: 38, of which 19 were waited for; matrix products, arithmetic and copies ran while one was open for 0% of the time, Pallas kernels for 2%

profile of v4, /device:TPU:0, one launch (start us, length us, event | category | flops | bytes accessed | tf_op | source)
XLA Modules:
  0.0 97.0 jit_solution(13648652166307926555)
XLA Ops:
  0.6 2.1 %shard_map.121 = (f32[3,8,64,128]{3,2,1,0:T(8,128)S(1)}, f32[8,128]{1,0:T(8,128)S(1)}, f32[200,128]{1,0:T(8,128)S(1)}, f32[2,144,128]{2,1,0:T(8,128)S(1)}, f32[2...) custom-call(f32[3,8,64,128]{3,2,1,0:T(8,128)} %bitcast.13, f32[1,32]{1,0:T(1,128)} %row_hbm.1, ...), custom_call_target="tpu_custom_call" | custom-call | tf_op jit(solution)/shard_map/pallas_call | solution.py:803
  2.8 5.5 %collective-permute-start = (f32[200,128]{1,0:T(8,128)S(1)}, f32[200,128]{1,0:T(8,128)S(1)}, u32[]{:S(2)}, u32[]{:S(2)}) collective-permute-start(f32[200,128]{1,0:T(8,128)S(1)} %get-tuple-element.75), channel_id=1, source_target_pairs={{2,4},{6,8},{10,12},{14,16},{18,20},{22,24},{26,28},{30,0},{4,2},{... | collective-permute-start | bytes 307208 | tf_op jit(solution)/shard_map/ppermute | solution.py:817
  8.3 1.5 %collective-permute-start.2 = (f32[2,144,128]{2,1,0:T(8,128)S(1)}, f32[2,144,128]{2,1,0:T(8,128)S(1)}, u32[]{:S(2)}, u32[]{:S(2)}) collective-permute-start(f32[2,144,128]{2,1,0:T(8,128)S(1)} %get-tuple-element.77), channel_id=1, source_target_pairs={{0,1},{1,0},{2,3},{3,2},{4,5},{5,4},{6,7},{7,6},{8,9},{9,8},{10,11... | collective-permute-start | bytes 442376 | tf_op jit(solution)/shard_map/ppermute | solution.py:825
  10.7 2.0 %collective-permute-start.3 = (f32[2,72,128]{2,1,0:T(8,128)S(1)}, f32[2,72,128]{2,1,0:T(8,128)S(1)}, u32[]{:S(2)}, u32[]{:S(2)}) collective-permute-start(f32[2,72,128]{2,1,0:T(8,128)S(1)} %shard_map.122), channel_id=1, source_target_pairs={{0,1},{1,0},{2,3},{3,2},{4,5},{5,4},{6,7},{7,6},{8,9},{9,8},{10,11... | collective-permute-start | bytes 221192 | tf_op jit(solution)/shard_map/ppermute | solution.py:825
  12.7 2.2 %collective-permute-done.2.early_ref = f32[2,144,128]{2,1,0:T(8,128)S(1)} collective-permute-done((f32[2,144,128]{2,1,0:T(8,128)S(1)}, f32[2,144,128]{2,1,0:T(8,128)S(1)}, u32[]{:S(2)}, u32[]{:S(2)}) %collective-permute-start.2) | collective-permute-done | bytes 147488 | tf_op jit(solution)/shard_map/ppermute | solution.py:825
  16.8 2.3 %collective-permute-start.4 = (f32[128,128]{1,0:T(8,128)S(1)}, f32[128,128]{1,0:T(8,128)S(1)}, u32[]{:S(2)}, u32[]{:S(2)}) collective-permute-start(f32[128,128]{1,0:T(8,128)S(1)} %get-tuple-element.81), channel_id=1, source_target_pairs={{2,4},{6,8},{10,12},{14,16},{18,20},{22,24},{26,28},{30,0},{4,2},{... | collective-permute-start | bytes 196616 | tf_op jit(solution)/shard_map/ppermute | solution.py:817
  19.1 1.5 %collective-permute-start.6 = (f32[2,96,128]{2,1,0:T(8,128)S(1)}, f32[2,96,128]{2,1,0:T(8,128)S(1)}, u32[]{:S(2)}, u32[]{:S(2)}) collective-permute-start(f32[2,96,128]{2,1,0:T(8,128)S(1)} %get-tuple-element.83), channel_id=1, source_target_pairs={{0,1},{1,0},{2,3},{3,2},{4,5},{5,4},{6,7},{7,6},{8,9},{9,8},{10,11... | collective-permute-start | bytes 294920 | tf_op jit(solution)/shard_map/ppermute | solution.py:825
  21.7 1.5 %collective-permute-done.4.out_ref = f32[128,128]{1,0:T(8,128)S(1)} collective-permute-done((f32[128,128]{1,0:T(8,128)S(1)}, f32[128,128]{1,0:T(8,128)S(1)}, u32[]{:S(2)}, u32[]{:S(2)}) %collective-permute-start.4) | collective-permute-done | bytes 65568 | tf_op jit(solution)/shard_map/ppermute | solution.py:817
  23.3 1.6 %collective-permute-start.9 = (f32[2,48,128]{2,1,0:T(8,128)S(1)}, f32[2,48,128]{2,1,0:T(8,128)S(1)}, u32[]{:S(2)}, u32[]{:S(2)}) collective-permute-start(f32[2,48,128]{2,1,0:T(8,128)S(1)} %get-tuple-element.86), channel_id=1, source_target_pairs={{0,1},{1,0},{2,3},{3,2},{4,5},{5,4},{6,7},{7,6},{8,9},{9,8},{10,11... | collective-permute-start | bytes 147464 | tf_op jit(solution)/shard_map/ppermute | solution.py:825
  25.0 3.4 %collective-permute-done.10 = f32[1,128]{1,0:T(1,128)S(1)} collective-permute-done((f32[1,128]{1,0:T(1,128)S(1)}, f32[1,128]{1,0:T(1,128)S(1)}, u32[]{:S(2)}, u32[]{:S(2)}) %collective-permute-start.10) | collective-permute-done | bytes 544 | tf_op jit(solution)/shard_map/ppermute | solution.py:850
  28.4 1.5 %shard_map.126 = (f32[10,144,128]{2,1,0:T(8,128)S(1)}, f32[10,144,128]{2,1,0:T(8,128)S(1)}, f32[8,64,128]{2,1,0:T(8,128)S(1)}, f32[144,128]{1,0:T(8,128)S(1)}, f...) custom-call(f32[8,64,128]{2,1,0:T(8,128)S(1)} %get-tuple-element.80.g_ref,, ...), custom_call_target="tpu_custom_call" | custom-call | tf_op jit(solution)/shard_map/pallas_call | solution.py:803
  31.8 2.8 %collective-permute-done.14 = f32[32,128]{1,0:T(8,128)S(1)} collective-permute-done((f32[32,128]{1,0:T(8,128)S(1)}, f32[32,128]{1,0:T(8,128)S(1)}, u32[]{:S(2)}, u32[]{:S(2)}) %collective-permute-start.14) | collective-permute-done | bytes 16416 | tf_op jit(solution)/shard_map/ppermute | solution.py:850
  34.6 1.9 %collective-permute-done.11.out_ref = f32[144,128]{1,0:T(8,128)S(1)} collective-permute-done((f32[144,128]{1,0:T(8,128)S(1)}, f32[144,128]{1,0:T(8,128)S(1)}, u32[]{:S(2)}, u32[]{:S(2)}) %collective-permute-start.11) | collective-permute-done | bytes 73760 | tf_op jit(solution)/shard_map/ppermute | solution.py:817
  37.1 1.5 %collective-permute-start.16 = (f32[1,128]{1,0:T(1,128)S(1)}, f32[1,128]{1,0:T(1,128)S(1)}, u32[]{:S(2)}, u32[]{:S(2)}) collective-permute-start(f32[1,128]{1,0:T(1,128)S(1)} %get-tuple-element.96), channel_id=1, source_target_pairs={{0,1},{1,0},{2,3},{3,2},{4,5},{5,4},{6,7},{7,6},{8,9},{9,8},{10,11... | collective-permute-start | bytes 1544 | tf_op jit(solution)/shard_map/ppermute | solution.py:850
  38.6 2.1 %collective-permute-done.16 = f32[1,128]{1,0:T(1,128)S(1)} collective-permute-done((f32[1,128]{1,0:T(1,128)S(1)}, f32[1,128]{1,0:T(1,128)S(1)}, u32[]{:S(2)}, u32[]{:S(2)}) %collective-permute-start.16) | collective-permute-done | bytes 544 | tf_op jit(solution)/shard_map/ppermute | solution.py:850
  41.8 2.0 %collective-permute-start.18 = (f32[128,128]{1,0:T(8,128)S(1)}, f32[128,128]{1,0:T(8,128)S(1)}, u32[]{:S(2)}, u32[]{:S(2)}) collective-permute-start(f32[128,128]{1,0:T(8,128)S(1)} %get-tuple-element.101), channel_id=1, source_target_pairs={{0,2},{2,0},{4,6},{6,4},{8,10},{10,8},{12,14},{14,12},{16,18},{18,... | collective-permute-start | bytes 196616 | tf_op jit(solution)/shard_map/ppermute | solution.py:818
  43.9 1.4 %collective-permute-start.19 = (f32[2,96,128]{2,1,0:T(8,128)S(1)}, f32[2,96,128]{2,1,0:T(8,128)S(1)}, u32[]{:S(2)}, u32[]{:S(2)}) collective-permute-start(f32[2,96,128]{2,1,0:T(8,128)S(1)} %get-tuple-element.102), channel_id=1, source_target_pairs={{0,1},{1,0},{2,3},{3,2},{4,5},{5,4},{6,7},{7,6},{8,9},{9,8},{10,11... | collective-permute-start | bytes 294920 | tf_op jit(solution)/shard_map/ppermute | solution.py:825
  46.6 1.6 %collective-permute-done.17.out_ref = f32[128,128]{1,0:T(8,128)S(1)} collective-permute-done((f32[128,128]{1,0:T(8,128)S(1)}, f32[128,128]{1,0:T(8,128)S(1)}, u32[]{:S(2)}, u32[]{:S(2)}) %collective-permute-start.17) | collective-permute-done | bytes 65568 | tf_op jit(solution)/shard_map/ppermute | solution.py:817
  48.2 1.5 %collective-permute-start.22 = (f32[2,48,128]{2,1,0:T(8,128)S(1)}, f32[2,48,128]{2,1,0:T(8,128)S(1)}, u32[]{:S(2)}, u32[]{:S(2)}) collective-permute-start(f32[2,48,128]{2,1,0:T(8,128)S(1)} %get-tuple-element.105), channel_id=1, source_target_pairs={{0,1},{1,0},{2,3},{3,2},{4,5},{5,4},{6,7},{7,6},{8,9},{9,8},{10,11... | collective-permute-start | bytes 147464 | tf_op jit(solution)/shard_map/ppermute | solution.py:825
  49.7 3.5 %collective-permute-done.23 = f32[1,128]{1,0:T(1,128)S(1)} collective-permute-done((f32[1,128]{1,0:T(1,128)S(1)}, f32[1,128]{1,0:T(1,128)S(1)}, u32[]{:S(2)}, u32[]{:S(2)}) %collective-permute-start.23) | collective-permute-done | bytes 544 | tf_op jit(solution)/shard_map/ppermute | solution.py:850
  53.2 1.5 %shard_map.130 = (f32[10,144,128]{2,1,0:T(8,128)S(1)}, f32[10,144,128]{2,1,0:T(8,128)S(1)}, f32[8,64,128]{2,1,0:T(8,128)S(1)}, f32[144,128]{1,0:T(8,128)S(1)}, f...) custom-call(f32[8,64,128]{2,1,0:T(8,128)S(1)} %get-tuple-element.99.g_ref,, ...), custom_call_target="tpu_custom_call" | custom-call | tf_op jit(solution)/shard_map/pallas_call | solution.py:803
  55.8 3.6 %collective-permute-done.27 = f32[32,128]{1,0:T(8,128)S(1)} collective-permute-done((f32[32,128]{1,0:T(8,128)S(1)}, f32[32,128]{1,0:T(8,128)S(1)}, u32[]{:S(2)}, u32[]{:S(2)}) %collective-permute-start.27) | collective-permute-done | bytes 16416 | tf_op jit(solution)/shard_map/ppermute | solution.py:850
  59.4 1.9 %collective-permute-done.24.out_ref = f32[144,128]{1,0:T(8,128)S(1)} collective-permute-done((f32[144,128]{1,0:T(8,128)S(1)}, f32[144,128]{1,0:T(8,128)S(1)}, u32[]{:S(2)}, u32[]{:S(2)}) %collective-permute-start.24) | collective-permute-done | bytes 73760 | tf_op jit(solution)/shard_map/ppermute | solution.py:817
  62.0 1.4 %collective-permute-start.29 = (f32[1,128]{1,0:T(1,128)S(1)}, f32[1,128]{1,0:T(1,128)S(1)}, u32[]{:S(2)}, u32[]{:S(2)}) collective-permute-start(f32[1,128]{1,0:T(1,128)S(1)} %get-tuple-element.114), channel_id=1, source_target_pairs={{0,1},{1,0},{2,3},{3,2},{4,5},{5,4},{6,7},{7,6},{8,9},{9,8},{10,11... | collective-permute-start | bytes 1544 | tf_op jit(solution)/shard_map/ppermute | solution.py:850
  63.5 2.2 %collective-permute-done.29 = f32[1,128]{1,0:T(1,128)S(1)} collective-permute-done((f32[1,128]{1,0:T(1,128)S(1)}, f32[1,128]{1,0:T(1,128)S(1)}, u32[]{:S(2)}, u32[]{:S(2)}) %collective-permute-start.29) | collective-permute-done | bytes 544 | tf_op jit(solution)/shard_map/ppermute | solution.py:850
  66.6 1.4 %collective-permute-start.32 = (f32[2,96,128]{2,1,0:T(8,128)S(1)}, f32[2,96,128]{2,1,0:T(8,128)S(1)}, u32[]{:S(2)}, u32[]{:S(2)}) collective-permute-start(f32[2,96,128]{2,1,0:T(8,128)S(1)} %get-tuple-element.120), channel_id=1, source_target_pairs={{0,1},{1,0},{2,3},{3,2},{4,5},{5,4},{6,7},{7,6},{8,9},{9,8},{10,11... | collective-permute-start | bytes 294920 | tf_op jit(solution)/shard_map/ppermute | solution.py:825
  68.7 4.2 %collective-permute-done.30.out_ref = f32[128,128]{1,0:T(8,128)S(1)} collective-permute-done((f32[128,128]{1,0:T(8,128)S(1)}, f32[128,128]{1,0:T(8,128)S(1)}, u32[]{:S(2)}, u32[]{:S(2)}) %collective-permute-start.30) | collective-permute-done | bytes 65568 | tf_op jit(solution)/shard_map/ppermute | solution.py:817
  72.9 1.4 %collective-permute-start.33 = (f32[2,48,128]{2,1,0:T(8,128)S(1)}, f32[2,48,128]{2,1,0:T(8,128)S(1)}, u32[]{:S(2)}, u32[]{:S(2)}) collective-permute-start(f32[2,48,128]{2,1,0:T(8,128)S(1)} %get-tuple-element.128), channel_id=1, source_target_pairs={{0,1},{1,0},{2,3},{3,2},{4,5},{5,4},{6,7},{7,6},{8,9},{9,8},{10,11... | collective-permute-start | bytes 147464 | tf_op jit(solution)/shard_map/ppermute | solution.py:825
  74.3 2.8 %collective-permute-done.33.late_ref = f32[2,48,128]{2,1,0:T(8,128)S(1)} collective-permute-done((f32[2,48,128]{2,1,0:T(8,128)S(1)}, f32[2,48,128]{2,1,0:T(8,128)S(1)}, u32[]{:S(2)}, u32[]{:S(2)}) %collective-permute-start.33) | collective-permute-done | bytes 49184 | tf_op jit(solution)/shard_map/ppermute | solution.py:825
  77.1 1.5 %shard_map.135 = (f32[10,144,128]{2,1,0:T(8,128)S(1)}, f32[10,144,128]{2,1,0:T(8,128)S(1)}, f32[8,64,128]{2,1,0:T(8,128)S(1)}, f32[144,128]{1,0:T(8,128)S(1)}, f...) custom-call(f32[8,64,128]{2,1,0:T(8,128)S(1)} %get-tuple-element.117.g_ref, ...), custom_call_target="tpu_custom_call" | custom-call | tf_op jit(solution)/shard_map/pallas_call | solution.py:803
  80.6 4.5 %collective-permute-done.34.out_ref = f32[144,128]{1,0:T(8,128)S(1)} collective-permute-done((f32[144,128]{1,0:T(8,128)S(1)}, f32[144,128]{1,0:T(8,128)S(1)}, u32[]{:S(2)}, u32[]{:S(2)}) %collective-permute-start.34) | collective-permute-done | bytes 73760 | tf_op jit(solution)/shard_map/ppermute | solution.py:817
  86.9 8.9 %all_to_all.8 = f32[32,1,128]{2,1,0:T(1,128)S(1)} all-to-all(f32[32,1,128]{2,1,0:T(1,128)S(1)} %broadcast_in_dim.2), channel_id=1, replica_groups=mesh['axial'=16,'azim'=2] {'axial','azim'}, dimensions={0} | all-to-all | bytes 32768 | tf_op jit(solution)/shard_map/all_to_all | solution.py:855
  (93 shorter events, 17.3 us)
Async XLA Ops:
  2.8 7.8 %collective-permute-start = (f32[200,128]{1,0:T(8,128)S(1)}, f32[200,128]{1,0:T(8,128)S(1)}, u32[]{:S(2)}, u32[]{:S(2)}) collective-permute-start(f32[200,128]{1,0:T(8,128)S(1)} %get-tuple-element.75), channel_id=1, source_target_pairs={{2,4},{6,8},{10,12},{14,16},{18,20},{22,24},{26,28},{30,0},{4,2},{... | collective-permute-start | bytes 307208 | tf_op jit(solution)/shard_map/ppermute | solution.py:817
  8.3 6.6 %collective-permute-start.2 = (f32[2,144,128]{2,1,0:T(8,128)S(1)}, f32[2,144,128]{2,1,0:T(8,128)S(1)}, u32[]{:S(2)}, u32[]{:S(2)}) collective-permute-start(f32[2,144,128]{2,1,0:T(8,128)S(1)} %get-tuple-element.77), channel_id=1, source_target_pairs={{0,1},{1,0},{2,3},{3,2},{4,5},{5,4},{6,7},{7,6},{8,9},{9,8},{10,11... | collective-permute-start | bytes 442376 | tf_op jit(solution)/shard_map/ppermute | solution.py:825
  10.7 5.5 %collective-permute-start.3 = (f32[2,72,128]{2,1,0:T(8,128)S(1)}, f32[2,72,128]{2,1,0:T(8,128)S(1)}, u32[]{:S(2)}, u32[]{:S(2)}) collective-permute-start(f32[2,72,128]{2,1,0:T(8,128)S(1)} %shard_map.122), channel_id=1, source_target_pairs={{0,1},{1,0},{2,3},{3,2},{4,5},{5,4},{6,7},{7,6},{8,9},{9,8},{10,11... | collective-permute-start | bytes 221192 | tf_op jit(solution)/shard_map/ppermute | solution.py:825
  16.7 3.9 %collective-permute-start.7 = (f32[32,128]{1,0:T(8,128)S(1)}, f32[32,128]{1,0:T(8,128)S(1)}, u32[]{:S(2)}, u32[]{:S(2)}) collective-permute-start(f32[32,128]{1,0:T(8,128)S(1)} %get-tuple-element.85), channel_id=1, source_target_pairs={{0,4},{1,5},{2,6},{3,7},{4,0},{5,1},{6,2},{7,3},{8,12},{9,13},{10,... | collective-permute-start | bytes 49160 | tf_op jit(solution)/shard_map/ppermute | solution.py:850
  16.8 6.5 %collective-permute-start.4 = (f32[128,128]{1,0:T(8,128)S(1)}, f32[128,128]{1,0:T(8,128)S(1)}, u32[]{:S(2)}, u32[]{:S(2)}) collective-permute-start(f32[128,128]{1,0:T(8,128)S(1)} %get-tuple-element.81), channel_id=1, source_target_pairs={{2,4},{6,8},{10,12},{14,16},{18,20},{22,24},{26,28},{30,0},{4,2},{... | collective-permute-start | bytes 196616 | tf_op jit(solution)/shard_map/ppermute | solution.py:817
  19.1 4.1 %collective-permute-start.5 = (f32[128,128]{1,0:T(8,128)S(1)}, f32[128,128]{1,0:T(8,128)S(1)}, u32[]{:S(2)}, u32[]{:S(2)}) collective-permute-start(f32[128,128]{1,0:T(8,128)S(1)} %get-tuple-element.82), channel_id=1, source_target_pairs={{0,2},{2,0},{4,6},{6,4},{8,10},{10,8},{12,14},{14,12},{16,18},{18,... | collective-permute-start | bytes 196616 | tf_op jit(solution)/shard_map/ppermute | solution.py:818
  19.1 9.3 %collective-permute-start.6 = (f32[2,96,128]{2,1,0:T(8,128)S(1)}, f32[2,96,128]{2,1,0:T(8,128)S(1)}, u32[]{:S(2)}, u32[]{:S(2)}) collective-permute-start(f32[2,96,128]{2,1,0:T(8,128)S(1)} %get-tuple-element.83), channel_id=1, source_target_pairs={{0,1},{1,0},{2,3},{3,2},{4,5},{5,4},{6,7},{7,6},{8,9},{9,8},{10,11... | collective-permute-start | bytes 294920 | tf_op jit(solution)/shard_map/ppermute | solution.py:825
  23.3 5.1 %collective-permute-start.9 = (f32[2,48,128]{2,1,0:T(8,128)S(1)}, f32[2,48,128]{2,1,0:T(8,128)S(1)}, u32[]{:S(2)}, u32[]{:S(2)}) collective-permute-start(f32[2,48,128]{2,1,0:T(8,128)S(1)} %get-tuple-element.86), channel_id=1, source_target_pairs={{0,1},{1,0},{2,3},{3,2},{4,5},{5,4},{6,7},{7,6},{8,9},{9,8},{10,11... | collective-permute-start | bytes 147464 | tf_op jit(solution)/shard_map/ppermute | solution.py:825
  29.9 4.7 %collective-permute-start.14 = (f32[32,128]{1,0:T(8,128)S(1)}, f32[32,128]{1,0:T(8,128)S(1)}, u32[]{:S(2)}, u32[]{:S(2)}) collective-permute-start(f32[32,128]{1,0:T(8,128)S(1)} %get-tuple-element.93), channel_id=1, source_target_pairs={{0,16},{1,17},{2,18},{3,19},{4,20},{5,21},{6,22},{7,23},{8,24},{9,... | collective-permute-start | bytes 49160 | tf_op jit(solution)/shard_map/ppermute | solution.py:850
  30.0 6.5 %collective-permute-start.11 = (f32[144,128]{1,0:T(8,128)S(1)}, f32[144,128]{1,0:T(8,128)S(1)}, u32[]{:S(2)}, u32[]{:S(2)}) collective-permute-start(f32[144,128]{1,0:T(8,128)S(1)} %get-tuple-element.89), channel_id=1, source_target_pairs={{2,4},{6,8},{10,12},{14,16},{18,20},{22,24},{26,28},{30,0},{4,2},{... | collective-permute-start | bytes 221192 | tf_op jit(solution)/shard_map/ppermute | solution.py:817
  30.8 5.7 %collective-permute-start.12 = (f32[144,128]{1,0:T(8,128)S(1)}, f32[144,128]{1,0:T(8,128)S(1)}, u32[]{:S(2)}, u32[]{:S(2)}) collective-permute-start(f32[144,128]{1,0:T(8,128)S(1)} %get-tuple-element.90), channel_id=1, source_target_pairs={{0,2},{2,0},{4,6},{6,4},{8,10},{10,8},{12,14},{14,12},{16,18},{18,... | collective-permute-start | bytes 221192 | tf_op jit(solution)/shard_map/ppermute | solution.py:818
  31.3 9.5 %collective-permute-start.13 = (f32[2,80,128]{2,1,0:T(8,128)S(1)}, f32[2,80,128]{2,1,0:T(8,128)S(1)}, u32[]{:S(2)}, u32[]{:S(2)}) collective-permute-start(f32[2,80,128]{2,1,0:T(8,128)S(1)} %get-tuple-element.91), channel_id=1, source_target_pairs={{0,1},{1,0},{2,3},{3,2},{4,5},{5,4},{6,7},{7,6},{8,9},{9,8},{10,11... | collective-permute-start | bytes 245768 | tf_op jit(solution)/shard_map/ppermute | solution.py:825
  36.5 4.2 %collective-permute-start.15 = (f32[2,48,128]{2,1,0:T(8,128)S(1)}, f32[2,48,128]{2,1,0:T(8,128)S(1)}, u32[]{:S(2)}, u32[]{:S(2)}) collective-permute-start(f32[2,48,128]{2,1,0:T(8,128)S(1)} %get-tuple-element.94), channel_id=1, source_target_pairs={{0,1},{1,0},{2,3},{3,2},{4,5},{5,4},{6,7},{7,6},{8,9},{9,8},{10,11... | collective-permute-start | bytes 147464 | tf_op jit(solution)/shard_map/ppermute | solution.py:825
  37.1 3.6 %collective-permute-start.16 = (f32[1,128]{1,0:T(1,128)S(1)}, f32[1,128]{1,0:T(1,128)S(1)}, u32[]{:S(2)}, u32[]{:S(2)}) collective-permute-start(f32[1,128]{1,0:T(1,128)S(1)} %get-tuple-element.96), channel_id=1, source_target_pairs={{0,1},{1,0},{2,3},{3,2},{4,5},{5,4},{6,7},{7,6},{8,9},{9,8},{10,11... | collective-permute-start | bytes 1544 | tf_op jit(solution)/shard_map/ppermute | solution.py:850
  41.7 3.8 %collective-permute-start.20 = (f32[32,128]{1,0:T(8,128)S(1)}, f32[32,128]{1,0:T(8,128)S(1)}, u32[]{:S(2)}, u32[]{:S(2)}) collective-permute-start(f32[32,128]{1,0:T(8,128)S(1)} %get-tuple-element.104), channel_id=1, source_target_pairs={{0,4},{1,5},{2,6},{3,7},{4,0},{5,1},{6,2},{7,3},{8,12},{9,13},{10,... | collective-permute-start | bytes 49160 | tf_op jit(solution)/shard_map/ppermute | solution.py:850
  41.7 6.5 %collective-permute-start.17 = (f32[128,128]{1,0:T(8,128)S(1)}, f32[128,128]{1,0:T(8,128)S(1)}, u32[]{:S(2)}, u32[]{:S(2)}) collective-permute-start(f32[128,128]{1,0:T(8,128)S(1)} %get-tuple-element.100), channel_id=1, source_target_pairs={{2,4},{6,8},{10,12},{14,16},{18,20},{22,24},{26,28},{30,0},{4,2},{... | collective-permute-start | bytes 196616 | tf_op jit(solution)/shard_map/ppermute | solution.py:817
  41.8 6.4 %collective-permute-start.18 = (f32[128,128]{1,0:T(8,128)S(1)}, f32[128,128]{1,0:T(8,128)S(1)}, u32[]{:S(2)}, u32[]{:S(2)}) collective-permute-start(f32[128,128]{1,0:T(8,128)S(1)} %get-tuple-element.101), channel_id=1, source_target_pairs={{0,2},{2,0},{4,6},{6,4},{8,10},{10,8},{12,14},{14,12},{16,18},{18,... | collective-permute-start | bytes 196616 | tf_op jit(solution)/shard_map/ppermute | solution.py:818
  43.9 9.4 %collective-permute-start.19 = (f32[2,96,128]{2,1,0:T(8,128)S(1)}, f32[2,96,128]{2,1,0:T(8,128)S(1)}, u32[]{:S(2)}, u32[]{:S(2)}) collective-permute-start(f32[2,96,128]{2,1,0:T(8,128)S(1)} %get-tuple-element.102), channel_id=1, source_target_pairs={{0,1},{1,0},{2,3},{3,2},{4,5},{5,4},{6,7},{7,6},{8,9},{9,8},{10,11... | collective-permute-start | bytes 294920 | tf_op jit(solution)/shard_map/ppermute | solution.py:825
  48.2 5.0 %collective-permute-start.22 = (f32[2,48,128]{2,1,0:T(8,128)S(1)}, f32[2,48,128]{2,1,0:T(8,128)S(1)}, u32[]{:S(2)}, u32[]{:S(2)}) collective-permute-start(f32[2,48,128]{2,1,0:T(8,128)S(1)} %get-tuple-element.105), channel_id=1, source_target_pairs={{0,1},{1,0},{2,3},{3,2},{4,5},{5,4},{6,7},{7,6},{8,9},{9,8},{10,11... | collective-permute-start | bytes 147464 | tf_op jit(solution)/shard_map/ppermute | solution.py:825
  54.7 4.7 %collective-permute-start.27 = (f32[32,128]{1,0:T(8,128)S(1)}, f32[32,128]{1,0:T(8,128)S(1)}, u32[]{:S(2)}, u32[]{:S(2)}) collective-permute-start(f32[32,128]{1,0:T(8,128)S(1)} %get-tuple-element.112), channel_id=1, source_target_pairs={{0,16},{1,17},{2,18},{3,19},{4,20},{5,21},{6,22},{7,23},{8,24},{9,... | collective-permute-start | bytes 49160 | tf_op jit(solution)/shard_map/ppermute | solution.py:850
  54.8 6.5 %collective-permute-start.24 = (f32[144,128]{1,0:T(8,128)S(1)}, f32[144,128]{1,0:T(8,128)S(1)}, u32[]{:S(2)}, u32[]{:S(2)}) collective-permute-start(f32[144,128]{1,0:T(8,128)S(1)} %get-tuple-element.108), channel_id=1, source_target_pairs={{2,4},{6,8},{10,12},{14,16},{18,20},{22,24},{26,28},{30,0},{4,2},{... | collective-permute-start | bytes 221192 | tf_op jit(solution)/shard_map/ppermute | solution.py:817
  54.9 6.5 %collective-permute-start.25 = (f32[144,128]{1,0:T(8,128)S(1)}, f32[144,128]{1,0:T(8,128)S(1)}, u32[]{:S(2)}, u32[]{:S(2)}) collective-permute-start(f32[144,128]{1,0:T(8,128)S(1)} %get-tuple-element.109), channel_id=1, source_target_pairs={{0,2},{2,0},{4,6},{6,4},{8,10},{10,8},{12,14},{14,12},{16,18},{18,... | collective-permute-start | bytes 221192 | tf_op jit(solution)/shard_map/ppermute | solution.py:818
  55.2 10.5 %collective-permute-start.26 = (f32[2,80,128]{2,1,0:T(8,128)S(1)}, f32[2,80,128]{2,1,0:T(8,128)S(1)}, u32[]{:S(2)}, u32[]{:S(2)}) collective-permute-start(f32[2,80,128]{2,1,0:T(8,128)S(1)} %get-tuple-element.110), channel_id=1, source_target_pairs={{0,1},{1,0},{2,3},{3,2},{4,5},{5,4},{6,7},{7,6},{8,9},{9,8},{10,11... | collective-permute-start | bytes 245768 | tf_op jit(solution)/shard_map/ppermute | solution.py:825
  61.4 4.3 %collective-permute-start.28 = (f32[2,48,128]{2,1,0:T(8,128)S(1)}, f32[2,48,128]{2,1,0:T(8,128)S(1)}, u32[]{:S(2)}, u32[]{:S(2)}) collective-permute-start(f32[2,48,128]{2,1,0:T(8,128)S(1)} %get-tuple-element.113), channel_id=1, source_target_pairs={{0,1},{1,0},{2,3},{3,2},{4,5},{5,4},{6,7},{7,6},{8,9},{9,8},{10,11... | collective-permute-start | bytes 147464 | tf_op jit(solution)/shard_map/ppermute | solution.py:825
  66.4 6.5 %collective-permute-start.30 = (f32[128,128]{1,0:T(8,128)S(1)}, f32[128,128]{1,0:T(8,128)S(1)}, u32[]{:S(2)}, u32[]{:S(2)}) collective-permute-start(f32[128,128]{1,0:T(8,128)S(1)} %get-tuple-element.118), channel_id=1, source_target_pairs={{2,4},{6,8},{10,12},{14,16},{18,20},{22,24},{26,28},{30,0},{4,2},{... | collective-permute-start | bytes 196616 | tf_op jit(solution)/shard_map/ppermute | solution.py:817
  66.5 6.4 %collective-permute-start.31 = (f32[128,128]{1,0:T(8,128)S(1)}, f32[128,128]{1,0:T(8,128)S(1)}, u32[]{:S(2)}, u32[]{:S(2)}) collective-permute-start(f32[128,128]{1,0:T(8,128)S(1)} %get-tuple-element.119), channel_id=1, source_target_pairs={{0,2},{2,0},{4,6},{6,4},{8,10},{10,8},{12,14},{14,12},{16,18},{18,... | collective-permute-start | bytes 196616 | tf_op jit(solution)/shard_map/ppermute | solution.py:818
  66.6 7.7 %collective-permute-start.32 = (f32[2,96,128]{2,1,0:T(8,128)S(1)}, f32[2,96,128]{2,1,0:T(8,128)S(1)}, u32[]{:S(2)}, u32[]{:S(2)}) collective-permute-start(f32[2,96,128]{2,1,0:T(8,128)S(1)} %get-tuple-element.120), channel_id=1, source_target_pairs={{0,1},{1,0},{2,3},{3,2},{4,5},{5,4},{6,7},{7,6},{8,9},{9,8},{10,11... | collective-permute-start | bytes 294920 | tf_op jit(solution)/shard_map/ppermute | solution.py:825
  72.9 4.2 %collective-permute-start.33 = (f32[2,48,128]{2,1,0:T(8,128)S(1)}, f32[2,48,128]{2,1,0:T(8,128)S(1)}, u32[]{:S(2)}, u32[]{:S(2)}) collective-permute-start(f32[2,48,128]{2,1,0:T(8,128)S(1)} %get-tuple-element.128), channel_id=1, source_target_pairs={{0,1},{1,0},{2,3},{3,2},{4,5},{5,4},{6,7},{7,6},{8,9},{9,8},{10,11... | collective-permute-start | bytes 147464 | tf_op jit(solution)/shard_map/ppermute | solution.py:825
  78.5 6.5 %collective-permute-start.34 = (f32[144,128]{1,0:T(8,128)S(1)}, f32[144,128]{1,0:T(8,128)S(1)}, u32[]{:S(2)}, u32[]{:S(2)}) collective-permute-start(f32[144,128]{1,0:T(8,128)S(1)} %get-tuple-element.131), channel_id=1, source_target_pairs={{2,4},{6,8},{10,12},{14,16},{18,20},{22,24},{26,28},{30,0},{4,2},{... | collective-permute-start | bytes 221192 | tf_op jit(solution)/shard_map/ppermute | solution.py:817
  78.6 6.5 %collective-permute-start.35 = (f32[144,128]{1,0:T(8,128)S(1)}, f32[144,128]{1,0:T(8,128)S(1)}, u32[]{:S(2)}, u32[]{:S(2)}) collective-permute-start(f32[144,128]{1,0:T(8,128)S(1)} %get-tuple-element.132), channel_id=1, source_target_pairs={{0,2},{2,0},{4,6},{6,4},{8,10},{10,8},{12,14},{14,12},{16,18},{18,... | collective-permute-start | bytes 221192 | tf_op jit(solution)/shard_map/ppermute | solution.py:818
  78.7 17.1 %collective-permute-start.36 = (f32[2,80,128]{2,1,0:T(8,128)S(1)}, f32[2,80,128]{2,1,0:T(8,128)S(1)}, u32[]{:S(2)}, u32[]{:S(2)}) collective-permute-start(f32[2,80,128]{2,1,0:T(8,128)S(1)} %get-tuple-element.133), channel_id=1, source_target_pairs={{0,1},{1,0},{2,3},{3,2},{4,5},{5,4},{6,7},{7,6},{8,9},{9,8},{10,11... | collective-permute-start | bytes 245768 | tf_op jit(solution)/shard_map/ppermute | solution.py:825
  85.6 10.2 %collective-permute-start.37 = (f32[2,48,128]{2,1,0:T(8,128)S(1)}, f32[2,48,128]{2,1,0:T(8,128)S(1)}, u32[]{:S(2)}, u32[]{:S(2)}) collective-permute-start(f32[2,48,128]{2,1,0:T(8,128)S(1)} %get-tuple-element.140), channel_id=1, source_target_pairs={{0,1},{1,0},{2,3},{3,2},{4,5},{5,4},{6,7},{7,6},{8,9},{9,8},{10,11... | collective-permute-start | bytes 147464 | tf_op jit(solution)/shard_map/ppermute | solution.py:825
  (15 other events, 69.0 us)

commit v5 on v4

--- a/solution.py
+++ b/solution.py
@@ -524,11 +524,13 @@
     return planes
 
 
-def solve_kernel(
-    g_ref, out_ref, in_ref, early_ref, late_ref, row_ref,
-    inverse_ref, into_ref, outof_ref,
-    planes_ref, solved_ref, part_ref, send_out_ref, send_early_ref, send_in_ref, send_late_ref,
-    pass_ref,
+def to_part(rows):
+    return radial_sum(rows[:64] + spread(rows[64:128], 1, 6)), radial_sum(rows[128:144])
+
+
+def solve_ends_kernel(
+    g_ref, out_ref, in_ref, early_ref, late_ref, row_ref, inverse_ref, into_ref, outof_ref,
+    planes_ref, middle_ref, ends_ref, send_out_ref, send_in_ref, pass_ref,
 ):
     pass_ref[...] = jnp.broadcast_to(row_ref[...], pass_ref.shape)
     planes = got_planes(g_ref, in_ref, out_ref, early_ref, late_ref)
@@ -538,16 +540,32 @@
     parts = to_spectral([flat[:, LANES * e : LANES * e + LANES] for e in range(10)])
     parts = [parts[i] * inverse_ref[i] for i in range(10)]
     parts = from_spectral(parts)
-    flat = product(outof_ref, jnp.concatenate(parts, axis=1))
-    solved = [flat[:, LANES * e : LANES * e + LANES] for e in range(10)]
+    flat = product(outof_ref, jnp.concatenate([parts[e] for e in (0, 1, 8, 9)], axis=1))
+    ends = [flat[:, LANES * k : LANES * k + LANES] for k in range(4)]
+    low, low_faces = to_part(ends[1])
+    high, high_faces = to_part(ends[2])
+    send_axial(
+        send_in_ref,
+        send_out_ref,
+        [low, radial_sum(ends[0][:64]), low_faces],
+        [high, radial_sum(ends[3][:64]), high_faces],
+    )
+    for k in range(4):
+        ends_ref[k] = ends[k]
+    for e in range(2, 8):
+        middle_ref[e - 2] = parts[e]
+
+
+def solve_rest_kernel(
+    middle_ref, ends_ref, outof_ref, solved_ref, part_ref, send_early_ref, send_late_ref,
+):
+    flat = product(outof_ref, jnp.concatenate([middle_ref[k] for k in range(6)], axis=1))
+    solved = [flat[:, LANES * k : LANES * k + LANES] for k in range(6)]
+    solved = [ends_ref[0], ends_ref[1]] + solved + [ends_ref[2], ends_ref[3]]
     for e in range(10):
         solved_ref[e] = solved[e]
-    outer_a = [radial_sum(solved[0][:64]), radial_sum(solved[9][:64])]
-    edges = []
     for a in range(8):
-        rows = solved[a + 1]
-        value = radial_sum(rows[:64] + spread(rows[64:128], 1, 6))
-        outer_b = radial_sum(rows[128:144])
+        value, outer_b = to_part(solved[a + 1])
         part_ref[a] = value
         for side in range(2):
             edge = value[56 * side : 56 * side + 8]
@@ -562,14 +580,6 @@
                 send_late_ref[side, start : start + 8] = face
             else:
                 send_early_ref[side, 24 + 8 * a : 32 + 8 * a] = face
-        if a in (0, 7):
-            edges.append((value, outer_b))
-    send_axial(
-        send_in_ref,
-        send_out_ref,
-        [edges[0][0], outer_a[0], edges[0][1]],
-        [edges[1][0], outer_a[1], edges[1][1]],
-    )
 
 
 def solved_side_kernel(out_ref, in_ref, late_ref, row_ref, send_ref, pass_ref):
@@ -760,7 +770,7 @@
 
 
 def last_kernel(
-    part_ref, out_ref, in_ref, early_ref, late_ref, near_ref, sums_ref, old_sums_ref, row_ref,
+    part_ref, out_ref, in_ref, early_ref, late_ref, near_ref, sums_ref, old_sums_ref, row_ref, _,
     y_ref, z0_ref, z1_ref, planes_r_ref, planes_q_ref, planes_w_ref,
     pressure_ref, residual_ref, direction_ref,
 ):
@@ -870,7 +880,6 @@
     field, sums, row_shape = (8, 64, LANES), (devices, width * LANES), (8, width * LANES)
     boxes = [(10, 144, LANES), (10, 144, LANES)]
     raw_sends = [(128, LANES), (2, 96, LANES), (128, LANES), (2, 32, LANES)]
-    solved_sends = [(144, LANES), (2, 80, LANES), (144, LANES), (2, 48, LANES)]
 
     far = pl.BlockSpec(memory_space=pltpu.HBM)
     conv, row, *sends = kernel_call(
@@ -908,13 +917,23 @@
     )
     solver = (inverse, into, outof)
     operator = (near, diff, plane, grad, div)
-    solve_shapes = boxes + [field] + solved_sends + [copies]
+
+    def solve(g, moved, pay):
+        ends = [(6, 112, LANES), (4, 144, LANES), (144, LANES), (144, LANES), copies]
+        planes, middle, ends, send_out, send_in, pay = kernel_call(
+            solve_ends_kernel, boxes[:1] + ends, g, *moved, pay, *solver
+        )
+        solved, part, send_early, send_late = kernel_call(
+            solve_rest_kernel,
+            boxes[:1] + [field, (2, 80, LANES), (2, 48, LANES)],
+            middle, ends, outof,
+        )
+        return planes, solved, part, send_out, send_early, send_in, send_late, pay
+
 
     *moved, pay = exchange(raw_side_kernel, 48, sends, partial_sum(pay, groups[0]), one)
     pay = partial_sum(pay, groups[1])
-    planes_r, solved_r, part, *sends, pay = kernel_call(
-        solve_kernel, solve_shapes, g, *moved, pay, *solver
-    )
+    planes_r, solved_r, part, *sends, pay = solve(g, moved, pay)
     *moved, pay = exchange(solved_side_kernel, 48, sends, partial_sum(pay, groups[2]), one)
     pay = partial_sum(pay, groups[3])
     z0, raw0, g, *sends, row_r, pay = kernel_call(
@@ -924,9 +943,7 @@
     )
     *moved, pay = exchange(raw_side_kernel, 48, sends, partial_sum(pay, groups[0]), one)
     pay = partial_sum(pay, groups[1])
-    planes_q, solved_q, part, *sends, pay = kernel_call(
-        solve_kernel, solve_shapes, g, *moved, pay, *solver
-    )
+    planes_q, solved_q, part, *sends, pay = solve(g, moved, pay)
     *moved, pay = exchange(solved_side_kernel, 48, sends, partial_sum(pay, groups[2]), one)
     first_sums = partial_sum(pay, groups[3])
     y, z1, raw1, g, *sends = kernel_call(
@@ -940,18 +957,16 @@
         first_sums, row_r, near, planes_r, planes_q, solved_r, solved_q, z1, raw1, raw0,
     )
     *moved, pay = exchange(raw_side_kernel, 48, sends, pay, one)
-    planes_w, solved_w, part, *sends, pay = kernel_call(
-        solve_kernel, solve_shapes, g, *moved, pay, *solver
-    )
+    planes_w, solved_w, part, *sends, pay = solve(g, moved, pay)
     (pay,) = kernel_call(
         second_dots_kernel, [one], pay[:1], planes_r, planes_q, planes_w, solved_r, solved_q, solved_w
     )
     gathered = gather_sums(jnp.broadcast_to(pay, sums))
-    *moved, _ = exchange(solved_side_kernel, 48, sends, pay, one)
+    *moved, passed = exchange(solved_side_kernel, 48, sends, pay, one)
     pressure, residual, direction = kernel_call(
         last_kernel,
         [field, field, field],
-        part, *moved, near, gathered, first_sums, row_r,
+        part, *moved, near, gathered, first_sums, row_r, passed,
         y, z0, z1, planes_r, planes_q, planes_w,
     )
     return pressure.reshape(shape), residual.reshape(shape), direction.reshape(shape)

time: 97.1 us -> 96.1 us (0.990)
  waiting for transfers between devices: 42.5 us -> 40.8 us
    ppermute x10, waiting for transfers between devices: 19.8 us -> 18.7 us  [partial_sum(): lax.ppermute(row, ALL, [(i, i ^ step) for i in range(count)])[:1]]
    pallas_call x18 -> x21, Pallas kernels: 11.8 us -> 12.1 us  [kernel_call(): pl.pallas_call(kernel, out_shape=outs, compiler_params=pltpu.CompilerPara...]
  transfers between devices with their start and end apart: 38 -> 38, of which waited for: 19 -> 19; matrix products, arithmetic and copies ran while one was open for 0% -> 0% of each run, Pallas kernels for 2% -> 3%
where the time goes in v5:
time: 96.1 us; the launch traced here: 95.9 us
  waiting for transfers between devices  40.8 us (42%)
  starting transfers between devices  33.1 us (34%)
  Pallas kernels  12.1 us (13%)
  blocking collectives  8.89 us (9%)
  between operations  0.97 us (1%)
    ppermute x10, waiting for transfers between devices, partial_sum(): lax.ppermute(row, ALL, [(i, i ^ step) for i in range(count)])[:1]  18.7 us
    ppermute x14, starting transfers between devices, azim_swap(): return lax.ppermute(sides, 'azim', [(0, 1), (1, 0)])  17.7 us
    ppermute x7, waiting for transfers between devices, axial_swap(): from_outer = lax.ppermute(outer_rows, 'axial', outer)  15.9 us
    pallas_call x21, Pallas kernels, kernel_call(): pl.pallas_call(kernel, out_shape=outs, compiler_params=pltpu.CompilerPara...  12.1 us
    ppermute x7, starting transfers between devices, axial_swap(): from_outer = lax.ppermute(outer_rows, 'axial', outer)  8.96 us
    all_to_all x1, blocking collectives, gather_sums(): return lax.all_to_all(rows, ALL, 0, 0, tiled=True)  8.89 us
    ppermute x14, waiting for transfers between devices, azim_swap(): return lax.ppermute(sides, 'azim', [(0, 1), (1, 0)])  6.18 us
    ppermute x10, starting transfers between devices, partial_sum(): lax.ppermute(row, ALL, [(i, i ^ step) for i in range(count)])[:1]  3.48 us
  transfers between devices with their start and end apart: 38, of which 19 were waited for; matrix products, arithmetic and copies ran while one was open for 0% of the time, Pallas kernels for 3%

profile of v5, /device:TPU:0, one launch (start us, length us, event | category | flops | bytes accessed | tf_op | source)
XLA Modules:
  0.0 95.9 jit_solution(11011420076759068545)
XLA Ops:
  0.6 2.1 %shard_map.121 = (f32[3,8,64,128]{3,2,1,0:T(8,128)S(1)}, f32[8,128]{1,0:T(8,128)S(1)}, f32[200,128]{1,0:T(8,128)S(1)}, f32[2,144,128]{2,1,0:T(8,128)S(1)}, f32[2...) custom-call(f32[3,8,64,128]{3,2,1,0:T(8,128)} %bitcast.13, f32[1,32]{1,0:T(1,128)} %row_hbm.1, ...), custom_call_target="tpu_custom_call" | custom-call | tf_op jit(solution)/shard_map/pallas_call | solution.py:813
  2.8 5.5 %collective-permute-start = (f32[200,128]{1,0:T(8,128)S(1)}, f32[200,128]{1,0:T(8,128)S(1)}, u32[]{:S(2)}, u32[]{:S(2)}) collective-permute-start(f32[200,128]{1,0:T(8,128)S(1)} %get-tuple-element.82), channel_id=1, source_target_pairs={{2,4},{6,8},{10,12},{14,16},{18,20},{22,24},{26,28},{30,0},{4,2},{... | collective-permute-start | bytes 307208 | tf_op jit(solution)/shard_map/ppermute | solution.py:827
  8.3 1.5 %collective-permute-start.2 = (f32[2,144,128]{2,1,0:T(8,128)S(1)}, f32[2,144,128]{2,1,0:T(8,128)S(1)}, u32[]{:S(2)}, u32[]{:S(2)}) collective-permute-start(f32[2,144,128]{2,1,0:T(8,128)S(1)} %get-tuple-element.84), channel_id=1, source_target_pairs={{0,1},{1,0},{2,3},{3,2},{4,5},{5,4},{6,7},{7,6},{8,9},{9,8},{10,11... | collective-permute-start | bytes 442376 | tf_op jit(solution)/shard_map/ppermute | solution.py:835
  10.7 2.0 %collective-permute-start.3 = (f32[2,72,128]{2,1,0:T(8,128)S(1)}, f32[2,72,128]{2,1,0:T(8,128)S(1)}, u32[]{:S(2)}, u32[]{:S(2)}) collective-permute-start(f32[2,72,128]{2,1,0:T(8,128)S(1)} %shard_map.122), channel_id=1, source_target_pairs={{0,1},{1,0},{2,3},{3,2},{4,5},{5,4},{6,7},{7,6},{8,9},{9,8},{10,11... | collective-permute-start | bytes 221192 | tf_op jit(solution)/shard_map/ppermute | solution.py:835
  12.7 2.2 %collective-permute-done.2.early_ref = f32[2,144,128]{2,1,0:T(8,128)S(1)} collective-permute-done((f32[2,144,128]{2,1,0:T(8,128)S(1)}, f32[2,144,128]{2,1,0:T(8,128)S(1)}, u32[]{:S(2)}, u32[]{:S(2)}) %collective-permute-start.2) | collective-permute-done | bytes 147488 | tf_op jit(solution)/shard_map/ppermute | solution.py:835
  16.8 2.3 %collective-permute-start.4 = (f32[128,128]{1,0:T(8,128)S(1)}, f32[128,128]{1,0:T(8,128)S(1)}, u32[]{:S(2)}, u32[]{:S(2)}) collective-permute-start(f32[128,128]{1,0:T(8,128)S(1)} %get-tuple-element.88), channel_id=1, source_target_pairs={{2,4},{6,8},{10,12},{14,16},{18,20},{22,24},{26,28},{30,0},{4,2},{... | collective-permute-start | bytes 196616 | tf_op jit(solution)/shard_map/ppermute | solution.py:827
  19.1 1.5 %collective-permute-start.6 = (f32[2,96,128]{2,1,0:T(8,128)S(1)}, f32[2,96,128]{2,1,0:T(8,128)S(1)}, u32[]{:S(2)}, u32[]{:S(2)}) collective-permute-start(f32[2,96,128]{2,1,0:T(8,128)S(1)} %get-tuple-element.90), channel_id=1, source_target_pairs={{0,1},{1,0},{2,3},{3,2},{4,5},{5,4},{6,7},{7,6},{8,9},{9,8},{10,11... | collective-permute-start | bytes 294920 | tf_op jit(solution)/shard_map/ppermute | solution.py:835
  21.7 1.5 %collective-permute-done.4.out_ref = f32[128,128]{1,0:T(8,128)S(1)} collective-permute-done((f32[128,128]{1,0:T(8,128)S(1)}, f32[128,128]{1,0:T(8,128)S(1)}, u32[]{:S(2)}, u32[]{:S(2)}) %collective-permute-start.4) | collective-permute-done | bytes 65568 | tf_op jit(solution)/shard_map/ppermute | solution.py:827
  23.3 1.6 %collective-permute-start.9 = (f32[2,48,128]{2,1,0:T(8,128)S(1)}, f32[2,48,128]{2,1,0:T(8,128)S(1)}, u32[]{:S(2)}, u32[]{:S(2)}) collective-permute-start(f32[2,48,128]{2,1,0:T(8,128)S(1)} %get-tuple-element.93), channel_id=1, source_target_pairs={{0,1},{1,0},{2,3},{3,2},{4,5},{5,4},{6,7},{7,6},{8,9},{9,8},{10,11... | collective-permute-start | bytes 147464 | tf_op jit(solution)/shard_map/ppermute | solution.py:835
  25.0 3.4 %collective-permute-done.10 = f32[1,128]{1,0:T(1,128)S(1)} collective-permute-done((f32[1,128]{1,0:T(1,128)S(1)}, f32[1,128]{1,0:T(1,128)S(1)}, u32[]{:S(2)}, u32[]{:S(2)}) %collective-permute-start.10) | collective-permute-done | bytes 544 | tf_op jit(solution)/shard_map/ppermute | solution.py:860
  32.2 2.2 %collective-permute-done.14 = f32[32,128]{1,0:T(8,128)S(1)} collective-permute-done((f32[32,128]{1,0:T(8,128)S(1)}, f32[32,128]{1,0:T(8,128)S(1)}, u32[]{:S(2)}, u32[]{:S(2)}) %collective-permute-start.14) | collective-permute-done | bytes 16416 | tf_op jit(solution)/shard_map/ppermute | solution.py:860
  34.4 1.9 %collective-permute-done.11.out_ref = f32[144,128]{1,0:T(8,128)S(1)} collective-permute-done((f32[144,128]{1,0:T(8,128)S(1)}, f32[144,128]{1,0:T(8,128)S(1)}, u32[]{:S(2)}, u32[]{:S(2)}) %collective-permute-start.11) | collective-permute-done | bytes 73760 | tf_op jit(solution)/shard_map/ppermute | solution.py:827
  36.9 1.5 %collective-permute-start.16 = (f32[1,128]{1,0:T(1,128)S(1)}, f32[1,128]{1,0:T(1,128)S(1)}, u32[]{:S(2)}, u32[]{:S(2)}) collective-permute-start(f32[1,128]{1,0:T(1,128)S(1)} %get-tuple-element.105), channel_id=1, source_target_pairs={{0,1},{1,0},{2,3},{3,2},{4,5},{5,4},{6,7},{7,6},{8,9},{9,8},{10,11... | collective-permute-start | bytes 1544 | tf_op jit(solution)/shard_map/ppermute | solution.py:860
  38.4 2.1 %collective-permute-done.16 = f32[1,128]{1,0:T(1,128)S(1)} collective-permute-done((f32[1,128]{1,0:T(1,128)S(1)}, f32[1,128]{1,0:T(1,128)S(1)}, u32[]{:S(2)}, u32[]{:S(2)}) %collective-permute-start.16) | collective-permute-done | bytes 544 | tf_op jit(solution)/shard_map/ppermute | solution.py:860
  41.6 2.0 %collective-permute-start.18 = (f32[128,128]{1,0:T(8,128)S(1)}, f32[128,128]{1,0:T(8,128)S(1)}, u32[]{:S(2)}, u32[]{:S(2)}) collective-permute-start(f32[128,128]{1,0:T(8,128)S(1)} %get-tuple-element.110), channel_id=1, source_target_pairs={{0,2},{2,0},{4,6},{6,4},{8,10},{10,8},{12,14},{14,12},{16,18},{18,... | collective-permute-start | bytes 196616 | tf_op jit(solution)/shard_map/ppermute | solution.py:828
  43.6 1.4 %collective-permute-start.19 = (f32[2,96,128]{2,1,0:T(8,128)S(1)}, f32[2,96,128]{2,1,0:T(8,128)S(1)}, u32[]{:S(2)}, u32[]{:S(2)}) collective-permute-start(f32[2,96,128]{2,1,0:T(8,128)S(1)} %get-tuple-element.111), channel_id=1, source_target_pairs={{0,1},{1,0},{2,3},{3,2},{4,5},{5,4},{6,7},{7,6},{8,9},{9,8},{10,11... | collective-permute-start | bytes 294920 | tf_op jit(solution)/shard_map/ppermute | solution.py:835
  46.3 1.6 %collective-permute-done.17.out_ref = f32[128,128]{1,0:T(8,128)S(1)} collective-permute-done((f32[128,128]{1,0:T(8,128)S(1)}, f32[128,128]{1,0:T(8,128)S(1)}, u32[]{:S(2)}, u32[]{:S(2)}) %collective-permute-start.17) | collective-permute-done | bytes 65568 | tf_op jit(solution)/shard_map/ppermute | solution.py:827
  48.0 1.5 %collective-permute-start.22 = (f32[2,48,128]{2,1,0:T(8,128)S(1)}, f32[2,48,128]{2,1,0:T(8,128)S(1)}, u32[]{:S(2)}, u32[]{:S(2)}) collective-permute-start(f32[2,48,128]{2,1,0:T(8,128)S(1)} %get-tuple-element.114), channel_id=1, source_target_pairs={{0,1},{1,0},{2,3},{3,2},{4,5},{5,4},{6,7},{7,6},{8,9},{9,8},{10,11... | collective-permute-start | bytes 147464 | tf_op jit(solution)/shard_map/ppermute | solution.py:835
  49.4 3.5 %collective-permute-done.23 = f32[1,128]{1,0:T(1,128)S(1)} collective-permute-done((f32[1,128]{1,0:T(1,128)S(1)}, f32[1,128]{1,0:T(1,128)S(1)}, u32[]{:S(2)}, u32[]{:S(2)}) %collective-permute-start.23) | collective-permute-done | bytes 544 | tf_op jit(solution)/shard_map/ppermute | solution.py:860
  53.0 1.3 %shard_map.131 = (f32[10,144,128]{2,1,0:T(8,128)S(1)}, f32[6,112,128]{2,1,0:T(8,128)S(1)}, f32[4,144,128]{2,1,0:T(8,128)S(1)}, f32[144,128]{1,0:T(8,128)S(1)}, f...) custom-call(f32[8,64,128]{2,1,0:T(8,128)S(1)} %get-tuple-element.108.g_ref, f32[128,128]{1,0:T(8,128)S(1)} %collective-permute-done.17.out_ref, ...), custom_call_target="tpu_custom_call" | custom-call | tf_op jit(solution)/shard_map/pallas_call | solution.py:813
  55.9 3.0 %collective-permute-done.27 = f32[32,128]{1,0:T(8,128)S(1)} collective-permute-done((f32[32,128]{1,0:T(8,128)S(1)}, f32[32,128]{1,0:T(8,128)S(1)}, u32[]{:S(2)}, u32[]{:S(2)}) %collective-permute-start.27) | collective-permute-done | bytes 16416 | tf_op jit(solution)/shard_map/ppermute | solution.py:860
  59.0 1.9 %collective-permute-done.24.out_ref = f32[144,128]{1,0:T(8,128)S(1)} collective-permute-done((f32[144,128]{1,0:T(8,128)S(1)}, f32[144,128]{1,0:T(8,128)S(1)}, u32[]{:S(2)}, u32[]{:S(2)}) %collective-permute-start.24) | collective-permute-done | bytes 73760 | tf_op jit(solution)/shard_map/ppermute | solution.py:827
  61.6 1.4 %collective-permute-start.29 = (f32[1,128]{1,0:T(1,128)S(1)}, f32[1,128]{1,0:T(1,128)S(1)}, u32[]{:S(2)}, u32[]{:S(2)}) collective-permute-start(f32[1,128]{1,0:T(1,128)S(1)} %get-tuple-element.125), channel_id=1, source_target_pairs={{0,1},{1,0},{2,3},{3,2},{4,5},{5,4},{6,7},{7,6},{8,9},{9,8},{10,11... | collective-permute-start | bytes 1544 | tf_op jit(solution)/shard_map/ppermute | solution.py:860
  63.0 2.2 %collective-permute-done.29 = f32[1,128]{1,0:T(1,128)S(1)} collective-permute-done((f32[1,128]{1,0:T(1,128)S(1)}, f32[1,128]{1,0:T(1,128)S(1)}, u32[]{:S(2)}, u32[]{:S(2)}) %collective-permute-start.29) | collective-permute-done | bytes 544 | tf_op jit(solution)/shard_map/ppermute | solution.py:860
  66.2 1.4 %collective-permute-start.32 = (f32[2,96,128]{2,1,0:T(8,128)S(1)}, f32[2,96,128]{2,1,0:T(8,128)S(1)}, u32[]{:S(2)}, u32[]{:S(2)}) collective-permute-start(f32[2,96,128]{2,1,0:T(8,128)S(1)} %get-tuple-element.131), channel_id=1, source_target_pairs={{0,1},{1,0},{2,3},{3,2},{4,5},{5,4},{6,7},{7,6},{8,9},{9,8},{10,11... | collective-permute-start | bytes 294920 | tf_op jit(solution)/shard_map/ppermute | solution.py:835
  68.2 4.2 %collective-permute-done.30.out_ref = f32[128,128]{1,0:T(8,128)S(1)} collective-permute-done((f32[128,128]{1,0:T(8,128)S(1)}, f32[128,128]{1,0:T(8,128)S(1)}, u32[]{:S(2)}, u32[]{:S(2)}) %collective-permute-start.30) | collective-permute-done | bytes 65568 | tf_op jit(solution)/shard_map/ppermute | solution.py:827
  72.5 1.4 %collective-permute-start.33 = (f32[2,48,128]{2,1,0:T(8,128)S(1)}, f32[2,48,128]{2,1,0:T(8,128)S(1)}, u32[]{:S(2)}, u32[]{:S(2)}) collective-permute-start(f32[2,48,128]{2,1,0:T(8,128)S(1)} %get-tuple-element.139), channel_id=1, source_target_pairs={{0,1},{1,0},{2,3},{3,2},{4,5},{5,4},{6,7},{7,6},{8,9},{9,8},{10,11... | collective-permute-start | bytes 147464 | tf_op jit(solution)/shard_map/ppermute | solution.py:835
  73.9 2.8 %collective-permute-done.33.late_ref = f32[2,48,128]{2,1,0:T(8,128)S(1)} collective-permute-done((f32[2,48,128]{2,1,0:T(8,128)S(1)}, f32[2,48,128]{2,1,0:T(8,128)S(1)}, u32[]{:S(2)}, u32[]{:S(2)}) %collective-permute-start.33) | collective-permute-done | bytes 49184 | tf_op jit(solution)/shard_map/ppermute | solution.py:835
  78.5 1.4 %collective-permute-start.36 = (f32[2,80,128]{2,1,0:T(8,128)S(1)}, f32[2,80,128]{2,1,0:T(8,128)S(1)}, u32[]{:S(2)}, u32[]{:S(2)}) collective-permute-start(f32[2,80,128]{2,1,0:T(8,128)S(1)} %get-tuple-element.146), channel_id=1, source_target_pairs={{0,1},{1,0},{2,3},{3,2},{4,5},{5,4},{6,7},{7,6},{8,9},{9,8},{10,11... | collective-permute-start | bytes 245768 | tf_op jit(solution)/shard_map/ppermute | solution.py:835
  80.5 3.9 %collective-permute-done.34.out_ref = f32[144,128]{1,0:T(8,128)S(1)} collective-permute-done((f32[144,128]{1,0:T(8,128)S(1)}, f32[144,128]{1,0:T(8,128)S(1)}, u32[]{:S(2)}, u32[]{:S(2)}) %collective-permute-start.34) | collective-permute-done | bytes 73760 | tf_op jit(solution)/shard_map/ppermute | solution.py:827
  84.5 1.4 %collective-permute-start.37 = (f32[2,48,128]{2,1,0:T(8,128)S(1)}, f32[2,48,128]{2,1,0:T(8,128)S(1)}, u32[]{:S(2)}, u32[]{:S(2)}) collective-permute-start(f32[2,48,128]{2,1,0:T(8,128)S(1)} %get-tuple-element.153), channel_id=1, source_target_pairs={{0,1},{1,0},{2,3},{3,2},{4,5},{5,4},{6,7},{7,6},{8,9},{9,8},{10,11... | collective-permute-start | bytes 147464 | tf_op jit(solution)/shard_map/ppermute | solution.py:835
  85.9 8.9 %all_to_all.8 = f32[32,1,128]{2,1,0:T(1,128)S(1)} all-to-all(f32[32,1,128]{2,1,0:T(1,128)S(1)} %broadcast_in_dim.2), channel_id=1, replica_groups=mesh['axial'=16,'azim'=2] {'axial','azim'}, dimensions={0} | all-to-all | bytes 32768 | tf_op jit(solution)/shard_map/all_to_all | solution.py:865
  (96 shorter events, 18.2 us)
Async XLA Ops:
  2.8 7.8 %collective-permute-start = (f32[200,128]{1,0:T(8,128)S(1)}, f32[200,128]{1,0:T(8,128)S(1)}, u32[]{:S(2)}, u32[]{:S(2)}) collective-permute-start(f32[200,128]{1,0:T(8,128)S(1)} %get-tuple-element.82), channel_id=1, source_target_pairs={{2,4},{6,8},{10,12},{14,16},{18,20},{22,24},{26,28},{30,0},{4,2},{... | collective-permute-start | bytes 307208 | tf_op jit(solution)/shard_map/ppermute | solution.py:827
  8.3 6.6 %collective-permute-start.2 = (f32[2,144,128]{2,1,0:T(8,128)S(1)}, f32[2,144,128]{2,1,0:T(8,128)S(1)}, u32[]{:S(2)}, u32[]{:S(2)}) collective-permute-start(f32[2,144,128]{2,1,0:T(8,128)S(1)} %get-tuple-element.84), channel_id=1, source_target_pairs={{0,1},{1,0},{2,3},{3,2},{4,5},{5,4},{6,7},{7,6},{8,9},{9,8},{10,11... | collective-permute-start | bytes 442376 | tf_op jit(solution)/shard_map/ppermute | solution.py:835
  10.7 5.5 %collective-permute-start.3 = (f32[2,72,128]{2,1,0:T(8,128)S(1)}, f32[2,72,128]{2,1,0:T(8,128)S(1)}, u32[]{:S(2)}, u32[]{:S(2)}) collective-permute-start(f32[2,72,128]{2,1,0:T(8,128)S(1)} %shard_map.122), channel_id=1, source_target_pairs={{0,1},{1,0},{2,3},{3,2},{4,5},{5,4},{6,7},{7,6},{8,9},{9,8},{10,11... | collective-permute-start | bytes 221192 | tf_op jit(solution)/shard_map/ppermute | solution.py:835
  16.7 3.9 %collective-permute-start.7 = (f32[32,128]{1,0:T(8,128)S(1)}, f32[32,128]{1,0:T(8,128)S(1)}, u32[]{:S(2)}, u32[]{:S(2)}) collective-permute-start(f32[32,128]{1,0:T(8,128)S(1)} %get-tuple-element.92), channel_id=1, source_target_pairs={{0,4},{1,5},{2,6},{3,7},{4,0},{5,1},{6,2},{7,3},{8,12},{9,13},{10,... | collective-permute-start | bytes 49160 | tf_op jit(solution)/shard_map/ppermute | solution.py:860
  16.8 6.5 %collective-permute-start.4 = (f32[128,128]{1,0:T(8,128)S(1)}, f32[128,128]{1,0:T(8,128)S(1)}, u32[]{:S(2)}, u32[]{:S(2)}) collective-permute-start(f32[128,128]{1,0:T(8,128)S(1)} %get-tuple-element.88), channel_id=1, source_target_pairs={{2,4},{6,8},{10,12},{14,16},{18,20},{22,24},{26,28},{30,0},{4,2},{... | collective-permute-start | bytes 196616 | tf_op jit(solution)/shard_map/ppermute | solution.py:827
  19.1 4.1 %collective-permute-start.5 = (f32[128,128]{1,0:T(8,128)S(1)}, f32[128,128]{1,0:T(8,128)S(1)}, u32[]{:S(2)}, u32[]{:S(2)}) collective-permute-start(f32[128,128]{1,0:T(8,128)S(1)} %get-tuple-element.89), channel_id=1, source_target_pairs={{0,2},{2,0},{4,6},{6,4},{8,10},{10,8},{12,14},{14,12},{16,18},{18,... | collective-permute-start | bytes 196616 | tf_op jit(solution)/shard_map/ppermute | solution.py:828
  19.1 9.3 %collective-permute-start.6 = (f32[2,96,128]{2,1,0:T(8,128)S(1)}, f32[2,96,128]{2,1,0:T(8,128)S(1)}, u32[]{:S(2)}, u32[]{:S(2)}) collective-permute-start(f32[2,96,128]{2,1,0:T(8,128)S(1)} %get-tuple-element.90), channel_id=1, source_target_pairs={{0,1},{1,0},{2,3},{3,2},{4,5},{5,4},{6,7},{7,6},{8,9},{9,8},{10,11... | collective-permute-start | bytes 294920 | tf_op jit(solution)/shard_map/ppermute | solution.py:835
  23.3 5.1 %collective-permute-start.9 = (f32[2,48,128]{2,1,0:T(8,128)S(1)}, f32[2,48,128]{2,1,0:T(8,128)S(1)}, u32[]{:S(2)}, u32[]{:S(2)}) collective-permute-start(f32[2,48,128]{2,1,0:T(8,128)S(1)} %get-tuple-element.93), channel_id=1, source_target_pairs={{0,1},{1,0},{2,3},{3,2},{4,5},{5,4},{6,7},{7,6},{8,9},{9,8},{10,11... | collective-permute-start | bytes 147464 | tf_op jit(solution)/shard_map/ppermute | solution.py:835
  29.7 4.7 %collective-permute-start.14 = (f32[32,128]{1,0:T(8,128)S(1)}, f32[32,128]{1,0:T(8,128)S(1)}, u32[]{:S(2)}, u32[]{:S(2)}) collective-permute-start(f32[32,128]{1,0:T(8,128)S(1)} %get-tuple-element.102), channel_id=1, source_target_pairs={{0,16},{1,17},{2,18},{3,19},{4,20},{5,21},{6,22},{7,23},{8,24},{9,... | collective-permute-start | bytes 49160 | tf_op jit(solution)/shard_map/ppermute | solution.py:860
  29.8 6.5 %collective-permute-start.11 = (f32[144,128]{1,0:T(8,128)S(1)}, f32[144,128]{1,0:T(8,128)S(1)}, u32[]{:S(2)}, u32[]{:S(2)}) collective-permute-start(f32[144,128]{1,0:T(8,128)S(1)} %get-tuple-element.98), channel_id=1, source_target_pairs={{2,4},{6,8},{10,12},{14,16},{18,20},{22,24},{26,28},{30,0},{4,2},{... | collective-permute-start | bytes 221192 | tf_op jit(solution)/shard_map/ppermute | solution.py:827
  30.6 5.6 %collective-permute-start.12 = (f32[144,128]{1,0:T(8,128)S(1)}, f32[144,128]{1,0:T(8,128)S(1)}, u32[]{:S(2)}, u32[]{:S(2)}) collective-permute-start(f32[144,128]{1,0:T(8,128)S(1)} %get-tuple-element.99), channel_id=1, source_target_pairs={{0,2},{2,0},{4,6},{6,4},{8,10},{10,8},{12,14},{14,12},{16,18},{18,... | collective-permute-start | bytes 221192 | tf_op jit(solution)/shard_map/ppermute | solution.py:828
  31.6 9.0 %collective-permute-start.13 = (f32[2,80,128]{2,1,0:T(8,128)S(1)}, f32[2,80,128]{2,1,0:T(8,128)S(1)}, u32[]{:S(2)}, u32[]{:S(2)}) collective-permute-start(f32[2,80,128]{2,1,0:T(8,128)S(1)} %get-tuple-element.100), channel_id=1, source_target_pairs={{0,1},{1,0},{2,3},{3,2},{4,5},{5,4},{6,7},{7,6},{8,9},{9,8},{10,11... | collective-permute-start | bytes 245768 | tf_op jit(solution)/shard_map/ppermute | solution.py:835
  36.3 4.2 %collective-permute-start.15 = (f32[2,48,128]{2,1,0:T(8,128)S(1)}, f32[2,48,128]{2,1,0:T(8,128)S(1)}, u32[]{:S(2)}, u32[]{:S(2)}) collective-permute-start(f32[2,48,128]{2,1,0:T(8,128)S(1)} %get-tuple-element.103), channel_id=1, source_target_pairs={{0,1},{1,0},{2,3},{3,2},{4,5},{5,4},{6,7},{7,6},{8,9},{9,8},{10,11... | collective-permute-start | bytes 147464 | tf_op jit(solution)/shard_map/ppermute | solution.py:835
  36.9 3.6 %collective-permute-start.16 = (f32[1,128]{1,0:T(1,128)S(1)}, f32[1,128]{1,0:T(1,128)S(1)}, u32[]{:S(2)}, u32[]{:S(2)}) collective-permute-start(f32[1,128]{1,0:T(1,128)S(1)} %get-tuple-element.105), channel_id=1, source_target_pairs={{0,1},{1,0},{2,3},{3,2},{4,5},{5,4},{6,7},{7,6},{8,9},{9,8},{10,11... | collective-permute-start | bytes 1544 | tf_op jit(solution)/shard_map/ppermute | solution.py:860
  41.4 3.8 %collective-permute-start.20 = (f32[32,128]{1,0:T(8,128)S(1)}, f32[32,128]{1,0:T(8,128)S(1)}, u32[]{:S(2)}, u32[]{:S(2)}) collective-permute-start(f32[32,128]{1,0:T(8,128)S(1)} %get-tuple-element.113), channel_id=1, source_target_pairs={{0,4},{1,5},{2,6},{3,7},{4,0},{5,1},{6,2},{7,3},{8,12},{9,13},{10,... | collective-permute-start | bytes 49160 | tf_op jit(solution)/shard_map/ppermute | solution.py:860
  41.5 6.5 %collective-permute-start.17 = (f32[128,128]{1,0:T(8,128)S(1)}, f32[128,128]{1,0:T(8,128)S(1)}, u32[]{:S(2)}, u32[]{:S(2)}) collective-permute-start(f32[128,128]{1,0:T(8,128)S(1)} %get-tuple-element.109), channel_id=1, source_target_pairs={{2,4},{6,8},{10,12},{14,16},{18,20},{22,24},{26,28},{30,0},{4,2},{... | collective-permute-start | bytes 196616 | tf_op jit(solution)/shard_map/ppermute | solution.py:827
  41.6 6.4 %collective-permute-start.18 = (f32[128,128]{1,0:T(8,128)S(1)}, f32[128,128]{1,0:T(8,128)S(1)}, u32[]{:S(2)}, u32[]{:S(2)}) collective-permute-start(f32[128,128]{1,0:T(8,128)S(1)} %get-tuple-element.110), channel_id=1, source_target_pairs={{0,2},{2,0},{4,6},{6,4},{8,10},{10,8},{12,14},{14,12},{16,18},{18,... | collective-permute-start | bytes 196616 | tf_op jit(solution)/shard_map/ppermute | solution.py:828
  43.6 9.4 %collective-permute-start.19 = (f32[2,96,128]{2,1,0:T(8,128)S(1)}, f32[2,96,128]{2,1,0:T(8,128)S(1)}, u32[]{:S(2)}, u32[]{:S(2)}) collective-permute-start(f32[2,96,128]{2,1,0:T(8,128)S(1)} %get-tuple-element.111), channel_id=1, source_target_pairs={{0,1},{1,0},{2,3},{3,2},{4,5},{5,4},{6,7},{7,6},{8,9},{9,8},{10,11... | collective-permute-start | bytes 294920 | tf_op jit(solution)/shard_map/ppermute | solution.py:835
  48.0 5.0 %collective-permute-start.22 = (f32[2,48,128]{2,1,0:T(8,128)S(1)}, f32[2,48,128]{2,1,0:T(8,128)S(1)}, u32[]{:S(2)}, u32[]{:S(2)}) collective-permute-start(f32[2,48,128]{2,1,0:T(8,128)S(1)} %get-tuple-element.114), channel_id=1, source_target_pairs={{0,1},{1,0},{2,3},{3,2},{4,5},{5,4},{6,7},{7,6},{8,9},{9,8},{10,11... | collective-permute-start | bytes 147464 | tf_op jit(solution)/shard_map/ppermute | solution.py:835
  54.3 4.7 %collective-permute-start.27 = (f32[32,128]{1,0:T(8,128)S(1)}, f32[32,128]{1,0:T(8,128)S(1)}, u32[]{:S(2)}, u32[]{:S(2)}) collective-permute-start(f32[32,128]{1,0:T(8,128)S(1)} %get-tuple-element.123), channel_id=1, source_target_pairs={{0,16},{1,17},{2,18},{3,19},{4,20},{5,21},{6,22},{7,23},{8,24},{9,... | collective-permute-start | bytes 49160 | tf_op jit(solution)/shard_map/ppermute | solution.py:860
  54.4 6.5 %collective-permute-start.24 = (f32[144,128]{1,0:T(8,128)S(1)}, f32[144,128]{1,0:T(8,128)S(1)}, u32[]{:S(2)}, u32[]{:S(2)}) collective-permute-start(f32[144,128]{1,0:T(8,128)S(1)} %get-tuple-element.119), channel_id=1, source_target_pairs={{2,4},{6,8},{10,12},{14,16},{18,20},{22,24},{26,28},{30,0},{4,2},{... | collective-permute-start | bytes 221192 | tf_op jit(solution)/shard_map/ppermute | solution.py:827
  54.4 6.5 %collective-permute-start.25 = (f32[144,128]{1,0:T(8,128)S(1)}, f32[144,128]{1,0:T(8,128)S(1)}, u32[]{:S(2)}, u32[]{:S(2)}) collective-permute-start(f32[144,128]{1,0:T(8,128)S(1)} %get-tuple-element.120), channel_id=1, source_target_pairs={{0,2},{2,0},{4,6},{6,4},{8,10},{10,8},{12,14},{14,12},{16,18},{18,... | collective-permute-start | bytes 221192 | tf_op jit(solution)/shard_map/ppermute | solution.py:828
  55.2 10.0 %collective-permute-start.26 = (f32[2,80,128]{2,1,0:T(8,128)S(1)}, f32[2,80,128]{2,1,0:T(8,128)S(1)}, u32[]{:S(2)}, u32[]{:S(2)}) collective-permute-start(f32[2,80,128]{2,1,0:T(8,128)S(1)} %get-tuple-element.121), channel_id=1, source_target_pairs={{0,1},{1,0},{2,3},{3,2},{4,5},{5,4},{6,7},{7,6},{8,9},{9,8},{10,11... | collective-permute-start | bytes 245768 | tf_op jit(solution)/shard_map/ppermute | solution.py:835
  60.9 4.3 %collective-permute-start.28 = (f32[2,48,128]{2,1,0:T(8,128)S(1)}, f32[2,48,128]{2,1,0:T(8,128)S(1)}, u32[]{:S(2)}, u32[]{:S(2)}) collective-permute-start(f32[2,48,128]{2,1,0:T(8,128)S(1)} %get-tuple-element.124), channel_id=1, source_target_pairs={{0,1},{1,0},{2,3},{3,2},{4,5},{5,4},{6,7},{7,6},{8,9},{9,8},{10,11... | collective-permute-start | bytes 147464 | tf_op jit(solution)/shard_map/ppermute | solution.py:835
  66.0 6.5 %collective-permute-start.30 = (f32[128,128]{1,0:T(8,128)S(1)}, f32[128,128]{1,0:T(8,128)S(1)}, u32[]{:S(2)}, u32[]{:S(2)}) collective-permute-start(f32[128,128]{1,0:T(8,128)S(1)} %get-tuple-element.129), channel_id=1, source_target_pairs={{2,4},{6,8},{10,12},{14,16},{18,20},{22,24},{26,28},{30,0},{4,2},{... | collective-permute-start | bytes 196616 | tf_op jit(solution)/shard_map/ppermute | solution.py:827
  66.1 6.4 %collective-permute-start.31 = (f32[128,128]{1,0:T(8,128)S(1)}, f32[128,128]{1,0:T(8,128)S(1)}, u32[]{:S(2)}, u32[]{:S(2)}) collective-permute-start(f32[128,128]{1,0:T(8,128)S(1)} %get-tuple-element.130), channel_id=1, source_target_pairs={{0,2},{2,0},{4,6},{6,4},{8,10},{10,8},{12,14},{14,12},{16,18},{18,... | collective-permute-start | bytes 196616 | tf_op jit(solution)/shard_map/ppermute | solution.py:828
  66.2 7.7 %collective-permute-start.32 = (f32[2,96,128]{2,1,0:T(8,128)S(1)}, f32[2,96,128]{2,1,0:T(8,128)S(1)}, u32[]{:S(2)}, u32[]{:S(2)}) collective-permute-start(f32[2,96,128]{2,1,0:T(8,128)S(1)} %get-tuple-element.131), channel_id=1, source_target_pairs={{0,1},{1,0},{2,3},{3,2},{4,5},{5,4},{6,7},{7,6},{8,9},{9,8},{10,11... | collective-permute-start | bytes 294920 | tf_op jit(solution)/shard_map/ppermute | solution.py:835
  72.5 4.2 %collective-permute-start.33 = (f32[2,48,128]{2,1,0:T(8,128)S(1)}, f32[2,48,128]{2,1,0:T(8,128)S(1)}, u32[]{:S(2)}, u32[]{:S(2)}) collective-permute-start(f32[2,48,128]{2,1,0:T(8,128)S(1)} %get-tuple-element.139), channel_id=1, source_target_pairs={{0,1},{1,0},{2,3},{3,2},{4,5},{5,4},{6,7},{7,6},{8,9},{9,8},{10,11... | collective-permute-start | bytes 147464 | tf_op jit(solution)/shard_map/ppermute | solution.py:835
  77.9 6.5 %collective-permute-start.34 = (f32[144,128]{1,0:T(8,128)S(1)}, f32[144,128]{1,0:T(8,128)S(1)}, u32[]{:S(2)}, u32[]{:S(2)}) collective-permute-start(f32[144,128]{1,0:T(8,128)S(1)} %get-tuple-element.144), channel_id=1, source_target_pairs={{2,4},{6,8},{10,12},{14,16},{18,20},{22,24},{26,28},{30,0},{4,2},{... | collective-permute-start | bytes 221192 | tf_op jit(solution)/shard_map/ppermute | solution.py:827
  78.0 6.5 %collective-permute-start.35 = (f32[144,128]{1,0:T(8,128)S(1)}, f32[144,128]{1,0:T(8,128)S(1)}, u32[]{:S(2)}, u32[]{:S(2)}) collective-permute-start(f32[144,128]{1,0:T(8,128)S(1)} %get-tuple-element.145), channel_id=1, source_target_pairs={{0,2},{2,0},{4,6},{6,4},{8,10},{10,8},{12,14},{14,12},{16,18},{18,... | collective-permute-start | bytes 221192 | tf_op jit(solution)/shard_map/ppermute | solution.py:828
  78.5 16.2 %collective-permute-start.36 = (f32[2,80,128]{2,1,0:T(8,128)S(1)}, f32[2,80,128]{2,1,0:T(8,128)S(1)}, u32[]{:S(2)}, u32[]{:S(2)}) collective-permute-start(f32[2,80,128]{2,1,0:T(8,128)S(1)} %get-tuple-element.146), channel_id=1, source_target_pairs={{0,1},{1,0},{2,3},{3,2},{4,5},{5,4},{6,7},{7,6},{8,9},{9,8},{10,11... | collective-permute-start | bytes 245768 | tf_op jit(solution)/shard_map/ppermute | solution.py:835
  84.5 10.3 %collective-permute-start.37 = (f32[2,48,128]{2,1,0:T(8,128)S(1)}, f32[2,48,128]{2,1,0:T(8,128)S(1)}, u32[]{:S(2)}, u32[]{:S(2)}) collective-permute-start(f32[2,48,128]{2,1,0:T(8,128)S(1)} %get-tuple-element.153), channel_id=1, source_target_pairs={{0,1},{1,0},{2,3},{3,2},{4,5},{5,4},{6,7},{7,6},{8,9},{9,8},{10,11... | collective-permute-start | bytes 147464 | tf_op jit(solution)/shard_map/ppermute | solution.py:835
  (15 other events, 69.0 us)

commit v6 on v5

--- a/solution.py
+++ b/solution.py
@@ -199,11 +199,11 @@
     return total
 
 
-def skew_apply(matrix, parts):
+def skew_apply(matrix, parts, rows=range(4)):
     plus = [parts[b] + parts[7 - b] for b in range(4)]
     minus = [parts[b] - parts[7 - b] for b in range(4)]
     result = [None] * 8
-    for a in range(4):
+    for a in rows:
         even = combine([0.5 * (matrix[a, b] + matrix[a, 7 - b]) for b in range(4)], plus)
         odd = combine([0.5 * (matrix[a, b] - matrix[a, 7 - b]) for b in range(4)], minus)
         result[a] = even + odd
@@ -369,9 +369,11 @@
             row = 64 * comp + 8 * b
             send_ref[side, first] = late_ref[side, first] + before(row, 8)
             send_ref[side, last] = late_ref[side, last] + after(row, 8)
+        send_ref[side, 48:] = jnp.zeros((send_ref.shape[1] - 48, LANES), F32)
         for place, rows in enumerate((before(192, count), row_ref[...], after(192, count))):
-            start = 48 + place * count
-            send_ref[side, start : start + count] = rows
+            width = min(count, (send_ref.shape[1] - 48) // 3)
+            start = 48 + place * width
+            send_ref[side, start : start + width] = rows[:width]
 
 
 def coarse_share(raw, near_ref):
@@ -411,11 +413,13 @@
     return jnp.where(place >= width - TAIL, 0.0, row), values
 
 
-def send_raw(raw, g_ref, in_ref, out_ref, early_ref, late_ref):
-    parts = [radial_sum(raw[a]) for a in range(8)]
+def send_raw_ends(parts, in_ref, out_ref):
+    send_axial(in_ref, out_ref, [parts[0], parts[1]], [parts[7], parts[6]])
+
+
+def send_raw_rest(parts, g_ref, early_ref, late_ref):
     for a in range(8):
         g_ref[a] = parts[a]
-    send_axial(in_ref, out_ref, [parts[0], parts[1]], [parts[7], parts[6]])
     for side, (edge, inner) in enumerate(((0, 1), (7, 6))):
         edges = [part[8 * edge : 8 * edge + 8] for part in parts]
         inners = [part[8 * inner : 8 * inner + 8] for part in parts]
@@ -428,6 +432,12 @@
         late_ref[side, 24:32] = inners[7]
 
 
+def send_raw(raw, g_ref, in_ref, out_ref, early_ref, late_ref):
+    parts = [radial_sum(raw[a]) for a in range(8)]
+    send_raw_ends(parts, in_ref, out_ref)
+    send_raw_rest(parts, g_ref, early_ref, late_ref)
+
+
 def raw_side_kernel(out_ref, in_ref, late_ref, row_ref, send_ref, pass_ref):
     pass_ref[...] = row_ref[...]
     before, after = got_axial(in_ref, out_ref)
@@ -441,7 +451,7 @@
 
 
 def divergence_kernel(
-    conv_ref, u_ref, out_ref, in_ref, early_ref, late_ref, row_ref, plane_ref, over_ref, div_ref,
+    early_ref, conv_ref, u_ref, out_ref, in_ref, late_ref, row_ref, plane_ref, over_ref, div_ref,
     g_ref, send_out_ref, send_early_ref, send_in_ref, send_late_ref, near_ref, pay_ref,
 ):
     before, after = got_axial(in_ref, out_ref)
@@ -477,10 +487,11 @@
     count = row_ref.shape[0]
     width = near_ref.shape[1] // LANES
     near_ref[...] = jnp.zeros(near_ref.shape, F32)
+    packed = min(count, (late_ref.shape[1] - 48) // 3)
     for i in range(3):
-        start = 48 + i * count
+        start = 48 + i * packed
         middle = (before(192, count), row_ref[...], after(192, count))[i]
-        sides = (late_ref[1, start : start + count], middle, late_ref[0, start : start + count])
+        sides = (late_ref[1, start : start + packed], middle, late_ref[0, start : start + packed])
         for j, rows in enumerate(sides):
             for k in range(width):
                 near_ref[3 * i + j : 3 * i + j + 1, LANES * k : LANES * k + LANES] = rows[k : k + 1]
@@ -640,26 +651,33 @@
     ]
 
 
-def apply_operator(values, diff_ref, plane_ref, grad_ref, div_ref):
+def flux_along(values, diff_ref, plane_ref):
     plane = plane_ref[...]
-    coef = [float(WEIGHTS[a]) * plane * diff_ref[a] for a in range(8)]
-    flat = product(grad_ref, jnp.concatenate(values, axis=1))
-    along_a = skew_apply(DERIV, values)
-    flux = jnp.concatenate(
-        [
-            jnp.concatenate([coef[a], coef[a]], axis=0) * flat[:, LANES * a : LANES * a + LANES]
-            for a in range(8)
-        ],
-        axis=1,
-    )
-    flat = product(div_ref, flux)
-    along_a = skew_apply(DERIV.T, [coef[a] * along_a[a] for a in range(8)])
+    slopes = skew_apply(DERIV, values)
+    return [float(WEIGHTS[a]) * plane * diff_ref[a] * slopes[a] for a in range(8)]
+
+
+def apply_layers(layers, values, flux, diff_ref, plane_ref, grad_ref, div_ref):
+    plane = plane_ref[...]
+    flat = product(grad_ref, jnp.concatenate([values[a] for a in layers], axis=1))
+    across = []
+    for k, a in enumerate(layers):
+        coef = float(WEIGHTS[a]) * plane * diff_ref[a]
+        coef = jnp.concatenate([coef, coef], axis=0)
+        across.append(coef * flat[:, LANES * k : LANES * k + LANES])
+    flat = product(div_ref, jnp.concatenate(across, axis=1))
+    along_a = skew_apply(DERIV.T, flux, [a for a in layers if a < 4])
     return [
         along_a[a]
-        + flat[:, LANES * a : LANES * a + LANES]
+        + flat[:, LANES * k : LANES * k + LANES]
         + (mass_shift * float(WEIGHTS[a])) * plane * values[a]
-        for a in range(8)
+        for k, a in enumerate(layers)
     ]
+
+
+def apply_operator(values, diff_ref, plane_ref, grad_ref, div_ref):
+    flux = flux_along(values, diff_ref, plane_ref)
+    return apply_layers(range(8), values, flux, diff_ref, plane_ref, grad_ref, div_ref)
 
 
 def dot_parts(first, second):
@@ -708,20 +726,40 @@
     return row_r, row_q, rz, curv, rz / curv
 
 
-def second_apply_kernel(
+END_LAYERS = (0, 1, 6, 7)
+
+
+def apply_ends_kernel(
     part_ref, out_ref, in_ref, early_ref, late_ref, near_ref, diff_ref, plane_ref, grad_ref, div_ref,
     sums_ref, row_ref, z0_ref,
-    y_ref, z_ref, raw_ref, g_ref, send_out_ref, send_early_ref, send_in_ref, send_late_ref,
+    y_ref, z_ref, flux_ref, ends_ref, send_out_ref, send_in_ref,
 ):
     _, row_q, _, _, alpha = first_step(sums_ref, row_ref)
     change = got_solved(part_ref, in_ref, out_ref, early_ref, late_ref)
     change = add_coarse(change, row_q, near_ref)
     values = [z0_ref[a] - alpha * change[a] for a in range(8)]
-    raw = apply_operator(values, diff_ref, plane_ref, grad_ref, div_ref)
-    send_raw(raw, g_ref, send_in_ref, send_out_ref, send_early_ref, send_late_ref)
+    flux = flux_along(values, diff_ref, plane_ref)
+    ends = apply_layers(END_LAYERS, values, flux, diff_ref, plane_ref, grad_ref, div_ref)
+    sent = {a: radial_sum(raw) for a, raw in zip(END_LAYERS, ends)}
+    send_raw_ends(sent, send_in_ref, send_out_ref)
     for a in range(8):
         y_ref[a] = change[a]
         z_ref[a] = values[a]
+        flux_ref[a] = flux[a]
+    for k in range(4):
+        ends_ref[k] = ends[k]
+
+
+def apply_rest_kernel(
+    z_ref, flux_ref, ends_ref, diff_ref, plane_ref, grad_ref, div_ref,
+    raw_ref, g_ref, send_early_ref, send_late_ref,
+):
+    values = [z_ref[a] for a in range(8)]
+    flux = [flux_ref[a] for a in range(8)]
+    raw = apply_layers((2, 3, 4, 5), values, flux, diff_ref, plane_ref, grad_ref, div_ref)
+    raw = [ends_ref[0], ends_ref[1]] + raw + [ends_ref[2], ends_ref[3]]
+    send_raw_rest([radial_sum(part) for part in raw], g_ref, send_early_ref, send_late_ref)
+    for a in range(8):
         raw_ref[a] = raw[a]
 
 
@@ -909,11 +947,11 @@
 
     one, copies = (1, width * LANES), (SUM_ROWS, width * LANES)
     groups = sum_steps()
-    moved = exchange(conv_side_kernel, 48 + 3 * count, sends, row)
+    moved = exchange(conv_side_kernel, 48 + 8 * -(-3 * width // 8), sends, row)
     g, *sends, near, pay = kernel_call(
         divergence_kernel,
         [field] + raw_sends + [(16, width * LANES), copies],
-        conv, u, *moved, row, plane, over, div,
+        moved[2], conv, u, *moved[:2], moved[3], row, plane, over, div,
     )
     solver = (inverse, into, outof)
     operator = (near, diff, plane, grad, div)
@@ -946,11 +984,17 @@
     planes_q, solved_q, part, *sends, pay = solve(g, moved, pay)
     *moved, pay = exchange(solved_side_kernel, 48, sends, partial_sum(pay, groups[2]), one)
     first_sums = partial_sum(pay, groups[3])
-    y, z1, raw1, g, *sends = kernel_call(
-        second_apply_kernel,
-        [field, field, field, field] + raw_sends,
+    y, z1, flux, ends, send_out, send_in = kernel_call(
+        apply_ends_kernel,
+        [field, field, field, (4, 64, LANES), (128, LANES), (128, LANES)],
         part, *moved, *operator, first_sums, row_r, z0,
     )
+    raw1, g, send_early, send_late = kernel_call(
+        apply_rest_kernel,
+        [field, field, (2, 96, LANES), (2, 32, LANES)],
+        z1, flux, ends, diff, plane, grad, div,
+    )
+    sends = send_out, send_early, send_in, send_late
     planes_r, solved_r, pay = kernel_call(
         first_dots_kernel,
         boxes + [one],

time: 96.1 us -> 95.8 us (level)
  waiting for transfers between devices: 40.8 us -> 39.8 us
    pallas_call x21 -> x22, Pallas kernels: 12.1 us -> 12.6 us  [kernel_call(): pl.pallas_call(kernel, out_shape=outs, compiler_params=pltpu.CompilerPara...]
  transfers between devices with their start and end apart: 38 -> 38, of which waited for: 19 -> 19; matrix products, arithmetic and copies ran while one was open for 0% -> 0% of each run, Pallas kernels for 3% -> 4%
where the time goes in v6:
time: 95.8 us; the launch traced here: 95.6 us
  waiting for transfers between devices  39.8 us (42%)
  starting transfers between devices  33.3 us (35%)
  Pallas kernels  12.6 us (13%)
  blocking collectives  8.89 us (9%)
  between operations  0.98 us (1%)
    ppermute x10, waiting for transfers between devices, partial_sum(): lax.ppermute(row, ALL, [(i, i ^ step) for i in range(count)])[:1]  18.6 us
    ppermute x14, starting transfers between devices, azim_swap(): return lax.ppermute(sides, 'azim', [(0, 1), (1, 0)])  17.7 us
    ppermute x7, waiting for transfers between devices, axial_swap(): from_outer = lax.ppermute(outer_rows, 'axial', outer)  15.3 us
    pallas_call x22, Pallas kernels, kernel_call(): pl.pallas_call(kernel, out_shape=outs, compiler_params=pltpu.CompilerPara...  12.6 us
    ppermute x7, starting transfers between devices, axial_swap(): from_outer = lax.ppermute(outer_rows, 'axial', outer)  9.12 us
    all_to_all x1, blocking collectives, gather_sums(): return lax.all_to_all(rows, ALL, 0, 0, tiled=True)  8.89 us
    ppermute x14, waiting for transfers between devices, azim_swap(): return lax.ppermute(sides, 'azim', [(0, 1), (1, 0)])  5.83 us
    ppermute x10, starting transfers between devices, partial_sum(): lax.ppermute(row, ALL, [(i, i ^ step) for i in range(count)])[:1]  3.66 us
  transfers between devices with their start and end apart: 38, of which 19 were waited for; matrix products, arithmetic and copies ran while one was open for 0% of the time, Pallas kernels for 4%

profile of v6, /device:TPU:0, one launch (start us, length us, event | category | flops | bytes accessed | tf_op | source)
XLA Modules:
  0.0 95.6 jit_solution(6788697806901919621)
XLA Ops:
  0.6 2.1 %shard_map.121 = (f32[3,8,64,128]{3,2,1,0:T(8,128)S(1)}, f32[8,128]{1,0:T(8,128)S(1)}, f32[200,128]{1,0:T(8,128)S(1)}, f32[2,144,128]{2,1,0:T(8,128)S(1)}, f32[2...) custom-call(f32[3,8,64,128]{3,2,1,0:T(8,128)} %bitcast.17, f32[1,32]{1,0:T(1,128)} %row_hbm.1, ...), custom_call_target="tpu_custom_call" | custom-call | tf_op jit(solution)/shard_map/pallas_call | solution.py:851
  2.8 5.5 %collective-permute-start.1 = (f32[200,128]{1,0:T(8,128)S(1)}, f32[200,128]{1,0:T(8,128)S(1)}, u32[]{:S(2)}, u32[]{:S(2)}) collective-permute-start(f32[200,128]{1,0:T(8,128)S(1)} %get-tuple-element.85), channel_id=1, source_target_pairs={{2,4},{6,8},{10,12},{14,16},{18,20},{22,24},{26,28},{30,0},{4,2},{... | collective-permute-start | bytes 307208 | tf_op jit(solution)/shard_map/ppermute | solution.py:865
  8.3 1.5 %collective-permute-start = (f32[2,144,128]{2,1,0:T(8,128)S(1)}, f32[2,144,128]{2,1,0:T(8,128)S(1)}, u32[]{:S(2)}, u32[]{:S(2)}) collective-permute-start(f32[2,144,128]{2,1,0:T(8,128)S(1)} %get-tuple-element.83), channel_id=1, source_target_pairs={{0,1},{1,0},{2,3},{3,2},{4,5},{5,4},{6,7},{7,6},{8,9},{9,8},{10,11... | collective-permute-start | bytes 442376 | tf_op jit(solution)/shard_map/ppermute | solution.py:873
  10.7 2.1 %collective-permute-start.3 = (f32[2,56,128]{2,1,0:T(8,128)S(1)}, f32[2,56,128]{2,1,0:T(8,128)S(1)}, u32[]{:S(2)}, u32[]{:S(2)}) collective-permute-start(f32[2,56,128]{2,1,0:T(8,128)S(1)} %shard_map.122), channel_id=1, source_target_pairs={{0,1},{1,0},{2,3},{3,2},{4,5},{5,4},{6,7},{7,6},{8,9},{9,8},{10,11... | collective-permute-start | bytes 172040 | tf_op jit(solution)/shard_map/ppermute | solution.py:873
  12.7 2.2 %collective-permute-done.early_ref = f32[2,144,128]{2,1,0:T(8,128)S(1)} collective-permute-done((f32[2,144,128]{2,1,0:T(8,128)S(1)}, f32[2,144,128]{2,1,0:T(8,128)S(1)}, u32[]{:S(2)}, u32[]{:S(2)}) %collective-permute-start) | collective-permute-done | bytes 147488 | tf_op jit(solution)/shard_map/ppermute | solution.py:873
  16.4 2.5 %collective-permute-start.4 = (f32[128,128]{1,0:T(8,128)S(1)}, f32[128,128]{1,0:T(8,128)S(1)}, u32[]{:S(2)}, u32[]{:S(2)}) collective-permute-start(f32[128,128]{1,0:T(8,128)S(1)} %get-tuple-element.90), channel_id=1, source_target_pairs={{2,4},{6,8},{10,12},{14,16},{18,20},{22,24},{26,28},{30,0},{4,2},{... | collective-permute-start | bytes 196616 | tf_op jit(solution)/shard_map/ppermute | solution.py:865
  18.9 1.5 %collective-permute-start.6 = (f32[2,96,128]{2,1,0:T(8,128)S(1)}, f32[2,96,128]{2,1,0:T(8,128)S(1)}, u32[]{:S(2)}, u32[]{:S(2)}) collective-permute-start(f32[2,96,128]{2,1,0:T(8,128)S(1)} %get-tuple-element.92), channel_id=1, source_target_pairs={{0,1},{1,0},{2,3},{3,2},{4,5},{5,4},{6,7},{7,6},{8,9},{9,8},{10,11... | collective-permute-start | bytes 294920 | tf_op jit(solution)/shard_map/ppermute | solution.py:873
  21.6 1.3 %collective-permute-done.4.out_ref = f32[128,128]{1,0:T(8,128)S(1)} collective-permute-done((f32[128,128]{1,0:T(8,128)S(1)}, f32[128,128]{1,0:T(8,128)S(1)}, u32[]{:S(2)}, u32[]{:S(2)}) %collective-permute-start.4) | collective-permute-done | bytes 65568 | tf_op jit(solution)/shard_map/ppermute | solution.py:865
  22.9 1.6 %collective-permute-start.9 = (f32[2,48,128]{2,1,0:T(8,128)S(1)}, f32[2,48,128]{2,1,0:T(8,128)S(1)}, u32[]{:S(2)}, u32[]{:S(2)}) collective-permute-start(f32[2,48,128]{2,1,0:T(8,128)S(1)} %get-tuple-element.95), channel_id=1, source_target_pairs={{0,1},{1,0},{2,3},{3,2},{4,5},{5,4},{6,7},{7,6},{8,9},{9,8},{10,11... | collective-permute-start | bytes 147464 | tf_op jit(solution)/shard_map/ppermute | solution.py:873
  24.6 3.4 %collective-permute-done.10 = f32[1,128]{1,0:T(1,128)S(1)} collective-permute-done((f32[1,128]{1,0:T(1,128)S(1)}, f32[1,128]{1,0:T(1,128)S(1)}, u32[]{:S(2)}, u32[]{:S(2)}) %collective-permute-start.10) | collective-permute-done | bytes 544 | tf_op jit(solution)/shard_map/ppermute | solution.py:898
  32.0 2.0 %collective-permute-done.14 = f32[32,128]{1,0:T(8,128)S(1)} collective-permute-done((f32[32,128]{1,0:T(8,128)S(1)}, f32[32,128]{1,0:T(8,128)S(1)}, u32[]{:S(2)}, u32[]{:S(2)}) %collective-permute-start.14) | collective-permute-done | bytes 16416 | tf_op jit(solution)/shard_map/ppermute | solution.py:898
  34.0 2.0 %collective-permute-done.11.out_ref = f32[144,128]{1,0:T(8,128)S(1)} collective-permute-done((f32[144,128]{1,0:T(8,128)S(1)}, f32[144,128]{1,0:T(8,128)S(1)}, u32[]{:S(2)}, u32[]{:S(2)}) %collective-permute-start.11) | collective-permute-done | bytes 73760 | tf_op jit(solution)/shard_map/ppermute | solution.py:865
  36.7 1.5 %collective-permute-start.16 = (f32[1,128]{1,0:T(1,128)S(1)}, f32[1,128]{1,0:T(1,128)S(1)}, u32[]{:S(2)}, u32[]{:S(2)}) collective-permute-start(f32[1,128]{1,0:T(1,128)S(1)} %get-tuple-element.107), channel_id=1, source_target_pairs={{0,1},{1,0},{2,3},{3,2},{4,5},{5,4},{6,7},{7,6},{8,9},{9,8},{10,11... | collective-permute-start | bytes 1544 | tf_op jit(solution)/shard_map/ppermute | solution.py:898
  38.2 2.1 %collective-permute-done.16 = f32[1,128]{1,0:T(1,128)S(1)} collective-permute-done((f32[1,128]{1,0:T(1,128)S(1)}, f32[1,128]{1,0:T(1,128)S(1)}, u32[]{:S(2)}, u32[]{:S(2)}) %collective-permute-start.16) | collective-permute-done | bytes 544 | tf_op jit(solution)/shard_map/ppermute | solution.py:898
  41.4 2.0 %collective-permute-start.18 = (f32[128,128]{1,0:T(8,128)S(1)}, f32[128,128]{1,0:T(8,128)S(1)}, u32[]{:S(2)}, u32[]{:S(2)}) collective-permute-start(f32[128,128]{1,0:T(8,128)S(1)} %get-tuple-element.112), channel_id=1, source_target_pairs={{0,2},{2,0},{4,6},{6,4},{8,10},{10,8},{12,14},{14,12},{16,18},{18,... | collective-permute-start | bytes 196616 | tf_op jit(solution)/shard_map/ppermute | solution.py:866
  43.4 1.4 %collective-permute-start.19 = (f32[2,96,128]{2,1,0:T(8,128)S(1)}, f32[2,96,128]{2,1,0:T(8,128)S(1)}, u32[]{:S(2)}, u32[]{:S(2)}) collective-permute-start(f32[2,96,128]{2,1,0:T(8,128)S(1)} %get-tuple-element.113), channel_id=1, source_target_pairs={{0,1},{1,0},{2,3},{3,2},{4,5},{5,4},{6,7},{7,6},{8,9},{9,8},{10,11... | collective-permute-start | bytes 294920 | tf_op jit(solution)/shard_map/ppermute | solution.py:873
  46.1 1.6 %collective-permute-done.17.out_ref = f32[128,128]{1,0:T(8,128)S(1)} collective-permute-done((f32[128,128]{1,0:T(8,128)S(1)}, f32[128,128]{1,0:T(8,128)S(1)}, u32[]{:S(2)}, u32[]{:S(2)}) %collective-permute-start.17) | collective-permute-done | bytes 65568 | tf_op jit(solution)/shard_map/ppermute | solution.py:865
  47.8 1.5 %collective-permute-start.22 = (f32[2,48,128]{2,1,0:T(8,128)S(1)}, f32[2,48,128]{2,1,0:T(8,128)S(1)}, u32[]{:S(2)}, u32[]{:S(2)}) collective-permute-start(f32[2,48,128]{2,1,0:T(8,128)S(1)} %get-tuple-element.116), channel_id=1, source_target_pairs={{0,1},{1,0},{2,3},{3,2},{4,5},{5,4},{6,7},{7,6},{8,9},{9,8},{10,11... | collective-permute-start | bytes 147464 | tf_op jit(solution)/shard_map/ppermute | solution.py:873
  49.2 3.5 %collective-permute-done.23 = f32[1,128]{1,0:T(1,128)S(1)} collective-permute-done((f32[1,128]{1,0:T(1,128)S(1)}, f32[1,128]{1,0:T(1,128)S(1)}, u32[]{:S(2)}, u32[]{:S(2)}) %collective-permute-start.23) | collective-permute-done | bytes 544 | tf_op jit(solution)/shard_map/ppermute | solution.py:898
  52.8 1.3 %shard_map.131 = (f32[10,144,128]{2,1,0:T(8,128)S(1)}, f32[6,112,128]{2,1,0:T(8,128)S(1)}, f32[4,144,128]{2,1,0:T(8,128)S(1)}, f32[144,128]{1,0:T(8,128)S(1)}, f...) custom-call(f32[8,64,128]{2,1,0:T(8,128)S(1)} %get-tuple-element.110.g_ref, f32[128,128]{1,0:T(8,128)S(1)} %collective-permute-done.17.out_ref, ...), custom_call_target="tpu_custom_call" | custom-call | tf_op jit(solution)/shard_map/pallas_call | solution.py:851
  55.6 3.1 %collective-permute-done.27 = f32[32,128]{1,0:T(8,128)S(1)} collective-permute-done((f32[32,128]{1,0:T(8,128)S(1)}, f32[32,128]{1,0:T(8,128)S(1)}, u32[]{:S(2)}, u32[]{:S(2)}) %collective-permute-start.27) | collective-permute-done | bytes 16416 | tf_op jit(solution)/shard_map/ppermute | solution.py:898
  58.8 1.9 %collective-permute-done.24.out_ref = f32[144,128]{1,0:T(8,128)S(1)} collective-permute-done((f32[144,128]{1,0:T(8,128)S(1)}, f32[144,128]{1,0:T(8,128)S(1)}, u32[]{:S(2)}, u32[]{:S(2)}) %collective-permute-start.24) | collective-permute-done | bytes 73760 | tf_op jit(solution)/shard_map/ppermute | solution.py:865
  61.4 1.4 %collective-permute-start.29 = (f32[1,128]{1,0:T(1,128)S(1)}, f32[1,128]{1,0:T(1,128)S(1)}, u32[]{:S(2)}, u32[]{:S(2)}) collective-permute-start(f32[1,128]{1,0:T(1,128)S(1)} %get-tuple-element.127), channel_id=1, source_target_pairs={{0,1},{1,0},{2,3},{3,2},{4,5},{5,4},{6,7},{7,6},{8,9},{9,8},{10,11... | collective-permute-start | bytes 1544 | tf_op jit(solution)/shard_map/ppermute | solution.py:898
  62.8 2.2 %collective-permute-done.29 = f32[1,128]{1,0:T(1,128)S(1)} collective-permute-done((f32[1,128]{1,0:T(1,128)S(1)}, f32[1,128]{1,0:T(1,128)S(1)}, u32[]{:S(2)}, u32[]{:S(2)}) %collective-permute-start.29) | collective-permute-done | bytes 544 | tf_op jit(solution)/shard_map/ppermute | solution.py:898
  66.3 1.4 %collective-permute-start.32 = (f32[2,96,128]{2,1,0:T(8,128)S(1)}, f32[2,96,128]{2,1,0:T(8,128)S(1)}, u32[]{:S(2)}, u32[]{:S(2)}) collective-permute-start(f32[2,96,128]{2,1,0:T(8,128)S(1)} %get-tuple-element.136), channel_id=1, source_target_pairs={{0,1},{1,0},{2,3},{3,2},{4,5},{5,4},{6,7},{7,6},{8,9},{9,8},{10,11... | collective-permute-start | bytes 294920 | tf_op jit(solution)/shard_map/ppermute | solution.py:873
  68.4 3.7 %collective-permute-done.30.out_ref = f32[128,128]{1,0:T(8,128)S(1)} collective-permute-done((f32[128,128]{1,0:T(8,128)S(1)}, f32[128,128]{1,0:T(8,128)S(1)}, u32[]{:S(2)}, u32[]{:S(2)}) %collective-permute-start.30) | collective-permute-done | bytes 65568 | tf_op jit(solution)/shard_map/ppermute | solution.py:865
  72.1 1.4 %collective-permute-start.33 = (f32[2,48,128]{2,1,0:T(8,128)S(1)}, f32[2,48,128]{2,1,0:T(8,128)S(1)}, u32[]{:S(2)}, u32[]{:S(2)}) collective-permute-start(f32[2,48,128]{2,1,0:T(8,128)S(1)} %get-tuple-element.143), channel_id=1, source_target_pairs={{0,1},{1,0},{2,3},{3,2},{4,5},{5,4},{6,7},{7,6},{8,9},{9,8},{10,11... | collective-permute-start | bytes 147464 | tf_op jit(solution)/shard_map/ppermute | solution.py:873
  73.5 2.8 %collective-permute-done.33.late_ref = f32[2,48,128]{2,1,0:T(8,128)S(1)} collective-permute-done((f32[2,48,128]{2,1,0:T(8,128)S(1)}, f32[2,48,128]{2,1,0:T(8,128)S(1)}, u32[]{:S(2)}, u32[]{:S(2)}) %collective-permute-start.33) | collective-permute-done | bytes 49184 | tf_op jit(solution)/shard_map/ppermute | solution.py:873
  78.2 1.4 %collective-permute-start.36 = (f32[2,80,128]{2,1,0:T(8,128)S(1)}, f32[2,80,128]{2,1,0:T(8,128)S(1)}, u32[]{:S(2)}, u32[]{:S(2)}) collective-permute-start(f32[2,80,128]{2,1,0:T(8,128)S(1)} %get-tuple-element.150), channel_id=1, source_target_pairs={{0,1},{1,0},{2,3},{3,2},{4,5},{5,4},{6,7},{7,6},{8,9},{9,8},{10,11... | collective-permute-start | bytes 245768 | tf_op jit(solution)/shard_map/ppermute | solution.py:873
  80.2 3.9 %collective-permute-done.34.out_ref = f32[144,128]{1,0:T(8,128)S(1)} collective-permute-done((f32[144,128]{1,0:T(8,128)S(1)}, f32[144,128]{1,0:T(8,128)S(1)}, u32[]{:S(2)}, u32[]{:S(2)}) %collective-permute-start.34) | collective-permute-done | bytes 73760 | tf_op jit(solution)/shard_map/ppermute | solution.py:865
  84.1 1.4 %collective-permute-start.37 = (f32[2,48,128]{2,1,0:T(8,128)S(1)}, f32[2,48,128]{2,1,0:T(8,128)S(1)}, u32[]{:S(2)}, u32[]{:S(2)}) collective-permute-start(f32[2,48,128]{2,1,0:T(8,128)S(1)} %get-tuple-element.157), channel_id=1, source_target_pairs={{0,1},{1,0},{2,3},{3,2},{4,5},{5,4},{6,7},{7,6},{8,9},{9,8},{10,11... | collective-permute-start | bytes 147464 | tf_op jit(solution)/shard_map/ppermute | solution.py:873
  85.5 8.9 %all_to_all.8 = f32[32,1,128]{2,1,0:T(1,128)S(1)} all-to-all(f32[32,1,128]{2,1,0:T(1,128)S(1)} %broadcast_in_dim.2), channel_id=1, replica_groups=mesh['axial'=16,'azim'=2] {'axial','azim'}, dimensions={0} | all-to-all | bytes 32768 | tf_op jit(solution)/shard_map/all_to_all | solution.py:903
  (97 shorter events, 18.3 us)
Async XLA Ops:
  2.8 7.8 %collective-permute-start.1 = (f32[200,128]{1,0:T(8,128)S(1)}, f32[200,128]{1,0:T(8,128)S(1)}, u32[]{:S(2)}, u32[]{:S(2)}) collective-permute-start(f32[200,128]{1,0:T(8,128)S(1)} %get-tuple-element.85), channel_id=1, source_target_pairs={{2,4},{6,8},{10,12},{14,16},{18,20},{22,24},{26,28},{30,0},{4,2},{... | collective-permute-start | bytes 307208 | tf_op jit(solution)/shard_map/ppermute | solution.py:865
  8.3 6.6 %collective-permute-start = (f32[2,144,128]{2,1,0:T(8,128)S(1)}, f32[2,144,128]{2,1,0:T(8,128)S(1)}, u32[]{:S(2)}, u32[]{:S(2)}) collective-permute-start(f32[2,144,128]{2,1,0:T(8,128)S(1)} %get-tuple-element.83), channel_id=1, source_target_pairs={{0,1},{1,0},{2,3},{3,2},{4,5},{5,4},{6,7},{7,6},{8,9},{9,8},{10,11... | collective-permute-start | bytes 442376 | tf_op jit(solution)/shard_map/ppermute | solution.py:873
  10.7 5.1 %collective-permute-start.3 = (f32[2,56,128]{2,1,0:T(8,128)S(1)}, f32[2,56,128]{2,1,0:T(8,128)S(1)}, u32[]{:S(2)}, u32[]{:S(2)}) collective-permute-start(f32[2,56,128]{2,1,0:T(8,128)S(1)} %shard_map.122), channel_id=1, source_target_pairs={{0,1},{1,0},{2,3},{3,2},{4,5},{5,4},{6,7},{7,6},{8,9},{9,8},{10,11... | collective-permute-start | bytes 172040 | tf_op jit(solution)/shard_map/ppermute | solution.py:873
  16.3 4.1 %collective-permute-start.7 = (f32[32,128]{1,0:T(8,128)S(1)}, f32[32,128]{1,0:T(8,128)S(1)}, u32[]{:S(2)}, u32[]{:S(2)}) collective-permute-start(f32[32,128]{1,0:T(8,128)S(1)} %get-tuple-element.94), channel_id=1, source_target_pairs={{0,4},{1,5},{2,6},{3,7},{4,0},{5,1},{6,2},{7,3},{8,12},{9,13},{10,... | collective-permute-start | bytes 49160 | tf_op jit(solution)/shard_map/ppermute | solution.py:898
  16.4 6.5 %collective-permute-start.4 = (f32[128,128]{1,0:T(8,128)S(1)}, f32[128,128]{1,0:T(8,128)S(1)}, u32[]{:S(2)}, u32[]{:S(2)}) collective-permute-start(f32[128,128]{1,0:T(8,128)S(1)} %get-tuple-element.90), channel_id=1, source_target_pairs={{2,4},{6,8},{10,12},{14,16},{18,20},{22,24},{26,28},{30,0},{4,2},{... | collective-permute-start | bytes 196616 | tf_op jit(solution)/shard_map/ppermute | solution.py:865
  18.9 4.0 %collective-permute-start.5 = (f32[128,128]{1,0:T(8,128)S(1)}, f32[128,128]{1,0:T(8,128)S(1)}, u32[]{:S(2)}, u32[]{:S(2)}) collective-permute-start(f32[128,128]{1,0:T(8,128)S(1)} %get-tuple-element.91), channel_id=1, source_target_pairs={{0,2},{2,0},{4,6},{6,4},{8,10},{10,8},{12,14},{14,12},{16,18},{18,... | collective-permute-start | bytes 196616 | tf_op jit(solution)/shard_map/ppermute | solution.py:866
  18.9 9.1 %collective-permute-start.6 = (f32[2,96,128]{2,1,0:T(8,128)S(1)}, f32[2,96,128]{2,1,0:T(8,128)S(1)}, u32[]{:S(2)}, u32[]{:S(2)}) collective-permute-start(f32[2,96,128]{2,1,0:T(8,128)S(1)} %get-tuple-element.92), channel_id=1, source_target_pairs={{0,1},{1,0},{2,3},{3,2},{4,5},{5,4},{6,7},{7,6},{8,9},{9,8},{10,11... | collective-permute-start | bytes 294920 | tf_op jit(solution)/shard_map/ppermute | solution.py:873
  22.9 5.1 %collective-permute-start.9 = (f32[2,48,128]{2,1,0:T(8,128)S(1)}, f32[2,48,128]{2,1,0:T(8,128)S(1)}, u32[]{:S(2)}, u32[]{:S(2)}) collective-permute-start(f32[2,48,128]{2,1,0:T(8,128)S(1)} %get-tuple-element.95), channel_id=1, source_target_pairs={{0,1},{1,0},{2,3},{3,2},{4,5},{5,4},{6,7},{7,6},{8,9},{9,8},{10,11... | collective-permute-start | bytes 147464 | tf_op jit(solution)/shard_map/ppermute | solution.py:873
  29.3 4.7 %collective-permute-start.14 = (f32[32,128]{1,0:T(8,128)S(1)}, f32[32,128]{1,0:T(8,128)S(1)}, u32[]{:S(2)}, u32[]{:S(2)}) collective-permute-start(f32[32,128]{1,0:T(8,128)S(1)} %get-tuple-element.104), channel_id=1, source_target_pairs={{0,16},{1,17},{2,18},{3,19},{4,20},{5,21},{6,22},{7,23},{8,24},{9,... | collective-permute-start | bytes 49160 | tf_op jit(solution)/shard_map/ppermute | solution.py:898
  29.6 6.5 %collective-permute-start.11 = (f32[144,128]{1,0:T(8,128)S(1)}, f32[144,128]{1,0:T(8,128)S(1)}, u32[]{:S(2)}, u32[]{:S(2)}) collective-permute-start(f32[144,128]{1,0:T(8,128)S(1)} %get-tuple-element.100), channel_id=1, source_target_pairs={{2,4},{6,8},{10,12},{14,16},{18,20},{22,24},{26,28},{30,0},{4,2},{... | collective-permute-start | bytes 221192 | tf_op jit(solution)/shard_map/ppermute | solution.py:865
  30.5 5.6 %collective-permute-start.12 = (f32[144,128]{1,0:T(8,128)S(1)}, f32[144,128]{1,0:T(8,128)S(1)}, u32[]{:S(2)}, u32[]{:S(2)}) collective-permute-start(f32[144,128]{1,0:T(8,128)S(1)} %get-tuple-element.101), channel_id=1, source_target_pairs={{0,2},{2,0},{4,6},{6,4},{8,10},{10,8},{12,14},{14,12},{16,18},{18,... | collective-permute-start | bytes 221192 | tf_op jit(solution)/shard_map/ppermute | solution.py:866
  31.4 8.9 %collective-permute-start.13 = (f32[2,80,128]{2,1,0:T(8,128)S(1)}, f32[2,80,128]{2,1,0:T(8,128)S(1)}, u32[]{:S(2)}, u32[]{:S(2)}) collective-permute-start(f32[2,80,128]{2,1,0:T(8,128)S(1)} %get-tuple-element.102), channel_id=1, source_target_pairs={{0,1},{1,0},{2,3},{3,2},{4,5},{5,4},{6,7},{7,6},{8,9},{9,8},{10,11... | collective-permute-start | bytes 245768 | tf_op jit(solution)/shard_map/ppermute | solution.py:873
  36.1 4.2 %collective-permute-start.15 = (f32[2,48,128]{2,1,0:T(8,128)S(1)}, f32[2,48,128]{2,1,0:T(8,128)S(1)}, u32[]{:S(2)}, u32[]{:S(2)}) collective-permute-start(f32[2,48,128]{2,1,0:T(8,128)S(1)} %get-tuple-element.105), channel_id=1, source_target_pairs={{0,1},{1,0},{2,3},{3,2},{4,5},{5,4},{6,7},{7,6},{8,9},{9,8},{10,11... | collective-permute-start | bytes 147464 | tf_op jit(solution)/shard_map/ppermute | solution.py:873
  36.7 3.6 %collective-permute-start.16 = (f32[1,128]{1,0:T(1,128)S(1)}, f32[1,128]{1,0:T(1,128)S(1)}, u32[]{:S(2)}, u32[]{:S(2)}) collective-permute-start(f32[1,128]{1,0:T(1,128)S(1)} %get-tuple-element.107), channel_id=1, source_target_pairs={{0,1},{1,0},{2,3},{3,2},{4,5},{5,4},{6,7},{7,6},{8,9},{9,8},{10,11... | collective-permute-start | bytes 1544 | tf_op jit(solution)/shard_map/ppermute | solution.py:898
  41.2 3.8 %collective-permute-start.20 = (f32[32,128]{1,0:T(8,128)S(1)}, f32[32,128]{1,0:T(8,128)S(1)}, u32[]{:S(2)}, u32[]{:S(2)}) collective-permute-start(f32[32,128]{1,0:T(8,128)S(1)} %get-tuple-element.115), channel_id=1, source_target_pairs={{0,4},{1,5},{2,6},{3,7},{4,0},{5,1},{6,2},{7,3},{8,12},{9,13},{10,... | collective-permute-start | bytes 49160 | tf_op jit(solution)/shard_map/ppermute | solution.py:898
  41.3 6.5 %collective-permute-start.17 = (f32[128,128]{1,0:T(8,128)S(1)}, f32[128,128]{1,0:T(8,128)S(1)}, u32[]{:S(2)}, u32[]{:S(2)}) collective-permute-start(f32[128,128]{1,0:T(8,128)S(1)} %get-tuple-element.111), channel_id=1, source_target_pairs={{2,4},{6,8},{10,12},{14,16},{18,20},{22,24},{26,28},{30,0},{4,2},{... | collective-permute-start | bytes 196616 | tf_op jit(solution)/shard_map/ppermute | solution.py:865
  41.4 6.4 %collective-permute-start.18 = (f32[128,128]{1,0:T(8,128)S(1)}, f32[128,128]{1,0:T(8,128)S(1)}, u32[]{:S(2)}, u32[]{:S(2)}) collective-permute-start(f32[128,128]{1,0:T(8,128)S(1)} %get-tuple-element.112), channel_id=1, source_target_pairs={{0,2},{2,0},{4,6},{6,4},{8,10},{10,8},{12,14},{14,12},{16,18},{18,... | collective-permute-start | bytes 196616 | tf_op jit(solution)/shard_map/ppermute | solution.py:866
  43.4 9.4 %collective-permute-start.19 = (f32[2,96,128]{2,1,0:T(8,128)S(1)}, f32[2,96,128]{2,1,0:T(8,128)S(1)}, u32[]{:S(2)}, u32[]{:S(2)}) collective-permute-start(f32[2,96,128]{2,1,0:T(8,128)S(1)} %get-tuple-element.113), channel_id=1, source_target_pairs={{0,1},{1,0},{2,3},{3,2},{4,5},{5,4},{6,7},{7,6},{8,9},{9,8},{10,11... | collective-permute-start | bytes 294920 | tf_op jit(solution)/shard_map/ppermute | solution.py:873
  47.8 5.0 %collective-permute-start.22 = (f32[2,48,128]{2,1,0:T(8,128)S(1)}, f32[2,48,128]{2,1,0:T(8,128)S(1)}, u32[]{:S(2)}, u32[]{:S(2)}) collective-permute-start(f32[2,48,128]{2,1,0:T(8,128)S(1)} %get-tuple-element.116), channel_id=1, source_target_pairs={{0,1},{1,0},{2,3},{3,2},{4,5},{5,4},{6,7},{7,6},{8,9},{9,8},{10,11... | collective-permute-start | bytes 147464 | tf_op jit(solution)/shard_map/ppermute | solution.py:873
  54.1 4.7 %collective-permute-start.27 = (f32[32,128]{1,0:T(8,128)S(1)}, f32[32,128]{1,0:T(8,128)S(1)}, u32[]{:S(2)}, u32[]{:S(2)}) collective-permute-start(f32[32,128]{1,0:T(8,128)S(1)} %get-tuple-element.125), channel_id=1, source_target_pairs={{0,16},{1,17},{2,18},{3,19},{4,20},{5,21},{6,22},{7,23},{8,24},{9,... | collective-permute-start | bytes 49160 | tf_op jit(solution)/shard_map/ppermute | solution.py:898
  54.1 6.5 %collective-permute-start.24 = (f32[144,128]{1,0:T(8,128)S(1)}, f32[144,128]{1,0:T(8,128)S(1)}, u32[]{:S(2)}, u32[]{:S(2)}) collective-permute-start(f32[144,128]{1,0:T(8,128)S(1)} %get-tuple-element.121), channel_id=1, source_target_pairs={{2,4},{6,8},{10,12},{14,16},{18,20},{22,24},{26,28},{30,0},{4,2},{... | collective-permute-start | bytes 221192 | tf_op jit(solution)/shard_map/ppermute | solution.py:865
  54.2 6.5 %collective-permute-start.25 = (f32[144,128]{1,0:T(8,128)S(1)}, f32[144,128]{1,0:T(8,128)S(1)}, u32[]{:S(2)}, u32[]{:S(2)}) collective-permute-start(f32[144,128]{1,0:T(8,128)S(1)} %get-tuple-element.122), channel_id=1, source_target_pairs={{0,2},{2,0},{4,6},{6,4},{8,10},{10,8},{12,14},{14,12},{16,18},{18,... | collective-permute-start | bytes 221192 | tf_op jit(solution)/shard_map/ppermute | solution.py:866
  54.9 10.1 %collective-permute-start.26 = (f32[2,80,128]{2,1,0:T(8,128)S(1)}, f32[2,80,128]{2,1,0:T(8,128)S(1)}, u32[]{:S(2)}, u32[]{:S(2)}) collective-permute-start(f32[2,80,128]{2,1,0:T(8,128)S(1)} %get-tuple-element.123), channel_id=1, source_target_pairs={{0,1},{1,0},{2,3},{3,2},{4,5},{5,4},{6,7},{7,6},{8,9},{9,8},{10,11... | collective-permute-start | bytes 245768 | tf_op jit(solution)/shard_map/ppermute | solution.py:873
  60.7 4.3 %collective-permute-start.28 = (f32[2,48,128]{2,1,0:T(8,128)S(1)}, f32[2,48,128]{2,1,0:T(8,128)S(1)}, u32[]{:S(2)}, u32[]{:S(2)}) collective-permute-start(f32[2,48,128]{2,1,0:T(8,128)S(1)} %get-tuple-element.126), channel_id=1, source_target_pairs={{0,1},{1,0},{2,3},{3,2},{4,5},{5,4},{6,7},{7,6},{8,9},{9,8},{10,11... | collective-permute-start | bytes 147464 | tf_op jit(solution)/shard_map/ppermute | solution.py:873
  65.7 6.5 %collective-permute-start.30 = (f32[128,128]{1,0:T(8,128)S(1)}, f32[128,128]{1,0:T(8,128)S(1)}, u32[]{:S(2)}, u32[]{:S(2)}) collective-permute-start(f32[128,128]{1,0:T(8,128)S(1)} %get-tuple-element.134), channel_id=1, source_target_pairs={{2,4},{6,8},{10,12},{14,16},{18,20},{22,24},{26,28},{30,0},{4,2},{... | collective-permute-start | bytes 196616 | tf_op jit(solution)/shard_map/ppermute | solution.py:865
  65.8 6.4 %collective-permute-start.31 = (f32[128,128]{1,0:T(8,128)S(1)}, f32[128,128]{1,0:T(8,128)S(1)}, u32[]{:S(2)}, u32[]{:S(2)}) collective-permute-start(f32[128,128]{1,0:T(8,128)S(1)} %get-tuple-element.135), channel_id=1, source_target_pairs={{0,2},{2,0},{4,6},{6,4},{8,10},{10,8},{12,14},{14,12},{16,18},{18,... | collective-permute-start | bytes 196616 | tf_op jit(solution)/shard_map/ppermute | solution.py:866
  66.3 7.2 %collective-permute-start.32 = (f32[2,96,128]{2,1,0:T(8,128)S(1)}, f32[2,96,128]{2,1,0:T(8,128)S(1)}, u32[]{:S(2)}, u32[]{:S(2)}) collective-permute-start(f32[2,96,128]{2,1,0:T(8,128)S(1)} %get-tuple-element.136), channel_id=1, source_target_pairs={{0,1},{1,0},{2,3},{3,2},{4,5},{5,4},{6,7},{7,6},{8,9},{9,8},{10,11... | collective-permute-start | bytes 294920 | tf_op jit(solution)/shard_map/ppermute | solution.py:873
  72.1 4.2 %collective-permute-start.33 = (f32[2,48,128]{2,1,0:T(8,128)S(1)}, f32[2,48,128]{2,1,0:T(8,128)S(1)}, u32[]{:S(2)}, u32[]{:S(2)}) collective-permute-start(f32[2,48,128]{2,1,0:T(8,128)S(1)} %get-tuple-element.143), channel_id=1, source_target_pairs={{0,1},{1,0},{2,3},{3,2},{4,5},{5,4},{6,7},{7,6},{8,9},{9,8},{10,11... | collective-permute-start | bytes 147464 | tf_op jit(solution)/shard_map/ppermute | solution.py:873
  77.6 6.5 %collective-permute-start.34 = (f32[144,128]{1,0:T(8,128)S(1)}, f32[144,128]{1,0:T(8,128)S(1)}, u32[]{:S(2)}, u32[]{:S(2)}) collective-permute-start(f32[144,128]{1,0:T(8,128)S(1)} %get-tuple-element.148), channel_id=1, source_target_pairs={{2,4},{6,8},{10,12},{14,16},{18,20},{22,24},{26,28},{30,0},{4,2},{... | collective-permute-start | bytes 221192 | tf_op jit(solution)/shard_map/ppermute | solution.py:865
  77.6 6.5 %collective-permute-start.35 = (f32[144,128]{1,0:T(8,128)S(1)}, f32[144,128]{1,0:T(8,128)S(1)}, u32[]{:S(2)}, u32[]{:S(2)}) collective-permute-start(f32[144,128]{1,0:T(8,128)S(1)} %get-tuple-element.149), channel_id=1, source_target_pairs={{0,2},{2,0},{4,6},{6,4},{8,10},{10,8},{12,14},{14,12},{16,18},{18,... | collective-permute-start | bytes 221192 | tf_op jit(solution)/shard_map/ppermute | solution.py:866
  78.2 16.2 %collective-permute-start.36 = (f32[2,80,128]{2,1,0:T(8,128)S(1)}, f32[2,80,128]{2,1,0:T(8,128)S(1)}, u32[]{:S(2)}, u32[]{:S(2)}) collective-permute-start(f32[2,80,128]{2,1,0:T(8,128)S(1)} %get-tuple-element.150), channel_id=1, source_target_pairs={{0,1},{1,0},{2,3},{3,2},{4,5},{5,4},{6,7},{7,6},{8,9},{9,8},{10,11... | collective-permute-start | bytes 245768 | tf_op jit(solution)/shard_map/ppermute | solution.py:873
  84.1 10.3 %collective-permute-start.37 = (f32[2,48,128]{2,1,0:T(8,128)S(1)}, f32[2,48,128]{2,1,0:T(8,128)S(1)}, u32[]{:S(2)}, u32[]{:S(2)}) collective-permute-start(f32[2,48,128]{2,1,0:T(8,128)S(1)} %get-tuple-element.157), channel_id=1, source_target_pairs={{0,1},{1,0},{2,3},{3,2},{4,5},{5,4},{6,7},{7,6},{8,9},{9,8},{10,11... | collective-permute-start | bytes 147464 | tf_op jit(solution)/shard_map/ppermute | solution.py:873
  (15 other events, 67.6 us)

commit v7 on v6

--- a/solution.py
+++ b/solution.py
@@ -606,6 +606,11 @@
         send_ref[side, 40:48] = late_ref[side, 40:48] + after(128 + 8 * side, 8)
 
 
+def last_side_kernel(out_ref, in_ref, late_ref, row_ref, bulk_ref, send_ref, pass_ref):
+    send_ref[:, 48:] = bulk_ref[...]
+    solved_side_kernel(out_ref, in_ref, late_ref, row_ref, send_ref, pass_ref)
+
+
 def got_solved(part_ref, in_ref, out_ref, early_ref, late_ref):
     before, after = got_axial(in_ref, out_ref)
     extra = {0: (before, 0), 1: (before, 64), 6: (after, 64), 7: (after, 0)}
@@ -808,7 +813,7 @@
 
 
 def last_kernel(
-    part_ref, out_ref, in_ref, early_ref, late_ref, near_ref, sums_ref, old_sums_ref, row_ref, _,
+    part_ref, out_ref, in_ref, late_ref, near_ref, sums_ref, old_sums_ref, row_ref, _,
     y_ref, z0_ref, z1_ref, planes_r_ref, planes_q_ref, planes_w_ref,
     pressure_ref, residual_ref, direction_ref,
 ):
@@ -833,7 +838,7 @@
         + norm(row_r)
     )
     beta1 = rz2 / rz1
-    change = got_solved(part_ref, in_ref, out_ref, early_ref, late_ref)
+    change = got_solved(part_ref, in_ref, out_ref, late_ref.at[:, 48:], late_ref)
     change = add_coarse(change, row_w, near_ref)
     for a in range(8):
         first = z0_ref[a]
@@ -1006,7 +1011,12 @@
         second_dots_kernel, [one], pay[:1], planes_r, planes_q, planes_w, solved_r, solved_q, solved_w
     )
     gathered = gather_sums(jnp.broadcast_to(pay, sums))
-    *moved, passed = exchange(solved_side_kernel, 48, sends, pay, one)
+    send_out, send_early, send_in, send_late = sends
+    inner, outer = axial_swap(send_in, send_out)
+    late, passed = kernel_call(
+        last_side_kernel, [(2, 128, LANES), one], outer, inner, send_late, pay, send_early
+    )
+    moved = outer, inner, azim_swap(late)
     pressure, residual, direction = kernel_call(
         last_kernel,
         [field, field, field],

time: 95.8 us -> 95.7 us (level)
  waiting for transfers between devices: 39.8 us -> 41.2 us
  starting transfers between devices: 33.3 us -> 31.9 us
    ppermute x14 -> x13, starting transfers between devices: 17.7 us -> 16.3 us  [azim_swap(): return lax.ppermute(sides, 'azim', [(0, 1), (1, 0)])]
    ppermute x7, waiting for transfers between devices: 15.3 us -> 16.7 us  [axial_swap(): from_outer = lax.ppermute(outer_rows, 'axial', outer)]
    ppermute x14 -> x13, waiting for transfers between devices: 5.83 us -> 5.82 us  [azim_swap(): return lax.ppermute(sides, 'azim', [(0, 1), (1, 0)])]
  transfers between devices with their start and end apart: 38 -> 37, of which waited for: 19 -> 19; matrix products, arithmetic and copies ran while one was open for 0% -> 0% of each run, Pallas kernels for 4% -> 4%
where the time goes in v7:
time: 95.7 us; the launch traced here: 95.6 us
  waiting for transfers between devices  41.2 us (43%)
  starting transfers between devices  31.9 us (33%)
  Pallas kernels  12.6 us (13%)
  blocking collectives  8.89 us (9%)
  between operations  0.98 us (1%)
    ppermute x10, waiting for transfers between devices, partial_sum(): lax.ppermute(row, ALL, [(i, i ^ step) for i in range(count)])[:1]  18.6 us
    ppermute x7, waiting for transfers between devices, axial_swap(): from_outer = lax.ppermute(outer_rows, 'axial', outer)  16.7 us
    ppermute x13, starting transfers between devices, azim_swap(): return lax.ppermute(sides, 'azim', [(0, 1), (1, 0)])  16.3 us
    pallas_call x22, Pallas kernels, kernel_call(): pl.pallas_call(kernel, out_shape=outs, compiler_params=pltpu.CompilerPara...  12.6 us
    ppermute x7, starting transfers between devices, axial_swap(): from_outer = lax.ppermute(outer_rows, 'axial', outer)  9.12 us
    all_to_all x1, blocking collectives, gather_sums(): return lax.all_to_all(rows, ALL, 0, 0, tiled=True)  8.89 us
    ppermute x13, waiting for transfers between devices, azim_swap(): return lax.ppermute(sides, 'azim', [(0, 1), (1, 0)])  5.82 us
    ppermute x10, starting transfers between devices, partial_sum(): lax.ppermute(row, ALL, [(i, i ^ step) for i in range(count)])[:1]  3.66 us
  transfers between devices with their start and end apart: 37, of which 19 were waited for; matrix products, arithmetic and copies ran while one was open for 0% of the time, Pallas kernels for 4%

profile of v7, /device:TPU:0, one launch (start us, length us, event | category | flops | bytes accessed | tf_op | source)
XLA Modules:
  0.0 95.6 jit_solution(3843858586963238107)
XLA Ops:
  0.6 2.1 %shard_map.121 = (f32[3,8,64,128]{3,2,1,0:T(8,128)S(1)}, f32[8,128]{1,0:T(8,128)S(1)}, f32[200,128]{1,0:T(8,128)S(1)}, f32[2,144,128]{2,1,0:T(8,128)S(1)}, f32[2...) custom-call(f32[3,8,64,128]{3,2,1,0:T(8,128)} %bitcast.17, f32[1,32]{1,0:T(1,128)} %row_hbm.1, ...), custom_call_target="tpu_custom_call" | custom-call | tf_op jit(solution)/shard_map/pallas_call | solution.py:856
  2.8 5.5 %collective-permute-start.1 = (f32[200,128]{1,0:T(8,128)S(1)}, f32[200,128]{1,0:T(8,128)S(1)}, u32[]{:S(2)}, u32[]{:S(2)}) collective-permute-start(f32[200,128]{1,0:T(8,128)S(1)} %get-tuple-element.85), channel_id=1, source_target_pairs={{2,4},{6,8},{10,12},{14,16},{18,20},{22,24},{26,28},{30,0},{4,2},{... | collective-permute-start | bytes 307208 | tf_op jit(solution)/shard_map/ppermute | solution.py:870
  8.3 1.5 %collective-permute-start = (f32[2,144,128]{2,1,0:T(8,128)S(1)}, f32[2,144,128]{2,1,0:T(8,128)S(1)}, u32[]{:S(2)}, u32[]{:S(2)}) collective-permute-start(f32[2,144,128]{2,1,0:T(8,128)S(1)} %get-tuple-element.83), channel_id=1, source_target_pairs={{0,1},{1,0},{2,3},{3,2},{4,5},{5,4},{6,7},{7,6},{8,9},{9,8},{10,11... | collective-permute-start | bytes 442376 | tf_op jit(solution)/shard_map/ppermute | solution.py:878
  10.7 2.1 %collective-permute-start.3 = (f32[2,56,128]{2,1,0:T(8,128)S(1)}, f32[2,56,128]{2,1,0:T(8,128)S(1)}, u32[]{:S(2)}, u32[]{:S(2)}) collective-permute-start(f32[2,56,128]{2,1,0:T(8,128)S(1)} %shard_map.122), channel_id=1, source_target_pairs={{0,1},{1,0},{2,3},{3,2},{4,5},{5,4},{6,7},{7,6},{8,9},{9,8},{10,11... | collective-permute-start | bytes 172040 | tf_op jit(solution)/shard_map/ppermute | solution.py:878
  12.7 2.2 %collective-permute-done.early_ref = f32[2,144,128]{2,1,0:T(8,128)S(1)} collective-permute-done((f32[2,144,128]{2,1,0:T(8,128)S(1)}, f32[2,144,128]{2,1,0:T(8,128)S(1)}, u32[]{:S(2)}, u32[]{:S(2)}) %collective-permute-start) | collective-permute-done | bytes 147488 | tf_op jit(solution)/shard_map/ppermute | solution.py:878
  16.4 2.5 %collective-permute-start.4 = (f32[128,128]{1,0:T(8,128)S(1)}, f32[128,128]{1,0:T(8,128)S(1)}, u32[]{:S(2)}, u32[]{:S(2)}) collective-permute-start(f32[128,128]{1,0:T(8,128)S(1)} %get-tuple-element.90), channel_id=1, source_target_pairs={{2,4},{6,8},{10,12},{14,16},{18,20},{22,24},{26,28},{30,0},{4,2},{... | collective-permute-start | bytes 196616 | tf_op jit(solution)/shard_map/ppermute | solution.py:870
  18.9 1.5 %collective-permute-start.6 = (f32[2,96,128]{2,1,0:T(8,128)S(1)}, f32[2,96,128]{2,1,0:T(8,128)S(1)}, u32[]{:S(2)}, u32[]{:S(2)}) collective-permute-start(f32[2,96,128]{2,1,0:T(8,128)S(1)} %get-tuple-element.92), channel_id=1, source_target_pairs={{0,1},{1,0},{2,3},{3,2},{4,5},{5,4},{6,7},{7,6},{8,9},{9,8},{10,11... | collective-permute-start | bytes 294920 | tf_op jit(solution)/shard_map/ppermute | solution.py:878
  21.6 1.3 %collective-permute-done.4.out_ref = f32[128,128]{1,0:T(8,128)S(1)} collective-permute-done((f32[128,128]{1,0:T(8,128)S(1)}, f32[128,128]{1,0:T(8,128)S(1)}, u32[]{:S(2)}, u32[]{:S(2)}) %collective-permute-start.4) | collective-permute-done | bytes 65568 | tf_op jit(solution)/shard_map/ppermute | solution.py:870
  22.9 1.6 %collective-permute-start.9 = (f32[2,48,128]{2,1,0:T(8,128)S(1)}, f32[2,48,128]{2,1,0:T(8,128)S(1)}, u32[]{:S(2)}, u32[]{:S(2)}) collective-permute-start(f32[2,48,128]{2,1,0:T(8,128)S(1)} %get-tuple-element.95), channel_id=1, source_target_pairs={{0,1},{1,0},{2,3},{3,2},{4,5},{5,4},{6,7},{7,6},{8,9},{9,8},{10,11... | collective-permute-start | bytes 147464 | tf_op jit(solution)/shard_map/ppermute | solution.py:878
  24.6 3.4 %collective-permute-done.10 = f32[1,128]{1,0:T(1,128)S(1)} collective-permute-done((f32[1,128]{1,0:T(1,128)S(1)}, f32[1,128]{1,0:T(1,128)S(1)}, u32[]{:S(2)}, u32[]{:S(2)}) %collective-permute-start.10) | collective-permute-done | bytes 544 | tf_op jit(solution)/shard_map/ppermute | solution.py:903
  28.1 1.3 %shard_map.126 = (f32[10,144,128]{2,1,0:T(8,128)S(1)}, f32[6,112,128]{2,1,0:T(8,128)S(1)}, f32[4,144,128]{2,1,0:T(8,128)S(1)}, f32[144,128]{1,0:T(8,128)S(1)}, f...) custom-call(f32[8,64,128]{2,1,0:T(8,128)S(1)} %get-tuple-element.89.g_ref, f32[128,128]{1,0:T(8,128)S(1)} %collective-permute-done.4.out_ref, ...), custom_call_target="tpu_custom_call" | custom-call | tf_op jit(solution)/shard_map/pallas_call | solution.py:856
  32.0 2.0 %collective-permute-done.14 = f32[32,128]{1,0:T(8,128)S(1)} collective-permute-done((f32[32,128]{1,0:T(8,128)S(1)}, f32[32,128]{1,0:T(8,128)S(1)}, u32[]{:S(2)}, u32[]{:S(2)}) %collective-permute-start.14) | collective-permute-done | bytes 16416 | tf_op jit(solution)/shard_map/ppermute | solution.py:903
  34.0 2.0 %collective-permute-done.11.out_ref = f32[144,128]{1,0:T(8,128)S(1)} collective-permute-done((f32[144,128]{1,0:T(8,128)S(1)}, f32[144,128]{1,0:T(8,128)S(1)}, u32[]{:S(2)}, u32[]{:S(2)}) %collective-permute-start.11) | collective-permute-done | bytes 73760 | tf_op jit(solution)/shard_map/ppermute | solution.py:870
  36.7 1.5 %collective-permute-start.16 = (f32[1,128]{1,0:T(1,128)S(1)}, f32[1,128]{1,0:T(1,128)S(1)}, u32[]{:S(2)}, u32[]{:S(2)}) collective-permute-start(f32[1,128]{1,0:T(1,128)S(1)} %get-tuple-element.107), channel_id=1, source_target_pairs={{0,1},{1,0},{2,3},{3,2},{4,5},{5,4},{6,7},{7,6},{8,9},{9,8},{10,11... | collective-permute-start | bytes 1544 | tf_op jit(solution)/shard_map/ppermute | solution.py:903
  38.2 2.1 %collective-permute-done.16 = f32[1,128]{1,0:T(1,128)S(1)} collective-permute-done((f32[1,128]{1,0:T(1,128)S(1)}, f32[1,128]{1,0:T(1,128)S(1)}, u32[]{:S(2)}, u32[]{:S(2)}) %collective-permute-start.16) | collective-permute-done | bytes 544 | tf_op jit(solution)/shard_map/ppermute | solution.py:903
  41.4 2.0 %collective-permute-start.18 = (f32[128,128]{1,0:T(8,128)S(1)}, f32[128,128]{1,0:T(8,128)S(1)}, u32[]{:S(2)}, u32[]{:S(2)}) collective-permute-start(f32[128,128]{1,0:T(8,128)S(1)} %get-tuple-element.112), channel_id=1, source_target_pairs={{0,2},{2,0},{4,6},{6,4},{8,10},{10,8},{12,14},{14,12},{16,18},{18,... | collective-permute-start | bytes 196616 | tf_op jit(solution)/shard_map/ppermute | solution.py:871
  43.4 1.4 %collective-permute-start.19 = (f32[2,96,128]{2,1,0:T(8,128)S(1)}, f32[2,96,128]{2,1,0:T(8,128)S(1)}, u32[]{:S(2)}, u32[]{:S(2)}) collective-permute-start(f32[2,96,128]{2,1,0:T(8,128)S(1)} %get-tuple-element.113), channel_id=1, source_target_pairs={{0,1},{1,0},{2,3},{3,2},{4,5},{5,4},{6,7},{7,6},{8,9},{9,8},{10,11... | collective-permute-start | bytes 294920 | tf_op jit(solution)/shard_map/ppermute | solution.py:878
  46.1 1.6 %collective-permute-done.17.out_ref = f32[128,128]{1,0:T(8,128)S(1)} collective-permute-done((f32[128,128]{1,0:T(8,128)S(1)}, f32[128,128]{1,0:T(8,128)S(1)}, u32[]{:S(2)}, u32[]{:S(2)}) %collective-permute-start.17) | collective-permute-done | bytes 65568 | tf_op jit(solution)/shard_map/ppermute | solution.py:870
  47.8 1.5 %collective-permute-start.22 = (f32[2,48,128]{2,1,0:T(8,128)S(1)}, f32[2,48,128]{2,1,0:T(8,128)S(1)}, u32[]{:S(2)}, u32[]{:S(2)}) collective-permute-start(f32[2,48,128]{2,1,0:T(8,128)S(1)} %get-tuple-element.116), channel_id=1, source_target_pairs={{0,1},{1,0},{2,3},{3,2},{4,5},{5,4},{6,7},{7,6},{8,9},{9,8},{10,11... | collective-permute-start | bytes 147464 | tf_op jit(solution)/shard_map/ppermute | solution.py:878
  49.2 3.5 %collective-permute-done.23 = f32[1,128]{1,0:T(1,128)S(1)} collective-permute-done((f32[1,128]{1,0:T(1,128)S(1)}, f32[1,128]{1,0:T(1,128)S(1)}, u32[]{:S(2)}, u32[]{:S(2)}) %collective-permute-start.23) | collective-permute-done | bytes 544 | tf_op jit(solution)/shard_map/ppermute | solution.py:903
  52.8 1.3 %shard_map.131 = (f32[10,144,128]{2,1,0:T(8,128)S(1)}, f32[6,112,128]{2,1,0:T(8,128)S(1)}, f32[4,144,128]{2,1,0:T(8,128)S(1)}, f32[144,128]{1,0:T(8,128)S(1)}, f...) custom-call(f32[8,64,128]{2,1,0:T(8,128)S(1)} %get-tuple-element.110.g_ref, f32[128,128]{1,0:T(8,128)S(1)} %collective-permute-done.17.out_ref, ...), custom_call_target="tpu_custom_call" | custom-call | tf_op jit(solution)/shard_map/pallas_call | solution.py:856
  55.6 3.1 %collective-permute-done.27 = f32[32,128]{1,0:T(8,128)S(1)} collective-permute-done((f32[32,128]{1,0:T(8,128)S(1)}, f32[32,128]{1,0:T(8,128)S(1)}, u32[]{:S(2)}, u32[]{:S(2)}) %collective-permute-start.27) | collective-permute-done | bytes 16416 | tf_op jit(solution)/shard_map/ppermute | solution.py:903
  58.8 1.9 %collective-permute-done.24.out_ref = f32[144,128]{1,0:T(8,128)S(1)} collective-permute-done((f32[144,128]{1,0:T(8,128)S(1)}, f32[144,128]{1,0:T(8,128)S(1)}, u32[]{:S(2)}, u32[]{:S(2)}) %collective-permute-start.24) | collective-permute-done | bytes 73760 | tf_op jit(solution)/shard_map/ppermute | solution.py:870
  61.4 1.4 %collective-permute-start.29 = (f32[1,128]{1,0:T(1,128)S(1)}, f32[1,128]{1,0:T(1,128)S(1)}, u32[]{:S(2)}, u32[]{:S(2)}) collective-permute-start(f32[1,128]{1,0:T(1,128)S(1)} %get-tuple-element.127), channel_id=1, source_target_pairs={{0,1},{1,0},{2,3},{3,2},{4,5},{5,4},{6,7},{7,6},{8,9},{9,8},{10,11... | collective-permute-start | bytes 1544 | tf_op jit(solution)/shard_map/ppermute | solution.py:903
  62.8 2.2 %collective-permute-done.29 = f32[1,128]{1,0:T(1,128)S(1)} collective-permute-done((f32[1,128]{1,0:T(1,128)S(1)}, f32[1,128]{1,0:T(1,128)S(1)}, u32[]{:S(2)}, u32[]{:S(2)}) %collective-permute-start.29) | collective-permute-done | bytes 544 | tf_op jit(solution)/shard_map/ppermute | solution.py:903
  66.3 1.4 %collective-permute-start.32 = (f32[2,96,128]{2,1,0:T(8,128)S(1)}, f32[2,96,128]{2,1,0:T(8,128)S(1)}, u32[]{:S(2)}, u32[]{:S(2)}) collective-permute-start(f32[2,96,128]{2,1,0:T(8,128)S(1)} %get-tuple-element.136), channel_id=1, source_target_pairs={{0,1},{1,0},{2,3},{3,2},{4,5},{5,4},{6,7},{7,6},{8,9},{9,8},{10,11... | collective-permute-start | bytes 294920 | tf_op jit(solution)/shard_map/ppermute | solution.py:878
  68.4 3.7 %collective-permute-done.30.out_ref = f32[128,128]{1,0:T(8,128)S(1)} collective-permute-done((f32[128,128]{1,0:T(8,128)S(1)}, f32[128,128]{1,0:T(8,128)S(1)}, u32[]{:S(2)}, u32[]{:S(2)}) %collective-permute-start.30) | collective-permute-done | bytes 65568 | tf_op jit(solution)/shard_map/ppermute | solution.py:870
  72.1 1.4 %collective-permute-start.33 = (f32[2,48,128]{2,1,0:T(8,128)S(1)}, f32[2,48,128]{2,1,0:T(8,128)S(1)}, u32[]{:S(2)}, u32[]{:S(2)}) collective-permute-start(f32[2,48,128]{2,1,0:T(8,128)S(1)} %get-tuple-element.143), channel_id=1, source_target_pairs={{0,1},{1,0},{2,3},{3,2},{4,5},{5,4},{6,7},{7,6},{8,9},{9,8},{10,11... | collective-permute-start | bytes 147464 | tf_op jit(solution)/shard_map/ppermute | solution.py:878
  73.5 2.8 %collective-permute-done.33.late_ref = f32[2,48,128]{2,1,0:T(8,128)S(1)} collective-permute-done((f32[2,48,128]{2,1,0:T(8,128)S(1)}, f32[2,48,128]{2,1,0:T(8,128)S(1)}, u32[]{:S(2)}, u32[]{:S(2)}) %collective-permute-start.33) | collective-permute-done | bytes 49184 | tf_op jit(solution)/shard_map/ppermute | solution.py:878
  78.8 5.3 %collective-permute-done.34.out_ref = f32[144,128]{1,0:T(8,128)S(1)} collective-permute-done((f32[144,128]{1,0:T(8,128)S(1)}, f32[144,128]{1,0:T(8,128)S(1)}, u32[]{:S(2)}, u32[]{:S(2)}) %collective-permute-start.34) | collective-permute-done | bytes 73760 | tf_op jit(solution)/shard_map/ppermute | solution.py:870
  84.1 1.4 %collective-permute-start.36 = (f32[2,128,128]{2,1,0:T(8,128)S(1)}, f32[2,128,128]{2,1,0:T(8,128)S(1)}, u32[]{:S(2)}, u32[]{:S(2)}) collective-permute-start(f32[2,128,128]{2,1,0:T(8,128)S(1)} %get-tuple-element.157), channel_id=1, source_target_pairs={{0,1},{1,0},{2,3},{3,2},{4,5},{5,4},{6,7},{7,6},{8,9},{9,8},{10,11... | collective-permute-start | bytes 393224 | tf_op jit(solution)/shard_map/ppermute | solution.py:878
  85.5 8.9 %all_to_all.8 = f32[32,1,128]{2,1,0:T(1,128)S(1)} all-to-all(f32[32,1,128]{2,1,0:T(1,128)S(1)} %broadcast_in_dim.2), channel_id=1, replica_groups=mesh['axial'=16,'azim'=2] {'axial','azim'}, dimensions={0} | all-to-all | bytes 32768 | tf_op jit(solution)/shard_map/all_to_all | solution.py:908
  (95 shorter events, 17.1 us)
Async XLA Ops:
  2.8 7.8 %collective-permute-start.1 = (f32[200,128]{1,0:T(8,128)S(1)}, f32[200,128]{1,0:T(8,128)S(1)}, u32[]{:S(2)}, u32[]{:S(2)}) collective-permute-start(f32[200,128]{1,0:T(8,128)S(1)} %get-tuple-element.85), channel_id=1, source_target_pairs={{2,4},{6,8},{10,12},{14,16},{18,20},{22,24},{26,28},{30,0},{4,2},{... | collective-permute-start | bytes 307208 | tf_op jit(solution)/shard_map/ppermute | solution.py:870
  8.3 6.6 %collective-permute-start = (f32[2,144,128]{2,1,0:T(8,128)S(1)}, f32[2,144,128]{2,1,0:T(8,128)S(1)}, u32[]{:S(2)}, u32[]{:S(2)}) collective-permute-start(f32[2,144,128]{2,1,0:T(8,128)S(1)} %get-tuple-element.83), channel_id=1, source_target_pairs={{0,1},{1,0},{2,3},{3,2},{4,5},{5,4},{6,7},{7,6},{8,9},{9,8},{10,11... | collective-permute-start | bytes 442376 | tf_op jit(solution)/shard_map/ppermute | solution.py:878
  10.7 5.1 %collective-permute-start.3 = (f32[2,56,128]{2,1,0:T(8,128)S(1)}, f32[2,56,128]{2,1,0:T(8,128)S(1)}, u32[]{:S(2)}, u32[]{:S(2)}) collective-permute-start(f32[2,56,128]{2,1,0:T(8,128)S(1)} %shard_map.122), channel_id=1, source_target_pairs={{0,1},{1,0},{2,3},{3,2},{4,5},{5,4},{6,7},{7,6},{8,9},{9,8},{10,11... | collective-permute-start | bytes 172040 | tf_op jit(solution)/shard_map/ppermute | solution.py:878
  16.3 4.1 %collective-permute-start.7 = (f32[32,128]{1,0:T(8,128)S(1)}, f32[32,128]{1,0:T(8,128)S(1)}, u32[]{:S(2)}, u32[]{:S(2)}) collective-permute-start(f32[32,128]{1,0:T(8,128)S(1)} %get-tuple-element.94), channel_id=1, source_target_pairs={{0,4},{1,5},{2,6},{3,7},{4,0},{5,1},{6,2},{7,3},{8,12},{9,13},{10,... | collective-permute-start | bytes 49160 | tf_op jit(solution)/shard_map/ppermute | solution.py:903
  16.4 6.5 %collective-permute-start.4 = (f32[128,128]{1,0:T(8,128)S(1)}, f32[128,128]{1,0:T(8,128)S(1)}, u32[]{:S(2)}, u32[]{:S(2)}) collective-permute-start(f32[128,128]{1,0:T(8,128)S(1)} %get-tuple-element.90), channel_id=1, source_target_pairs={{2,4},{6,8},{10,12},{14,16},{18,20},{22,24},{26,28},{30,0},{4,2},{... | collective-permute-start | bytes 196616 | tf_op jit(solution)/shard_map/ppermute | solution.py:870
  18.9 4.0 %collective-permute-start.5 = (f32[128,128]{1,0:T(8,128)S(1)}, f32[128,128]{1,0:T(8,128)S(1)}, u32[]{:S(2)}, u32[]{:S(2)}) collective-permute-start(f32[128,128]{1,0:T(8,128)S(1)} %get-tuple-element.91), channel_id=1, source_target_pairs={{0,2},{2,0},{4,6},{6,4},{8,10},{10,8},{12,14},{14,12},{16,18},{18,... | collective-permute-start | bytes 196616 | tf_op jit(solution)/shard_map/ppermute | solution.py:871
  18.9 9.1 %collective-permute-start.6 = (f32[2,96,128]{2,1,0:T(8,128)S(1)}, f32[2,96,128]{2,1,0:T(8,128)S(1)}, u32[]{:S(2)}, u32[]{:S(2)}) collective-permute-start(f32[2,96,128]{2,1,0:T(8,128)S(1)} %get-tuple-element.92), channel_id=1, source_target_pairs={{0,1},{1,0},{2,3},{3,2},{4,5},{5,4},{6,7},{7,6},{8,9},{9,8},{10,11... | collective-permute-start | bytes 294920 | tf_op jit(solution)/shard_map/ppermute | solution.py:878
  22.9 5.1 %collective-permute-start.9 = (f32[2,48,128]{2,1,0:T(8,128)S(1)}, f32[2,48,128]{2,1,0:T(8,128)S(1)}, u32[]{:S(2)}, u32[]{:S(2)}) collective-permute-start(f32[2,48,128]{2,1,0:T(8,128)S(1)} %get-tuple-element.95), channel_id=1, source_target_pairs={{0,1},{1,0},{2,3},{3,2},{4,5},{5,4},{6,7},{7,6},{8,9},{9,8},{10,11... | collective-permute-start | bytes 147464 | tf_op jit(solution)/shard_map/ppermute | solution.py:878
  29.3 4.7 %collective-permute-start.14 = (f32[32,128]{1,0:T(8,128)S(1)}, f32[32,128]{1,0:T(8,128)S(1)}, u32[]{:S(2)}, u32[]{:S(2)}) collective-permute-start(f32[32,128]{1,0:T(8,128)S(1)} %get-tuple-element.104), channel_id=1, source_target_pairs={{0,16},{1,17},{2,18},{3,19},{4,20},{5,21},{6,22},{7,23},{8,24},{9,... | collective-permute-start | bytes 49160 | tf_op jit(solution)/shard_map/ppermute | solution.py:903
  29.6 6.5 %collective-permute-start.11 = (f32[144,128]{1,0:T(8,128)S(1)}, f32[144,128]{1,0:T(8,128)S(1)}, u32[]{:S(2)}, u32[]{:S(2)}) collective-permute-start(f32[144,128]{1,0:T(8,128)S(1)} %get-tuple-element.100), channel_id=1, source_target_pairs={{2,4},{6,8},{10,12},{14,16},{18,20},{22,24},{26,28},{30,0},{4,2},{... | collective-permute-start | bytes 221192 | tf_op jit(solution)/shard_map/ppermute | solution.py:870
  30.5 5.6 %collective-permute-start.12 = (f32[144,128]{1,0:T(8,128)S(1)}, f32[144,128]{1,0:T(8,128)S(1)}, u32[]{:S(2)}, u32[]{:S(2)}) collective-permute-start(f32[144,128]{1,0:T(8,128)S(1)} %get-tuple-element.101), channel_id=1, source_target_pairs={{0,2},{2,0},{4,6},{6,4},{8,10},{10,8},{12,14},{14,12},{16,18},{18,... | collective-permute-start | bytes 221192 | tf_op jit(solution)/shard_map/ppermute | solution.py:871
  31.4 8.9 %collective-permute-start.13 = (f32[2,80,128]{2,1,0:T(8,128)S(1)}, f32[2,80,128]{2,1,0:T(8,128)S(1)}, u32[]{:S(2)}, u32[]{:S(2)}) collective-permute-start(f32[2,80,128]{2,1,0:T(8,128)S(1)} %get-tuple-element.102), channel_id=1, source_target_pairs={{0,1},{1,0},{2,3},{3,2},{4,5},{5,4},{6,7},{7,6},{8,9},{9,8},{10,11... | collective-permute-start | bytes 245768 | tf_op jit(solution)/shard_map/ppermute | solution.py:878
  36.1 4.2 %collective-permute-start.15 = (f32[2,48,128]{2,1,0:T(8,128)S(1)}, f32[2,48,128]{2,1,0:T(8,128)S(1)}, u32[]{:S(2)}, u32[]{:S(2)}) collective-permute-start(f32[2,48,128]{2,1,0:T(8,128)S(1)} %get-tuple-element.105), channel_id=1, source_target_pairs={{0,1},{1,0},{2,3},{3,2},{4,5},{5,4},{6,7},{7,6},{8,9},{9,8},{10,11... | collective-permute-start | bytes 147464 | tf_op jit(solution)/shard_map/ppermute | solution.py:878
  36.7 3.6 %collective-permute-start.16 = (f32[1,128]{1,0:T(1,128)S(1)}, f32[1,128]{1,0:T(1,128)S(1)}, u32[]{:S(2)}, u32[]{:S(2)}) collective-permute-start(f32[1,128]{1,0:T(1,128)S(1)} %get-tuple-element.107), channel_id=1, source_target_pairs={{0,1},{1,0},{2,3},{3,2},{4,5},{5,4},{6,7},{7,6},{8,9},{9,8},{10,11... | collective-permute-start | bytes 1544 | tf_op jit(solution)/shard_map/ppermute | solution.py:903
  41.2 3.8 %collective-permute-start.20 = (f32[32,128]{1,0:T(8,128)S(1)}, f32[32,128]{1,0:T(8,128)S(1)}, u32[]{:S(2)}, u32[]{:S(2)}) collective-permute-start(f32[32,128]{1,0:T(8,128)S(1)} %get-tuple-element.115), channel_id=1, source_target_pairs={{0,4},{1,5},{2,6},{3,7},{4,0},{5,1},{6,2},{7,3},{8,12},{9,13},{10,... | collective-permute-start | bytes 49160 | tf_op jit(solution)/shard_map/ppermute | solution.py:903
  41.3 6.5 %collective-permute-start.17 = (f32[128,128]{1,0:T(8,128)S(1)}, f32[128,128]{1,0:T(8,128)S(1)}, u32[]{:S(2)}, u32[]{:S(2)}) collective-permute-start(f32[128,128]{1,0:T(8,128)S(1)} %get-tuple-element.111), channel_id=1, source_target_pairs={{2,4},{6,8},{10,12},{14,16},{18,20},{22,24},{26,28},{30,0},{4,2},{... | collective-permute-start | bytes 196616 | tf_op jit(solution)/shard_map/ppermute | solution.py:870
  41.4 6.4 %collective-permute-start.18 = (f32[128,128]{1,0:T(8,128)S(1)}, f32[128,128]{1,0:T(8,128)S(1)}, u32[]{:S(2)}, u32[]{:S(2)}) collective-permute-start(f32[128,128]{1,0:T(8,128)S(1)} %get-tuple-element.112), channel_id=1, source_target_pairs={{0,2},{2,0},{4,6},{6,4},{8,10},{10,8},{12,14},{14,12},{16,18},{18,... | collective-permute-start | bytes 196616 | tf_op jit(solution)/shard_map/ppermute | solution.py:871
  43.4 9.4 %collective-permute-start.19 = (f32[2,96,128]{2,1,0:T(8,128)S(1)}, f32[2,96,128]{2,1,0:T(8,128)S(1)}, u32[]{:S(2)}, u32[]{:S(2)}) collective-permute-start(f32[2,96,128]{2,1,0:T(8,128)S(1)} %get-tuple-element.113), channel_id=1, source_target_pairs={{0,1},{1,0},{2,3},{3,2},{4,5},{5,4},{6,7},{7,6},{8,9},{9,8},{10,11... | collective-permute-start | bytes 294920 | tf_op jit(solution)/shard_map/ppermute | solution.py:878
  47.8 5.0 %collective-permute-start.22 = (f32[2,48,128]{2,1,0:T(8,128)S(1)}, f32[2,48,128]{2,1,0:T(8,128)S(1)}, u32[]{:S(2)}, u32[]{:S(2)}) collective-permute-start(f32[2,48,128]{2,1,0:T(8,128)S(1)} %get-tuple-element.116), channel_id=1, source_target_pairs={{0,1},{1,0},{2,3},{3,2},{4,5},{5,4},{6,7},{7,6},{8,9},{9,8},{10,11... | collective-permute-start | bytes 147464 | tf_op jit(solution)/shard_map/ppermute | solution.py:878
  54.1 4.7 %collective-permute-start.27 = (f32[32,128]{1,0:T(8,128)S(1)}, f32[32,128]{1,0:T(8,128)S(1)}, u32[]{:S(2)}, u32[]{:S(2)}) collective-permute-start(f32[32,128]{1,0:T(8,128)S(1)} %get-tuple-element.125), channel_id=1, source_target_pairs={{0,16},{1,17},{2,18},{3,19},{4,20},{5,21},{6,22},{7,23},{8,24},{9,... | collective-permute-start | bytes 49160 | tf_op jit(solution)/shard_map/ppermute | solution.py:903
  54.1 6.5 %collective-permute-start.24 = (f32[144,128]{1,0:T(8,128)S(1)}, f32[144,128]{1,0:T(8,128)S(1)}, u32[]{:S(2)}, u32[]{:S(2)}) collective-permute-start(f32[144,128]{1,0:T(8,128)S(1)} %get-tuple-element.121), channel_id=1, source_target_pairs={{2,4},{6,8},{10,12},{14,16},{18,20},{22,24},{26,28},{30,0},{4,2},{... | collective-permute-start | bytes 221192 | tf_op jit(solution)/shard_map/ppermute | solution.py:870
  54.2 6.5 %collective-permute-start.25 = (f32[144,128]{1,0:T(8,128)S(1)}, f32[144,128]{1,0:T(8,128)S(1)}, u32[]{:S(2)}, u32[]{:S(2)}) collective-permute-start(f32[144,128]{1,0:T(8,128)S(1)} %get-tuple-element.122), channel_id=1, source_target_pairs={{0,2},{2,0},{4,6},{6,4},{8,10},{10,8},{12,14},{14,12},{16,18},{18,... | collective-permute-start | bytes 221192 | tf_op jit(solution)/shard_map/ppermute | solution.py:871
  54.9 10.1 %collective-permute-start.26 = (f32[2,80,128]{2,1,0:T(8,128)S(1)}, f32[2,80,128]{2,1,0:T(8,128)S(1)}, u32[]{:S(2)}, u32[]{:S(2)}) collective-permute-start(f32[2,80,128]{2,1,0:T(8,128)S(1)} %get-tuple-element.123), channel_id=1, source_target_pairs={{0,1},{1,0},{2,3},{3,2},{4,5},{5,4},{6,7},{7,6},{8,9},{9,8},{10,11... | collective-permute-start | bytes 245768 | tf_op jit(solution)/shard_map/ppermute | solution.py:878
  60.7 4.3 %collective-permute-start.28 = (f32[2,48,128]{2,1,0:T(8,128)S(1)}, f32[2,48,128]{2,1,0:T(8,128)S(1)}, u32[]{:S(2)}, u32[]{:S(2)}) collective-permute-start(f32[2,48,128]{2,1,0:T(8,128)S(1)} %get-tuple-element.126), channel_id=1, source_target_pairs={{0,1},{1,0},{2,3},{3,2},{4,5},{5,4},{6,7},{7,6},{8,9},{9,8},{10,11... | collective-permute-start | bytes 147464 | tf_op jit(solution)/shard_map/ppermute | solution.py:878
  61.4 3.6 %collective-permute-start.29 = (f32[1,128]{1,0:T(1,128)S(1)}, f32[1,128]{1,0:T(1,128)S(1)}, u32[]{:S(2)}, u32[]{:S(2)}) collective-permute-start(f32[1,128]{1,0:T(1,128)S(1)} %get-tuple-element.127), channel_id=1, source_target_pairs={{0,1},{1,0},{2,3},{3,2},{4,5},{5,4},{6,7},{7,6},{8,9},{9,8},{10,11... | collective-permute-start | bytes 1544 | tf_op jit(solution)/shard_map/ppermute | solution.py:903
  65.7 6.5 %collective-permute-start.30 = (f32[128,128]{1,0:T(8,128)S(1)}, f32[128,128]{1,0:T(8,128)S(1)}, u32[]{:S(2)}, u32[]{:S(2)}) collective-permute-start(f32[128,128]{1,0:T(8,128)S(1)} %get-tuple-element.134), channel_id=1, source_target_pairs={{2,4},{6,8},{10,12},{14,16},{18,20},{22,24},{26,28},{30,0},{4,2},{... | collective-permute-start | bytes 196616 | tf_op jit(solution)/shard_map/ppermute | solution.py:870
  65.8 6.4 %collective-permute-start.31 = (f32[128,128]{1,0:T(8,128)S(1)}, f32[128,128]{1,0:T(8,128)S(1)}, u32[]{:S(2)}, u32[]{:S(2)}) collective-permute-start(f32[128,128]{1,0:T(8,128)S(1)} %get-tuple-element.135), channel_id=1, source_target_pairs={{0,2},{2,0},{4,6},{6,4},{8,10},{10,8},{12,14},{14,12},{16,18},{18,... | collective-permute-start | bytes 196616 | tf_op jit(solution)/shard_map/ppermute | solution.py:871
  66.3 7.2 %collective-permute-start.32 = (f32[2,96,128]{2,1,0:T(8,128)S(1)}, f32[2,96,128]{2,1,0:T(8,128)S(1)}, u32[]{:S(2)}, u32[]{:S(2)}) collective-permute-start(f32[2,96,128]{2,1,0:T(8,128)S(1)} %get-tuple-element.136), channel_id=1, source_target_pairs={{0,1},{1,0},{2,3},{3,2},{4,5},{5,4},{6,7},{7,6},{8,9},{9,8},{10,11... | collective-permute-start | bytes 294920 | tf_op jit(solution)/shard_map/ppermute | solution.py:878
  72.1 4.2 %collective-permute-start.33 = (f32[2,48,128]{2,1,0:T(8,128)S(1)}, f32[2,48,128]{2,1,0:T(8,128)S(1)}, u32[]{:S(2)}, u32[]{:S(2)}) collective-permute-start(f32[2,48,128]{2,1,0:T(8,128)S(1)} %get-tuple-element.143), channel_id=1, source_target_pairs={{0,1},{1,0},{2,3},{3,2},{4,5},{5,4},{6,7},{7,6},{8,9},{9,8},{10,11... | collective-permute-start | bytes 147464 | tf_op jit(solution)/shard_map/ppermute | solution.py:878
  77.6 6.5 %collective-permute-start.34 = (f32[144,128]{1,0:T(8,128)S(1)}, f32[144,128]{1,0:T(8,128)S(1)}, u32[]{:S(2)}, u32[]{:S(2)}) collective-permute-start(f32[144,128]{1,0:T(8,128)S(1)} %get-tuple-element.148), channel_id=1, source_target_pairs={{2,4},{6,8},{10,12},{14,16},{18,20},{22,24},{26,28},{30,0},{4,2},{... | collective-permute-start | bytes 221192 | tf_op jit(solution)/shard_map/ppermute | solution.py:870
  77.6 6.5 %collective-permute-start.35 = (f32[144,128]{1,0:T(8,128)S(1)}, f32[144,128]{1,0:T(8,128)S(1)}, u32[]{:S(2)}, u32[]{:S(2)}) collective-permute-start(f32[144,128]{1,0:T(8,128)S(1)} %get-tuple-element.149), channel_id=1, source_target_pairs={{0,2},{2,0},{4,6},{6,4},{8,10},{10,8},{12,14},{14,12},{16,18},{18,... | collective-permute-start | bytes 221192 | tf_op jit(solution)/shard_map/ppermute | solution.py:871
  84.1 10.3 %collective-permute-start.36 = (f32[2,128,128]{2,1,0:T(8,128)S(1)}, f32[2,128,128]{2,1,0:T(8,128)S(1)}, u32[]{:S(2)}, u32[]{:S(2)}) collective-permute-start(f32[2,128,128]{2,1,0:T(8,128)S(1)} %get-tuple-element.157), channel_id=1, source_target_pairs={{0,1},{1,0},{2,3},{3,2},{4,5},{5,4},{6,7},{7,6},{8,9},{9,8},{10,11... | collective-permute-start | bytes 393224 | tf_op jit(solution)/shard_map/ppermute | solution.py:878
  (14 other events, 63.9 us)

commit v8 on v7

--- a/solution.py
+++ b/solution.py
@@ -593,6 +593,16 @@
                 send_early_ref[side, 24 + 8 * a : 32 + 8 * a] = face
 
 
+def first_rest_kernel(
+    middle_ref, ends_ref, outof_ref, planes_ref,
+    solved_ref, part_ref, send_early_ref, send_late_ref, dot_ref,
+):
+    solve_rest_kernel(
+        middle_ref, ends_ref, outof_ref, solved_ref, part_ref, send_early_ref, send_late_ref
+    )
+    dot_ref[...] = jnp.broadcast_to(dot_planes(planes_ref, solved_ref), dot_ref.shape)
+
+
 def solved_side_kernel(out_ref, in_ref, late_ref, row_ref, send_ref, pass_ref):
     pass_ref[...] = row_ref[...]
     before, after = got_axial(in_ref, out_ref)
@@ -708,7 +718,7 @@
 
 def first_apply_kernel(
     part_ref, out_ref, in_ref, early_ref, late_ref, near_ref, diff_ref, plane_ref, grad_ref, div_ref,
-    sums_ref, planes_ref, solved_ref,
+    sums_ref, dot_ref,
     z_ref, raw_ref, g_ref, send_out_ref, send_early_ref, send_in_ref, send_late_ref, row_ref, pay_ref,
 ):
     row, _ = got_sums(sums_ref, 0)
@@ -720,7 +730,7 @@
         z_ref[a] = values[a]
         raw_ref[a] = raw[a]
     row_ref[0:1] = row
-    scalars = [dot_planes(planes_ref, solved_ref), dot_parts(values, raw)]
+    scalars = [dot_ref[0:1, 0:1], dot_parts(values, raw)]
     send_sums(pay_ref, coarse_share(raw, near_ref), scalars)
 
 
@@ -961,28 +971,32 @@
     solver = (inverse, into, outof)
     operator = (near, diff, plane, grad, div)
 
-    def solve(g, moved, pay):
+    def solve(g, moved, pay, first=False):
         ends = [(6, 112, LANES), (4, 144, LANES), (144, LANES), (144, LANES), copies]
         planes, middle, ends, send_out, send_in, pay = kernel_call(
             solve_ends_kernel, boxes[:1] + ends, g, *moved, pay, *solver
         )
+        shapes = boxes[:1] + [field, (2, 80, LANES), (2, 48, LANES)]
+        if first:
+            solved, part, send_early, send_late, dot = kernel_call(
+                first_rest_kernel, shapes + [(8, LANES)], middle, ends, outof, planes
+            )
+            return dot, planes, solved, part, send_out, send_early, send_in, send_late, pay
         solved, part, send_early, send_late = kernel_call(
-            solve_rest_kernel,
-            boxes[:1] + [field, (2, 80, LANES), (2, 48, LANES)],
-            middle, ends, outof,
+            solve_rest_kernel, shapes, middle, ends, outof
         )
         return planes, solved, part, send_out, send_early, send_in, send_late, pay
 
 
     *moved, pay = exchange(raw_side_kernel, 48, sends, partial_sum(pay, groups[0]), one)
     pay = partial_sum(pay, groups[1])
-    planes_r, solved_r, part, *sends, pay = solve(g, moved, pay)
+    dot, planes_r, solved_r, part, *sends, pay = solve(g, moved, pay, True)
     *moved, pay = exchange(solved_side_kernel, 48, sends, partial_sum(pay, groups[2]), one)
     pay = partial_sum(pay, groups[3])
     z0, raw0, g, *sends, row_r, pay = kernel_call(
         first_apply_kernel,
         [field, field, field] + raw_sends + [row_shape, copies],
-        part, *moved, *operator, pay, planes_r, solved_r,
+        part, *moved, *operator, pay, dot,
     )
     *moved, pay = exchange(raw_side_kernel, 48, sends, partial_sum(pay, groups[0]), one)
     pay = partial_sum(pay, groups[1])

time: 95.7 us -> 95.7 us (level)
  no operation moved by 1% of the time
where the time goes in v8:
time: 95.7 us; the launch traced here: 95.5 us
  waiting for transfers between devices  41.2 us (43%)
  starting transfers between devices  31.9 us (33%)
  Pallas kernels  12.5 us (13%)
  blocking collectives  8.89 us (9%)
  between operations  0.98 us (1%)
    ppermute x10, waiting for transfers between devices, partial_sum(): lax.ppermute(row, ALL, [(i, i ^ step) for i in range(count)])[:1]  18.6 us
    ppermute x7, waiting for transfers between devices, axial_swap(): from_outer = lax.ppermute(outer_rows, 'axial', outer)  16.7 us
    ppermute x13, starting transfers between devices, azim_swap(): return lax.ppermute(sides, 'azim', [(0, 1), (1, 0)])  16.3 us
    pallas_call x22, Pallas kernels, kernel_call(): pl.pallas_call(kernel, out_shape=outs, compiler_params=pltpu.CompilerPara...  12.5 us
    ppermute x7, starting transfers between devices, axial_swap(): from_outer = lax.ppermute(outer_rows, 'axial', outer)  9.13 us
    all_to_all x1, blocking collectives, gather_sums(): return lax.all_to_all(rows, ALL, 0, 0, tiled=True)  8.89 us
    ppermute x13, waiting for transfers between devices, azim_swap(): return lax.ppermute(sides, 'azim', [(0, 1), (1, 0)])  5.82 us
    ppermute x10, starting transfers between devices, partial_sum(): lax.ppermute(row, ALL, [(i, i ^ step) for i in range(count)])[:1]  3.67 us
  transfers between devices with their start and end apart: 37, of which 19 were waited for; matrix products, arithmetic and copies ran while one was open for 0% of the time, Pallas kernels for 4%

profile of v8, /device:TPU:0, one launch (start us, length us, event | category | flops | bytes accessed | tf_op | source)
XLA Modules:
  0.0 95.5 jit_solution(13023493269902023209)
XLA Ops:
  0.6 2.1 %shard_map.121 = (f32[3,8,64,128]{3,2,1,0:T(8,128)S(1)}, f32[8,128]{1,0:T(8,128)S(1)}, f32[200,128]{1,0:T(8,128)S(1)}, f32[2,144,128]{2,1,0:T(8,128)S(1)}, f32[2...) custom-call(f32[3,8,64,128]{3,2,1,0:T(8,128)} %bitcast.17, f32[1,32]{1,0:T(1,128)} %row_hbm.1, ...), custom_call_target="tpu_custom_call" | custom-call | tf_op jit(solution)/shard_map/pallas_call | solution.py:866
  2.8 5.5 %collective-permute-start.1 = (f32[200,128]{1,0:T(8,128)S(1)}, f32[200,128]{1,0:T(8,128)S(1)}, u32[]{:S(2)}, u32[]{:S(2)}) collective-permute-start(f32[200,128]{1,0:T(8,128)S(1)} %get-tuple-element.86), channel_id=1, source_target_pairs={{2,4},{6,8},{10,12},{14,16},{18,20},{22,24},{26,28},{30,0},{4,2},{... | collective-permute-start | bytes 307208 | tf_op jit(solution)/shard_map/ppermute | solution.py:880
  8.3 1.5 %collective-permute-start = (f32[2,144,128]{2,1,0:T(8,128)S(1)}, f32[2,144,128]{2,1,0:T(8,128)S(1)}, u32[]{:S(2)}, u32[]{:S(2)}) collective-permute-start(f32[2,144,128]{2,1,0:T(8,128)S(1)} %get-tuple-element.84), channel_id=1, source_target_pairs={{0,1},{1,0},{2,3},{3,2},{4,5},{5,4},{6,7},{7,6},{8,9},{9,8},{10,11... | collective-permute-start | bytes 442376 | tf_op jit(solution)/shard_map/ppermute | solution.py:888
  10.7 2.0 %collective-permute-start.3 = (f32[2,56,128]{2,1,0:T(8,128)S(1)}, f32[2,56,128]{2,1,0:T(8,128)S(1)}, u32[]{:S(2)}, u32[]{:S(2)}) collective-permute-start(f32[2,56,128]{2,1,0:T(8,128)S(1)} %shard_map.122), channel_id=1, source_target_pairs={{0,1},{1,0},{2,3},{3,2},{4,5},{5,4},{6,7},{7,6},{8,9},{9,8},{10,11... | collective-permute-start | bytes 172040 | tf_op jit(solution)/shard_map/ppermute | solution.py:888
  12.7 2.2 %collective-permute-done.early_ref = f32[2,144,128]{2,1,0:T(8,128)S(1)} collective-permute-done((f32[2,144,128]{2,1,0:T(8,128)S(1)}, f32[2,144,128]{2,1,0:T(8,128)S(1)}, u32[]{:S(2)}, u32[]{:S(2)}) %collective-permute-start) | collective-permute-done | bytes 147488 | tf_op jit(solution)/shard_map/ppermute | solution.py:888
  16.4 2.5 %collective-permute-start.4 = (f32[128,128]{1,0:T(8,128)S(1)}, f32[128,128]{1,0:T(8,128)S(1)}, u32[]{:S(2)}, u32[]{:S(2)}) collective-permute-start(f32[128,128]{1,0:T(8,128)S(1)} %get-tuple-element.91), channel_id=1, source_target_pairs={{2,4},{6,8},{10,12},{14,16},{18,20},{22,24},{26,28},{30,0},{4,2},{... | collective-permute-start | bytes 196616 | tf_op jit(solution)/shard_map/ppermute | solution.py:880
  18.9 1.5 %collective-permute-start.6 = (f32[2,96,128]{2,1,0:T(8,128)S(1)}, f32[2,96,128]{2,1,0:T(8,128)S(1)}, u32[]{:S(2)}, u32[]{:S(2)}) collective-permute-start(f32[2,96,128]{2,1,0:T(8,128)S(1)} %get-tuple-element.93), channel_id=1, source_target_pairs={{0,1},{1,0},{2,3},{3,2},{4,5},{5,4},{6,7},{7,6},{8,9},{9,8},{10,11... | collective-permute-start | bytes 294920 | tf_op jit(solution)/shard_map/ppermute | solution.py:888
  21.6 1.3 %collective-permute-done.4.out_ref = f32[128,128]{1,0:T(8,128)S(1)} collective-permute-done((f32[128,128]{1,0:T(8,128)S(1)}, f32[128,128]{1,0:T(8,128)S(1)}, u32[]{:S(2)}, u32[]{:S(2)}) %collective-permute-start.4) | collective-permute-done | bytes 65568 | tf_op jit(solution)/shard_map/ppermute | solution.py:880
  22.9 1.6 %collective-permute-start.9 = (f32[2,48,128]{2,1,0:T(8,128)S(1)}, f32[2,48,128]{2,1,0:T(8,128)S(1)}, u32[]{:S(2)}, u32[]{:S(2)}) collective-permute-start(f32[2,48,128]{2,1,0:T(8,128)S(1)} %get-tuple-element.96), channel_id=1, source_target_pairs={{0,1},{1,0},{2,3},{3,2},{4,5},{5,4},{6,7},{7,6},{8,9},{9,8},{10,11... | collective-permute-start | bytes 147464 | tf_op jit(solution)/shard_map/ppermute | solution.py:888
  24.6 3.4 %collective-permute-done.10 = f32[1,128]{1,0:T(1,128)S(1)} collective-permute-done((f32[1,128]{1,0:T(1,128)S(1)}, f32[1,128]{1,0:T(1,128)S(1)}, u32[]{:S(2)}, u32[]{:S(2)}) %collective-permute-start.10) | collective-permute-done | bytes 544 | tf_op jit(solution)/shard_map/ppermute | solution.py:913
  28.0 1.3 %shard_map.126 = (f32[10,144,128]{2,1,0:T(8,128)S(1)}, f32[6,112,128]{2,1,0:T(8,128)S(1)}, f32[4,144,128]{2,1,0:T(8,128)S(1)}, f32[144,128]{1,0:T(8,128)S(1)}, f...) custom-call(f32[8,64,128]{2,1,0:T(8,128)S(1)} %get-tuple-element.90.g_ref, f32[128,128]{1,0:T(8,128)S(1)} %collective-permute-done.4.out_ref, ...), custom_call_target="tpu_custom_call" | custom-call | tf_op jit(solution)/shard_map/pallas_call | solution.py:866
  32.0 2.0 %collective-permute-done.14 = f32[32,128]{1,0:T(8,128)S(1)} collective-permute-done((f32[32,128]{1,0:T(8,128)S(1)}, f32[32,128]{1,0:T(8,128)S(1)}, u32[]{:S(2)}, u32[]{:S(2)}) %collective-permute-start.14) | collective-permute-done | bytes 16416 | tf_op jit(solution)/shard_map/ppermute | solution.py:913
  34.0 2.0 %collective-permute-done.11.out_ref = f32[144,128]{1,0:T(8,128)S(1)} collective-permute-done((f32[144,128]{1,0:T(8,128)S(1)}, f32[144,128]{1,0:T(8,128)S(1)}, u32[]{:S(2)}, u32[]{:S(2)}) %collective-permute-start.11) | collective-permute-done | bytes 73760 | tf_op jit(solution)/shard_map/ppermute | solution.py:880
  36.7 1.5 %collective-permute-start.16 = (f32[1,128]{1,0:T(1,128)S(1)}, f32[1,128]{1,0:T(1,128)S(1)}, u32[]{:S(2)}, u32[]{:S(2)}) collective-permute-start(f32[1,128]{1,0:T(1,128)S(1)} %get-tuple-element.109), channel_id=1, source_target_pairs={{0,1},{1,0},{2,3},{3,2},{4,5},{5,4},{6,7},{7,6},{8,9},{9,8},{10,11... | collective-permute-start | bytes 1544 | tf_op jit(solution)/shard_map/ppermute | solution.py:913
  38.2 2.1 %collective-permute-done.16 = f32[1,128]{1,0:T(1,128)S(1)} collective-permute-done((f32[1,128]{1,0:T(1,128)S(1)}, f32[1,128]{1,0:T(1,128)S(1)}, u32[]{:S(2)}, u32[]{:S(2)}) %collective-permute-start.16) | collective-permute-done | bytes 544 | tf_op jit(solution)/shard_map/ppermute | solution.py:913
  41.3 2.0 %collective-permute-start.18 = (f32[128,128]{1,0:T(8,128)S(1)}, f32[128,128]{1,0:T(8,128)S(1)}, u32[]{:S(2)}, u32[]{:S(2)}) collective-permute-start(f32[128,128]{1,0:T(8,128)S(1)} %get-tuple-element.113), channel_id=1, source_target_pairs={{0,2},{2,0},{4,6},{6,4},{8,10},{10,8},{12,14},{14,12},{16,18},{18,... | collective-permute-start | bytes 196616 | tf_op jit(solution)/shard_map/ppermute | solution.py:881
  43.4 1.4 %collective-permute-start.19 = (f32[2,96,128]{2,1,0:T(8,128)S(1)}, f32[2,96,128]{2,1,0:T(8,128)S(1)}, u32[]{:S(2)}, u32[]{:S(2)}) collective-permute-start(f32[2,96,128]{2,1,0:T(8,128)S(1)} %get-tuple-element.114), channel_id=1, source_target_pairs={{0,1},{1,0},{2,3},{3,2},{4,5},{5,4},{6,7},{7,6},{8,9},{9,8},{10,11... | collective-permute-start | bytes 294920 | tf_op jit(solution)/shard_map/ppermute | solution.py:888
  46.1 1.6 %collective-permute-done.17.out_ref = f32[128,128]{1,0:T(8,128)S(1)} collective-permute-done((f32[128,128]{1,0:T(8,128)S(1)}, f32[128,128]{1,0:T(8,128)S(1)}, u32[]{:S(2)}, u32[]{:S(2)}) %collective-permute-start.17) | collective-permute-done | bytes 65568 | tf_op jit(solution)/shard_map/ppermute | solution.py:880
  47.7 1.5 %collective-permute-start.22 = (f32[2,48,128]{2,1,0:T(8,128)S(1)}, f32[2,48,128]{2,1,0:T(8,128)S(1)}, u32[]{:S(2)}, u32[]{:S(2)}) collective-permute-start(f32[2,48,128]{2,1,0:T(8,128)S(1)} %get-tuple-element.117), channel_id=1, source_target_pairs={{0,1},{1,0},{2,3},{3,2},{4,5},{5,4},{6,7},{7,6},{8,9},{9,8},{10,11... | collective-permute-start | bytes 147464 | tf_op jit(solution)/shard_map/ppermute | solution.py:888
  49.2 3.5 %collective-permute-done.23 = f32[1,128]{1,0:T(1,128)S(1)} collective-permute-done((f32[1,128]{1,0:T(1,128)S(1)}, f32[1,128]{1,0:T(1,128)S(1)}, u32[]{:S(2)}, u32[]{:S(2)}) %collective-permute-start.23) | collective-permute-done | bytes 544 | tf_op jit(solution)/shard_map/ppermute | solution.py:913
  52.7 1.3 %shard_map.131 = (f32[10,144,128]{2,1,0:T(8,128)S(1)}, f32[6,112,128]{2,1,0:T(8,128)S(1)}, f32[4,144,128]{2,1,0:T(8,128)S(1)}, f32[144,128]{1,0:T(8,128)S(1)}, f...) custom-call(f32[8,64,128]{2,1,0:T(8,128)S(1)} %get-tuple-element.111.g_ref, f32[128,128]{1,0:T(8,128)S(1)} %collective-permute-done.17.out_ref, ...), custom_call_target="tpu_custom_call" | custom-call | tf_op jit(solution)/shard_map/pallas_call | solution.py:866
  55.6 3.2 %collective-permute-done.27 = f32[32,128]{1,0:T(8,128)S(1)} collective-permute-done((f32[32,128]{1,0:T(8,128)S(1)}, f32[32,128]{1,0:T(8,128)S(1)}, u32[]{:S(2)}, u32[]{:S(2)}) %collective-permute-start.27) | collective-permute-done | bytes 16416 | tf_op jit(solution)/shard_map/ppermute | solution.py:913
  58.7 1.9 %collective-permute-done.24.out_ref = f32[144,128]{1,0:T(8,128)S(1)} collective-permute-done((f32[144,128]{1,0:T(8,128)S(1)}, f32[144,128]{1,0:T(8,128)S(1)}, u32[]{:S(2)}, u32[]{:S(2)}) %collective-permute-start.24) | collective-permute-done | bytes 73760 | tf_op jit(solution)/shard_map/ppermute | solution.py:880
  61.3 1.4 %collective-permute-start.29 = (f32[1,128]{1,0:T(1,128)S(1)}, f32[1,128]{1,0:T(1,128)S(1)}, u32[]{:S(2)}, u32[]{:S(2)}) collective-permute-start(f32[1,128]{1,0:T(1,128)S(1)} %get-tuple-element.128), channel_id=1, source_target_pairs={{0,1},{1,0},{2,3},{3,2},{4,5},{5,4},{6,7},{7,6},{8,9},{9,8},{10,11... | collective-permute-start | bytes 1544 | tf_op jit(solution)/shard_map/ppermute | solution.py:913
  62.8 2.2 %collective-permute-done.29 = f32[1,128]{1,0:T(1,128)S(1)} collective-permute-done((f32[1,128]{1,0:T(1,128)S(1)}, f32[1,128]{1,0:T(1,128)S(1)}, u32[]{:S(2)}, u32[]{:S(2)}) %collective-permute-start.29) | collective-permute-done | bytes 544 | tf_op jit(solution)/shard_map/ppermute | solution.py:913
  66.3 1.4 %collective-permute-start.32 = (f32[2,96,128]{2,1,0:T(8,128)S(1)}, f32[2,96,128]{2,1,0:T(8,128)S(1)}, u32[]{:S(2)}, u32[]{:S(2)}) collective-permute-start(f32[2,96,128]{2,1,0:T(8,128)S(1)} %get-tuple-element.137), channel_id=1, source_target_pairs={{0,1},{1,0},{2,3},{3,2},{4,5},{5,4},{6,7},{7,6},{8,9},{9,8},{10,11... | collective-permute-start | bytes 294920 | tf_op jit(solution)/shard_map/ppermute | solution.py:888
  68.4 3.7 %collective-permute-done.30.out_ref = f32[128,128]{1,0:T(8,128)S(1)} collective-permute-done((f32[128,128]{1,0:T(8,128)S(1)}, f32[128,128]{1,0:T(8,128)S(1)}, u32[]{:S(2)}, u32[]{:S(2)}) %collective-permute-start.30) | collective-permute-done | bytes 65568 | tf_op jit(solution)/shard_map/ppermute | solution.py:880
  72.1 1.4 %collective-permute-start.33 = (f32[2,48,128]{2,1,0:T(8,128)S(1)}, f32[2,48,128]{2,1,0:T(8,128)S(1)}, u32[]{:S(2)}, u32[]{:S(2)}) collective-permute-start(f32[2,48,128]{2,1,0:T(8,128)S(1)} %get-tuple-element.145), channel_id=1, source_target_pairs={{0,1},{1,0},{2,3},{3,2},{4,5},{5,4},{6,7},{7,6},{8,9},{9,8},{10,11... | collective-permute-start | bytes 147464 | tf_op jit(solution)/shard_map/ppermute | solution.py:888
  73.5 2.7 %collective-permute-done.33.late_ref = f32[2,48,128]{2,1,0:T(8,128)S(1)} collective-permute-done((f32[2,48,128]{2,1,0:T(8,128)S(1)}, f32[2,48,128]{2,1,0:T(8,128)S(1)}, u32[]{:S(2)}, u32[]{:S(2)}) %collective-permute-start.33) | collective-permute-done | bytes 49184 | tf_op jit(solution)/shard_map/ppermute | solution.py:888
  78.7 5.3 %collective-permute-done.34.out_ref = f32[144,128]{1,0:T(8,128)S(1)} collective-permute-done((f32[144,128]{1,0:T(8,128)S(1)}, f32[144,128]{1,0:T(8,128)S(1)}, u32[]{:S(2)}, u32[]{:S(2)}) %collective-permute-start.34) | collective-permute-done | bytes 73760 | tf_op jit(solution)/shard_map/ppermute | solution.py:880
  84.1 1.4 %collective-permute-start.36 = (f32[2,128,128]{2,1,0:T(8,128)S(1)}, f32[2,128,128]{2,1,0:T(8,128)S(1)}, u32[]{:S(2)}, u32[]{:S(2)}) collective-permute-start(f32[2,128,128]{2,1,0:T(8,128)S(1)} %get-tuple-element.159), channel_id=1, source_target_pairs={{0,1},{1,0},{2,3},{3,2},{4,5},{5,4},{6,7},{7,6},{8,9},{9,8},{10,11... | collective-permute-start | bytes 393224 | tf_op jit(solution)/shard_map/ppermute | solution.py:888
  85.5 8.9 %all_to_all.8 = f32[32,1,128]{2,1,0:T(1,128)S(1)} all-to-all(f32[32,1,128]{2,1,0:T(1,128)S(1)} %broadcast_in_dim.2), channel_id=1, replica_groups=mesh['axial'=16,'azim'=2] {'axial','azim'}, dimensions={0} | all-to-all | bytes 32768 | tf_op jit(solution)/shard_map/all_to_all | solution.py:918
  (95 shorter events, 17.0 us)
Async XLA Ops:
  2.8 7.8 %collective-permute-start.1 = (f32[200,128]{1,0:T(8,128)S(1)}, f32[200,128]{1,0:T(8,128)S(1)}, u32[]{:S(2)}, u32[]{:S(2)}) collective-permute-start(f32[200,128]{1,0:T(8,128)S(1)} %get-tuple-element.86), channel_id=1, source_target_pairs={{2,4},{6,8},{10,12},{14,16},{18,20},{22,24},{26,28},{30,0},{4,2},{... | collective-permute-start | bytes 307208 | tf_op jit(solution)/shard_map/ppermute | solution.py:880
  8.3 6.6 %collective-permute-start = (f32[2,144,128]{2,1,0:T(8,128)S(1)}, f32[2,144,128]{2,1,0:T(8,128)S(1)}, u32[]{:S(2)}, u32[]{:S(2)}) collective-permute-start(f32[2,144,128]{2,1,0:T(8,128)S(1)} %get-tuple-element.84), channel_id=1, source_target_pairs={{0,1},{1,0},{2,3},{3,2},{4,5},{5,4},{6,7},{7,6},{8,9},{9,8},{10,11... | collective-permute-start | bytes 442376 | tf_op jit(solution)/shard_map/ppermute | solution.py:888
  10.7 5.1 %collective-permute-start.3 = (f32[2,56,128]{2,1,0:T(8,128)S(1)}, f32[2,56,128]{2,1,0:T(8,128)S(1)}, u32[]{:S(2)}, u32[]{:S(2)}) collective-permute-start(f32[2,56,128]{2,1,0:T(8,128)S(1)} %shard_map.122), channel_id=1, source_target_pairs={{0,1},{1,0},{2,3},{3,2},{4,5},{5,4},{6,7},{7,6},{8,9},{9,8},{10,11... | collective-permute-start | bytes 172040 | tf_op jit(solution)/shard_map/ppermute | solution.py:888
  16.3 4.1 %collective-permute-start.7 = (f32[32,128]{1,0:T(8,128)S(1)}, f32[32,128]{1,0:T(8,128)S(1)}, u32[]{:S(2)}, u32[]{:S(2)}) collective-permute-start(f32[32,128]{1,0:T(8,128)S(1)} %get-tuple-element.95), channel_id=1, source_target_pairs={{0,4},{1,5},{2,6},{3,7},{4,0},{5,1},{6,2},{7,3},{8,12},{9,13},{10,... | collective-permute-start | bytes 49160 | tf_op jit(solution)/shard_map/ppermute | solution.py:913
  16.4 6.5 %collective-permute-start.4 = (f32[128,128]{1,0:T(8,128)S(1)}, f32[128,128]{1,0:T(8,128)S(1)}, u32[]{:S(2)}, u32[]{:S(2)}) collective-permute-start(f32[128,128]{1,0:T(8,128)S(1)} %get-tuple-element.91), channel_id=1, source_target_pairs={{2,4},{6,8},{10,12},{14,16},{18,20},{22,24},{26,28},{30,0},{4,2},{... | collective-permute-start | bytes 196616 | tf_op jit(solution)/shard_map/ppermute | solution.py:880
  18.9 4.0 %collective-permute-start.5 = (f32[128,128]{1,0:T(8,128)S(1)}, f32[128,128]{1,0:T(8,128)S(1)}, u32[]{:S(2)}, u32[]{:S(2)}) collective-permute-start(f32[128,128]{1,0:T(8,128)S(1)} %get-tuple-element.92), channel_id=1, source_target_pairs={{0,2},{2,0},{4,6},{6,4},{8,10},{10,8},{12,14},{14,12},{16,18},{18,... | collective-permute-start | bytes 196616 | tf_op jit(solution)/shard_map/ppermute | solution.py:881
  18.9 9.1 %collective-permute-start.6 = (f32[2,96,128]{2,1,0:T(8,128)S(1)}, f32[2,96,128]{2,1,0:T(8,128)S(1)}, u32[]{:S(2)}, u32[]{:S(2)}) collective-permute-start(f32[2,96,128]{2,1,0:T(8,128)S(1)} %get-tuple-element.93), channel_id=1, source_target_pairs={{0,1},{1,0},{2,3},{3,2},{4,5},{5,4},{6,7},{7,6},{8,9},{9,8},{10,11... | collective-permute-start | bytes 294920 | tf_op jit(solution)/shard_map/ppermute | solution.py:888
  22.9 5.1 %collective-permute-start.9 = (f32[2,48,128]{2,1,0:T(8,128)S(1)}, f32[2,48,128]{2,1,0:T(8,128)S(1)}, u32[]{:S(2)}, u32[]{:S(2)}) collective-permute-start(f32[2,48,128]{2,1,0:T(8,128)S(1)} %get-tuple-element.96), channel_id=1, source_target_pairs={{0,1},{1,0},{2,3},{3,2},{4,5},{5,4},{6,7},{7,6},{8,9},{9,8},{10,11... | collective-permute-start | bytes 147464 | tf_op jit(solution)/shard_map/ppermute | solution.py:888
  29.3 4.7 %collective-permute-start.14 = (f32[32,128]{1,0:T(8,128)S(1)}, f32[32,128]{1,0:T(8,128)S(1)}, u32[]{:S(2)}, u32[]{:S(2)}) collective-permute-start(f32[32,128]{1,0:T(8,128)S(1)} %get-tuple-element.106), channel_id=1, source_target_pairs={{0,16},{1,17},{2,18},{3,19},{4,20},{5,21},{6,22},{7,23},{8,24},{9,... | collective-permute-start | bytes 49160 | tf_op jit(solution)/shard_map/ppermute | solution.py:913
  29.6 6.5 %collective-permute-start.11 = (f32[144,128]{1,0:T(8,128)S(1)}, f32[144,128]{1,0:T(8,128)S(1)}, u32[]{:S(2)}, u32[]{:S(2)}) collective-permute-start(f32[144,128]{1,0:T(8,128)S(1)} %get-tuple-element.102), channel_id=1, source_target_pairs={{2,4},{6,8},{10,12},{14,16},{18,20},{22,24},{26,28},{30,0},{4,2},{... | collective-permute-start | bytes 221192 | tf_op jit(solution)/shard_map/ppermute | solution.py:880
  30.5 5.6 %collective-permute-start.12 = (f32[144,128]{1,0:T(8,128)S(1)}, f32[144,128]{1,0:T(8,128)S(1)}, u32[]{:S(2)}, u32[]{:S(2)}) collective-permute-start(f32[144,128]{1,0:T(8,128)S(1)} %get-tuple-element.103), channel_id=1, source_target_pairs={{0,2},{2,0},{4,6},{6,4},{8,10},{10,8},{12,14},{14,12},{16,18},{18,... | collective-permute-start | bytes 221192 | tf_op jit(solution)/shard_map/ppermute | solution.py:881
  31.4 8.9 %collective-permute-start.13 = (f32[2,80,128]{2,1,0:T(8,128)S(1)}, f32[2,80,128]{2,1,0:T(8,128)S(1)}, u32[]{:S(2)}, u32[]{:S(2)}) collective-permute-start(f32[2,80,128]{2,1,0:T(8,128)S(1)} %get-tuple-element.104), channel_id=1, source_target_pairs={{0,1},{1,0},{2,3},{3,2},{4,5},{5,4},{6,7},{7,6},{8,9},{9,8},{10,11... | collective-permute-start | bytes 245768 | tf_op jit(solution)/shard_map/ppermute | solution.py:888
  36.1 4.2 %collective-permute-start.15 = (f32[2,48,128]{2,1,0:T(8,128)S(1)}, f32[2,48,128]{2,1,0:T(8,128)S(1)}, u32[]{:S(2)}, u32[]{:S(2)}) collective-permute-start(f32[2,48,128]{2,1,0:T(8,128)S(1)} %get-tuple-element.107), channel_id=1, source_target_pairs={{0,1},{1,0},{2,3},{3,2},{4,5},{5,4},{6,7},{7,6},{8,9},{9,8},{10,11... | collective-permute-start | bytes 147464 | tf_op jit(solution)/shard_map/ppermute | solution.py:888
  36.7 3.6 %collective-permute-start.16 = (f32[1,128]{1,0:T(1,128)S(1)}, f32[1,128]{1,0:T(1,128)S(1)}, u32[]{:S(2)}, u32[]{:S(2)}) collective-permute-start(f32[1,128]{1,0:T(1,128)S(1)} %get-tuple-element.109), channel_id=1, source_target_pairs={{0,1},{1,0},{2,3},{3,2},{4,5},{5,4},{6,7},{7,6},{8,9},{9,8},{10,11... | collective-permute-start | bytes 1544 | tf_op jit(solution)/shard_map/ppermute | solution.py:913
  41.2 3.8 %collective-permute-start.20 = (f32[32,128]{1,0:T(8,128)S(1)}, f32[32,128]{1,0:T(8,128)S(1)}, u32[]{:S(2)}, u32[]{:S(2)}) collective-permute-start(f32[32,128]{1,0:T(8,128)S(1)} %get-tuple-element.116), channel_id=1, source_target_pairs={{0,4},{1,5},{2,6},{3,7},{4,0},{5,1},{6,2},{7,3},{8,12},{9,13},{10,... | collective-permute-start | bytes 49160 | tf_op jit(solution)/shard_map/ppermute | solution.py:913
  41.2 6.5 %collective-permute-start.17 = (f32[128,128]{1,0:T(8,128)S(1)}, f32[128,128]{1,0:T(8,128)S(1)}, u32[]{:S(2)}, u32[]{:S(2)}) collective-permute-start(f32[128,128]{1,0:T(8,128)S(1)} %get-tuple-element.112), channel_id=1, source_target_pairs={{2,4},{6,8},{10,12},{14,16},{18,20},{22,24},{26,28},{30,0},{4,2},{... | collective-permute-start | bytes 196616 | tf_op jit(solution)/shard_map/ppermute | solution.py:880
  41.3 6.4 %collective-permute-start.18 = (f32[128,128]{1,0:T(8,128)S(1)}, f32[128,128]{1,0:T(8,128)S(1)}, u32[]{:S(2)}, u32[]{:S(2)}) collective-permute-start(f32[128,128]{1,0:T(8,128)S(1)} %get-tuple-element.113), channel_id=1, source_target_pairs={{0,2},{2,0},{4,6},{6,4},{8,10},{10,8},{12,14},{14,12},{16,18},{18,... | collective-permute-start | bytes 196616 | tf_op jit(solution)/shard_map/ppermute | solution.py:881
  43.4 9.4 %collective-permute-start.19 = (f32[2,96,128]{2,1,0:T(8,128)S(1)}, f32[2,96,128]{2,1,0:T(8,128)S(1)}, u32[]{:S(2)}, u32[]{:S(2)}) collective-permute-start(f32[2,96,128]{2,1,0:T(8,128)S(1)} %get-tuple-element.114), channel_id=1, source_target_pairs={{0,1},{1,0},{2,3},{3,2},{4,5},{5,4},{6,7},{7,6},{8,9},{9,8},{10,11... | collective-permute-start | bytes 294920 | tf_op jit(solution)/shard_map/ppermute | solution.py:888
  47.7 5.0 %collective-permute-start.22 = (f32[2,48,128]{2,1,0:T(8,128)S(1)}, f32[2,48,128]{2,1,0:T(8,128)S(1)}, u32[]{:S(2)}, u32[]{:S(2)}) collective-permute-start(f32[2,48,128]{2,1,0:T(8,128)S(1)} %get-tuple-element.117), channel_id=1, source_target_pairs={{0,1},{1,0},{2,3},{3,2},{4,5},{5,4},{6,7},{7,6},{8,9},{9,8},{10,11... | collective-permute-start | bytes 147464 | tf_op jit(solution)/shard_map/ppermute | solution.py:888
  54.0 4.7 %collective-permute-start.27 = (f32[32,128]{1,0:T(8,128)S(1)}, f32[32,128]{1,0:T(8,128)S(1)}, u32[]{:S(2)}, u32[]{:S(2)}) collective-permute-start(f32[32,128]{1,0:T(8,128)S(1)} %get-tuple-element.126), channel_id=1, source_target_pairs={{0,16},{1,17},{2,18},{3,19},{4,20},{5,21},{6,22},{7,23},{8,24},{9,... | collective-permute-start | bytes 49160 | tf_op jit(solution)/shard_map/ppermute | solution.py:913
  54.1 6.5 %collective-permute-start.24 = (f32[144,128]{1,0:T(8,128)S(1)}, f32[144,128]{1,0:T(8,128)S(1)}, u32[]{:S(2)}, u32[]{:S(2)}) collective-permute-start(f32[144,128]{1,0:T(8,128)S(1)} %get-tuple-element.122), channel_id=1, source_target_pairs={{2,4},{6,8},{10,12},{14,16},{18,20},{22,24},{26,28},{30,0},{4,2},{... | collective-permute-start | bytes 221192 | tf_op jit(solution)/shard_map/ppermute | solution.py:880
  54.2 6.5 %collective-permute-start.25 = (f32[144,128]{1,0:T(8,128)S(1)}, f32[144,128]{1,0:T(8,128)S(1)}, u32[]{:S(2)}, u32[]{:S(2)}) collective-permute-start(f32[144,128]{1,0:T(8,128)S(1)} %get-tuple-element.123), channel_id=1, source_target_pairs={{0,2},{2,0},{4,6},{6,4},{8,10},{10,8},{12,14},{14,12},{16,18},{18,... | collective-permute-start | bytes 221192 | tf_op jit(solution)/shard_map/ppermute | solution.py:881
  54.8 10.1 %collective-permute-start.26 = (f32[2,80,128]{2,1,0:T(8,128)S(1)}, f32[2,80,128]{2,1,0:T(8,128)S(1)}, u32[]{:S(2)}, u32[]{:S(2)}) collective-permute-start(f32[2,80,128]{2,1,0:T(8,128)S(1)} %get-tuple-element.124), channel_id=1, source_target_pairs={{0,1},{1,0},{2,3},{3,2},{4,5},{5,4},{6,7},{7,6},{8,9},{9,8},{10,11... | collective-permute-start | bytes 245768 | tf_op jit(solution)/shard_map/ppermute | solution.py:888
  60.7 4.3 %collective-permute-start.28 = (f32[2,48,128]{2,1,0:T(8,128)S(1)}, f32[2,48,128]{2,1,0:T(8,128)S(1)}, u32[]{:S(2)}, u32[]{:S(2)}) collective-permute-start(f32[2,48,128]{2,1,0:T(8,128)S(1)} %get-tuple-element.127), channel_id=1, source_target_pairs={{0,1},{1,0},{2,3},{3,2},{4,5},{5,4},{6,7},{7,6},{8,9},{9,8},{10,11... | collective-permute-start | bytes 147464 | tf_op jit(solution)/shard_map/ppermute | solution.py:888
  61.3 3.6 %collective-permute-start.29 = (f32[1,128]{1,0:T(1,128)S(1)}, f32[1,128]{1,0:T(1,128)S(1)}, u32[]{:S(2)}, u32[]{:S(2)}) collective-permute-start(f32[1,128]{1,0:T(1,128)S(1)} %get-tuple-element.128), channel_id=1, source_target_pairs={{0,1},{1,0},{2,3},{3,2},{4,5},{5,4},{6,7},{7,6},{8,9},{9,8},{10,11... | collective-permute-start | bytes 1544 | tf_op jit(solution)/shard_map/ppermute | solution.py:913
  65.6 6.5 %collective-permute-start.30 = (f32[128,128]{1,0:T(8,128)S(1)}, f32[128,128]{1,0:T(8,128)S(1)}, u32[]{:S(2)}, u32[]{:S(2)}) collective-permute-start(f32[128,128]{1,0:T(8,128)S(1)} %get-tuple-element.135), channel_id=1, source_target_pairs={{2,4},{6,8},{10,12},{14,16},{18,20},{22,24},{26,28},{30,0},{4,2},{... | collective-permute-start | bytes 196616 | tf_op jit(solution)/shard_map/ppermute | solution.py:880
  65.7 6.4 %collective-permute-start.31 = (f32[128,128]{1,0:T(8,128)S(1)}, f32[128,128]{1,0:T(8,128)S(1)}, u32[]{:S(2)}, u32[]{:S(2)}) collective-permute-start(f32[128,128]{1,0:T(8,128)S(1)} %get-tuple-element.136), channel_id=1, source_target_pairs={{0,2},{2,0},{4,6},{6,4},{8,10},{10,8},{12,14},{14,12},{16,18},{18,... | collective-permute-start | bytes 196616 | tf_op jit(solution)/shard_map/ppermute | solution.py:881
  66.3 7.2 %collective-permute-start.32 = (f32[2,96,128]{2,1,0:T(8,128)S(1)}, f32[2,96,128]{2,1,0:T(8,128)S(1)}, u32[]{:S(2)}, u32[]{:S(2)}) collective-permute-start(f32[2,96,128]{2,1,0:T(8,128)S(1)} %get-tuple-element.137), channel_id=1, source_target_pairs={{0,1},{1,0},{2,3},{3,2},{4,5},{5,4},{6,7},{7,6},{8,9},{9,8},{10,11... | collective-permute-start | bytes 294920 | tf_op jit(solution)/shard_map/ppermute | solution.py:888
  72.1 4.2 %collective-permute-start.33 = (f32[2,48,128]{2,1,0:T(8,128)S(1)}, f32[2,48,128]{2,1,0:T(8,128)S(1)}, u32[]{:S(2)}, u32[]{:S(2)}) collective-permute-start(f32[2,48,128]{2,1,0:T(8,128)S(1)} %get-tuple-element.145), channel_id=1, source_target_pairs={{0,1},{1,0},{2,3},{3,2},{4,5},{5,4},{6,7},{7,6},{8,9},{9,8},{10,11... | collective-permute-start | bytes 147464 | tf_op jit(solution)/shard_map/ppermute | solution.py:888
  77.5 6.5 %collective-permute-start.34 = (f32[144,128]{1,0:T(8,128)S(1)}, f32[144,128]{1,0:T(8,128)S(1)}, u32[]{:S(2)}, u32[]{:S(2)}) collective-permute-start(f32[144,128]{1,0:T(8,128)S(1)} %get-tuple-element.150), channel_id=1, source_target_pairs={{2,4},{6,8},{10,12},{14,16},{18,20},{22,24},{26,28},{30,0},{4,2},{... | collective-permute-start | bytes 221192 | tf_op jit(solution)/shard_map/ppermute | solution.py:880
  77.6 6.5 %collective-permute-start.35 = (f32[144,128]{1,0:T(8,128)S(1)}, f32[144,128]{1,0:T(8,128)S(1)}, u32[]{:S(2)}, u32[]{:S(2)}) collective-permute-start(f32[144,128]{1,0:T(8,128)S(1)} %get-tuple-element.151), channel_id=1, source_target_pairs={{0,2},{2,0},{4,6},{6,4},{8,10},{10,8},{12,14},{14,12},{16,18},{18,... | collective-permute-start | bytes 221192 | tf_op jit(solution)/shard_map/ppermute | solution.py:881
  84.1 10.3 %collective-permute-start.36 = (f32[2,128,128]{2,1,0:T(8,128)S(1)}, f32[2,128,128]{2,1,0:T(8,128)S(1)}, u32[]{:S(2)}, u32[]{:S(2)}) collective-permute-start(f32[2,128,128]{2,1,0:T(8,128)S(1)} %get-tuple-element.159), channel_id=1, source_target_pairs={{0,1},{1,0},{2,3},{3,2},{4,5},{5,4},{6,7},{7,6},{8,9},{9,8},{10,11... | collective-permute-start | bytes 393224 | tf_op jit(solution)/shard_map/ppermute | solution.py:888
  (14 other events, 63.9 us)
